TPU v7x, 32 devices: a whole 2x2x4 slice. The times are simulated.
32 devices in a mesh: energy: 4 (over y, x), domain: 8 (over z, core).
Axes of the slice: x: 2, y: 2, z: 4, core: 2. Of those that a mesh axis runs over, the one named last changes fastest.
Arguments:
- retarded: bfloat16 [4, 16, 256, 512], P('energy', 'domain'), may hold values from -1 to 2
- coupling: bfloat16 [16, 256, 512], P('domain'), may hold values from -1 to 2
- sigma_lesser: bfloat16 [4, 16, 256, 512], P('energy', 'domain'), may hold values from -4 to 4
- sigma_greater: bfloat16 [4, 16, 256, 512], P('energy', 'domain'), may hold values from -4 to 4
- tiles: int32 [16, 2], P('domain'), may hold values from 0 to 3, all different within a row
- offsets: int32 [4], replicated, may hold values from -2 to 2, as said below
Outputs:
- polarization: bfloat16 [4, 16, 2, 128, 256], P('energy', 'domain')
Inputs may be any that keep to these rules, and one draw needn't show every extreme that they name: Each row names 2 different tiles. `offsets`: both ends of the range occur in every draw.
All inputs are finite; a program needn't handle non-finite values.
Results may differ from a plain program's by a relative error of at most 0.039.
Values may be sent and summed in bfloat16 or wider, within the bound.
No kernel may reach another device: no remote copies, remote signals or barrier semaphores. Data moves between devices by JAX's collectives and lax.ppermute only.
A program may use at most 64 MiB of HBM per device.

v0:
```python
import functools
import math

import jax
import jax.numpy as jnp
from jax import lax
from jax.experimental import pallas as pl
from jax.experimental.pallas import tpu as pltpu
from jax.sharding import PartitionSpec as P


VMEM_LIMIT = 16 << 20
F32 = jnp.float32
BF16 = jnp.bfloat16
VMEM = pl.BlockSpec(memory_space=pltpu.VMEM)
SMEM = pl.BlockSpec(memory_space=pltpu.SMEM)
HBM = pl.BlockSpec(memory_space=pltpu.HBM)


def stacked(block):
    order = block.shape[-1] // 2
    real, imag = block[:, :order], block[:, order:]
    return jnp.concatenate([block, jnp.concatenate([-imag, real], axis=1)], axis=0)


def times(factor, second_stacked):
    return lax.dot_general(
        factor, second_stacked, (((1,), (0,)), ((), ())), preferred_element_type=F32
    )


def times_adjoint(factor, second_stacked):
    return lax.dot_general(
        factor, second_stacked, (((1,), (1,)), ((), ())), preferred_element_type=F32
    )


def product(factor, second):
    return times(factor, stacked(second)).astype(BF16)


def injected(retarded, sigma):
    return times_adjoint(product(retarded, sigma), stacked(retarded)).astype(BF16)


def advance(state, step, source):
    return (times_adjoint(product(step, state), stacked(step)) + source.astype(F32)).astype(
        BF16
    )


def kernel_call(body, outs, operands, flops, in_specs=None, scratch=(), out_specs=None):
    moved = sum(x.size * x.dtype.itemsize for x in operands)
    moved += sum(math.prod(o.shape) * o.dtype.itemsize for o in outs)
    return pl.pallas_call(
        body,
        out_shape=outs,
        in_specs=in_specs or [VMEM] * len(operands),
        out_specs=out_specs or [VMEM] * len(outs),
        scratch_shapes=list(scratch),
        compiler_params=pltpu.CompilerParams(vmem_limit_bytes=VMEM_LIMIT),
        cost_estimate=pl.CostEstimate(
            flops=int(flops), bytes_accessed=moved, transcendentals=0
        ),
    )(*operands)


def first_kernel(
    blocks,
    place,
    tiles,
    offsets,
    retarded,
    coupling,
    lesser,
    greater,
    held_retarded,
    held_coupling,
    held_greater,
    later_steps,
    sources,
    total,
    scalars,
    held_lesser,
    held_tiles,
    held_offsets,
    sem,
):
    copies = {}
    for k in range(blocks):
        copies["r", k] = (retarded.at[0, k], held_retarded.at[k])
        copies["l", k] = (lesser.at[0, k], held_lesser.at[k])
        if k > 0:
            copies["c", k] = (coupling.at[k], held_coupling.at[k])
    copies["c", 0] = (coupling.at[0], held_coupling.at[0])
    for k in range(blocks):
        copies["g", k] = (greater.at[0, k], held_greater.at[k])
    copies["t", 0] = (tiles, held_tiles)
    copies["o", 0] = (offsets, held_offsets)
    for index, key in enumerate(copies):
        copies[key] = pltpu.make_async_copy(*copies[key], sem.at[index])
        copies[key].start()
    state = None
    for k in range(blocks):
        copies["r", k].wait()
        copies["l", k].wait()
        source = injected(held_retarded[k], held_lesser[k])
        sources[k] = source
        if k > 0:
            copies["c", k].wait()
            step = product(held_retarded[k], held_coupling[k])
            later_steps[k - 1] = step
        state = source if k == 0 else advance(state, step, source)
    total[...] = state
    copies["c", 0].wait()
    for k in range(blocks):
        copies["g", k].wait()
    copies["t", 0].wait()
    copies["o", 0].wait()
    chosen = held_tiles.shape[1]
    values = [place[i] for i in range(place.shape[0])]
    values += [held_tiles[k, j] for k in range(blocks) for j in range(chosen)]
    values += [held_offsets[i] for i in range(held_offsets.shape[0])]
    for i, value in enumerate(values):
        scalars[i] = value


def second_kernel(
    blocks, retarded, coupling, greater, later_steps, first_step, sources, totals
):
    state = chain = None
    for k in range(blocks):
        source = injected(retarded[k], greater[k])
        sources[k] = source
        if k == 0:
            chain = product(retarded[0], coupling[0])
            first_step[...] = chain
            state = source
        else:
            step = later_steps[k - 1]
            chain = product(step, chain)
            state = advance(state, step, source)
    totals[0] = state
    totals[1] = chain


def join_lesser_kernel(lower, totals, upper, out):
    out[...] = advance(lower[...], totals[1], upper[...])


def join_greater_kernel(lower, upper, out, whole):
    out[...] = advance(lower[0], upper[1], upper[0])
    whole[...] = product(upper[1], lower[1])


def keep(z, scalars, state, kept, out):
    @pl.when(scalars[1] == z)
    def _():
        out[...] = state[...]

    @pl.when(scalars[1] != z)
    def _():
        out[...] = jnp.zeros_like(out) if kept is None else kept[...]


def advance_kernel(z, scalars, state, step, source, *refs):
    kept, (out, chosen) = (refs[0] if len(refs) == 3 else None), refs[-2:]
    out[...] = advance(state[...], step[...], source[...])
    keep(z, scalars, state, kept, chosen)


def keep_kernel(z, scalars, state, *refs):
    keep(z, scalars, state, refs[0] if len(refs) == 2 else None, refs[-1])


def piece_of(scalars, k, chosen, half, rows):
    first = (scalars[2] ^ k) * rows
    block = first // (chosen * half)
    tile = scalars[3 + first // half]
    return block, tile, first % half


def prepare_kernel(
    blocks,
    energies,
    chosen,
    scalars,
    first_step,
    later_steps,
    lesser_sources,
    greater_sources,
    lower_lesser,
    lower_totals,
    lefts,
    rights,
    lesser_parts,
    greater_parts,
    chains,
    lessers,
    greaters,
):
    order = first_step.shape[0]
    half = order // 2
    rows = blocks * chosen * half // energies

    @pl.when(scalars[0] == 0)
    def _():
        chains[0] = first_step[...]
        lessers[0] = lesser_sources[0]
        greaters[0] = greater_sources[0]

    @pl.when(scalars[0] == 1)
    def _():
        chains[0] = product(first_step[...], lower_totals[1])
        lessers[0] = advance(lower_lesser[...], first_step[...], lesser_sources[0])
        greaters[0] = advance(lower_totals[0], first_step[...], greater_sources[0])

    for k in range(1, blocks):
        step = later_steps[k - 1]
        chains[k] = product(step, chains[k - 1])
        lessers[k] = advance(lessers[k - 1], step, lesser_sources[k])
        greaters[k] = advance(greaters[k - 1], step, greater_sources[k])
    for k in range(energies):
        block, tile, start = piece_of(scalars, k, chosen, half, rows)
        row = pl.multiple_of((tile // 2) * half + start, 16)
        column = pl.multiple_of((tile % 2) * half, half)
        mine = slice(k * rows, (k + 1) * rows)
        lefts[mine] = chains[block, pl.ds(row, rows), :]
        rights[k] = stacked(chains[block, pl.ds(column, half), :])
        for whole, parts in ((lessers, lesser_parts), (greaters, greater_parts)):
            for part in range(2):
                at = pl.ds(pl.multiple_of(column + part * order, half), half)
                parts[mine, part * half : (part + 1) * half] = whole[
                    block, pl.ds(row, rows), at
                ]


def finish_kernel(energies, scalars, arrived, near, lefts, rights, parts, *refs):
    pieces, doubled = refs[:energies], refs[energies]
    rows = parts.shape[0] // energies

    @pl.when(scalars[0] == 1)
    def _():
        doubled[...] = stacked(arrived[...])

    @pl.when(scalars[0] == 0)
    def _():
        doubled[...] = stacked(near[...])

    moved = times(lefts[...], doubled[...]).astype(BF16)
    for k in range(energies):
        mine = slice(k * rows, (k + 1) * rows)
        pieces[k][...] = (
            times_adjoint(moved[mine], rights[k]) + parts[mine].astype(F32)
        ).astype(BF16)


def convolve_kernel(energies, at_offsets, scalars, *refs):
    less, great = refs[:energies], refs[energies : 2 * energies]
    outs = refs[2 * energies : 3 * energies]
    held_less, held_great = refs[3 * energies :]
    group = scalars[2]
    rows, width = less[0].shape
    half = width // 2
    for k in range(energies):
        held_less[group ^ k] = less[k][...].astype(F32)
        held_great[energies + (group ^ k)] = great[k][...].astype(F32)
        held_great[k] = jnp.zeros((rows, width), F32)
        held_great[2 * energies + k] = jnp.zeros((rows, width), F32)
    chunk = 16
    for start in range(0, rows, chunk):
        at = slice(start, start + chunk)
        for k in range(energies):
            shift = energies - scalars[at_offsets + (group ^ k)]
            real = jnp.zeros((chunk, half), F32)
            imag = jnp.zeros((chunk, half), F32)
            for e in range(energies):
                other = held_great.at[shift + e]
                lr, li = held_less[e, at, :half], held_less[e, at, half:]
                gr, gi = other[at, :half], other[at, half:]
                real = real + (lr * gr - li * gi)
                imag = imag + (lr * gi + li * gr)
            outs[k][at, :half] = (real / energies).astype(BF16)
            outs[k][at, half:] = (imag / energies).astype(BF16)


def gather_kernel(energies, scalars, *refs):
    shares, (out, sem) = refs[:energies], refs[energies:]
    copies = [
        pltpu.make_async_copy(shares[k], out.at[scalars[2] ^ k], sem.at[k])
        for k in range(energies)
    ]
    for copy in copies:
        copy.start()
    for copy in copies:
        copy.wait()


def shards(retarded, coupling, sigma_lesser, sigma_greater, tiles, offsets):
    blocks, order = retarded.shape[1], retarded.shape[2]
    half = order // 2
    chosen = tiles.shape[1]
    domains, energies = lax.axis_size("domain"), lax.axis_size("energy")
    chips = domains // 2
    rows = blocks * chosen * half // energies
    unit = 8 * order**3
    block = jax.ShapeDtypeStruct((order, 2 * order), BF16)
    piece = jax.ShapeDtypeStruct((rows, order), BF16)

    def series(count):
        return jax.ShapeDtypeStruct((count, order, 2 * order), BF16)

    domain = lax.axis_index("domain")
    place = jnp.stack([domain & 1, domain >> 1, lax.axis_index("energy")])
    at_offsets = place.size + tiles.size

    def swap(x):
        return lax.ppermute(x, "domain", [(d, d ^ 1) for d in range(domains)])

    def hop(x, z):
        last = 2 * z - 1
        ring = [last, last + 2, last + 1, last - 1]
        route = dict(zip(ring, ring[1:] + ring[:1]))
        return lax.ppermute(
            x, "domain", [(d, route.get(d, d ^ 1)) for d in range(domains)]
        )

    def across(x, k):
        return lax.ppermute(x, "energy", [(e, e ^ k) for e in range(energies)])

    inputs = (tiles, offsets, retarded, coupling, sigma_lesser, sigma_greater)
    (
        held_retarded,
        held_coupling,
        held_greater,
        later_steps,
        less_sources,
        less_total,
        scalars,
    ) = kernel_call(
        functools.partial(first_kernel, blocks),
        [series(blocks)] * 3
        + [series(blocks - 1), series(blocks), block]
        + [jax.ShapeDtypeStruct((at_offsets + offsets.size,), jnp.int32)],
        (place,)
        + tuple(pltpu.with_memory_space_constraint(x, pltpu.HBM) for x in inputs),
        (5 * blocks - 3) * unit,
        in_specs=[SMEM] + [HBM] * len(inputs),
        out_specs=[VMEM] * 6 + [SMEM],
        scratch=[
            pltpu.VMEM((blocks, order, 2 * order), BF16),
            pltpu.SMEM(tiles.shape, jnp.int32),
            pltpu.SMEM(offsets.shape, jnp.int32),
            pltpu.SemaphoreType.DMA((4 * blocks + 2,)),
        ],
    )
    lower_less = swap(less_total)
    first_step, great_sources, totals = kernel_call(
        functools.partial(second_kernel, blocks),
        [block, series(blocks), series(2)],
        (held_retarded, held_coupling, held_greater, later_steps),
        (5 * blocks - 2) * unit,
    )
    lower_totals = swap(totals)
    (chip_less,) = kernel_call(
        join_lesser_kernel, [block], (lower_less, totals, less_total), 2 * unit
    )
    chip_great, chip_whole = kernel_call(
        join_greater_kernel, [block] * 2, (lower_totals, totals), 3 * unit
    )
    lefts, rights, less_parts, great_parts = kernel_call(
        functools.partial(prepare_kernel, blocks, energies, chosen),
        [
            jax.ShapeDtypeStruct((energies * rows, 2 * order), BF16),
            jax.ShapeDtypeStruct((energies, order, 2 * order), BF16),
            jax.ShapeDtypeStruct((energies * rows, order), BF16),
            jax.ShapeDtypeStruct((energies * rows, order), BF16),
        ],
        (
            scalars,
            first_step,
            later_steps,
            less_sources,
            great_sources,
            lower_less,
            lower_totals,
        ),
        5 * blocks * unit,
        in_specs=[SMEM] + [VMEM] * 6,
        scratch=[pltpu.VMEM((blocks, order, 2 * order), BF16)] * 3,
    )

    def step_on(z, state, kept, source):
        return kernel_call(
            functools.partial(advance_kernel, z),
            [block, block],
            (scalars, state, chip_whole, source, *kept),
            2 * unit,
            in_specs=[SMEM] + [VMEM] * (3 + len(kept)),
        )

    def keep_last(state, kept):
        return kernel_call(
            functools.partial(keep_kernel, chips - 1),
            [block],
            (scalars, state, *kept),
            0,
            in_specs=[SMEM] + [VMEM] * (1 + len(kept)),
        )

    def finish(arrived, parts):
        near = swap(arrived)
        pieces = kernel_call(
            functools.partial(finish_kernel, energies),
            [piece] * energies,
            (scalars, arrived, near, lefts, rights, parts),
            3 * unit,
            in_specs=[SMEM] + [VMEM] * 5,
            scratch=[pltpu.VMEM((2 * order, 2 * order), BF16)],
        )
        return [pieces[0]] + [across(pieces[k], k) for k in range(1, energies)]

    less, great = chip_less, chip_great
    less_in, great_in = (), ()
    for z in range(1, chips):
        less, great = hop(less, z), hop(great, z)
        if z < chips - 1:
            less, *less_in = step_on(z, less, less_in, chip_less)
            great, *great_in = step_on(z, great, great_in, chip_great)
        else:
            less_in = keep_last(less, less_in)
            great_in = keep_last(great, great_in)
    less_pieces = finish(less_in[0], less_parts)
    great_pieces = finish(great_in[0], great_parts)
    shares = kernel_call(
        functools.partial(convolve_kernel, energies, at_offsets),
        [piece] * energies,
        (scalars, *less_pieces, *great_pieces),
        8 * energies * energies * rows * half,
        in_specs=[SMEM] + [VMEM] * (2 * energies),
        scratch=[
            pltpu.VMEM((energies, rows, order), F32),
            pltpu.VMEM((3 * energies, rows, order), F32),
        ],
    )
    shares = [shares[0]] + [across(shares[k], k) for k in range(1, energies)]
    (result,) = kernel_call(
        functools.partial(gather_kernel, energies),
        [jax.ShapeDtypeStruct((energies, rows, order), BF16)],
        (scalars, *shares),
        0,
        in_specs=[SMEM] + [VMEM] * energies,
        out_specs=[HBM],
        scratch=[pltpu.SemaphoreType.DMA((energies,))],
    )
    return result.reshape(1, blocks, chosen, half, order)


def solution(mesh):
    placed = (
        P("energy", "domain", None, None),
        P("domain", None, None),
        P("energy", "domain", None, None),
        P("energy", "domain", None, None),
        P("domain", None),
        P(),
    )

    return jax.shard_map(
        shards,
        mesh=mesh,
        in_specs=placed,
        out_specs=P("energy", "domain", None, None, None),
        check_vma=False,
    )
```

profile of v0, /device:TPU:16, one launch (start us, length us, event | category | flops | bytes accessed | tf_op | source)
XLA Modules:
  0.0 54.1 jit_solution(1376400015504318145)
XLA Ops:
  0.0 0.1 pad_add_fusion.place
  0.1 4.0 %shard_map.64 = (bf16[2,256,512]{2,1,0:T(8,128)(2,1)S(1)}, bf16[2,256,512]{2,1,0:T(8,128)(2,1)S(1)}, bf16[2,256,512]{2,1,0:T(8,128)(2,1)S(1)}, bf16[1,256,512]{2...) custom-call(s32[3]{0:T(128)S(1)} %pad_add_fusion.place, ...), custom_call_target="tpu_custom_call" | custom-call | flops 939524096 | bytes 4718680 | tf_op jit(solution)/shard_map/pallas_call | solution.py:55
  4.1 1.5 %shard_map.65 = (bf16[256,512]{1,0:T(8,128)(2,1)S(1)}, bf16[2,256,512]{2,1,0:T(8,128)(2,1)S(1)}, bf16[2,256,512]{2,1,0:T(8,128)(2,1)S(1)}) custom-call(bf16[2,256,512]{2,1,0:T(8,128)(2,1)S(1)} %get-tuple-element.43.retarded, bf16[2,256,512]{2,1,0:T(8,128)(2,1)S(1)} %get-tuple-element.44.coupling, bf16[2,256,512]{2,1,0:T(8,128)(2,1)S(1)} %get-tuple-element.45.greater, ...), custom_call_target="tpu_custom_call" | custom-call | flops 1073741824 | bytes 3145728 | tf_op jit(solution)/shard_map/pallas_call | solution.py:55
  5.6 0.1 collective-permute-start.2
  5.7 0.5 collective-permute-start
  6.2 1.8 %collective-permute-done.lower.lower_lesser = bf16[256,512]{1,0:T(8,128)(2,1)S(1)} collective-permute-done((bf16[256,512]{1,0:T(8,128)(2,1)S(1)}, bf16[256,512]{1,0:T(8,128)(2,1)S(1)}, u32[]{:S(2)}, u32[]{:S(2)}) %collective-permute-start) | collective-permute-done | bytes 262176 | tf_op jit(solution)/shard_map/ppermute | solution.py:318
  8.0 0.5 shard_map.66.source
  8.5 0.2 collective-permute-start.1
  8.7 0.0 collective-permute-done.2.lower.lower_totals
  8.7 0.6 %shard_map.67 = (bf16[256,512]{1,0:T(8,128)(2,1)S(1)}, bf16[256,512]{1,0:T(8,128)(2,1)S(1)}) custom-call(bf16[2,256,512]{2,1,0:T(8,128)(2,1)S(1)} %collective-permute-done.2.lower.lower_totals, bf16[2,256,512]{2,1,0:T(8,128)(2,1)S(1)} %get-tuple-element.47.totals.upper), custom_call_target="tpu_custom_call" | custom-call | flops 402653184 | bytes 1572864 | tf_op jit(solution)/shard_map/pallas_call | solution.py:55
  9.4 0.4 collective-permute-start.9
  9.8 0.3 collective-permute-done.1.state
  10.1 1.1 %shard_map.68 = (bf16[256,512]{1,0:T(8,128)(2,1)S(1)}, bf16[256,512]{1,0:T(8,128)(2,1)S(1)}) custom-call(s32[11]{0:T(128)S(1)} %get-tuple-element.41.scalars, bf16[256,512]{1,0:T(8,128)(2,1)S(1)} %collective-permute-done.1.state, bf16[256,512]{1,0:T(8,128)(2,1)S(1)} %get-tuple-element.48.step, bf16[256,512]{1,0:T(8,128)(2,1)S(1)} %shard_map.66.source), custom_call_target="tpu_custom_call" | custom-call | flops 268435456 | bytes 1310764 | tf_op jit(solution)/shard_map/pallas_call | solution.py:55
  11.2 2.9 %collective-permute-start.3 = (bf16[256,512]{1,0:T(8,128)(2,1)S(1)}, bf16[256,512]{1,0:T(8,128)(2,1)S(1)}, u32[]{:S(2)}, u32[]{:S(2)}) collective-permute-start(bf16[256,512]{1,0:T(8,128)(2,1)S(1)} %get-tuple-element.49), channel_id=1, source_target_pairs={{0,1},{1,0},{2,3},{3,5},{4,2},{5,4},{6,7},{7,6},{8,9},{9,8},{10,11... | collective-permute-start | bytes 786440 | tf_op jit(solution)/shard_map/ppermute | solution.py:324
  14.1 0.0 collective-permute-done.9.state
  14.1 1.1 %shard_map.73 = (bf16[256,512]{1,0:T(8,128)(2,1)S(1)}, bf16[256,512]{1,0:T(8,128)(2,1)S(1)}) custom-call(s32[11]{0:T(128)S(1)} %get-tuple-element.41.scalars, bf16[256,512]{1,0:T(8,128)(2,1)S(1)} %collective-permute-done.9.state, bf16[256,512]{1,0:T(8,128)(2,1)S(1)} %get-tuple-element.48.step, bf16[256,512]{1,0:T(8,128)(2,1)S(1)} %get-tuple-element.63.source), custom_call_target="tpu_custom_call" | custom-call | flops 268435456 | bytes 1310764 | tf_op jit(solution)/shard_map/pallas_call | solution.py:55
  15.2 1.7 %collective-permute-start.10 = (bf16[256,512]{1,0:T(8,128)(2,1)S(1)}, bf16[256,512]{1,0:T(8,128)(2,1)S(1)}, u32[]{:S(2)}, u32[]{:S(2)}) collective-permute-start(bf16[256,512]{1,0:T(8,128)(2,1)S(1)} %get-tuple-element.64), channel_id=1, source_target_pairs={{0,1},{1,0},{2,3},{3,5},{4,2},{5,4},{6,7},{7,6},{8,9},{9,8},{10,11... | collective-permute-start | bytes 786440 | tf_op jit(solution)/shard_map/ppermute | solution.py:324
  16.9 1.1 %collective-permute-done.3.state = bf16[256,512]{1,0:T(8,128)(2,1)S(1)} collective-permute-done((bf16[256,512]{1,0:T(8,128)(2,1)S(1)}, bf16[256,512]{1,0:T(8,128)(2,1)S(1)}, u32[]{:S(2)}, u32[]{:S(2)}) %collective-permute-start.3) | collective-permute-done | bytes 262176 | tf_op jit(solution)/shard_map/ppermute | solution.py:324
  18.0 1.1 %shard_map.69 = (bf16[256,512]{1,0:T(8,128)(2,1)S(1)}, bf16[256,512]{1,0:T(8,128)(2,1)S(1)}) custom-call(s32[11]{0:T(128)S(1)} %get-tuple-element.41.scalars, bf16[256,512]{1,0:T(8,128)(2,1)S(1)} %collective-permute-done.3.state, bf16[256,512]{1,0:T(8,128)(2,1)S(1)} %get-tuple-element.48.step, bf16[256,512]{1,0:T(8,128)(2,1)S(1)} %shard_map.66.source, ...), custom_call_target="tpu_custom_call" | custom-call | flops 268435456 | bytes 1572908 | tf_op jit(solution)/shard_map/pallas_call | solution.py:55
  19.1 1.1 %collective-permute-start.4 = (bf16[256,512]{1,0:T(8,128)(2,1)S(1)}, bf16[256,512]{1,0:T(8,128)(2,1)S(1)}, u32[]{:S(2)}, u32[]{:S(2)}) collective-permute-start(bf16[256,512]{1,0:T(8,128)(2,1)S(1)} %get-tuple-element.51), channel_id=1, source_target_pairs={{0,1},{1,0},{2,3},{3,2},{4,5},{5,7},{6,4},{7,6},{8,9},{9,8},{10,11... | collective-permute-start | bytes 786440 | tf_op jit(solution)/shard_map/ppermute | solution.py:324
  20.2 0.6 %collective-permute-done.10.state = bf16[256,512]{1,0:T(8,128)(2,1)S(1)} collective-permute-done((bf16[256,512]{1,0:T(8,128)(2,1)S(1)}, bf16[256,512]{1,0:T(8,128)(2,1)S(1)}, u32[]{:S(2)}, u32[]{:S(2)}) %collective-permute-start.10) | collective-permute-done | bytes 262176 | tf_op jit(solution)/shard_map/ppermute | solution.py:324
  20.8 1.1 %shard_map.74 = (bf16[256,512]{1,0:T(8,128)(2,1)S(1)}, bf16[256,512]{1,0:T(8,128)(2,1)S(1)}) custom-call(s32[11]{0:T(128)S(1)} %get-tuple-element.41.scalars, bf16[256,512]{1,0:T(8,128)(2,1)S(1)} %collective-permute-done.10.state, bf16[256,512]{1,0:T(8,128)(2,1)S(1)} %get-tuple-element.48.step, bf16[256,512]{1,0:T(8,128)(2,1)S(1)} %get-tuple-element.63.source, ...), custom_call_target="tpu_custom_call" | custom-call | flops 268435456 | bytes 1572908 | tf_op jit(solution)/shard_map/pallas_call | solution.py:55
  21.9 1.1 %collective-permute-start.11 = (bf16[256,512]{1,0:T(8,128)(2,1)S(1)}, bf16[256,512]{1,0:T(8,128)(2,1)S(1)}, u32[]{:S(2)}, u32[]{:S(2)}) collective-permute-start(bf16[256,512]{1,0:T(8,128)(2,1)S(1)} %get-tuple-element.66), channel_id=1, source_target_pairs={{0,1},{1,0},{2,3},{3,2},{4,5},{5,7},{6,4},{7,6},{8,9},{9,8},{10,11... | collective-permute-start | bytes 786440 | tf_op jit(solution)/shard_map/ppermute | solution.py:324
  23.0 2.5 %collective-permute-done.4.state = bf16[256,512]{1,0:T(8,128)(2,1)S(1)} collective-permute-done((bf16[256,512]{1,0:T(8,128)(2,1)S(1)}, bf16[256,512]{1,0:T(8,128)(2,1)S(1)}, u32[]{:S(2)}, u32[]{:S(2)}) %collective-permute-start.4) | collective-permute-done | bytes 262176 | tf_op jit(solution)/shard_map/ppermute | solution.py:324
  25.5 0.6 %shard_map.70.arrived = bf16[256,512]{1,0:T(8,128)(2,1)S(1)} custom-call(s32[11]{0:T(128)S(1)} %get-tuple-element.41.scalars, bf16[256,512]{1,0:T(8,128)(2,1)S(1)} %collective-permute-done.4.state, bf16[256,512]{1,0:T(8,128)(2,1)S(1)} %get-tuple-element.52.refs_0_), custom_call_target="tpu_custom_call" | custom-call | bytes 786476 | tf_op jit(solution)/shard_map/pallas_call | solution.py:55
  26.1 0.1 collective-permute-start.5
  26.2 2.2 %collective-permute-done.11.state = bf16[256,512]{1,0:T(8,128)(2,1)S(1)} collective-permute-done((bf16[256,512]{1,0:T(8,128)(2,1)S(1)}, bf16[256,512]{1,0:T(8,128)(2,1)S(1)}, u32[]{:S(2)}, u32[]{:S(2)}) %collective-permute-start.11) | collective-permute-done | bytes 262176 | tf_op jit(solution)/shard_map/ppermute | solution.py:324
  28.3 0.6 %shard_map.75.arrived = bf16[256,512]{1,0:T(8,128)(2,1)S(1)} custom-call(s32[11]{0:T(128)S(1)} %get-tuple-element.41.scalars, bf16[256,512]{1,0:T(8,128)(2,1)S(1)} %collective-permute-done.11.state, bf16[256,512]{1,0:T(8,128)(2,1)S(1)} %get-tuple-element.67.refs_0_), custom_call_target="tpu_custom_call" | custom-call | bytes 786476 | tf_op jit(solution)/shard_map/pallas_call | solution.py:55
  28.9 0.1 collective-permute-start.12
  29.0 1.7 %shard_map.71 = (bf16[512,512]{1,0:T(8,128)(2,1)S(1)}, bf16[4,256,512]{2,1,0:T(8,128)(2,1)S(1)}, bf16[512,256]{1,0:T(8,128)(2,1)S(1)}, bf16[512,256]{1,0:T(8,128)(2,1)S(1)}) custom-call(s32[11]{0:T(128)S(1)} %get-tuple-element.41.scalars, bf16[256,512]{1,0:T(8,128)(2,1)S(1)} %get-tuple-element.53.first_step, ...), custom_call_target="tpu_custom_call" | custom-call | flops 1342177280 | bytes 4456492 | tf_op jit(solution)/shard_map/pallas_call | solution.py:55
  30.7 0.0 collective-permute-done.5.near
  30.7 1.3 %shard_map.72 = (bf16[128,256]{1,0:T(8,128)(2,1)S(1)}, bf16[128,256]{1,0:T(8,128)(2,1)S(1)}, bf16[128,256]{1,0:T(8,128)(2,1)S(1)}, bf16[128,256]{1,0:T(8,128)(2,1)S(1)}) custom-call(s32[11]{0:T(128)S(1)} %get-tuple-element.41.scalars, bf16[256,512]{1,0:T(8,128)(2,1)S(1)} %shard_map.70.arrived, bf16[256,512]{1,0:T(8,128)(2,1)S(1)} %collective-permute-done.5.near, ...), custom_call_target="tpu_custom_call" | custom-call | flops 402653184 | bytes 2621484 | tf_op jit(solution)/shard_map/pallas_call | solution.py:55
  32.0 2.0 %collective-permute-start.6 = (bf16[128,256]{1,0:T(8,128)(2,1)S(1)}, bf16[128,256]{1,0:T(8,128)(2,1)S(1)}, u32[]{:S(2)}, u32[]{:S(2)}) collective-permute-start(bf16[128,256]{1,0:T(8,128)(2,1)S(1)} %get-tuple-element.60), channel_id=1, source_target_pairs={{0,8},{8,0},{16,24},{24,16},{1,9},{9,1},{17,25},{25,17},{2,10},{10... | collective-permute-start | bytes 196616 | tf_op jit(solution)/shard_map/ppermute | solution.py:329
  34.0 1.5 %collective-permute-start.7 = (bf16[128,256]{1,0:T(8,128)(2,1)S(1)}, bf16[128,256]{1,0:T(8,128)(2,1)S(1)}, u32[]{:S(2)}, u32[]{:S(2)}) collective-permute-start(bf16[128,256]{1,0:T(8,128)(2,1)S(1)} %get-tuple-element.61), channel_id=1, source_target_pairs={{0,16},{8,24},{16,0},{24,8},{1,17},{9,25},{17,1},{25,9},{2,18},{10... | collective-permute-start | bytes 196616 | tf_op jit(solution)/shard_map/ppermute | solution.py:329
  35.5 0.0 collective-permute-start.8
  35.6 0.0 collective-permute-done.12.near
  35.6 1.3 %shard_map.76 = (bf16[128,256]{1,0:T(8,128)(2,1)S(1)}, bf16[128,256]{1,0:T(8,128)(2,1)S(1)}, bf16[128,256]{1,0:T(8,128)(2,1)S(1)}, bf16[128,256]{1,0:T(8,128)(2,1)S(1)}) custom-call(s32[11]{0:T(128)S(1)} %get-tuple-element.41.scalars, bf16[256,512]{1,0:T(8,128)(2,1)S(1)} %shard_map.75.arrived, bf16[256,512]{1,0:T(8,128)(2,1)S(1)} %collective-permute-done.12.near, ...), custom_call_target="tpu_custom_call" | custom-call | flops 402653184 | bytes 2621484 | tf_op jit(solution)/shard_map/pallas_call | solution.py:55
  36.9 2.0 %collective-permute-start.13 = (bf16[128,256]{1,0:T(8,128)(2,1)S(1)}, bf16[128,256]{1,0:T(8,128)(2,1)S(1)}, u32[]{:S(2)}, u32[]{:S(2)}) collective-permute-start(bf16[128,256]{1,0:T(8,128)(2,1)S(1)} %get-tuple-element.70), channel_id=1, source_target_pairs={{0,8},{8,0},{16,24},{24,16},{1,9},{9,1},{17,25},{25,17},{2,10},{10... | collective-permute-start | bytes 196616 | tf_op jit(solution)/shard_map/ppermute | solution.py:329
  38.9 1.5 %collective-permute-start.14 = (bf16[128,256]{1,0:T(8,128)(2,1)S(1)}, bf16[128,256]{1,0:T(8,128)(2,1)S(1)}, u32[]{:S(2)}, u32[]{:S(2)}) collective-permute-start(bf16[128,256]{1,0:T(8,128)(2,1)S(1)} %get-tuple-element.71), channel_id=1, source_target_pairs={{0,16},{8,24},{16,0},{24,8},{1,17},{9,25},{17,1},{25,9},{2,18},{10... | collective-permute-start | bytes 196616 | tf_op jit(solution)/shard_map/ppermute | solution.py:329
  40.4 0.0 collective-permute-done.6.refs_1_
  40.4 0.0 collective-permute-start.15
  40.4 0.0 collective-permute-done.7.refs_2_
  40.4 0.9 %collective-permute-done.8.refs_3_ = bf16[128,256]{1,0:T(8,128)(2,1)S(1)} collective-permute-done((bf16[128,256]{1,0:T(8,128)(2,1)S(1)}, bf16[128,256]{1,0:T(8,128)(2,1)S(1)}, u32[]{:S(2)}, u32[]{:S(2)}) %collective-permute-start.8) | collective-permute-done | bytes 65568 | tf_op jit(solution)/shard_map/ppermute | solution.py:329
  41.3 0.5 collective-permute-done.13.refs_5_
  41.8 1.4 %collective-permute-done.14.refs_6_ = bf16[128,256]{1,0:T(8,128)(2,1)S(1)} collective-permute-done((bf16[128,256]{1,0:T(8,128)(2,1)S(1)}, bf16[128,256]{1,0:T(8,128)(2,1)S(1)}, u32[]{:S(2)}, u32[]{:S(2)}) %collective-permute-start.14) | collective-permute-done | bytes 65568 | tf_op jit(solution)/shard_map/ppermute | solution.py:329
  43.2 2.4 %collective-permute-done.15.refs_7_ = bf16[128,256]{1,0:T(8,128)(2,1)S(1)} collective-permute-done((bf16[128,256]{1,0:T(8,128)(2,1)S(1)}, bf16[128,256]{1,0:T(8,128)(2,1)S(1)}, u32[]{:S(2)}, u32[]{:S(2)}) %collective-permute-start.15) | collective-permute-done | bytes 65568 | tf_op jit(solution)/shard_map/ppermute | solution.py:329
  45.6 1.0 %shard_map.77 = (bf16[128,256]{1,0:T(8,128)(2,1)S(1)}, bf16[128,256]{1,0:T(8,128)(2,1)S(1)}, bf16[128,256]{1,0:T(8,128)(2,1)S(1)}, bf16[128,256]{1,0:T(8,128)(2,1)S(1)}) custom-call(s32[11]{0:T(128)S(1)} %get-tuple-element.41.scalars, bf16[128,256]{1,0:T(8,128)(2,1)S(1)} %get-tuple-element.59.refs_0_, bf16[128,256]{1,0:T(8,128)(2,1)S(1)} %collective-permute-done.6.refs_1_, ...), custom_call_target="tpu_custom_call" | custom-call | flops 2097152 | bytes 786476 | tf_op jit(solution)/shard_map/pallas_call | solution.py:55
  46.5 0.6 %collective-permute-start.16 = (bf16[128,256]{1,0:T(8,128)(2,1)S(1)}, bf16[128,256]{1,0:T(8,128)(2,1)S(1)}, u32[]{:S(2)}, u32[]{:S(2)}) collective-permute-start(bf16[128,256]{1,0:T(8,128)(2,1)S(1)} %get-tuple-element.74), channel_id=1, source_target_pairs={{0,8},{8,0},{16,24},{24,16},{1,9},{9,1},{17,25},{25,17},{2,10},{10... | collective-permute-start | bytes 196616 | tf_op jit(solution)/shard_map/ppermute | solution.py:329
  47.1 0.6 %collective-permute-start.17 = (bf16[128,256]{1,0:T(8,128)(2,1)S(1)}, bf16[128,256]{1,0:T(8,128)(2,1)S(1)}, u32[]{:S(2)}, u32[]{:S(2)}) collective-permute-start(bf16[128,256]{1,0:T(8,128)(2,1)S(1)} %get-tuple-element.75), channel_id=1, source_target_pairs={{0,16},{8,24},{16,0},{24,8},{1,17},{9,25},{17,1},{25,9},{2,18},{10... | collective-permute-start | bytes 196616 | tf_op jit(solution)/shard_map/ppermute | solution.py:329
  47.7 2.4 %collective-permute-start.18 = (bf16[128,256]{1,0:T(8,128)(2,1)S(1)}, bf16[128,256]{1,0:T(8,128)(2,1)S(1)}, u32[]{:S(2)}, u32[]{:S(2)}) collective-permute-start(bf16[128,256]{1,0:T(8,128)(2,1)S(1)} %get-tuple-element.76), channel_id=1, source_target_pairs={{0,24},{8,16},{16,8},{24,0},{1,25},{9,17},{17,9},{25,1},{2,26},{10... | collective-permute-start | bytes 196616 | tf_op jit(solution)/shard_map/ppermute | solution.py:329
  50.1 0.8 %collective-permute-done.16.refs_1_ = bf16[128,256]{1,0:T(8,128)(2,1)S(1)} collective-permute-done((bf16[128,256]{1,0:T(8,128)(2,1)S(1)}, bf16[128,256]{1,0:T(8,128)(2,1)S(1)}, u32[]{:S(2)}, u32[]{:S(2)}) %collective-permute-start.16) | collective-permute-done | bytes 65568 | tf_op jit(solution)/shard_map/ppermute | solution.py:329
  50.9 0.6 %collective-permute-done.17.refs_2_ = bf16[128,256]{1,0:T(8,128)(2,1)S(1)} collective-permute-done((bf16[128,256]{1,0:T(8,128)(2,1)S(1)}, bf16[128,256]{1,0:T(8,128)(2,1)S(1)}, u32[]{:S(2)}, u32[]{:S(2)}) %collective-permute-start.17) | collective-permute-done | bytes 65568 | tf_op jit(solution)/shard_map/ppermute | solution.py:329
  51.6 1.3 %collective-permute-done.18.refs_3_ = bf16[128,256]{1,0:T(8,128)(2,1)S(1)} collective-permute-done((bf16[128,256]{1,0:T(8,128)(2,1)S(1)}, bf16[128,256]{1,0:T(8,128)(2,1)S(1)}, u32[]{:S(2)}, u32[]{:S(2)}) %collective-permute-start.18) | collective-permute-done | bytes 65568 | tf_op jit(solution)/shard_map/ppermute | solution.py:329
  52.9 1.3 %shard_map.78 = bf16[4,128,256]{2,1,0:T(8,128)(2,1)} custom-call(s32[11]{0:T(128)S(1)} %get-tuple-element.41.scalars, bf16[128,256]{1,0:T(8,128)(2,1)S(1)} %get-tuple-element.73.refs_0_, bf16[128,256]{1,0:T(8,128)(2,1)S(1)} %collective-permute-done.16.refs_1_, bf16[128,256]{1,0:T(8,128)(2,1)S(1)} %collective-permute-done.17.refs_2_, ...), custom_call_target="tpu_custom_call" | custom-call | bytes 524332 | tf_op jit(solution)/shard_map/pallas_call | solution.py:55
Async XLA Ops:
  5.6 3.1 %collective-permute-start.2 = (bf16[2,256,512]{2,1,0:T(8,128)(2,1)S(1)}, bf16[2,256,512]{2,1,0:T(8,128)(2,1)S(1)}, u32[]{:S(2)}, u32[]{:S(2)}) collective-permute-start(bf16[2,256,512]{2,1,0:T(8,128)(2,1)S(1)} %get-tuple-element.47.totals.upper), channel_id=1, source_target_pairs={{0,1},{1,0},{2,3},{3,2},{4,5},{5,4},{6,7},{7,6},{8,9},{9,8},{10,11... | collective-permute-start | bytes 1572872 | tf_op jit(solution)/shard_map/ppermute | solution.py:318
  5.7 2.3 %collective-permute-start = (bf16[256,512]{1,0:T(8,128)(2,1)S(1)}, bf16[256,512]{1,0:T(8,128)(2,1)S(1)}, u32[]{:S(2)}, u32[]{:S(2)}) collective-permute-start(bf16[256,512]{1,0:T(8,128)(2,1)S(1)} %get-tuple-element.42.upper), channel_id=1, source_target_pairs={{0,1},{1,0},{2,3},{3,2},{4,5},{5,4},{6,7},{7,6},{8,9},{9,8},{10,11... | collective-permute-start | bytes 786440 | tf_op jit(solution)/shard_map/ppermute | solution.py:318
  8.5 1.6 %collective-permute-start.1 = (bf16[256,512]{1,0:T(8,128)(2,1)S(1)}, bf16[256,512]{1,0:T(8,128)(2,1)S(1)}, u32[]{:S(2)}, u32[]{:S(2)}) collective-permute-start(bf16[256,512]{1,0:T(8,128)(2,1)S(1)} %shard_map.66.source), channel_id=1, source_target_pairs={{0,1},{1,3},{2,0},{3,2},{4,5},{5,4},{6,7},{7,6},{8,9},{9,11},{10,8... | collective-permute-start | bytes 786440 | tf_op jit(solution)/shard_map/ppermute | solution.py:324
  9.4 4.7 %collective-permute-start.9 = (bf16[256,512]{1,0:T(8,128)(2,1)S(1)}, bf16[256,512]{1,0:T(8,128)(2,1)S(1)}, u32[]{:S(2)}, u32[]{:S(2)}) collective-permute-start(bf16[256,512]{1,0:T(8,128)(2,1)S(1)} %get-tuple-element.63.source), channel_id=1, source_target_pairs={{0,1},{1,3},{2,0},{3,2},{4,5},{5,4},{6,7},{7,6},{8,9},{9,11},{10,8... | collective-permute-start | bytes 786440 | tf_op jit(solution)/shard_map/ppermute | solution.py:324
  11.2 6.8 %collective-permute-start.3 = (bf16[256,512]{1,0:T(8,128)(2,1)S(1)}, bf16[256,512]{1,0:T(8,128)(2,1)S(1)}, u32[]{:S(2)}, u32[]{:S(2)}) collective-permute-start(bf16[256,512]{1,0:T(8,128)(2,1)S(1)} %get-tuple-element.49), channel_id=1, source_target_pairs={{0,1},{1,0},{2,3},{3,5},{4,2},{5,4},{6,7},{7,6},{8,9},{9,8},{10,11... | collective-permute-start | bytes 786440 | tf_op jit(solution)/shard_map/ppermute | solution.py:324
  15.2 5.6 %collective-permute-start.10 = (bf16[256,512]{1,0:T(8,128)(2,1)S(1)}, bf16[256,512]{1,0:T(8,128)(2,1)S(1)}, u32[]{:S(2)}, u32[]{:S(2)}) collective-permute-start(bf16[256,512]{1,0:T(8,128)(2,1)S(1)} %get-tuple-element.64), channel_id=1, source_target_pairs={{0,1},{1,0},{2,3},{3,5},{4,2},{5,4},{6,7},{7,6},{8,9},{9,8},{10,11... | collective-permute-start | bytes 786440 | tf_op jit(solution)/shard_map/ppermute | solution.py:324
  19.1 6.5 %collective-permute-start.4 = (bf16[256,512]{1,0:T(8,128)(2,1)S(1)}, bf16[256,512]{1,0:T(8,128)(2,1)S(1)}, u32[]{:S(2)}, u32[]{:S(2)}) collective-permute-start(bf16[256,512]{1,0:T(8,128)(2,1)S(1)} %get-tuple-element.51), channel_id=1, source_target_pairs={{0,1},{1,0},{2,3},{3,2},{4,5},{5,7},{6,4},{7,6},{8,9},{9,8},{10,11... | collective-permute-start | bytes 786440 | tf_op jit(solution)/shard_map/ppermute | solution.py:324
  21.9 6.5 %collective-permute-start.11 = (bf16[256,512]{1,0:T(8,128)(2,1)S(1)}, bf16[256,512]{1,0:T(8,128)(2,1)S(1)}, u32[]{:S(2)}, u32[]{:S(2)}) collective-permute-start(bf16[256,512]{1,0:T(8,128)(2,1)S(1)} %get-tuple-element.66), channel_id=1, source_target_pairs={{0,1},{1,0},{2,3},{3,2},{4,5},{5,7},{6,4},{7,6},{8,9},{9,8},{10,11... | collective-permute-start | bytes 786440 | tf_op jit(solution)/shard_map/ppermute | solution.py:324
  26.1 4.6 %collective-permute-start.5 = (bf16[256,512]{1,0:T(8,128)(2,1)S(1)}, bf16[256,512]{1,0:T(8,128)(2,1)S(1)}, u32[]{:S(2)}, u32[]{:S(2)}) collective-permute-start(bf16[256,512]{1,0:T(8,128)(2,1)S(1)} %shard_map.70.arrived), channel_id=1, source_target_pairs={{0,1},{1,0},{2,3},{3,2},{4,5},{5,4},{6,7},{7,6},{8,9},{9,8},{10,11... | collective-permute-start | bytes 786440 | tf_op jit(solution)/shard_map/ppermute | solution.py:318
  28.9 6.7 %collective-permute-start.12 = (bf16[256,512]{1,0:T(8,128)(2,1)S(1)}, bf16[256,512]{1,0:T(8,128)(2,1)S(1)}, u32[]{:S(2)}, u32[]{:S(2)}) collective-permute-start(bf16[256,512]{1,0:T(8,128)(2,1)S(1)} %shard_map.75.arrived), channel_id=1, source_target_pairs={{0,1},{1,0},{2,3},{3,2},{4,5},{5,4},{6,7},{7,6},{8,9},{9,8},{10,11... | collective-permute-start | bytes 786440 | tf_op jit(solution)/shard_map/ppermute | solution.py:318
  32.0 8.4 %collective-permute-start.6 = (bf16[128,256]{1,0:T(8,128)(2,1)S(1)}, bf16[128,256]{1,0:T(8,128)(2,1)S(1)}, u32[]{:S(2)}, u32[]{:S(2)}) collective-permute-start(bf16[128,256]{1,0:T(8,128)(2,1)S(1)} %get-tuple-element.60), channel_id=1, source_target_pairs={{0,8},{8,0},{16,24},{24,16},{1,9},{9,1},{17,25},{25,17},{2,10},{10... | collective-permute-start | bytes 196616 | tf_op jit(solution)/shard_map/ppermute | solution.py:329
  34.0 6.4 %collective-permute-start.7 = (bf16[128,256]{1,0:T(8,128)(2,1)S(1)}, bf16[128,256]{1,0:T(8,128)(2,1)S(1)}, u32[]{:S(2)}, u32[]{:S(2)}) collective-permute-start(bf16[128,256]{1,0:T(8,128)(2,1)S(1)} %get-tuple-element.61), channel_id=1, source_target_pairs={{0,16},{8,24},{16,0},{24,8},{1,17},{9,25},{17,1},{25,9},{2,18},{10... | collective-permute-start | bytes 196616 | tf_op jit(solution)/shard_map/ppermute | solution.py:329
  35.5 5.8 %collective-permute-start.8 = (bf16[128,256]{1,0:T(8,128)(2,1)S(1)}, bf16[128,256]{1,0:T(8,128)(2,1)S(1)}, u32[]{:S(2)}, u32[]{:S(2)}) collective-permute-start(bf16[128,256]{1,0:T(8,128)(2,1)S(1)} %get-tuple-element.62), channel_id=1, source_target_pairs={{0,24},{8,16},{16,8},{24,0},{1,25},{9,17},{17,9},{25,1},{2,26},{10... | collective-permute-start | bytes 196616 | tf_op jit(solution)/shard_map/ppermute | solution.py:329
  36.9 4.9 %collective-permute-start.13 = (bf16[128,256]{1,0:T(8,128)(2,1)S(1)}, bf16[128,256]{1,0:T(8,128)(2,1)S(1)}, u32[]{:S(2)}, u32[]{:S(2)}) collective-permute-start(bf16[128,256]{1,0:T(8,128)(2,1)S(1)} %get-tuple-element.70), channel_id=1, source_target_pairs={{0,8},{8,0},{16,24},{24,16},{1,9},{9,1},{17,25},{25,17},{2,10},{10... | collective-permute-start | bytes 196616 | tf_op jit(solution)/shard_map/ppermute | solution.py:329
  38.9 4.3 %collective-permute-start.14 = (bf16[128,256]{1,0:T(8,128)(2,1)S(1)}, bf16[128,256]{1,0:T(8,128)(2,1)S(1)}, u32[]{:S(2)}, u32[]{:S(2)}) collective-permute-start(bf16[128,256]{1,0:T(8,128)(2,1)S(1)} %get-tuple-element.71), channel_id=1, source_target_pairs={{0,16},{8,24},{16,0},{24,8},{1,17},{9,25},{17,1},{25,9},{2,18},{10... | collective-permute-start | bytes 196616 | tf_op jit(solution)/shard_map/ppermute | solution.py:329
  40.4 5.2 %collective-permute-start.15 = (bf16[128,256]{1,0:T(8,128)(2,1)S(1)}, bf16[128,256]{1,0:T(8,128)(2,1)S(1)}, u32[]{:S(2)}, u32[]{:S(2)}) collective-permute-start(bf16[128,256]{1,0:T(8,128)(2,1)S(1)} %get-tuple-element.72), channel_id=1, source_target_pairs={{0,24},{8,16},{16,8},{24,0},{1,25},{9,17},{17,9},{25,1},{2,26},{10... | collective-permute-start | bytes 196616 | tf_op jit(solution)/shard_map/ppermute | solution.py:329
  46.5 4.4 %collective-permute-start.16 = (bf16[128,256]{1,0:T(8,128)(2,1)S(1)}, bf16[128,256]{1,0:T(8,128)(2,1)S(1)}, u32[]{:S(2)}, u32[]{:S(2)}) collective-permute-start(bf16[128,256]{1,0:T(8,128)(2,1)S(1)} %get-tuple-element.74), channel_id=1, source_target_pairs={{0,8},{8,0},{16,24},{24,16},{1,9},{9,1},{17,25},{25,17},{2,10},{10... | collective-permute-start | bytes 196616 | tf_op jit(solution)/shard_map/ppermute | solution.py:329
  47.1 4.4 %collective-permute-start.17 = (bf16[128,256]{1,0:T(8,128)(2,1)S(1)}, bf16[128,256]{1,0:T(8,128)(2,1)S(1)}, u32[]{:S(2)}, u32[]{:S(2)}) collective-permute-start(bf16[128,256]{1,0:T(8,128)(2,1)S(1)} %get-tuple-element.75), channel_id=1, source_target_pairs={{0,16},{8,24},{16,0},{24,8},{1,17},{9,25},{17,1},{25,9},{2,18},{10... | collective-permute-start | bytes 196616 | tf_op jit(solution)/shard_map/ppermute | solution.py:329
  47.7 5.2 %collective-permute-start.18 = (bf16[128,256]{1,0:T(8,128)(2,1)S(1)}, bf16[128,256]{1,0:T(8,128)(2,1)S(1)}, u32[]{:S(2)}, u32[]{:S(2)}) collective-permute-start(bf16[128,256]{1,0:T(8,128)(2,1)S(1)} %get-tuple-element.76), channel_id=1, source_target_pairs={{0,24},{8,16},{16,8},{24,0},{1,25},{9,17},{17,9},{25,1},{2,26},{10... | collective-permute-start | bytes 196616 | tf_op jit(solution)/shard_map/ppermute | solution.py:329
where the time goes:
time: 54.3 us; the launch traced here: 54.1 us
  starting transfers between devices  18.9 us (35%)
  Pallas kernels  18.7 us (34%)
  waiting for transfers between devices  16.3 us (30%)
    pallas_call x15, Pallas kernels, kernel_call(): pl.pallas_call(body, out_shape=outs, in_specs=in_specs or [VMEM] * len(op...  18.7 us
    ppermute x9, starting transfers between devices, across(): return lax.ppermute(x, 'energy', [(e, e ^ k) for e in range(energies)])  10.7 us
    ppermute x9, waiting for transfers between devices, across(): return lax.ppermute(x, 'energy', [(e, e ^ k) for e in range(energies)])  7.9 us
    ppermute x6, starting transfers between devices, hop(): lax.ppermute(x, 'domain', [(d, route.get(d, d ^ 1)) for d in range(domain...  7.5 us
    ppermute x6, waiting for transfers between devices, hop(): lax.ppermute(x, 'domain', [(d, route.get(d, d ^ 1)) for d in range(domain...  6.66 us
    ppermute x4, waiting for transfers between devices, swap(): return lax.ppermute(x, 'domain', [(d, d ^ 1) for d in range(domains)])  1.78 us
  transfers between devices with their start and end apart: 19, of which 13 were waited for; matrix products, arithmetic and copies ran while one was open for 0% of the time, Pallas kernels for 20%

commit v1 on v0

--- a/solution.py
+++ b/solution.py
@@ -13,7 +13,6 @@
 F32 = jnp.float32
 BF16 = jnp.bfloat16
 VMEM = pl.BlockSpec(memory_space=pltpu.VMEM)
-SMEM = pl.BlockSpec(memory_space=pltpu.SMEM)
 HBM = pl.BlockSpec(memory_space=pltpu.HBM)
 
 
@@ -65,11 +64,26 @@
     )(*operands)
 
 
+class Copies:
+    def __init__(self, source, target, sems):
+        parts = sems.shape[0]
+        rows = target.shape[0] // parts
+        self.parts = [
+            pltpu.make_async_copy(
+                source.at[pl.ds(i * rows, rows)], target.at[pl.ds(i * rows, rows)], sems.at[i]
+            )
+            for i in range(parts)
+        ]
+        for part in self.parts:
+            part.start()
+
+    def wait(self):
+        for part in self.parts:
+            part.wait()
+
+
 def first_kernel(
     blocks,
-    place,
-    tiles,
-    offsets,
     retarded,
     coupling,
     lesser,
@@ -80,10 +94,7 @@
     later_steps,
     sources,
     total,
-    scalars,
     held_lesser,
-    held_tiles,
-    held_offsets,
     sem,
 ):
     copies = {}
@@ -95,11 +106,8 @@
     copies["c", 0] = (coupling.at[0], held_coupling.at[0])
     for k in range(blocks):
         copies["g", k] = (greater.at[0, k], held_greater.at[k])
-    copies["t", 0] = (tiles, held_tiles)
-    copies["o", 0] = (offsets, held_offsets)
-    for index, key in enumerate(copies):
-        copies[key] = pltpu.make_async_copy(*copies[key], sem.at[index])
-        copies[key].start()
+    for index, (key, (source, target)) in enumerate(copies.items()):
+        copies[key] = Copies(source, target, sem.at[index])
     state = None
     for k in range(blocks):
         copies["r", k].wait()
@@ -115,14 +123,6 @@
     copies["c", 0].wait()
     for k in range(blocks):
         copies["g", k].wait()
-    copies["t", 0].wait()
-    copies["o", 0].wait()
-    chosen = held_tiles.shape[1]
-    values = [place[i] for i in range(place.shape[0])]
-    values += [held_tiles[k, j] for k in range(blocks) for j in range(chosen)]
-    values += [held_offsets[i] for i in range(held_offsets.shape[0])]
-    for i, value in enumerate(values):
-        scalars[i] = value
 
 
 def second_kernel(
@@ -153,38 +153,34 @@
     whole[...] = product(upper[1], lower[1])
 
 
-def keep(z, scalars, state, kept, out):
-    @pl.when(scalars[1] == z)
+def keep(z, state, kept, out):
+    chip = lax.axis_index("domain") >> 1
+
+    @pl.when(chip == z)
     def _():
         out[...] = state[...]
 
-    @pl.when(scalars[1] != z)
+    @pl.when(chip != z)
     def _():
         out[...] = jnp.zeros_like(out) if kept is None else kept[...]
 
 
-def advance_kernel(z, scalars, state, step, source, *refs):
+def advance_kernel(z, state, step, source, *refs):
     kept, (out, chosen) = (refs[0] if len(refs) == 3 else None), refs[-2:]
     out[...] = advance(state[...], step[...], source[...])
-    keep(z, scalars, state, kept, chosen)
-
-
-def keep_kernel(z, scalars, state, *refs):
-    keep(z, scalars, state, refs[0] if len(refs) == 2 else None, refs[-1])
-
-
-def piece_of(scalars, k, chosen, half, rows):
-    first = (scalars[2] ^ k) * rows
-    block = first // (chosen * half)
-    tile = scalars[3 + first // half]
-    return block, tile, first % half
+    keep(z, state, kept, chosen)
+
+
+def keep_kernel(z, state, *refs):
+    keep(z, state, refs[0] if len(refs) == 2 else None, refs[-1])
 
 
 def prepare_kernel(
     blocks,
     energies,
     chosen,
-    scalars,
+    tiles,
+    offsets,
     first_step,
     later_steps,
     lesser_sources,
@@ -195,21 +191,33 @@
     rights,
     lesser_parts,
     greater_parts,
+    shifts,
     chains,
     lessers,
     greaters,
+    held_tiles,
+    held_offsets,
+    sem,
 ):
+    copies = [
+        pltpu.make_async_copy(tiles, held_tiles, sem.at[0]),
+        pltpu.make_async_copy(offsets, held_offsets, sem.at[1]),
+    ]
+    for copy in copies:
+        copy.start()
+    upper = lax.axis_index("domain") & 1
+    group = lax.axis_index("energy")
     order = first_step.shape[0]
     half = order // 2
     rows = blocks * chosen * half // energies
 
-    @pl.when(scalars[0] == 0)
+    @pl.when(upper == 0)
     def _():
         chains[0] = first_step[...]
         lessers[0] = lesser_sources[0]
         greaters[0] = greater_sources[0]
 
-    @pl.when(scalars[0] == 1)
+    @pl.when(upper == 1)
     def _():
         chains[0] = product(first_step[...], lower_totals[1])
         lessers[0] = advance(lower_lesser[...], first_step[...], lesser_sources[0])
@@ -220,8 +228,14 @@
         chains[k] = product(step, chains[k - 1])
         lessers[k] = advance(lessers[k - 1], step, lesser_sources[k])
         greaters[k] = advance(greaters[k - 1], step, greater_sources[k])
+    for copy in copies:
+        copy.wait()
     for k in range(energies):
-        block, tile, start = piece_of(scalars, k, chosen, half, rows)
+        shifts[k] = jnp.full(shifts.shape[1:], held_offsets[group ^ k], jnp.int32)
+        first = (group ^ k) * rows
+        block = first // (chosen * half)
+        tile = held_tiles[block, (first // half) % chosen]
+        start = first % half
         row = pl.multiple_of((tile // 2) * half + start, 16)
         column = pl.multiple_of((tile % 2) * half, half)
         mine = slice(k * rows, (k + 1) * rows)
@@ -235,15 +249,16 @@
                 ]
 
 
-def finish_kernel(energies, scalars, arrived, near, lefts, rights, parts, *refs):
+def finish_kernel(energies, arrived, near, lefts, rights, parts, *refs):
     pieces, doubled = refs[:energies], refs[energies]
     rows = parts.shape[0] // energies
-
-    @pl.when(scalars[0] == 1)
+    upper = lax.axis_index("domain") & 1
+
+    @pl.when(upper == 1)
     def _():
         doubled[...] = stacked(arrived[...])
 
-    @pl.when(scalars[0] == 0)
+    @pl.when(upper == 0)
     def _():
         doubled[...] = stacked(near[...])
 
@@ -255,39 +270,51 @@
         ).astype(BF16)
 
 
-def convolve_kernel(energies, at_offsets, scalars, *refs):
+def convolve_kernel(energies, shifts, *refs):
     less, great = refs[:energies], refs[energies : 2 * energies]
     outs = refs[2 * energies : 3 * energies]
     held_less, held_great = refs[3 * energies :]
-    group = scalars[2]
+    group = lax.axis_index("energy")
     rows, width = less[0].shape
     half = width // 2
+    reach = energies // 2
     for k in range(energies):
-        held_less[group ^ k] = less[k][...].astype(F32)
-        held_great[energies + (group ^ k)] = great[k][...].astype(F32)
-        held_great[k] = jnp.zeros((rows, width), F32)
-        held_great[2 * energies + k] = jnp.zeros((rows, width), F32)
+        held_less[group ^ k] = less[k][...]
+        held_great[group ^ k] = great[k][...]
     chunk = 16
     for start in range(0, rows, chunk):
         at = slice(start, start + chunk)
+        totals = [None] * energies
+        wanted = [jnp.broadcast_to(shifts[k, :1], (chunk, half)) for k in range(energies)]
+        for distance in range(-reach, reach + 1):
+            real = imag = None
+            for e in range(max(0, distance), min(energies, energies + distance)):
+                lr = held_less[e, at, :half].astype(F32)
+                li = held_less[e, at, half:].astype(F32)
+                gr = held_great[e - distance, at, :half].astype(F32)
+                gi = held_great[e - distance, at, half:].astype(F32)
+                more_real, more_imag = lr * gr - li * gi, lr * gi + li * gr
+                real = more_real if real is None else real + more_real
+                imag = more_imag if imag is None else imag + more_imag
+            for k in range(energies):
+                if totals[k] is None:
+                    totals[k] = (real, imag)
+                else:
+                    match = wanted[k] == distance
+                    totals[k] = (
+                        jnp.where(match, real, totals[k][0]),
+                        jnp.where(match, imag, totals[k][1]),
+                    )
         for k in range(energies):
-            shift = energies - scalars[at_offsets + (group ^ k)]
-            real = jnp.zeros((chunk, half), F32)
-            imag = jnp.zeros((chunk, half), F32)
-            for e in range(energies):
-                other = held_great.at[shift + e]
-                lr, li = held_less[e, at, :half], held_less[e, at, half:]
-                gr, gi = other[at, :half], other[at, half:]
-                real = real + (lr * gr - li * gi)
-                imag = imag + (lr * gi + li * gr)
-            outs[k][at, :half] = (real / energies).astype(BF16)
-            outs[k][at, half:] = (imag / energies).astype(BF16)
-
-
-def gather_kernel(energies, scalars, *refs):
+            outs[k][at, :half] = (totals[k][0] / energies).astype(BF16)
+            outs[k][at, half:] = (totals[k][1] / energies).astype(BF16)
+
+
+def gather_kernel(energies, *refs):
     shares, (out, sem) = refs[:energies], refs[energies:]
+    group = lax.axis_index("energy")
     copies = [
-        pltpu.make_async_copy(shares[k], out.at[scalars[2] ^ k], sem.at[k])
+        pltpu.make_async_copy(shares[k], out.at[group ^ k], sem.at[k])
         for k in range(energies)
     ]
     for copy in copies:
@@ -310,9 +337,8 @@
     def series(count):
         return jax.ShapeDtypeStruct((count, order, 2 * order), BF16)
 
-    domain = lax.axis_index("domain")
-    place = jnp.stack([domain & 1, domain >> 1, lax.axis_index("energy")])
-    at_offsets = place.size + tiles.size
+    def in_place(*arrays):
+        return tuple(pltpu.with_memory_space_constraint(x, pltpu.HBM) for x in arrays)
 
     def swap(x):
         return lax.ppermute(x, "domain", [(d, d ^ 1) for d in range(domains)])
@@ -328,31 +354,18 @@
     def across(x, k):
         return lax.ppermute(x, "energy", [(e, e ^ k) for e in range(energies)])
 
-    inputs = (tiles, offsets, retarded, coupling, sigma_lesser, sigma_greater)
-    (
-        held_retarded,
-        held_coupling,
-        held_greater,
-        later_steps,
-        less_sources,
-        less_total,
-        scalars,
-    ) = kernel_call(
-        functools.partial(first_kernel, blocks),
-        [series(blocks)] * 3
-        + [series(blocks - 1), series(blocks), block]
-        + [jax.ShapeDtypeStruct((at_offsets + offsets.size,), jnp.int32)],
-        (place,)
-        + tuple(pltpu.with_memory_space_constraint(x, pltpu.HBM) for x in inputs),
-        (5 * blocks - 3) * unit,
-        in_specs=[SMEM] + [HBM] * len(inputs),
-        out_specs=[VMEM] * 6 + [SMEM],
-        scratch=[
-            pltpu.VMEM((blocks, order, 2 * order), BF16),
-            pltpu.SMEM(tiles.shape, jnp.int32),
-            pltpu.SMEM(offsets.shape, jnp.int32),
-            pltpu.SemaphoreType.DMA((4 * blocks + 2,)),
-        ],
+    held_retarded, held_coupling, held_greater, later_steps, less_sources, less_total = (
+        kernel_call(
+            functools.partial(first_kernel, blocks),
+            [series(blocks)] * 3 + [series(blocks - 1), series(blocks), block],
+            in_place(retarded, coupling, sigma_lesser, sigma_greater),
+            (5 * blocks - 3) * unit,
+            in_specs=[HBM] * 4,
+            scratch=[
+                pltpu.VMEM((blocks, order, 2 * order), BF16),
+                pltpu.SemaphoreType.DMA((4 * blocks, 2)),
+            ],
+        )
     )
     lower_less = swap(less_total)
     first_step, great_sources, totals = kernel_call(
@@ -368,16 +381,17 @@
     chip_great, chip_whole = kernel_call(
         join_greater_kernel, [block] * 2, (lower_totals, totals), 3 * unit
     )
-    lefts, rights, less_parts, great_parts = kernel_call(
+    lefts, rights, less_parts, great_parts, shifts = kernel_call(
         functools.partial(prepare_kernel, blocks, energies, chosen),
         [
             jax.ShapeDtypeStruct((energies * rows, 2 * order), BF16),
             jax.ShapeDtypeStruct((energies, order, 2 * order), BF16),
             jax.ShapeDtypeStruct((energies * rows, order), BF16),
             jax.ShapeDtypeStruct((energies * rows, order), BF16),
+            jax.ShapeDtypeStruct((energies, 8, half), jnp.int32),
         ],
         (
-            scalars,
+            *in_place(tiles, offsets),
             first_step,
             later_steps,
             less_sources,
@@ -386,26 +400,26 @@
             lower_totals,
         ),
         5 * blocks * unit,
-        in_specs=[SMEM] + [VMEM] * 6,
-        scratch=[pltpu.VMEM((blocks, order, 2 * order), BF16)] * 3,
+        in_specs=[HBM] * 2 + [VMEM] * 6,
+        scratch=[pltpu.VMEM((blocks, order, 2 * order), BF16)] * 3
+        + [
+            pltpu.SMEM(tiles.shape, jnp.int32),
+            pltpu.SMEM(offsets.shape, jnp.int32),
+            pltpu.SemaphoreType.DMA((2,)),
+        ],
     )
 
     def step_on(z, state, kept, source):
         return kernel_call(
             functools.partial(advance_kernel, z),
             [block, block],
-            (scalars, state, chip_whole, source, *kept),
+            (state, chip_whole, source, *kept),
             2 * unit,
-            in_specs=[SMEM] + [VMEM] * (3 + len(kept)),
         )
 
     def keep_last(state, kept):
         return kernel_call(
-            functools.partial(keep_kernel, chips - 1),
-            [block],
-            (scalars, state, *kept),
-            0,
-            in_specs=[SMEM] + [VMEM] * (1 + len(kept)),
+            functools.partial(keep_kernel, chips - 1), [block], (state, *kept), 0
         )
 
     def finish(arrived, parts):
@@ -413,9 +427,8 @@
         pieces = kernel_call(
             functools.partial(finish_kernel, energies),
             [piece] * energies,
-            (scalars, arrived, near, lefts, rights, parts),
+            (arrived, near, lefts, rights, parts),
             3 * unit,
-            in_specs=[SMEM] + [VMEM] * 5,
             scratch=[pltpu.VMEM((2 * order, 2 * order), BF16)],
         )
         return [pieces[0]] + [across(pieces[k], k) for k in range(1, energies)]
@@ -433,23 +446,18 @@
     less_pieces = finish(less_in[0], less_parts)
     great_pieces = finish(great_in[0], great_parts)
     shares = kernel_call(
-        functools.partial(convolve_kernel, energies, at_offsets),
+        functools.partial(convolve_kernel, energies),
         [piece] * energies,
-        (scalars, *less_pieces, *great_pieces),
+        (shifts, *less_pieces, *great_pieces),
         8 * energies * energies * rows * half,
-        in_specs=[SMEM] + [VMEM] * (2 * energies),
-        scratch=[
-            pltpu.VMEM((energies, rows, order), F32),
-            pltpu.VMEM((3 * energies, rows, order), F32),
-        ],
+        scratch=[pltpu.VMEM((energies, rows, order), BF16)] * 2,
     )
     shares = [shares[0]] + [across(shares[k], k) for k in range(1, energies)]
     (result,) = kernel_call(
         functools.partial(gather_kernel, energies),
         [jax.ShapeDtypeStruct((energies, rows, order), BF16)],
-        (scalars, *shares),
+        shares,
         0,
-        in_specs=[SMEM] + [VMEM] * energies,
         out_specs=[HBM],
         scratch=[pltpu.SemaphoreType.DMA((energies,))],
     )

time: 54.3 us -> 48.9 us (0.901)
  Pallas kernels: 18.7 us -> 11.8 us
  starting transfers between devices: 18.9 us -> 20 us
  waiting for transfers between devices: 16.3 us -> 16.9 us
    pallas_call x15, Pallas kernels: 18.7 us -> 11.8 us  [kernel_call(): pl.pallas_call(body, out_shape=outs, in_specs=in_specs or [VMEM] * len(op...]
    ppermute x6, starting transfers between devices: 7.5 us -> 8.62 us  [hop(): lax.ppermute(x, 'domain', [(d, route.get(d, d ^ 1)) for d in range(domain...]
  transfers between devices with their start and end apart: 19 -> 19, of which waited for: 13 -> 13; matrix products, arithmetic and copies ran while one was open for 0% -> 0% of each run, Pallas kernels for 20% -> 13%
where the time goes in v1:
time: 48.9 us; the launch traced here: 48.8 us
  starting transfers between devices  20 us (41%)
  waiting for transfers between devices  16.9 us (35%)
  Pallas kernels  11.8 us (24%)
    pallas_call x15, Pallas kernels, kernel_call(): pl.pallas_call(body, out_shape=outs, in_specs=in_specs or [VMEM] * len(op...  11.8 us
    ppermute x9, starting transfers between devices, across(): return lax.ppermute(x, 'energy', [(e, e ^ k) for e in range(energies)])  10.7 us
    ppermute x6, starting transfers between devices, hop(): lax.ppermute(x, 'domain', [(d, route.get(d, d ^ 1)) for d in range(domain...  8.62 us
    ppermute x9, waiting for transfers between devices, across(): return lax.ppermute(x, 'energy', [(e, e ^ k) for e in range(energies)])  7.89 us
    ppermute x6, waiting for transfers between devices, hop(): lax.ppermute(x, 'domain', [(d, route.get(d, d ^ 1)) for d in range(domain...  7.18 us
    ppermute x4, waiting for transfers between devices, swap(): return lax.ppermute(x, 'domain', [(d, d ^ 1) for d in range(domains)])  1.78 us
  transfers between devices with their start and end apart: 19, of which 13 were waited for; matrix products, arithmetic and copies ran while one was open for 0% of the time, Pallas kernels for 13%

profile of v1, /device:TPU:16, one launch (start us, length us, event | category | flops | bytes accessed | tf_op | source)
XLA Modules:
  0.0 48.8 jit_solution(10982843378619785990)
XLA Ops:
  0.0 3.0 %shard_map.64 = (bf16[2,256,512]{2,1,0:T(8,128)(2,1)S(1)}, bf16[2,256,512]{2,1,0:T(8,128)(2,1)S(1)}, bf16[2,256,512]{2,1,0:T(8,128)(2,1)S(1)}, bf16[1,256,512]{2...) custom-call(bf16[1,2,256,512]{3,2,1,0:T(8,128)(2,1)} %retarded.1, ...), custom_call_target="tpu_custom_call" | custom-call | flops 939524096 | bytes 4718592 | tf_op jit(solution)/shard_map/pallas_call | solution.py:54
  3.0 1.5 %shard_map.65 = (bf16[256,512]{1,0:T(8,128)(2,1)S(1)}, bf16[2,256,512]{2,1,0:T(8,128)(2,1)S(1)}, bf16[2,256,512]{2,1,0:T(8,128)(2,1)S(1)}) custom-call(bf16[2,256,512]{2,1,0:T(8,128)(2,1)S(1)} %get-tuple-element.41.retarded, bf16[2,256,512]{2,1,0:T(8,128)(2,1)S(1)} %get-tuple-element.42.coupling, bf16[2,256,512]{2,1,0:T(8,128)(2,1)S(1)} %get-tuple-element.43.greater, ...), custom_call_target="tpu_custom_call" | custom-call | flops 1073741824 | bytes 3145728 | tf_op jit(solution)/shard_map/pallas_call | solution.py:54
  4.5 0.1 collective-permute-start.1
  4.6 0.5 %collective-permute-start = (bf16[256,512]{1,0:T(8,128)(2,1)S(1)}, bf16[256,512]{1,0:T(8,128)(2,1)S(1)}, u32[]{:S(2)}, u32[]{:S(2)}) collective-permute-start(bf16[256,512]{1,0:T(8,128)(2,1)S(1)} %get-tuple-element.48.upper), channel_id=1, source_target_pairs={{0,1},{1,0},{2,3},{3,2},{4,5},{5,4},{6,7},{7,6},{8,9},{9,8},{10,11... | collective-permute-start | bytes 786440 | tf_op jit(solution)/shard_map/ppermute | solution.py:344
  5.1 1.8 %collective-permute-done.lower_lesser.lower = bf16[256,512]{1,0:T(8,128)(2,1)S(1)} collective-permute-done((bf16[256,512]{1,0:T(8,128)(2,1)S(1)}, bf16[256,512]{1,0:T(8,128)(2,1)S(1)}, u32[]{:S(2)}, u32[]{:S(2)}) %collective-permute-start) | collective-permute-done | bytes 262176 | tf_op jit(solution)/shard_map/ppermute | solution.py:344
  6.9 0.5 %shard_map.67.source = bf16[256,512]{1,0:T(8,128)(2,1)S(1)} custom-call(bf16[256,512]{1,0:T(8,128)(2,1)S(1)} %collective-permute-done.lower_lesser.lower, bf16[2,256,512]{2,1,0:T(8,128)(2,1)S(1)} %get-tuple-element.49.totals.upper, bf16[256,512]{1,0:T(8,128)(2,1)S(1)} %get-tuple-element.48.upper), custom_call_target="tpu_custom_call" | custom-call | flops 268435456 | bytes 1310720 | tf_op jit(solution)/shard_map/pallas_call | solution.py:54
  7.4 0.2 collective-permute-start.2
  7.6 0.0 collective-permute-done.1.lower_totals.lower
  7.6 0.7 %shard_map.68 = (bf16[256,512]{1,0:T(8,128)(2,1)S(1)}, bf16[256,512]{1,0:T(8,128)(2,1)S(1)}) custom-call(bf16[2,256,512]{2,1,0:T(8,128)(2,1)S(1)} %collective-permute-done.1.lower_totals.lower, bf16[2,256,512]{2,1,0:T(8,128)(2,1)S(1)} %get-tuple-element.49.totals.upper), custom_call_target="tpu_custom_call" | custom-call | flops 402653184 | bytes 1572864 | tf_op jit(solution)/shard_map/pallas_call | solution.py:54
  8.2 0.4 collective-permute-start.9
  8.7 0.3 collective-permute-done.2.state
  9.0 0.5 %shard_map.69 = (bf16[256,512]{1,0:T(8,128)(2,1)S(1)}, bf16[256,512]{1,0:T(8,128)(2,1)S(1)}) custom-call(bf16[256,512]{1,0:T(8,128)(2,1)S(1)} %collective-permute-done.2.state, bf16[256,512]{1,0:T(8,128)(2,1)S(1)} %get-tuple-element.51.step, bf16[256,512]{1,0:T(8,128)(2,1)S(1)} %shard_map.67.source), custom_call_target="tpu_custom_call" | custom-call | flops 268435456 | bytes 1310720 | tf_op jit(solution)/shard_map/pallas_call | solution.py:54
  9.5 2.9 %collective-permute-start.3 = (bf16[256,512]{1,0:T(8,128)(2,1)S(1)}, bf16[256,512]{1,0:T(8,128)(2,1)S(1)}, u32[]{:S(2)}, u32[]{:S(2)}) collective-permute-start(bf16[256,512]{1,0:T(8,128)(2,1)S(1)} %get-tuple-element.52), channel_id=1, source_target_pairs={{0,1},{1,0},{2,3},{3,5},{4,2},{5,4},{6,7},{7,6},{8,9},{9,8},{10,11... | collective-permute-start | bytes 786440 | tf_op jit(solution)/shard_map/ppermute | solution.py:350
  12.4 0.0 collective-permute-done.9.state
  12.4 0.5 %shard_map.73 = (bf16[256,512]{1,0:T(8,128)(2,1)S(1)}, bf16[256,512]{1,0:T(8,128)(2,1)S(1)}) custom-call(bf16[256,512]{1,0:T(8,128)(2,1)S(1)} %collective-permute-done.9.state, bf16[256,512]{1,0:T(8,128)(2,1)S(1)} %get-tuple-element.51.step, bf16[256,512]{1,0:T(8,128)(2,1)S(1)} %get-tuple-element.63.source), custom_call_target="tpu_custom_call" | custom-call | flops 268435456 | bytes 1310720 | tf_op jit(solution)/shard_map/pallas_call | solution.py:54
  13.0 2.3 %collective-permute-start.10 = (bf16[256,512]{1,0:T(8,128)(2,1)S(1)}, bf16[256,512]{1,0:T(8,128)(2,1)S(1)}, u32[]{:S(2)}, u32[]{:S(2)}) collective-permute-start(bf16[256,512]{1,0:T(8,128)(2,1)S(1)} %get-tuple-element.64), channel_id=1, source_target_pairs={{0,1},{1,0},{2,3},{3,5},{4,2},{5,4},{6,7},{7,6},{8,9},{9,8},{10,11... | collective-permute-start | bytes 786440 | tf_op jit(solution)/shard_map/ppermute | solution.py:350
  15.2 1.1 %collective-permute-done.3.state = bf16[256,512]{1,0:T(8,128)(2,1)S(1)} collective-permute-done((bf16[256,512]{1,0:T(8,128)(2,1)S(1)}, bf16[256,512]{1,0:T(8,128)(2,1)S(1)}, u32[]{:S(2)}, u32[]{:S(2)}) %collective-permute-start.3) | collective-permute-done | bytes 262176 | tf_op jit(solution)/shard_map/ppermute | solution.py:350
  16.3 0.5 %shard_map.70 = (bf16[256,512]{1,0:T(8,128)(2,1)S(1)}, bf16[256,512]{1,0:T(8,128)(2,1)S(1)}) custom-call(bf16[256,512]{1,0:T(8,128)(2,1)S(1)} %collective-permute-done.3.state, bf16[256,512]{1,0:T(8,128)(2,1)S(1)} %get-tuple-element.51.step, bf16[256,512]{1,0:T(8,128)(2,1)S(1)} %shard_map.67.source, bf16[256,512]{1,0:T(8,128)(2,1)S(1)} %get-tuple-element.53.refs_0_), custom_call_target="tpu_custom_call" | custom-call | flops 268435456 | bytes 1572864 | tf_op jit(solution)/shard_map/pallas_call | solution.py:54
  16.9 1.1 %collective-permute-start.4 = (bf16[256,512]{1,0:T(8,128)(2,1)S(1)}, bf16[256,512]{1,0:T(8,128)(2,1)S(1)}, u32[]{:S(2)}, u32[]{:S(2)}) collective-permute-start(bf16[256,512]{1,0:T(8,128)(2,1)S(1)} %get-tuple-element.54), channel_id=1, source_target_pairs={{0,1},{1,0},{2,3},{3,2},{4,5},{5,7},{6,4},{7,6},{8,9},{9,8},{10,11... | collective-permute-start | bytes 786440 | tf_op jit(solution)/shard_map/ppermute | solution.py:350
  18.0 1.1 %collective-permute-done.10.state = bf16[256,512]{1,0:T(8,128)(2,1)S(1)} collective-permute-done((bf16[256,512]{1,0:T(8,128)(2,1)S(1)}, bf16[256,512]{1,0:T(8,128)(2,1)S(1)}, u32[]{:S(2)}, u32[]{:S(2)}) %collective-permute-start.10) | collective-permute-done | bytes 262176 | tf_op jit(solution)/shard_map/ppermute | solution.py:350
  19.1 0.5 %shard_map.74 = (bf16[256,512]{1,0:T(8,128)(2,1)S(1)}, bf16[256,512]{1,0:T(8,128)(2,1)S(1)}) custom-call(bf16[256,512]{1,0:T(8,128)(2,1)S(1)} %collective-permute-done.10.state, bf16[256,512]{1,0:T(8,128)(2,1)S(1)} %get-tuple-element.51.step, bf16[256,512]{1,0:T(8,128)(2,1)S(1)} %get-tuple-element.63.source, bf16[256,512]{1,0:T(8,128)(2,1)S(1)} %get-tuple-element.65.refs_0_), custom_call_target="tpu_custom_call" | custom-call | flops 268435456 | bytes 1572864 | tf_op jit(solution)/shard_map/pallas_call | solution.py:54
  19.7 1.7 %collective-permute-start.11 = (bf16[256,512]{1,0:T(8,128)(2,1)S(1)}, bf16[256,512]{1,0:T(8,128)(2,1)S(1)}, u32[]{:S(2)}, u32[]{:S(2)}) collective-permute-start(bf16[256,512]{1,0:T(8,128)(2,1)S(1)} %get-tuple-element.66), channel_id=1, source_target_pairs={{0,1},{1,0},{2,3},{3,2},{4,5},{5,7},{6,4},{7,6},{8,9},{9,8},{10,11... | collective-permute-start | bytes 786440 | tf_op jit(solution)/shard_map/ppermute | solution.py:350
  21.4 1.9 %collective-permute-done.4.state = bf16[256,512]{1,0:T(8,128)(2,1)S(1)} collective-permute-done((bf16[256,512]{1,0:T(8,128)(2,1)S(1)}, bf16[256,512]{1,0:T(8,128)(2,1)S(1)}, u32[]{:S(2)}, u32[]{:S(2)}) %collective-permute-start.4) | collective-permute-done | bytes 262176 | tf_op jit(solution)/shard_map/ppermute | solution.py:350
  23.3 0.1 collective-permute-start.5
  23.4 2.7 %collective-permute-done.11.state = bf16[256,512]{1,0:T(8,128)(2,1)S(1)} collective-permute-done((bf16[256,512]{1,0:T(8,128)(2,1)S(1)}, bf16[256,512]{1,0:T(8,128)(2,1)S(1)}, u32[]{:S(2)}, u32[]{:S(2)}) %collective-permute-start.11) | collective-permute-done | bytes 262176 | tf_op jit(solution)/shard_map/ppermute | solution.py:350
  26.2 0.1 collective-permute-start.12
  26.2 1.3 %shard_map.66 = (bf16[512,512]{1,0:T(8,128)(2,1)S(1)}, bf16[4,256,512]{2,1,0:T(8,128)(2,1)S(1)}, bf16[512,256]{1,0:T(8,128)(2,1)S(1)}, bf16[512,256]{1,0:T(8,128)(2,1)S(1)}, s32[4,8,128]{2,1,0:T(8,128)S(1)}) custom-call(s32[2,2]{1,0:T(2,128)} %tiles.1, s32[4]{0:T(128)} %offsets.1, bf16[256,512]{1,0:T(8,128)(2,1)S(1)} %get-tuple-element.45.first_step, ...), custom_call_target="tpu_custom_call" | custom-call | flops 1342177280 | bytes 4472864 | tf_op jit(solution)/shard_map/pallas_call | solution.py:54
  27.6 0.0 collective-permute-done.5.near
  27.6 0.8 %shard_map.72 = (bf16[128,256]{1,0:T(8,128)(2,1)S(1)}, bf16[128,256]{1,0:T(8,128)(2,1)S(1)}, bf16[128,256]{1,0:T(8,128)(2,1)S(1)}, bf16[128,256]{1,0:T(8,128)(2,1)S(1)}) custom-call(bf16[256,512]{1,0:T(8,128)(2,1)S(1)} %shard_map.71.arrived, bf16[256,512]{1,0:T(8,128)(2,1)S(1)} %collective-permute-done.5.near, bf16[512,512]{1,0:T(8,128)(2,1)S(1)} %get-tuple-element.56.lefts, ...), custom_call_target="tpu_custom_call" | custom-call | flops 402653184 | bytes 2621440 | tf_op jit(solution)/shard_map/pallas_call | solution.py:54
  28.4 2.0 %collective-permute-start.6 = (bf16[128,256]{1,0:T(8,128)(2,1)S(1)}, bf16[128,256]{1,0:T(8,128)(2,1)S(1)}, u32[]{:S(2)}, u32[]{:S(2)}) collective-permute-start(bf16[128,256]{1,0:T(8,128)(2,1)S(1)} %get-tuple-element.60), channel_id=1, source_target_pairs={{0,8},{8,0},{16,24},{24,16},{1,9},{9,1},{17,25},{25,17},{2,10},{10... | collective-permute-start | bytes 196616 | tf_op jit(solution)/shard_map/ppermute | solution.py:355
  30.4 1.5 %collective-permute-start.7 = (bf16[128,256]{1,0:T(8,128)(2,1)S(1)}, bf16[128,256]{1,0:T(8,128)(2,1)S(1)}, u32[]{:S(2)}, u32[]{:S(2)}) collective-permute-start(bf16[128,256]{1,0:T(8,128)(2,1)S(1)} %get-tuple-element.61), channel_id=1, source_target_pairs={{0,16},{8,24},{16,0},{24,8},{1,17},{9,25},{17,1},{25,9},{2,18},{10... | collective-permute-start | bytes 196616 | tf_op jit(solution)/shard_map/ppermute | solution.py:355
  31.9 0.0 collective-permute-start.8
  31.9 0.0 collective-permute-done.12.near
  31.9 0.7 %shard_map.76 = (bf16[128,256]{1,0:T(8,128)(2,1)S(1)}, bf16[128,256]{1,0:T(8,128)(2,1)S(1)}, bf16[128,256]{1,0:T(8,128)(2,1)S(1)}, bf16[128,256]{1,0:T(8,128)(2,1)S(1)}) custom-call(bf16[256,512]{1,0:T(8,128)(2,1)S(1)} %shard_map.75.arrived, bf16[256,512]{1,0:T(8,128)(2,1)S(1)} %collective-permute-done.12.near, ...), custom_call_target="tpu_custom_call" | custom-call | flops 402653184 | bytes 2621440 | tf_op jit(solution)/shard_map/pallas_call | solution.py:54
  32.7 2.0 %collective-permute-start.13 = (bf16[128,256]{1,0:T(8,128)(2,1)S(1)}, bf16[128,256]{1,0:T(8,128)(2,1)S(1)}, u32[]{:S(2)}, u32[]{:S(2)}) collective-permute-start(bf16[128,256]{1,0:T(8,128)(2,1)S(1)} %get-tuple-element.70), channel_id=1, source_target_pairs={{0,8},{8,0},{16,24},{24,16},{1,9},{9,1},{17,25},{25,17},{2,10},{10... | collective-permute-start | bytes 196616 | tf_op jit(solution)/shard_map/ppermute | solution.py:355
  34.7 1.5 %collective-permute-start.14 = (bf16[128,256]{1,0:T(8,128)(2,1)S(1)}, bf16[128,256]{1,0:T(8,128)(2,1)S(1)}, u32[]{:S(2)}, u32[]{:S(2)}) collective-permute-start(bf16[128,256]{1,0:T(8,128)(2,1)S(1)} %get-tuple-element.71), channel_id=1, source_target_pairs={{0,16},{8,24},{16,0},{24,8},{1,17},{9,25},{17,1},{25,9},{2,18},{10... | collective-permute-start | bytes 196616 | tf_op jit(solution)/shard_map/ppermute | solution.py:355
  36.2 0.0 collective-permute-done.6.refs_1_
  36.2 0.0 collective-permute-start.15
  36.2 0.0 collective-permute-done.7.refs_2_
  36.2 1.5 %collective-permute-done.8.refs_3_ = bf16[128,256]{1,0:T(8,128)(2,1)S(1)} collective-permute-done((bf16[128,256]{1,0:T(8,128)(2,1)S(1)}, bf16[128,256]{1,0:T(8,128)(2,1)S(1)}, u32[]{:S(2)}, u32[]{:S(2)}) %collective-permute-start.8) | collective-permute-done | bytes 65568 | tf_op jit(solution)/shard_map/ppermute | solution.py:355
  37.7 0.4 collective-permute-done.13.refs_5_
  38.1 0.9 %collective-permute-done.14.refs_6_ = bf16[128,256]{1,0:T(8,128)(2,1)S(1)} collective-permute-done((bf16[128,256]{1,0:T(8,128)(2,1)S(1)}, bf16[128,256]{1,0:T(8,128)(2,1)S(1)}, u32[]{:S(2)}, u32[]{:S(2)}) %collective-permute-start.14) | collective-permute-done | bytes 65568 | tf_op jit(solution)/shard_map/ppermute | solution.py:355
  39.1 2.3 %collective-permute-done.15.refs_7_ = bf16[128,256]{1,0:T(8,128)(2,1)S(1)} collective-permute-done((bf16[128,256]{1,0:T(8,128)(2,1)S(1)}, bf16[128,256]{1,0:T(8,128)(2,1)S(1)}, u32[]{:S(2)}, u32[]{:S(2)}) %collective-permute-start.15) | collective-permute-done | bytes 65568 | tf_op jit(solution)/shard_map/ppermute | solution.py:355
  41.3 0.4 shard_map.77
  41.8 0.6 %collective-permute-start.16 = (bf16[128,256]{1,0:T(8,128)(2,1)S(1)}, bf16[128,256]{1,0:T(8,128)(2,1)S(1)}, u32[]{:S(2)}, u32[]{:S(2)}) collective-permute-start(bf16[128,256]{1,0:T(8,128)(2,1)S(1)} %get-tuple-element.74), channel_id=1, source_target_pairs={{0,8},{8,0},{16,24},{24,16},{1,9},{9,1},{17,25},{25,17},{2,10},{10... | collective-permute-start | bytes 196616 | tf_op jit(solution)/shard_map/ppermute | solution.py:355
  42.4 0.5 %collective-permute-start.17 = (bf16[128,256]{1,0:T(8,128)(2,1)S(1)}, bf16[128,256]{1,0:T(8,128)(2,1)S(1)}, u32[]{:S(2)}, u32[]{:S(2)}) collective-permute-start(bf16[128,256]{1,0:T(8,128)(2,1)S(1)} %get-tuple-element.75), channel_id=1, source_target_pairs={{0,16},{8,24},{16,0},{24,8},{1,17},{9,25},{17,1},{25,9},{2,18},{10... | collective-permute-start | bytes 196616 | tf_op jit(solution)/shard_map/ppermute | solution.py:355
  42.9 2.4 %collective-permute-start.18 = (bf16[128,256]{1,0:T(8,128)(2,1)S(1)}, bf16[128,256]{1,0:T(8,128)(2,1)S(1)}, u32[]{:S(2)}, u32[]{:S(2)}) collective-permute-start(bf16[128,256]{1,0:T(8,128)(2,1)S(1)} %get-tuple-element.76), channel_id=1, source_target_pairs={{0,24},{8,16},{16,8},{24,0},{1,25},{9,17},{17,9},{25,1},{2,26},{10... | collective-permute-start | bytes 196616 | tf_op jit(solution)/shard_map/ppermute | solution.py:355
  45.3 0.8 %collective-permute-done.16.refs_1_ = bf16[128,256]{1,0:T(8,128)(2,1)S(1)} collective-permute-done((bf16[128,256]{1,0:T(8,128)(2,1)S(1)}, bf16[128,256]{1,0:T(8,128)(2,1)S(1)}, u32[]{:S(2)}, u32[]{:S(2)}) %collective-permute-start.16) | collective-permute-done | bytes 65568 | tf_op jit(solution)/shard_map/ppermute | solution.py:355
  46.1 0.6 %collective-permute-done.17.refs_2_ = bf16[128,256]{1,0:T(8,128)(2,1)S(1)} collective-permute-done((bf16[128,256]{1,0:T(8,128)(2,1)S(1)}, bf16[128,256]{1,0:T(8,128)(2,1)S(1)}, u32[]{:S(2)}, u32[]{:S(2)}) %collective-permute-start.17) | collective-permute-done | bytes 65568 | tf_op jit(solution)/shard_map/ppermute | solution.py:355
  46.8 1.3 %collective-permute-done.18.refs_3_ = bf16[128,256]{1,0:T(8,128)(2,1)S(1)} collective-permute-done((bf16[128,256]{1,0:T(8,128)(2,1)S(1)}, bf16[128,256]{1,0:T(8,128)(2,1)S(1)}, u32[]{:S(2)}, u32[]{:S(2)}) %collective-permute-start.18) | collective-permute-done | bytes 65568 | tf_op jit(solution)/shard_map/ppermute | solution.py:355
  48.1 0.7 %shard_map.78 = bf16[4,128,256]{2,1,0:T(8,128)(2,1)} custom-call(bf16[128,256]{1,0:T(8,128)(2,1)S(1)} %get-tuple-element.73.refs_0_, bf16[128,256]{1,0:T(8,128)(2,1)S(1)} %collective-permute-done.16.refs_1_, bf16[128,256]{1,0:T(8,128)(2,1)S(1)} %collective-permute-done.17.refs_2_, bf16[128,256]{1,0:T(8,128)(2,1)S(1)} %collective-permute-done.18.refs_3_), custom_call_target="tpu_custom_call" | custom-call | bytes 524288 | tf_op jit(solution)/shard_map/pallas_call | solution.py:54
  (2 shorter events, 0.0 us)
Async XLA Ops:
  4.5 3.1 %collective-permute-start.1 = (bf16[2,256,512]{2,1,0:T(8,128)(2,1)S(1)}, bf16[2,256,512]{2,1,0:T(8,128)(2,1)S(1)}, u32[]{:S(2)}, u32[]{:S(2)}) collective-permute-start(bf16[2,256,512]{2,1,0:T(8,128)(2,1)S(1)} %get-tuple-element.49.totals.upper), channel_id=1, source_target_pairs={{0,1},{1,0},{2,3},{3,2},{4,5},{5,4},{6,7},{7,6},{8,9},{9,8},{10,11... | collective-permute-start | bytes 1572872 | tf_op jit(solution)/shard_map/ppermute | solution.py:344
  4.6 2.3 %collective-permute-start = (bf16[256,512]{1,0:T(8,128)(2,1)S(1)}, bf16[256,512]{1,0:T(8,128)(2,1)S(1)}, u32[]{:S(2)}, u32[]{:S(2)}) collective-permute-start(bf16[256,512]{1,0:T(8,128)(2,1)S(1)} %get-tuple-element.48.upper), channel_id=1, source_target_pairs={{0,1},{1,0},{2,3},{3,2},{4,5},{5,4},{6,7},{7,6},{8,9},{9,8},{10,11... | collective-permute-start | bytes 786440 | tf_op jit(solution)/shard_map/ppermute | solution.py:344
  7.4 1.6 %collective-permute-start.2 = (bf16[256,512]{1,0:T(8,128)(2,1)S(1)}, bf16[256,512]{1,0:T(8,128)(2,1)S(1)}, u32[]{:S(2)}, u32[]{:S(2)}) collective-permute-start(bf16[256,512]{1,0:T(8,128)(2,1)S(1)} %shard_map.67.source), channel_id=1, source_target_pairs={{0,1},{1,3},{2,0},{3,2},{4,5},{5,4},{6,7},{7,6},{8,9},{9,11},{10,8... | collective-permute-start | bytes 786440 | tf_op jit(solution)/shard_map/ppermute | solution.py:350
  8.2 4.2 %collective-permute-start.9 = (bf16[256,512]{1,0:T(8,128)(2,1)S(1)}, bf16[256,512]{1,0:T(8,128)(2,1)S(1)}, u32[]{:S(2)}, u32[]{:S(2)}) collective-permute-start(bf16[256,512]{1,0:T(8,128)(2,1)S(1)} %get-tuple-element.63.source), channel_id=1, source_target_pairs={{0,1},{1,3},{2,0},{3,2},{4,5},{5,4},{6,7},{7,6},{8,9},{9,11},{10,8... | collective-permute-start | bytes 786440 | tf_op jit(solution)/shard_map/ppermute | solution.py:350
  9.5 6.8 %collective-permute-start.3 = (bf16[256,512]{1,0:T(8,128)(2,1)S(1)}, bf16[256,512]{1,0:T(8,128)(2,1)S(1)}, u32[]{:S(2)}, u32[]{:S(2)}) collective-permute-start(bf16[256,512]{1,0:T(8,128)(2,1)S(1)} %get-tuple-element.52), channel_id=1, source_target_pairs={{0,1},{1,0},{2,3},{3,5},{4,2},{5,4},{6,7},{7,6},{8,9},{9,8},{10,11... | collective-permute-start | bytes 786440 | tf_op jit(solution)/shard_map/ppermute | solution.py:350
  13.0 6.2 %collective-permute-start.10 = (bf16[256,512]{1,0:T(8,128)(2,1)S(1)}, bf16[256,512]{1,0:T(8,128)(2,1)S(1)}, u32[]{:S(2)}, u32[]{:S(2)}) collective-permute-start(bf16[256,512]{1,0:T(8,128)(2,1)S(1)} %get-tuple-element.64), channel_id=1, source_target_pairs={{0,1},{1,0},{2,3},{3,5},{4,2},{5,4},{6,7},{7,6},{8,9},{9,8},{10,11... | collective-permute-start | bytes 786440 | tf_op jit(solution)/shard_map/ppermute | solution.py:350
  16.9 6.5 %collective-permute-start.4 = (bf16[256,512]{1,0:T(8,128)(2,1)S(1)}, bf16[256,512]{1,0:T(8,128)(2,1)S(1)}, u32[]{:S(2)}, u32[]{:S(2)}) collective-permute-start(bf16[256,512]{1,0:T(8,128)(2,1)S(1)} %get-tuple-element.54), channel_id=1, source_target_pairs={{0,1},{1,0},{2,3},{3,2},{4,5},{5,7},{6,4},{7,6},{8,9},{9,8},{10,11... | collective-permute-start | bytes 786440 | tf_op jit(solution)/shard_map/ppermute | solution.py:350
  19.7 6.5 %collective-permute-start.11 = (bf16[256,512]{1,0:T(8,128)(2,1)S(1)}, bf16[256,512]{1,0:T(8,128)(2,1)S(1)}, u32[]{:S(2)}, u32[]{:S(2)}) collective-permute-start(bf16[256,512]{1,0:T(8,128)(2,1)S(1)} %get-tuple-element.66), channel_id=1, source_target_pairs={{0,1},{1,0},{2,3},{3,2},{4,5},{5,7},{6,4},{7,6},{8,9},{9,8},{10,11... | collective-permute-start | bytes 786440 | tf_op jit(solution)/shard_map/ppermute | solution.py:350
  23.3 4.2 %collective-permute-start.5 = (bf16[256,512]{1,0:T(8,128)(2,1)S(1)}, bf16[256,512]{1,0:T(8,128)(2,1)S(1)}, u32[]{:S(2)}, u32[]{:S(2)}) collective-permute-start(bf16[256,512]{1,0:T(8,128)(2,1)S(1)} %shard_map.71.arrived), channel_id=1, source_target_pairs={{0,1},{1,0},{2,3},{3,2},{4,5},{5,4},{6,7},{7,6},{8,9},{9,8},{10,11... | collective-permute-start | bytes 786440 | tf_op jit(solution)/shard_map/ppermute | solution.py:344
  26.2 5.8 %collective-permute-start.12 = (bf16[256,512]{1,0:T(8,128)(2,1)S(1)}, bf16[256,512]{1,0:T(8,128)(2,1)S(1)}, u32[]{:S(2)}, u32[]{:S(2)}) collective-permute-start(bf16[256,512]{1,0:T(8,128)(2,1)S(1)} %shard_map.75.arrived), channel_id=1, source_target_pairs={{0,1},{1,0},{2,3},{3,2},{4,5},{5,4},{6,7},{7,6},{8,9},{9,8},{10,11... | collective-permute-start | bytes 786440 | tf_op jit(solution)/shard_map/ppermute | solution.py:344
  28.4 7.8 %collective-permute-start.6 = (bf16[128,256]{1,0:T(8,128)(2,1)S(1)}, bf16[128,256]{1,0:T(8,128)(2,1)S(1)}, u32[]{:S(2)}, u32[]{:S(2)}) collective-permute-start(bf16[128,256]{1,0:T(8,128)(2,1)S(1)} %get-tuple-element.60), channel_id=1, source_target_pairs={{0,8},{8,0},{16,24},{24,16},{1,9},{9,1},{17,25},{25,17},{2,10},{10... | collective-permute-start | bytes 196616 | tf_op jit(solution)/shard_map/ppermute | solution.py:355
  30.4 5.9 %collective-permute-start.7 = (bf16[128,256]{1,0:T(8,128)(2,1)S(1)}, bf16[128,256]{1,0:T(8,128)(2,1)S(1)}, u32[]{:S(2)}, u32[]{:S(2)}) collective-permute-start(bf16[128,256]{1,0:T(8,128)(2,1)S(1)} %get-tuple-element.61), channel_id=1, source_target_pairs={{0,16},{8,24},{16,0},{24,8},{1,17},{9,25},{17,1},{25,9},{2,18},{10... | collective-permute-start | bytes 196616 | tf_op jit(solution)/shard_map/ppermute | solution.py:355
  31.9 5.9 %collective-permute-start.8 = (bf16[128,256]{1,0:T(8,128)(2,1)S(1)}, bf16[128,256]{1,0:T(8,128)(2,1)S(1)}, u32[]{:S(2)}, u32[]{:S(2)}) collective-permute-start(bf16[128,256]{1,0:T(8,128)(2,1)S(1)} %get-tuple-element.62), channel_id=1, source_target_pairs={{0,24},{8,16},{16,8},{24,0},{1,25},{9,17},{17,9},{25,1},{2,26},{10... | collective-permute-start | bytes 196616 | tf_op jit(solution)/shard_map/ppermute | solution.py:355
  32.7 5.5 %collective-permute-start.13 = (bf16[128,256]{1,0:T(8,128)(2,1)S(1)}, bf16[128,256]{1,0:T(8,128)(2,1)S(1)}, u32[]{:S(2)}, u32[]{:S(2)}) collective-permute-start(bf16[128,256]{1,0:T(8,128)(2,1)S(1)} %get-tuple-element.70), channel_id=1, source_target_pairs={{0,8},{8,0},{16,24},{24,16},{1,9},{9,1},{17,25},{25,17},{2,10},{10... | collective-permute-start | bytes 196616 | tf_op jit(solution)/shard_map/ppermute | solution.py:355
  34.7 4.4 %collective-permute-start.14 = (bf16[128,256]{1,0:T(8,128)(2,1)S(1)}, bf16[128,256]{1,0:T(8,128)(2,1)S(1)}, u32[]{:S(2)}, u32[]{:S(2)}) collective-permute-start(bf16[128,256]{1,0:T(8,128)(2,1)S(1)} %get-tuple-element.71), channel_id=1, source_target_pairs={{0,16},{8,24},{16,0},{24,8},{1,17},{9,25},{17,1},{25,9},{2,18},{10... | collective-permute-start | bytes 196616 | tf_op jit(solution)/shard_map/ppermute | solution.py:355
  36.2 5.2 %collective-permute-start.15 = (bf16[128,256]{1,0:T(8,128)(2,1)S(1)}, bf16[128,256]{1,0:T(8,128)(2,1)S(1)}, u32[]{:S(2)}, u32[]{:S(2)}) collective-permute-start(bf16[128,256]{1,0:T(8,128)(2,1)S(1)} %get-tuple-element.72), channel_id=1, source_target_pairs={{0,24},{8,16},{16,8},{24,0},{1,25},{9,17},{17,9},{25,1},{2,26},{10... | collective-permute-start | bytes 196616 | tf_op jit(solution)/shard_map/ppermute | solution.py:355
  41.8 4.4 %collective-permute-start.16 = (bf16[128,256]{1,0:T(8,128)(2,1)S(1)}, bf16[128,256]{1,0:T(8,128)(2,1)S(1)}, u32[]{:S(2)}, u32[]{:S(2)}) collective-permute-start(bf16[128,256]{1,0:T(8,128)(2,1)S(1)} %get-tuple-element.74), channel_id=1, source_target_pairs={{0,8},{8,0},{16,24},{24,16},{1,9},{9,1},{17,25},{25,17},{2,10},{10... | collective-permute-start | bytes 196616 | tf_op jit(solution)/shard_map/ppermute | solution.py:355
  42.4 4.4 %collective-permute-start.17 = (bf16[128,256]{1,0:T(8,128)(2,1)S(1)}, bf16[128,256]{1,0:T(8,128)(2,1)S(1)}, u32[]{:S(2)}, u32[]{:S(2)}) collective-permute-start(bf16[128,256]{1,0:T(8,128)(2,1)S(1)} %get-tuple-element.75), channel_id=1, source_target_pairs={{0,16},{8,24},{16,0},{24,8},{1,17},{9,25},{17,1},{25,9},{2,18},{10... | collective-permute-start | bytes 196616 | tf_op jit(solution)/shard_map/ppermute | solution.py:355
  42.9 5.2 %collective-permute-start.18 = (bf16[128,256]{1,0:T(8,128)(2,1)S(1)}, bf16[128,256]{1,0:T(8,128)(2,1)S(1)}, u32[]{:S(2)}, u32[]{:S(2)}) collective-permute-start(bf16[128,256]{1,0:T(8,128)(2,1)S(1)} %get-tuple-element.76), channel_id=1, source_target_pairs={{0,24},{8,16},{16,8},{24,0},{1,25},{9,17},{17,9},{25,1},{2,26},{10... | collective-permute-start | bytes 196616 | tf_op jit(solution)/shard_map/ppermute | solution.py:355

commit v2 on v1

--- a/solution.py
+++ b/solution.py
@@ -126,7 +126,7 @@
 
 
 def second_kernel(
-    blocks, retarded, coupling, greater, later_steps, first_step, sources, totals
+    blocks, retarded, coupling, greater, later_steps, first_step, sources, total, whole
 ):
     state = chain = None
     for k in range(blocks):
@@ -140,17 +140,16 @@
             step = later_steps[k - 1]
             chain = product(step, chain)
             state = advance(state, step, source)
-    totals[0] = state
-    totals[1] = chain
-
-
-def join_lesser_kernel(lower, totals, upper, out):
-    out[...] = advance(lower[...], totals[1], upper[...])
-
-
-def join_greater_kernel(lower, upper, out, whole):
-    out[...] = advance(lower[0], upper[1], upper[0])
-    whole[...] = product(upper[1], lower[1])
+    total[...] = state
+    whole[...] = chain
+
+
+def join_kernel(lower, whole, upper, out):
+    out[...] = advance(lower[...], whole[...], upper[...])
+
+
+def chain_kernel(later, earlier, out):
+    out[...] = product(later[...], earlier[...])
 
 
 def keep(z, state, kept, out):
@@ -173,6 +172,29 @@
 
 def keep_kernel(z, state, *refs):
     keep(z, state, refs[0] if len(refs) == 2 else None, refs[-1])
+
+
+def states_of(blocks, first_step, later_steps, sources, lower, total, chip, states):
+    upper = lax.axis_index("domain") & 1
+
+    @pl.when(upper == 0)
+    def _():
+        states[0] = sources[0]
+        if blocks > 1:
+            states[blocks - 1] = total[...]
+
+    @pl.when(upper == 1)
+    def _():
+        if blocks > 1:
+            states[0] = advance(lower[...], first_step[...], sources[0])
+        states[blocks - 1] = chip[...]
+
+    for k in range(1, blocks - 1):
+        states[k] = advance(states[k - 1], later_steps[k - 1], sources[k])
+
+
+def prepare_lesser_kernel(blocks, *refs):
+    states_of(blocks, *refs)
 
 
 def prepare_kernel(
@@ -183,17 +205,20 @@
     offsets,
     first_step,
     later_steps,
-    lesser_sources,
     greater_sources,
-    lower_lesser,
-    lower_totals,
+    lower_great,
+    great_total,
+    chip_great,
+    lower_whole,
+    whole,
+    chip_whole,
+    lessers,
     lefts,
     rights,
     lesser_parts,
     greater_parts,
     shifts,
     chains,
-    lessers,
     greaters,
     held_tiles,
     held_offsets,
@@ -210,24 +235,30 @@
     order = first_step.shape[0]
     half = order // 2
     rows = blocks * chosen * half // energies
+    states_of(
+        blocks,
+        first_step,
+        later_steps,
+        greater_sources,
+        lower_great,
+        great_total,
+        chip_great,
+        greaters,
+    )
 
     @pl.when(upper == 0)
     def _():
         chains[0] = first_step[...]
-        lessers[0] = lesser_sources[0]
-        greaters[0] = greater_sources[0]
+        chains[blocks - 1] = whole[...]
 
     @pl.when(upper == 1)
     def _():
-        chains[0] = product(first_step[...], lower_totals[1])
-        lessers[0] = advance(lower_lesser[...], first_step[...], lesser_sources[0])
-        greaters[0] = advance(lower_totals[0], first_step[...], greater_sources[0])
-
-    for k in range(1, blocks):
-        step = later_steps[k - 1]
-        chains[k] = product(step, chains[k - 1])
-        lessers[k] = advance(lessers[k - 1], step, lesser_sources[k])
-        greaters[k] = advance(greaters[k - 1], step, greater_sources[k])
+        if blocks > 1:
+            chains[0] = product(first_step[...], lower_whole[...])
+        chains[blocks - 1] = chip_whole[...]
+
+    for k in range(1, blocks - 1):
+        chains[k] = product(later_steps[k - 1], chains[k - 1])
     for copy in copies:
         copy.wait()
     for k in range(energies):
@@ -241,16 +272,15 @@
         mine = slice(k * rows, (k + 1) * rows)
         lefts[mine] = chains[block, pl.ds(row, rows), :]
         rights[k] = stacked(chains[block, pl.ds(column, half), :])
-        for whole, parts in ((lessers, lesser_parts), (greaters, greater_parts)):
+        for states, parts in ((lessers, lesser_parts), (greaters, greater_parts)):
             for part in range(2):
                 at = pl.ds(pl.multiple_of(column + part * order, half), half)
-                parts[mine, part * half : (part + 1) * half] = whole[
+                parts[mine, part * half : (part + 1) * half] = states[
                     block, pl.ds(row, rows), at
                 ]
 
 
-def finish_kernel(energies, arrived, near, lefts, rights, parts, *refs):
-    pieces, doubled = refs[:energies], refs[energies]
+def finish(energies, arrived, near, lefts, rights, parts, doubled, write):
     rows = parts.shape[0] // energies
     upper = lax.axis_index("domain") & 1
 
@@ -265,22 +295,39 @@
     moved = times(lefts[...], doubled[...]).astype(BF16)
     for k in range(energies):
         mine = slice(k * rows, (k + 1) * rows)
-        pieces[k][...] = (
-            times_adjoint(moved[mine], rights[k]) + parts[mine].astype(F32)
-        ).astype(BF16)
+        write(
+            k,
+            (times_adjoint(moved[mine], rights[k]) + parts[mine].astype(F32)).astype(BF16),
+        )
+
+
+def finish_lesser_kernel(energies, arrived, near, lefts, rights, parts, out, doubled):
+    def write(k, value):
+        out[k] = value
+
+    finish(energies, arrived, near, lefts, rights, parts, doubled, write)
+
+
+def finish_greater_kernel(energies, arrived, near, lefts, rights, parts, lesser, *refs):
+    pieces, doubled = refs[:energies], refs[energies]
+
+    def write(k, value):
+        pieces[k][0] = lesser[k]
+        pieces[k][1] = value
+
+    finish(energies, arrived, near, lefts, rights, parts, doubled, write)
 
 
 def convolve_kernel(energies, shifts, *refs):
-    less, great = refs[:energies], refs[energies : 2 * energies]
-    outs = refs[2 * energies : 3 * energies]
-    held_less, held_great = refs[3 * energies :]
+    pieces, outs = refs[:energies], refs[energies : 2 * energies]
+    held_less, held_great = refs[2 * energies :]
     group = lax.axis_index("energy")
-    rows, width = less[0].shape
+    rows, width = outs[0].shape
     half = width // 2
     reach = energies // 2
     for k in range(energies):
-        held_less[group ^ k] = less[k][...]
-        held_great[group ^ k] = great[k][...]
+        held_less[group ^ k] = pieces[k][0]
+        held_great[group ^ k] = pieces[k][1]
     chunk = 16
     for start in range(0, rows, chunk):
         at = slice(start, start + chunk)
@@ -368,40 +415,53 @@
         )
     )
     lower_less = swap(less_total)
-    first_step, great_sources, totals = kernel_call(
+    first_step, great_sources, great_total, whole = kernel_call(
         functools.partial(second_kernel, blocks),
-        [block, series(blocks), series(2)],
+        [block, series(blocks), block, block],
         (held_retarded, held_coupling, held_greater, later_steps),
         (5 * blocks - 2) * unit,
     )
-    lower_totals = swap(totals)
+    lower_great = swap(great_total)
+    lower_whole = swap(whole)
     (chip_less,) = kernel_call(
-        join_lesser_kernel, [block], (lower_less, totals, less_total), 2 * unit
-    )
-    chip_great, chip_whole = kernel_call(
-        join_greater_kernel, [block] * 2, (lower_totals, totals), 3 * unit
-    )
+        join_kernel, [block], (lower_less, whole, less_total), 2 * unit
+    )
+    (chip_great,) = kernel_call(
+        join_kernel, [block], (lower_great, whole, great_total), 2 * unit
+    )
+    (chip_whole,) = kernel_call(chain_kernel, [block], (whole, lower_whole), unit)
+    (lessers,) = kernel_call(
+        functools.partial(prepare_lesser_kernel, blocks),
+        [series(blocks)],
+        (first_step, later_steps, less_sources, lower_less, less_total, chip_less),
+        2 * unit,
+    )
+    part = jax.ShapeDtypeStruct((energies * rows, order), BF16)
     lefts, rights, less_parts, great_parts, shifts = kernel_call(
         functools.partial(prepare_kernel, blocks, energies, chosen),
         [
             jax.ShapeDtypeStruct((energies * rows, 2 * order), BF16),
             jax.ShapeDtypeStruct((energies, order, 2 * order), BF16),
-            jax.ShapeDtypeStruct((energies * rows, order), BF16),
-            jax.ShapeDtypeStruct((energies * rows, order), BF16),
+            part,
+            part,
             jax.ShapeDtypeStruct((energies, 8, half), jnp.int32),
         ],
         (
             *in_place(tiles, offsets),
             first_step,
             later_steps,
-            less_sources,
             great_sources,
-            lower_less,
-            lower_totals,
+            lower_great,
+            great_total,
+            chip_great,
+            lower_whole,
+            whole,
+            chip_whole,
+            lessers,
         ),
-        5 * blocks * unit,
-        in_specs=[HBM] * 2 + [VMEM] * 6,
-        scratch=[pltpu.VMEM((blocks, order, 2 * order), BF16)] * 3
+        3 * unit,
+        in_specs=[HBM] * 2 + [VMEM] * 10,
+        scratch=[pltpu.VMEM((blocks, order, 2 * order), BF16)] * 2
         + [
             pltpu.SMEM(tiles.shape, jnp.int32),
             pltpu.SMEM(offsets.shape, jnp.int32),
@@ -421,17 +481,6 @@
         return kernel_call(
             functools.partial(keep_kernel, chips - 1), [block], (state, *kept), 0
         )
-
-    def finish(arrived, parts):
-        near = swap(arrived)
-        pieces = kernel_call(
-            functools.partial(finish_kernel, energies),
-            [piece] * energies,
-            (arrived, near, lefts, rights, parts),
-            3 * unit,
-            scratch=[pltpu.VMEM((2 * order, 2 * order), BF16)],
-        )
-        return [pieces[0]] + [across(pieces[k], k) for k in range(1, energies)]
 
     less, great = chip_less, chip_great
     less_in, great_in = (), ()
@@ -443,12 +492,33 @@
         else:
             less_in = keep_last(less, less_in)
             great_in = keep_last(great, great_in)
-    less_pieces = finish(less_in[0], less_parts)
-    great_pieces = finish(great_in[0], great_parts)
+    doubled = [pltpu.VMEM((2 * order, 2 * order), BF16)]
+    (less_pieces,) = kernel_call(
+        functools.partial(finish_lesser_kernel, energies),
+        [jax.ShapeDtypeStruct((energies, rows, order), BF16)],
+        (*less_in, swap(*less_in), lefts, rights, less_parts),
+        3 * unit,
+        scratch=doubled,
+    )
+    pieces = kernel_call(
+        functools.partial(finish_greater_kernel, energies),
+        [jax.ShapeDtypeStruct((2, rows, order), BF16)] * energies,
+        (
+            *great_in,
+            swap(*great_in),
+            lefts,
+            rights,
+            great_parts,
+            less_pieces,
+        ),
+        3 * unit,
+        scratch=doubled,
+    )
+    pieces = [pieces[0]] + [across(pieces[k], k) for k in range(1, energies)]
     shares = kernel_call(
         functools.partial(convolve_kernel, energies),
         [piece] * energies,
-        (shifts, *less_pieces, *great_pieces),
+        (shifts, *pieces),
         8 * energies * energies * rows * half,
         scratch=[pltpu.VMEM((energies, rows, order), BF16)] * 2,
     )

time: 48.9 us -> 46.8 us (0.957)
  starting transfers between devices: 20 us -> 17.2 us
  waiting for transfers between devices: 16.9 us -> 17.6 us
    ppermute x9 -> x6, starting transfers between devices: 10.7 us -> 7.11 us  [across(): return lax.ppermute(x, 'energy', [(e, e ^ k) for e in range(energies)])]
    ppermute x9 -> x6, waiting for transfers between devices: 7.89 us -> 11.2 us  [across(): return lax.ppermute(x, 'energy', [(e, e ^ k) for e in range(energies)])]
    ppermute x4 -> x5, waiting for transfers between devices: 1.78 us -> 0.1 us  [swap(): return lax.ppermute(x, 'domain', [(d, d ^ 1) for d in range(domains)])]
    ppermute x6, waiting for transfers between devices: 7.18 us -> 6.24 us  [hop(): lax.ppermute(x, 'domain', [(d, route.get(d, d ^ 1)) for d in range(domain...]
    ppermute x6, starting transfers between devices: 8.62 us -> 9.27 us  [hop(): lax.ppermute(x, 'domain', [(d, route.get(d, d ^ 1)) for d in range(domain...]
    pallas_call x15 -> x17, Pallas kernels: 11.8 us -> 11.7 us  [kernel_call(): pl.pallas_call(body, out_shape=outs, in_specs=in_specs or [VMEM] * len(op...]
  transfers between devices with their start and end apart: 19 -> 17, of which waited for: 13 -> 10; matrix products, arithmetic and copies ran while one was open for 0% -> 0% of each run, Pallas kernels for 13% -> 15%
where the time goes in v2:
time: 46.8 us; the launch traced here: 46.6 us
  waiting for transfers between devices  17.6 us (38%)
  starting transfers between devices  17.2 us (37%)
  Pallas kernels  11.7 us (25%)
    pallas_call x17, Pallas kernels, kernel_call(): pl.pallas_call(body, out_shape=outs, in_specs=in_specs or [VMEM] * len(op...  11.7 us
    ppermute x6, waiting for transfers between devices, across(): return lax.ppermute(x, 'energy', [(e, e ^ k) for e in range(energies)])  11.2 us
    ppermute x6, starting transfers between devices, hop(): lax.ppermute(x, 'domain', [(d, route.get(d, d ^ 1)) for d in range(domain...  9.27 us
    ppermute x6, starting transfers between devices, across(): return lax.ppermute(x, 'energy', [(e, e ^ k) for e in range(energies)])  7.11 us
    ppermute x6, waiting for transfers between devices, hop(): lax.ppermute(x, 'domain', [(d, route.get(d, d ^ 1)) for d in range(domain...  6.24 us
  transfers between devices with their start and end apart: 17, of which 10 were waited for; matrix products, arithmetic and copies ran while one was open for 0% of the time, Pallas kernels for 15%

profile of v2, /device:TPU:16, one launch (start us, length us, event | category | flops | bytes accessed | tf_op | source)
XLA Modules:
  0.0 46.6 jit_solution(12970939701328319124)
XLA Ops:
  0.0 3.0 %shard_map.64 = (bf16[2,256,512]{2,1,0:T(8,128)(2,1)S(1)}, bf16[2,256,512]{2,1,0:T(8,128)(2,1)S(1)}, bf16[2,256,512]{2,1,0:T(8,128)(2,1)S(1)}, bf16[1,256,512]{2...) custom-call(bf16[1,2,256,512]{3,2,1,0:T(8,128)(2,1)} %retarded.1, ...), custom_call_target="tpu_custom_call" | custom-call | flops 939524096 | bytes 4718592 | tf_op jit(solution)/shard_map/pallas_call | solution.py:54
  3.0 0.1 collective-permute-start.2
  3.1 1.5 %shard_map.65 = (bf16[256,512]{1,0:T(8,128)(2,1)S(1)}, bf16[2,256,512]{2,1,0:T(8,128)(2,1)S(1)}, bf16[256,512]{1,0:T(8,128)(2,1)S(1)}, bf16[256,512]{1,0:T(8,128)(2,1)S(1)}) custom-call(bf16[2,256,512]{2,1,0:T(8,128)(2,1)S(1)} %get-tuple-element.36.retarded, bf16[2,256,512]{2,1,0:T(8,128)(2,1)S(1)} %get-tuple-element.37.coupling, ...), custom_call_target="tpu_custom_call" | custom-call | flops 1073741824 | bytes 3145728 | tf_op jit(solution)/shard_map/pallas_call | solution.py:54
  4.6 0.6 %collective-permute-start = (bf16[256,512]{1,0:T(8,128)(2,1)S(1)}, bf16[256,512]{1,0:T(8,128)(2,1)S(1)}, u32[]{:S(2)}, u32[]{:S(2)}) collective-permute-start(bf16[256,512]{1,0:T(8,128)(2,1)S(1)} %get-tuple-element.42.upper.great_total), channel_id=1, source_target_pairs={{0,1},{1,0},{2,3},{3,2},{4,5},{5,4},{6,7},{7,6},{8,9},{9,8},{10,11... | collective-permute-start | bytes 786440 | tf_op jit(solution)/shard_map/ppermute | solution.py:391
  5.2 0.1 collective-permute-start.1
  5.2 0.0 collective-permute-done.2.lower.refs_3_
  5.2 0.5 %shard_map.68.refs_5_.source = bf16[256,512]{1,0:T(8,128)(2,1)S(1)} custom-call(bf16[256,512]{1,0:T(8,128)(2,1)S(1)} %collective-permute-done.2.lower.refs_3_, bf16[256,512]{1,0:T(8,128)(2,1)S(1)} %get-tuple-element.43.whole.later, bf16[256,512]{1,0:T(8,128)(2,1)S(1)} %get-tuple-element.45.upper.refs_4_), custom_call_target="tpu_custom_call" | custom-call | flops 268435456 | bytes 1048576 | tf_op jit(solution)/shard_map/pallas_call | solution.py:54
  5.8 0.5 collective-permute-start.7
  6.2 0.1 collective-permute-done.lower.lower_great
  6.3 0.5 %shard_map.66.chip_great.source = bf16[256,512]{1,0:T(8,128)(2,1)S(1)} custom-call(bf16[256,512]{1,0:T(8,128)(2,1)S(1)} %collective-permute-done.lower.lower_great, bf16[256,512]{1,0:T(8,128)(2,1)S(1)} %get-tuple-element.43.whole.later, bf16[256,512]{1,0:T(8,128)(2,1)S(1)} %get-tuple-element.42.upper.great_total), custom_call_target="tpu_custom_call" | custom-call | flops 268435456 | bytes 1048576 | tf_op jit(solution)/shard_map/pallas_call | solution.py:54
  6.8 0.4 collective-permute-start.3
  7.3 0.0 collective-permute-done.1.earlier.lower_whole
  7.3 0.3 shard_map.67.chip_whole.step
  7.6 0.0 collective-permute-done.7.state
  7.6 0.5 %shard_map.74 = (bf16[256,512]{1,0:T(8,128)(2,1)S(1)}, bf16[256,512]{1,0:T(8,128)(2,1)S(1)}) custom-call(bf16[256,512]{1,0:T(8,128)(2,1)S(1)} %collective-permute-done.7.state, bf16[256,512]{1,0:T(8,128)(2,1)S(1)} %shard_map.67.chip_whole.step, bf16[256,512]{1,0:T(8,128)(2,1)S(1)} %shard_map.68.refs_5_.source), custom_call_target="tpu_custom_call" | custom-call | flops 268435456 | bytes 1310720 | tf_op jit(solution)/shard_map/pallas_call | solution.py:54
  8.1 2.6 %collective-permute-start.8 = (bf16[256,512]{1,0:T(8,128)(2,1)S(1)}, bf16[256,512]{1,0:T(8,128)(2,1)S(1)}, u32[]{:S(2)}, u32[]{:S(2)}) collective-permute-start(bf16[256,512]{1,0:T(8,128)(2,1)S(1)} %get-tuple-element.54), channel_id=1, source_target_pairs={{0,1},{1,0},{2,3},{3,5},{4,2},{5,4},{6,7},{7,6},{8,9},{9,8},{10,11... | collective-permute-start | bytes 786440 | tf_op jit(solution)/shard_map/ppermute | solution.py:397
  10.8 0.0 collective-permute-done.3.state
  10.8 0.5 %shard_map.71 = (bf16[256,512]{1,0:T(8,128)(2,1)S(1)}, bf16[256,512]{1,0:T(8,128)(2,1)S(1)}) custom-call(bf16[256,512]{1,0:T(8,128)(2,1)S(1)} %collective-permute-done.3.state, bf16[256,512]{1,0:T(8,128)(2,1)S(1)} %shard_map.67.chip_whole.step, bf16[256,512]{1,0:T(8,128)(2,1)S(1)} %shard_map.66.chip_great.source), custom_call_target="tpu_custom_call" | custom-call | flops 268435456 | bytes 1310720 | tf_op jit(solution)/shard_map/pallas_call | solution.py:54
  11.3 2.3 %collective-permute-start.4 = (bf16[256,512]{1,0:T(8,128)(2,1)S(1)}, bf16[256,512]{1,0:T(8,128)(2,1)S(1)}, u32[]{:S(2)}, u32[]{:S(2)}) collective-permute-start(bf16[256,512]{1,0:T(8,128)(2,1)S(1)} %get-tuple-element.47), channel_id=1, source_target_pairs={{0,1},{1,0},{2,3},{3,5},{4,2},{5,4},{6,7},{7,6},{8,9},{9,8},{10,11... | collective-permute-start | bytes 786440 | tf_op jit(solution)/shard_map/ppermute | solution.py:397
  13.6 1.1 %collective-permute-done.8.state = bf16[256,512]{1,0:T(8,128)(2,1)S(1)} collective-permute-done((bf16[256,512]{1,0:T(8,128)(2,1)S(1)}, bf16[256,512]{1,0:T(8,128)(2,1)S(1)}, u32[]{:S(2)}, u32[]{:S(2)}) %collective-permute-start.8) | collective-permute-done | bytes 262176 | tf_op jit(solution)/shard_map/ppermute | solution.py:397
  14.7 0.5 %shard_map.75 = (bf16[256,512]{1,0:T(8,128)(2,1)S(1)}, bf16[256,512]{1,0:T(8,128)(2,1)S(1)}) custom-call(bf16[256,512]{1,0:T(8,128)(2,1)S(1)} %collective-permute-done.8.state, bf16[256,512]{1,0:T(8,128)(2,1)S(1)} %shard_map.67.chip_whole.step, bf16[256,512]{1,0:T(8,128)(2,1)S(1)} %shard_map.68.refs_5_.source, bf16[256,512]{1,0:T(8,128)(2,1)S(1)} %get-tuple-element.55.refs_0_), custom_call_target="tpu_custom_call" | custom-call | flops 268435456 | bytes 1572864 | tf_op jit(solution)/shard_map/pallas_call | solution.py:54
  15.2 1.4 %collective-permute-start.9 = (bf16[256,512]{1,0:T(8,128)(2,1)S(1)}, bf16[256,512]{1,0:T(8,128)(2,1)S(1)}, u32[]{:S(2)}, u32[]{:S(2)}) collective-permute-start(bf16[256,512]{1,0:T(8,128)(2,1)S(1)} %get-tuple-element.56), channel_id=1, source_target_pairs={{0,1},{1,0},{2,3},{3,2},{4,5},{5,7},{6,4},{7,6},{8,9},{9,8},{10,11... | collective-permute-start | bytes 786440 | tf_op jit(solution)/shard_map/ppermute | solution.py:397
  16.7 0.8 %collective-permute-done.4.state = bf16[256,512]{1,0:T(8,128)(2,1)S(1)} collective-permute-done((bf16[256,512]{1,0:T(8,128)(2,1)S(1)}, bf16[256,512]{1,0:T(8,128)(2,1)S(1)}, u32[]{:S(2)}, u32[]{:S(2)}) %collective-permute-start.4) | collective-permute-done | bytes 262176 | tf_op jit(solution)/shard_map/ppermute | solution.py:397
  17.5 0.5 %shard_map.72 = (bf16[256,512]{1,0:T(8,128)(2,1)S(1)}, bf16[256,512]{1,0:T(8,128)(2,1)S(1)}) custom-call(bf16[256,512]{1,0:T(8,128)(2,1)S(1)} %collective-permute-done.4.state, bf16[256,512]{1,0:T(8,128)(2,1)S(1)} %shard_map.67.chip_whole.step, bf16[256,512]{1,0:T(8,128)(2,1)S(1)} %shard_map.66.chip_great.source, bf16[256,512]{1,0:T(8,128)(2,1)S(1)} %get-tuple-element.48.refs_0_), custom_call_target="tpu_custom_call" | custom-call | flops 268435456 | bytes 1572864 | tf_op jit(solution)/shard_map/pallas_call | solution.py:54
  18.0 2.0 %collective-permute-start.5 = (bf16[256,512]{1,0:T(8,128)(2,1)S(1)}, bf16[256,512]{1,0:T(8,128)(2,1)S(1)}, u32[]{:S(2)}, u32[]{:S(2)}) collective-permute-start(bf16[256,512]{1,0:T(8,128)(2,1)S(1)} %get-tuple-element.49), channel_id=1, source_target_pairs={{0,1},{1,0},{2,3},{3,2},{4,5},{5,7},{6,4},{7,6},{8,9},{9,8},{10,11... | collective-permute-start | bytes 786440 | tf_op jit(solution)/shard_map/ppermute | solution.py:397
  20.1 1.6 %collective-permute-done.9.state = bf16[256,512]{1,0:T(8,128)(2,1)S(1)} collective-permute-done((bf16[256,512]{1,0:T(8,128)(2,1)S(1)}, bf16[256,512]{1,0:T(8,128)(2,1)S(1)}, u32[]{:S(2)}, u32[]{:S(2)}) %collective-permute-start.9) | collective-permute-done | bytes 262176 | tf_op jit(solution)/shard_map/ppermute | solution.py:397
  21.7 0.1 collective-permute-start.10
  21.8 2.7 %collective-permute-done.5.state = bf16[256,512]{1,0:T(8,128)(2,1)S(1)} collective-permute-done((bf16[256,512]{1,0:T(8,128)(2,1)S(1)}, bf16[256,512]{1,0:T(8,128)(2,1)S(1)}, u32[]{:S(2)}, u32[]{:S(2)}) %collective-permute-start.5) | collective-permute-done | bytes 262176 | tf_op jit(solution)/shard_map/ppermute | solution.py:397
  24.5 0.1 collective-permute-start.6
  24.6 0.1 shard_map.69.lessers
  24.6 1.0 %shard_map.70 = (bf16[512,512]{1,0:T(8,128)(2,1)S(1)}, bf16[4,256,512]{2,1,0:T(8,128)(2,1)S(1)}, bf16[512,256]{1,0:T(8,128)(2,1)S(1)}, bf16[512,256]{1,0:T(8,128)(2,1)S(1)}, s32[4,8,128]{2,1,0:T(8,128)S(1)}) custom-call(s32[2,2]{1,0:T(2,128)} %tiles.1, s32[4]{0:T(128)} %offsets.1, bf16[256,512]{1,0:T(8,128)(2,1)S(1)} %get-tuple-element.40.refs_0_.first_step, ...), custom_call_target="tpu_custom_call" | custom-call | flops 402653184 | bytes 5259296 | tf_op jit(solution)/shard_map/pallas_call | solution.py:54
  25.6 0.0 collective-permute-done.10.near
  25.6 0.8 %shard_map.77.lesser = bf16[4,128,256]{2,1,0:T(8,128)(2,1)S(1)} custom-call(bf16[256,512]{1,0:T(8,128)(2,1)S(1)} %shard_map.76.arrived, bf16[256,512]{1,0:T(8,128)(2,1)S(1)} %collective-permute-done.10.near, bf16[512,512]{1,0:T(8,128)(2,1)S(1)} %get-tuple-element.51.lefts, bf16[4,256,512]{2,1,0:T(8,128)(2,1)S(1)} %get-tuple-element.52.rights, ...), custom_call_target="tpu_custom_call" | custom-call | flops 402653184 | bytes 2621440 | tf_op jit(solution)/shard_map/pallas_call | solution.py:54
  26.4 0.0 collective-permute-done.6.near
  26.4 0.8 %shard_map.78 = (bf16[2,128,256]{2,1,0:T(8,128)(2,1)S(1)}, bf16[2,128,256]{2,1,0:T(8,128)(2,1)S(1)}, bf16[2,128,256]{2,1,0:T(8,128)(2,1)S(1)}, bf16[2,128,256]{2,1,0:T(8,128)(2,1)S(1)}) custom-call(bf16[256,512]{1,0:T(8,128)(2,1)S(1)} %shard_map.73.arrived, bf16[256,512]{1,0:T(8,128)(2,1)S(1)} %collective-permute-done.6.near, ...), custom_call_target="tpu_custom_call" | custom-call | flops 402653184 | bytes 3145728 | tf_op jit(solution)/shard_map/pallas_call | solution.py:54
  27.2 2.0 %collective-permute-start.11 = (bf16[2,128,256]{2,1,0:T(8,128)(2,1)S(1)}, bf16[2,128,256]{2,1,0:T(8,128)(2,1)S(1)}, u32[]{:S(2)}, u32[]{:S(2)}) collective-permute-start(bf16[2,128,256]{2,1,0:T(8,128)(2,1)S(1)} %get-tuple-element.60), channel_id=1, source_target_pairs={{0,8},{8,0},{16,24},{24,16},{1,9},{9,1},{17,25},{25,17},{2,10},{10... | collective-permute-start | bytes 393224 | tf_op jit(solution)/shard_map/ppermute | solution.py:402
  29.2 1.5 %collective-permute-start.12 = (bf16[2,128,256]{2,1,0:T(8,128)(2,1)S(1)}, bf16[2,128,256]{2,1,0:T(8,128)(2,1)S(1)}, u32[]{:S(2)}, u32[]{:S(2)}) collective-permute-start(bf16[2,128,256]{2,1,0:T(8,128)(2,1)S(1)} %get-tuple-element.61), channel_id=1, source_target_pairs={{0,16},{8,24},{16,0},{24,8},{1,17},{9,25},{17,1},{25,9},{2,18},{10... | collective-permute-start | bytes 393224 | tf_op jit(solution)/shard_map/ppermute | solution.py:402
  30.7 0.0 collective-permute-start.13
  30.7 2.5 %collective-permute-done.11.refs_1_ = bf16[2,128,256]{2,1,0:T(8,128)(2,1)S(1)} collective-permute-done((bf16[2,128,256]{2,1,0:T(8,128)(2,1)S(1)}, bf16[2,128,256]{2,1,0:T(8,128)(2,1)S(1)}, u32[]{:S(2)}, u32[]{:S(2)}) %collective-permute-start.11) | collective-permute-done | bytes 131104 | tf_op jit(solution)/shard_map/ppermute | solution.py:402
  33.3 5.0 %collective-permute-done.12.refs_2_ = bf16[2,128,256]{2,1,0:T(8,128)(2,1)S(1)} collective-permute-done((bf16[2,128,256]{2,1,0:T(8,128)(2,1)S(1)}, bf16[2,128,256]{2,1,0:T(8,128)(2,1)S(1)}, u32[]{:S(2)}, u32[]{:S(2)}) %collective-permute-start.12) | collective-permute-done | bytes 131104 | tf_op jit(solution)/shard_map/ppermute | solution.py:402
  38.2 0.0 collective-permute-done.13.refs_3_
  38.2 0.4 shard_map.79
  38.6 1.0 %collective-permute-start.14 = (bf16[128,256]{1,0:T(8,128)(2,1)S(1)}, bf16[128,256]{1,0:T(8,128)(2,1)S(1)}, u32[]{:S(2)}, u32[]{:S(2)}) collective-permute-start(bf16[128,256]{1,0:T(8,128)(2,1)S(1)} %get-tuple-element.64), channel_id=1, source_target_pairs={{0,8},{8,0},{16,24},{24,16},{1,9},{9,1},{17,25},{25,17},{2,10},{10... | collective-permute-start | bytes 196616 | tf_op jit(solution)/shard_map/ppermute | solution.py:402
  39.6 1.1 %collective-permute-start.15 = (bf16[128,256]{1,0:T(8,128)(2,1)S(1)}, bf16[128,256]{1,0:T(8,128)(2,1)S(1)}, u32[]{:S(2)}, u32[]{:S(2)}) collective-permute-start(bf16[128,256]{1,0:T(8,128)(2,1)S(1)} %get-tuple-element.65), channel_id=1, source_target_pairs={{0,16},{8,24},{16,0},{24,8},{1,17},{9,25},{17,1},{25,9},{2,18},{10... | collective-permute-start | bytes 196616 | tf_op jit(solution)/shard_map/ppermute | solution.py:402
  40.8 1.4 %collective-permute-start.16 = (bf16[128,256]{1,0:T(8,128)(2,1)S(1)}, bf16[128,256]{1,0:T(8,128)(2,1)S(1)}, u32[]{:S(2)}, u32[]{:S(2)}) collective-permute-start(bf16[128,256]{1,0:T(8,128)(2,1)S(1)} %get-tuple-element.66), channel_id=1, source_target_pairs={{0,24},{8,16},{16,8},{24,0},{1,25},{9,17},{17,9},{25,1},{2,26},{10... | collective-permute-start | bytes 196616 | tf_op jit(solution)/shard_map/ppermute | solution.py:402
  42.2 0.8 %collective-permute-done.14.refs_1_ = bf16[128,256]{1,0:T(8,128)(2,1)S(1)} collective-permute-done((bf16[128,256]{1,0:T(8,128)(2,1)S(1)}, bf16[128,256]{1,0:T(8,128)(2,1)S(1)}, u32[]{:S(2)}, u32[]{:S(2)}) %collective-permute-start.14) | collective-permute-done | bytes 65568 | tf_op jit(solution)/shard_map/ppermute | solution.py:402
  43.0 1.1 %collective-permute-done.15.refs_2_ = bf16[128,256]{1,0:T(8,128)(2,1)S(1)} collective-permute-done((bf16[128,256]{1,0:T(8,128)(2,1)S(1)}, bf16[128,256]{1,0:T(8,128)(2,1)S(1)}, u32[]{:S(2)}, u32[]{:S(2)}) %collective-permute-start.15) | collective-permute-done | bytes 65568 | tf_op jit(solution)/shard_map/ppermute | solution.py:402
  44.1 1.8 %collective-permute-done.16.refs_3_ = bf16[128,256]{1,0:T(8,128)(2,1)S(1)} collective-permute-done((bf16[128,256]{1,0:T(8,128)(2,1)S(1)}, bf16[128,256]{1,0:T(8,128)(2,1)S(1)}, u32[]{:S(2)}, u32[]{:S(2)}) %collective-permute-start.16) | collective-permute-done | bytes 65568 | tf_op jit(solution)/shard_map/ppermute | solution.py:402
  45.9 0.7 %shard_map.80 = bf16[4,128,256]{2,1,0:T(8,128)(2,1)} custom-call(bf16[128,256]{1,0:T(8,128)(2,1)S(1)} %get-tuple-element.63.refs_0_, bf16[128,256]{1,0:T(8,128)(2,1)S(1)} %collective-permute-done.14.refs_1_, bf16[128,256]{1,0:T(8,128)(2,1)S(1)} %collective-permute-done.15.refs_2_, bf16[128,256]{1,0:T(8,128)(2,1)S(1)} %collective-permute-done.16.refs_3_), custom_call_target="tpu_custom_call" | custom-call | bytes 524288 | tf_op jit(solution)/shard_map/pallas_call | solution.py:54
  (2 shorter events, 0.0 us)
Async XLA Ops:
  3.0 2.2 %collective-permute-start.2 = (bf16[256,512]{1,0:T(8,128)(2,1)S(1)}, bf16[256,512]{1,0:T(8,128)(2,1)S(1)}, u32[]{:S(2)}, u32[]{:S(2)}) collective-permute-start(bf16[256,512]{1,0:T(8,128)(2,1)S(1)} %get-tuple-element.45.upper.refs_4_), channel_id=1, source_target_pairs={{0,1},{1,0},{2,3},{3,2},{4,5},{5,4},{6,7},{7,6},{8,9},{9,8},{10,11... | collective-permute-start | bytes 786440 | tf_op jit(solution)/shard_map/ppermute | solution.py:391
  4.6 1.7 %collective-permute-start = (bf16[256,512]{1,0:T(8,128)(2,1)S(1)}, bf16[256,512]{1,0:T(8,128)(2,1)S(1)}, u32[]{:S(2)}, u32[]{:S(2)}) collective-permute-start(bf16[256,512]{1,0:T(8,128)(2,1)S(1)} %get-tuple-element.42.upper.great_total), channel_id=1, source_target_pairs={{0,1},{1,0},{2,3},{3,2},{4,5},{5,4},{6,7},{7,6},{8,9},{9,8},{10,11... | collective-permute-start | bytes 786440 | tf_op jit(solution)/shard_map/ppermute | solution.py:391
  5.2 2.1 %collective-permute-start.1 = (bf16[256,512]{1,0:T(8,128)(2,1)S(1)}, bf16[256,512]{1,0:T(8,128)(2,1)S(1)}, u32[]{:S(2)}, u32[]{:S(2)}) collective-permute-start(bf16[256,512]{1,0:T(8,128)(2,1)S(1)} %get-tuple-element.43.whole.later), channel_id=1, source_target_pairs={{0,1},{1,0},{2,3},{3,2},{4,5},{5,4},{6,7},{7,6},{8,9},{9,8},{10,11... | collective-permute-start | bytes 786440 | tf_op jit(solution)/shard_map/ppermute | solution.py:391
  5.8 1.8 %collective-permute-start.7 = (bf16[256,512]{1,0:T(8,128)(2,1)S(1)}, bf16[256,512]{1,0:T(8,128)(2,1)S(1)}, u32[]{:S(2)}, u32[]{:S(2)}) collective-permute-start(bf16[256,512]{1,0:T(8,128)(2,1)S(1)} %shard_map.68.refs_5_.source), channel_id=1, source_target_pairs={{0,1},{1,3},{2,0},{3,2},{4,5},{5,4},{6,7},{7,6},{8,9},{9,11},{10,8... | collective-permute-start | bytes 786440 | tf_op jit(solution)/shard_map/ppermute | solution.py:397
  6.8 3.9 %collective-permute-start.3 = (bf16[256,512]{1,0:T(8,128)(2,1)S(1)}, bf16[256,512]{1,0:T(8,128)(2,1)S(1)}, u32[]{:S(2)}, u32[]{:S(2)}) collective-permute-start(bf16[256,512]{1,0:T(8,128)(2,1)S(1)} %shard_map.66.chip_great.source), channel_id=1, source_target_pairs={{0,1},{1,3},{2,0},{3,2},{4,5},{5,4},{6,7},{7,6},{8,9},{9,11},{10,8... | collective-permute-start | bytes 786440 | tf_op jit(solution)/shard_map/ppermute | solution.py:397
  8.1 6.5 %collective-permute-start.8 = (bf16[256,512]{1,0:T(8,128)(2,1)S(1)}, bf16[256,512]{1,0:T(8,128)(2,1)S(1)}, u32[]{:S(2)}, u32[]{:S(2)}) collective-permute-start(bf16[256,512]{1,0:T(8,128)(2,1)S(1)} %get-tuple-element.54), channel_id=1, source_target_pairs={{0,1},{1,0},{2,3},{3,5},{4,2},{5,4},{6,7},{7,6},{8,9},{9,8},{10,11... | collective-permute-start | bytes 786440 | tf_op jit(solution)/shard_map/ppermute | solution.py:397
  11.3 6.2 %collective-permute-start.4 = (bf16[256,512]{1,0:T(8,128)(2,1)S(1)}, bf16[256,512]{1,0:T(8,128)(2,1)S(1)}, u32[]{:S(2)}, u32[]{:S(2)}) collective-permute-start(bf16[256,512]{1,0:T(8,128)(2,1)S(1)} %get-tuple-element.47), channel_id=1, source_target_pairs={{0,1},{1,0},{2,3},{3,5},{4,2},{5,4},{6,7},{7,6},{8,9},{9,8},{10,11... | collective-permute-start | bytes 786440 | tf_op jit(solution)/shard_map/ppermute | solution.py:397
  15.2 6.5 %collective-permute-start.9 = (bf16[256,512]{1,0:T(8,128)(2,1)S(1)}, bf16[256,512]{1,0:T(8,128)(2,1)S(1)}, u32[]{:S(2)}, u32[]{:S(2)}) collective-permute-start(bf16[256,512]{1,0:T(8,128)(2,1)S(1)} %get-tuple-element.56), channel_id=1, source_target_pairs={{0,1},{1,0},{2,3},{3,2},{4,5},{5,7},{6,4},{7,6},{8,9},{9,8},{10,11... | collective-permute-start | bytes 786440 | tf_op jit(solution)/shard_map/ppermute | solution.py:397
  18.0 6.5 %collective-permute-start.5 = (bf16[256,512]{1,0:T(8,128)(2,1)S(1)}, bf16[256,512]{1,0:T(8,128)(2,1)S(1)}, u32[]{:S(2)}, u32[]{:S(2)}) collective-permute-start(bf16[256,512]{1,0:T(8,128)(2,1)S(1)} %get-tuple-element.49), channel_id=1, source_target_pairs={{0,1},{1,0},{2,3},{3,2},{4,5},{5,7},{6,4},{7,6},{8,9},{9,8},{10,11... | collective-permute-start | bytes 786440 | tf_op jit(solution)/shard_map/ppermute | solution.py:397
  21.7 3.9 %collective-permute-start.10 = (bf16[256,512]{1,0:T(8,128)(2,1)S(1)}, bf16[256,512]{1,0:T(8,128)(2,1)S(1)}, u32[]{:S(2)}, u32[]{:S(2)}) collective-permute-start(bf16[256,512]{1,0:T(8,128)(2,1)S(1)} %shard_map.76.arrived), channel_id=1, source_target_pairs={{0,1},{1,0},{2,3},{3,2},{4,5},{5,4},{6,7},{7,6},{8,9},{9,8},{10,11... | collective-permute-start | bytes 786440 | tf_op jit(solution)/shard_map/ppermute | solution.py:391
  24.5 1.9 %collective-permute-start.6 = (bf16[256,512]{1,0:T(8,128)(2,1)S(1)}, bf16[256,512]{1,0:T(8,128)(2,1)S(1)}, u32[]{:S(2)}, u32[]{:S(2)}) collective-permute-start(bf16[256,512]{1,0:T(8,128)(2,1)S(1)} %shard_map.73.arrived), channel_id=1, source_target_pairs={{0,1},{1,0},{2,3},{3,2},{4,5},{5,4},{6,7},{7,6},{8,9},{9,8},{10,11... | collective-permute-start | bytes 786440 | tf_op jit(solution)/shard_map/ppermute | solution.py:391
  27.2 6.1 %collective-permute-start.11 = (bf16[2,128,256]{2,1,0:T(8,128)(2,1)S(1)}, bf16[2,128,256]{2,1,0:T(8,128)(2,1)S(1)}, u32[]{:S(2)}, u32[]{:S(2)}) collective-permute-start(bf16[2,128,256]{2,1,0:T(8,128)(2,1)S(1)} %get-tuple-element.60), channel_id=1, source_target_pairs={{0,8},{8,0},{16,24},{24,16},{1,9},{9,1},{17,25},{25,17},{2,10},{10... | collective-permute-start | bytes 393224 | tf_op jit(solution)/shard_map/ppermute | solution.py:402
  29.2 9.1 %collective-permute-start.12 = (bf16[2,128,256]{2,1,0:T(8,128)(2,1)S(1)}, bf16[2,128,256]{2,1,0:T(8,128)(2,1)S(1)}, u32[]{:S(2)}, u32[]{:S(2)}) collective-permute-start(bf16[2,128,256]{2,1,0:T(8,128)(2,1)S(1)} %get-tuple-element.61), channel_id=1, source_target_pairs={{0,16},{8,24},{16,0},{24,8},{1,17},{9,25},{17,1},{25,9},{2,18},{10... | collective-permute-start | bytes 393224 | tf_op jit(solution)/shard_map/ppermute | solution.py:402
  30.7 7.5 %collective-permute-start.13 = (bf16[2,128,256]{2,1,0:T(8,128)(2,1)S(1)}, bf16[2,128,256]{2,1,0:T(8,128)(2,1)S(1)}, u32[]{:S(2)}, u32[]{:S(2)}) collective-permute-start(bf16[2,128,256]{2,1,0:T(8,128)(2,1)S(1)} %get-tuple-element.62), channel_id=1, source_target_pairs={{0,24},{8,16},{16,8},{24,0},{1,25},{9,17},{17,9},{25,1},{2,26},{10... | collective-permute-start | bytes 393224 | tf_op jit(solution)/shard_map/ppermute | solution.py:402
  38.6 4.3 %collective-permute-start.14 = (bf16[128,256]{1,0:T(8,128)(2,1)S(1)}, bf16[128,256]{1,0:T(8,128)(2,1)S(1)}, u32[]{:S(2)}, u32[]{:S(2)}) collective-permute-start(bf16[128,256]{1,0:T(8,128)(2,1)S(1)} %get-tuple-element.64), channel_id=1, source_target_pairs={{0,8},{8,0},{16,24},{24,16},{1,9},{9,1},{17,25},{25,17},{2,10},{10... | collective-permute-start | bytes 196616 | tf_op jit(solution)/shard_map/ppermute | solution.py:402
  39.6 4.5 %collective-permute-start.15 = (bf16[128,256]{1,0:T(8,128)(2,1)S(1)}, bf16[128,256]{1,0:T(8,128)(2,1)S(1)}, u32[]{:S(2)}, u32[]{:S(2)}) collective-permute-start(bf16[128,256]{1,0:T(8,128)(2,1)S(1)} %get-tuple-element.65), channel_id=1, source_target_pairs={{0,16},{8,24},{16,0},{24,8},{1,17},{9,25},{17,1},{25,9},{2,18},{10... | collective-permute-start | bytes 196616 | tf_op jit(solution)/shard_map/ppermute | solution.py:402
  40.8 5.2 %collective-permute-start.16 = (bf16[128,256]{1,0:T(8,128)(2,1)S(1)}, bf16[128,256]{1,0:T(8,128)(2,1)S(1)}, u32[]{:S(2)}, u32[]{:S(2)}) collective-permute-start(bf16[128,256]{1,0:T(8,128)(2,1)S(1)} %get-tuple-element.66), channel_id=1, source_target_pairs={{0,24},{8,16},{16,8},{24,0},{1,25},{9,17},{17,9},{25,1},{2,26},{10... | collective-permute-start | bytes 196616 | tf_op jit(solution)/shard_map/ppermute | solution.py:402

commit v3 on v2

--- a/solution.py
+++ b/solution.py
@@ -144,8 +144,14 @@
     whole[...] = chain
 
 
-def join_kernel(lower, whole, upper, out):
-    out[...] = advance(lower[...], whole[...], upper[...])
+def join_kernel(every_chip, lower, whole, upper, out):
+    needed = (lax.axis_index("domain") & 1) == 1
+    if not every_chip:
+        needed &= (lax.axis_index("domain") >> 1) == 0
+
+    @pl.when(needed)
+    def _():
+        out[...] = advance(lower[...], whole[...], upper[...])
 
 
 def chain_kernel(later, earlier, out):
@@ -174,6 +180,11 @@
     keep(z, state, refs[0] if len(refs) == 2 else None, refs[-1])
 
 
+def parts_at(energies, rows, half, k):
+    below = energies * (rows + half)
+    return below + (k // 2) * rows, (k % 2) * 2 * half
+
+
 def states_of(blocks, first_step, later_steps, sources, lower, total, chip, states):
     upper = lax.axis_index("domain") & 1
 
@@ -193,8 +204,29 @@
         states[k] = advance(states[k - 1], later_steps[k - 1], sources[k])
 
 
-def prepare_lesser_kernel(blocks, *refs):
-    states_of(blocks, *refs)
+def prepare_lesser_kernel(
+    blocks,
+    whole,
+    joined,
+    first_step,
+    later_steps,
+    sources,
+    lower,
+    total,
+    states,
+    chip,
+):
+    first_chip = (lax.axis_index("domain") >> 1) == 0
+
+    @pl.when(first_chip)
+    def _():
+        chip[...] = joined[...]
+
+    @pl.when(jnp.logical_not(first_chip))
+    def _():
+        chip[...] = advance(lower[...], whole[...], total[...])
+
+    states_of(blocks, first_step, later_steps, sources, lower, total, chip, states)
 
 
 def prepare_kernel(
@@ -213,10 +245,8 @@
     whole,
     chip_whole,
     lessers,
-    lefts,
-    rights,
-    lesser_parts,
-    greater_parts,
+    given,
+    own_parts,
     shifts,
     chains,
     greaters,
@@ -270,64 +300,93 @@
         row = pl.multiple_of((tile // 2) * half + start, 16)
         column = pl.multiple_of((tile % 2) * half, half)
         mine = slice(k * rows, (k + 1) * rows)
-        lefts[mine] = chains[block, pl.ds(row, rows), :]
-        rights[k] = stacked(chains[block, pl.ds(column, half), :])
-        for states, parts in ((lessers, lesser_parts), (greaters, greater_parts)):
-            for part in range(2):
-                at = pl.ds(pl.multiple_of(column + part * order, half), half)
-                parts[mine, part * half : (part + 1) * half] = states[
-                    block, pl.ds(row, rows), at
-                ]
-
-
-def finish(energies, arrived, near, lefts, rights, parts, doubled, write):
-    rows = parts.shape[0] // energies
+        given[mine] = chains[block, pl.ds(row, rows), :]
+        others = slice(energies * rows + k * half, energies * rows + (k + 1) * half)
+        given[others] = chains[block, pl.ds(column, half), :]
+
+        def pick(states):
+            return jnp.concatenate(
+                [
+                    states[
+                        block,
+                        pl.ds(row, rows),
+                        pl.ds(pl.multiple_of(column + part * order, half), half),
+                    ]
+                    for part in range(2)
+                ],
+                axis=1,
+            )
+
+        base, side = parts_at(energies, rows, half, k)
+
+        @pl.when(upper == 0)
+        def _():
+            own_parts[mine] = pick(lessers)
+            given[base : base + rows, side : side + order] = pick(greaters)
+
+        @pl.when(upper == 1)
+        def _():
+            own_parts[mine] = pick(greaters)
+            given[base : base + rows, side : side + order] = pick(lessers)
+
+
+def finish_kernel(energies, lesser, greater, given, taken, own_parts, *refs):
+    pieces, doubled = refs[:energies], refs[energies]
+    rows, order = pieces[0].shape[1:]
+    half = order // 2
     upper = lax.axis_index("domain") & 1
 
+    @pl.when(upper == 0)
+    def _():
+        doubled[...] = stacked(lesser[...])
+
     @pl.when(upper == 1)
     def _():
-        doubled[...] = stacked(arrived[...])
-
-    @pl.when(upper == 0)
-    def _():
-        doubled[...] = stacked(near[...])
-
-    moved = times(lefts[...], doubled[...]).astype(BF16)
+        doubled[...] = stacked(greater[...])
+
+    for source, slot in ((given, upper), (taken, 1 - upper)):
+        moved = times(source[: energies * rows], doubled[...]).astype(BF16)
+        for k in range(energies):
+            first = energies * rows + k * half
+            right = stacked(source[first : first + half])
+            if source is given:
+                part = own_parts[k * rows : (k + 1) * rows]
+            else:
+                base, side = parts_at(energies, rows, half, k)
+                part = source[base : base + rows, side : side + order]
+            pieces[k][slot] = (
+                times_adjoint(moved[k * rows : (k + 1) * rows], right) + part.astype(F32)
+            ).astype(BF16)
+
+
+def pack_kernel(energies, *refs):
+    pieces, out = refs[:energies], refs[energies]
+    other = 1 - (lax.axis_index("domain") & 1)
     for k in range(energies):
-        mine = slice(k * rows, (k + 1) * rows)
-        write(
-            k,
-            (times_adjoint(moved[mine], rights[k]) + parts[mine].astype(F32)).astype(BF16),
-        )
-
-
-def finish_lesser_kernel(energies, arrived, near, lefts, rights, parts, out, doubled):
-    def write(k, value):
-        out[k] = value
-
-    finish(energies, arrived, near, lefts, rights, parts, doubled, write)
-
-
-def finish_greater_kernel(energies, arrived, near, lefts, rights, parts, lesser, *refs):
-    pieces, doubled = refs[:energies], refs[energies]
-
-    def write(k, value):
-        pieces[k][0] = lesser[k]
-        pieces[k][1] = value
-
-    finish(energies, arrived, near, lefts, rights, parts, doubled, write)
-
-
-def convolve_kernel(energies, shifts, *refs):
+        out[k] = pieces[k][other]
+
+
+def convolve_kernel(energies, shifts, swapped, *refs):
     pieces, outs = refs[:energies], refs[energies : 2 * energies]
+    upper = lax.axis_index("domain") & 1
     held_less, held_great = refs[2 * energies :]
     group = lax.axis_index("energy")
     rows, width = outs[0].shape
     half = width // 2
     reach = energies // 2
-    for k in range(energies):
-        held_less[group ^ k] = pieces[k][0]
-        held_great[group ^ k] = pieces[k][1]
+
+    @pl.when(upper == 0)
+    def _():
+        for k in range(energies):
+            held_less[group ^ k] = pieces[k][0]
+            held_great[group ^ k] = swapped[k]
+
+    @pl.when(upper == 1)
+    def _():
+        for k in range(energies):
+            held_less[group ^ k] = swapped[k]
+            held_great[group ^ k] = pieces[k][1]
+
     chunk = 16
     for start in range(0, rows, chunk):
         at = slice(start, start + chunk)
@@ -392,11 +451,22 @@
 
     def hop(x, z):
         last = 2 * z - 1
-        ring = [last, last + 2, last + 1, last - 1]
-        route = dict(zip(ring, ring[1:] + ring[:1]))
-        return lax.ppermute(
-            x, "domain", [(d, route.get(d, d ^ 1)) for d in range(domains)]
-        )
+        if z < chips - 1 or energies % 2:
+            ring = [last, last + 2, last + 1, last - 1]
+        else:
+            ring = [last, last + 2, last - 1]
+        onward = dict(zip(ring, ring[1:] + ring[:1]))
+        route = []
+        for e in range(energies):
+            for d in range(domains):
+                if d in onward:
+                    target = (e, onward[d])
+                elif d == last + 1:
+                    target = (e ^ 1, d)
+                else:
+                    target = (e, d ^ 1)
+                route.append((e * domains + d, target[0] * domains + target[1]))
+        return lax.ppermute(x, ("energy", "domain"), route)
 
     def across(x, k):
         return lax.ppermute(x, "energy", [(e, e ^ k) for e in range(energies)])
@@ -423,27 +493,32 @@
     )
     lower_great = swap(great_total)
     lower_whole = swap(whole)
-    (chip_less,) = kernel_call(
-        join_kernel, [block], (lower_less, whole, less_total), 2 * unit
+    (joined_less,) = kernel_call(
+        functools.partial(join_kernel, False),
+        [block],
+        (lower_less, whole, less_total),
+        2 * unit,
     )
     (chip_great,) = kernel_call(
-        join_kernel, [block], (lower_great, whole, great_total), 2 * unit
+        functools.partial(join_kernel, True),
+        [block],
+        (lower_great, whole, great_total),
+        2 * unit,
     )
     (chip_whole,) = kernel_call(chain_kernel, [block], (whole, lower_whole), unit)
-    (lessers,) = kernel_call(
+    lessers, chip_less = kernel_call(
         functools.partial(prepare_lesser_kernel, blocks),
-        [series(blocks)],
-        (first_step, later_steps, less_sources, lower_less, less_total, chip_less),
-        2 * unit,
-    )
-    part = jax.ShapeDtypeStruct((energies * rows, order), BF16)
-    lefts, rights, less_parts, great_parts, shifts = kernel_call(
+        [series(blocks), block],
+        (whole, joined_less, first_step, later_steps, less_sources, lower_less, less_total),
+        4 * unit,
+    )
+    given, own_parts, shifts = kernel_call(
         functools.partial(prepare_kernel, blocks, energies, chosen),
         [
-            jax.ShapeDtypeStruct((energies * rows, 2 * order), BF16),
-            jax.ShapeDtypeStruct((energies, order, 2 * order), BF16),
-            part,
-            part,
+            jax.ShapeDtypeStruct(
+                (energies * (rows + half) + pl.cdiv(energies, 2) * rows, 2 * order), BF16
+            ),
+            jax.ShapeDtypeStruct((energies * rows, order), BF16),
             jax.ShapeDtypeStruct((energies, 8, half), jnp.int32),
         ],
         (
@@ -469,6 +544,8 @@
         ],
     )
 
+    taken = swap(given)
+
     def step_on(z, state, kept, source):
         return kernel_call(
             functools.partial(advance_kernel, z),
@@ -482,7 +559,7 @@
             functools.partial(keep_kernel, chips - 1), [block], (state, *kept), 0
         )
 
-    less, great = chip_less, chip_great
+    less, great = joined_less, chip_great
     less_in, great_in = (), ()
     for z in range(1, chips):
         less, great = hop(less, z), hop(great, z)
@@ -492,33 +569,24 @@
         else:
             less_in = keep_last(less, less_in)
             great_in = keep_last(great, great_in)
-    doubled = [pltpu.VMEM((2 * order, 2 * order), BF16)]
-    (less_pieces,) = kernel_call(
-        functools.partial(finish_lesser_kernel, energies),
+    pieces = kernel_call(
+        functools.partial(finish_kernel, energies),
+        [jax.ShapeDtypeStruct((2, rows, order), BF16)] * energies,
+        (swap(*less_in), *great_in, given, taken, own_parts),
+        6 * unit,
+        scratch=[pltpu.VMEM((2 * order, 2 * order), BF16)],
+    )
+    pieces = [pieces[0]] + [across(pieces[k], k) for k in range(1, energies)]
+    (packed,) = kernel_call(
+        functools.partial(pack_kernel, energies),
         [jax.ShapeDtypeStruct((energies, rows, order), BF16)],
-        (*less_in, swap(*less_in), lefts, rights, less_parts),
-        3 * unit,
-        scratch=doubled,
-    )
-    pieces = kernel_call(
-        functools.partial(finish_greater_kernel, energies),
-        [jax.ShapeDtypeStruct((2, rows, order), BF16)] * energies,
-        (
-            *great_in,
-            swap(*great_in),
-            lefts,
-            rights,
-            great_parts,
-            less_pieces,
-        ),
-        3 * unit,
-        scratch=doubled,
-    )
-    pieces = [pieces[0]] + [across(pieces[k], k) for k in range(1, energies)]
+        pieces,
+        0,
+    )
     shares = kernel_call(
         functools.partial(convolve_kernel, energies),
         [piece] * energies,
-        (shifts, *pieces),
+        (shifts, swap(packed), *pieces),
         8 * energies * energies * rows * half,
         scratch=[pltpu.VMEM((energies, rows, order), BF16)] * 2,
     )

time: 46.8 us -> 48.2 us (1.030)
  the two profiles are of different devices: /device:TPU:16 before, /device:TPU:24 now
where the time goes in v3:
time: 48.2 us; the launch traced here: 47.4 us
  waiting for transfers between devices  21.4 us (44%)
  starting transfers between devices  14.9 us (31%)
  Pallas kernels  10.9 us (23%)
    pallas_call x17, Pallas kernels, kernel_call(): pl.pallas_call(body, out_shape=outs, in_specs=in_specs or [VMEM] * len(op...  10.9 us
    ppermute x6, waiting for transfers between devices, across(): return lax.ppermute(x, 'energy', [(e, e ^ k) for e in range(energies)])  10.8 us
    ppermute x6, starting transfers between devices, across(): return lax.ppermute(x, 'energy', [(e, e ^ k) for e in range(energies)])  7.11 us
    ppermute x6, waiting for transfers between devices, hop(): return lax.ppermute(x, ('energy', 'domain'), route)  6.87 us
    ppermute x6, starting transfers between devices, swap(): return lax.ppermute(x, 'domain', [(d, d ^ 1) for d in range(domains)])  4.48 us
    ppermute x6, waiting for transfers between devices, swap(): return lax.ppermute(x, 'domain', [(d, d ^ 1) for d in range(domains)])  3.76 us
    ppermute x6, starting transfers between devices, hop(): return lax.ppermute(x, ('energy', 'domain'), route)  3.32 us
  transfers between devices with their start and end apart: 18, of which 14 were waited for; matrix products, arithmetic and copies ran while one was open for 0% of the time, Pallas kernels for 5%

profile of v3, /device:TPU:24, one launch (start us, length us, event | category | flops | bytes accessed | tf_op | source)
XLA Modules:
  0.0 47.4 jit_solution(1360435971440545748)
XLA Ops:
  0.0 3.0 %shard_map.64 = (bf16[2,256,512]{2,1,0:T(8,128)(2,1)S(1)}, bf16[2,256,512]{2,1,0:T(8,128)(2,1)S(1)}, bf16[2,256,512]{2,1,0:T(8,128)(2,1)S(1)}, bf16[1,256,512]{2...) custom-call(bf16[1,2,256,512]{3,2,1,0:T(8,128)(2,1)} %retarded.1, ...), custom_call_target="tpu_custom_call" | custom-call | flops 939524096 | bytes 4718592 | tf_op jit(solution)/shard_map/pallas_call | solution.py:54
  3.0 1.5 %shard_map.65 = (bf16[256,512]{1,0:T(8,128)(2,1)S(1)}, bf16[2,256,512]{2,1,0:T(8,128)(2,1)S(1)}, bf16[256,512]{1,0:T(8,128)(2,1)S(1)}, bf16[256,512]{1,0:T(8,128)(2,1)S(1)}) custom-call(bf16[2,256,512]{2,1,0:T(8,128)(2,1)S(1)} %get-tuple-element.36.retarded, bf16[2,256,512]{2,1,0:T(8,128)(2,1)S(1)} %get-tuple-element.37.coupling, ...), custom_call_target="tpu_custom_call" | custom-call | flops 1073741824 | bytes 3145728 | tf_op jit(solution)/shard_map/pallas_call | solution.py:54
  4.5 0.1 collective-permute-start.1
  4.6 0.5 %collective-permute-start = (bf16[256,512]{1,0:T(8,128)(2,1)S(1)}, bf16[256,512]{1,0:T(8,128)(2,1)S(1)}, u32[]{:S(2)}, u32[]{:S(2)}) collective-permute-start(bf16[256,512]{1,0:T(8,128)(2,1)S(1)} %get-tuple-element.42.upper.great_total), channel_id=1, source_target_pairs={{0,1},{1,0},{2,3},{3,2},{4,5},{5,4},{6,7},{7,6},{8,9},{9,8},{10,11... | collective-permute-start | bytes 786440 | tf_op jit(solution)/shard_map/ppermute | solution.py:450
  5.1 0.1 collective-permute-start.2
  5.2 0.9 %collective-permute-done.1.earlier.lower_whole = bf16[256,512]{1,0:T(8,128)(2,1)S(1)} collective-permute-done((bf16[256,512]{1,0:T(8,128)(2,1)S(1)}, bf16[256,512]{1,0:T(8,128)(2,1)S(1)}, u32[]{:S(2)}, u32[]{:S(2)}) %collective-permute-start.1) | collective-permute-done | bytes 262176 | tf_op jit(solution)/shard_map/ppermute | solution.py:450
  6.1 0.3 shard_map.67.chip_whole.step
  6.4 0.1 collective-permute-done.lower.lower_great
  6.5 0.4 collective-permute-done.2.lower
  6.9 0.6 %shard_map.69 = (bf16[2,256,512]{2,1,0:T(8,128)(2,1)S(1)}, bf16[256,512]{1,0:T(8,128)(2,1)S(1)}) custom-call(bf16[256,512]{1,0:T(8,128)(2,1)S(1)} %get-tuple-element.43.whole.later, bf16[256,512]{1,0:T(8,128)(2,1)S(1)} %shard_map.68.joined, bf16[256,512]{1,0:T(8,128)(2,1)S(1)} %get-tuple-element.40.first_step, ...), custom_call_target="tpu_custom_call" | custom-call | flops 536870912 | bytes 2883584 | tf_op jit(solution)/shard_map/pallas_call | solution.py:54
  7.4 1.0 %shard_map.70 = (bf16[1280,512]{1,0:T(8,128)(2,1)S(1)}, bf16[512,256]{1,0:T(8,128)(2,1)S(1)}, s32[4,8,128]{2,1,0:T(8,128)S(1)}) custom-call(s32[2,2]{1,0:T(2,128)} %tiles.1, s32[4]{0:T(128)} %offsets.1, bf16[256,512]{1,0:T(8,128)(2,1)S(1)} %get-tuple-element.40.first_step, bf16[1,256,512]{2,1,0:T(8,128)(2,1)S(1)} %get-tuple-element.39.later_steps, ...), custom_call_target="tpu_custom_call" | custom-call | flops 402653184 | bytes 4735008 | tf_op jit(solution)/shard_map/pallas_call | solution.py:54
  8.4 1.1 %collective-permute-start.10 = (bf16[1280,512]{1,0:T(8,128)(2,1)S(1)}, bf16[1280,512]{1,0:T(8,128)(2,1)S(1)}, u32[]{:S(2)}, u32[]{:S(2)}) collective-permute-start(bf16[1280,512]{1,0:T(8,128)(2,1)S(1)} %get-tuple-element.57.given), channel_id=1, source_target_pairs={{0,1},{1,0},{2,3},{3,2},{4,5},{5,4},{6,7},{7,6},{8,9},{9,8},{10,11... | collective-permute-start | bytes 3932168 | tf_op jit(solution)/shard_map/ppermute | solution.py:450
  9.5 0.1 collective-permute-start.3
  9.5 0.5 collective-permute-start.7
  10.0 2.5 %collective-permute-done.3.state = bf16[256,512]{1,0:T(8,128)(2,1)S(1)} collective-permute-done((bf16[256,512]{1,0:T(8,128)(2,1)S(1)}, bf16[256,512]{1,0:T(8,128)(2,1)S(1)}, u32[]{:S(2)}, u32[]{:S(2)}) %collective-permute-start.3) | collective-permute-done | bytes 262176 | tf_op jit(solution)/shard_map/ppermute | solution.py:469
  12.5 0.5 %shard_map.71 = (bf16[256,512]{1,0:T(8,128)(2,1)S(1)}, bf16[256,512]{1,0:T(8,128)(2,1)S(1)}) custom-call(bf16[256,512]{1,0:T(8,128)(2,1)S(1)} %collective-permute-done.3.state, bf16[256,512]{1,0:T(8,128)(2,1)S(1)} %shard_map.67.chip_whole.step, bf16[256,512]{1,0:T(8,128)(2,1)S(1)} %get-tuple-element.48.source), custom_call_target="tpu_custom_call" | custom-call | flops 268435456 | bytes 1310720 | tf_op jit(solution)/shard_map/pallas_call | solution.py:54
  13.0 0.4 collective-permute-start.4
  13.5 0.0 collective-permute-done.7.state
  13.5 0.5 %shard_map.74 = (bf16[256,512]{1,0:T(8,128)(2,1)S(1)}, bf16[256,512]{1,0:T(8,128)(2,1)S(1)}) custom-call(bf16[256,512]{1,0:T(8,128)(2,1)S(1)} %collective-permute-done.7.state, bf16[256,512]{1,0:T(8,128)(2,1)S(1)} %shard_map.67.chip_whole.step, bf16[256,512]{1,0:T(8,128)(2,1)S(1)} %shard_map.66.chip_great.source), custom_call_target="tpu_custom_call" | custom-call | flops 268435456 | bytes 1310720 | tf_op jit(solution)/shard_map/pallas_call | solution.py:54
  14.0 0.2 collective-permute-start.8
  14.2 0.4 collective-permute-done.4.state
  14.6 0.5 %shard_map.72 = (bf16[256,512]{1,0:T(8,128)(2,1)S(1)}, bf16[256,512]{1,0:T(8,128)(2,1)S(1)}) custom-call(bf16[256,512]{1,0:T(8,128)(2,1)S(1)} %collective-permute-done.4.state, bf16[256,512]{1,0:T(8,128)(2,1)S(1)} %shard_map.67.chip_whole.step, bf16[256,512]{1,0:T(8,128)(2,1)S(1)} %get-tuple-element.48.source, bf16[256,512]{1,0:T(8,128)(2,1)S(1)} %get-tuple-element.50.refs_0_), custom_call_target="tpu_custom_call" | custom-call | flops 268435456 | bytes 1572864 | tf_op jit(solution)/shard_map/pallas_call | solution.py:54
  15.2 1.6 %collective-permute-start.5 = (bf16[256,512]{1,0:T(8,128)(2,1)S(1)}, bf16[256,512]{1,0:T(8,128)(2,1)S(1)}, u32[]{:S(2)}, u32[]{:S(2)}) collective-permute-start(bf16[256,512]{1,0:T(8,128)(2,1)S(1)} %get-tuple-element.51), channel_id=1, source_target_pairs={{0,1},{1,0},{2,3},{3,2},{4,5},{5,7},{6,14},{7,4},{8,9},{9,8},{10,1... | collective-permute-start | bytes 786440 | tf_op jit(solution)/shard_map/ppermute | solution.py:469
  16.8 0.0 collective-permute-done.8.state
  16.8 0.5 %shard_map.75 = (bf16[256,512]{1,0:T(8,128)(2,1)S(1)}, bf16[256,512]{1,0:T(8,128)(2,1)S(1)}) custom-call(bf16[256,512]{1,0:T(8,128)(2,1)S(1)} %collective-permute-done.8.state, bf16[256,512]{1,0:T(8,128)(2,1)S(1)} %shard_map.67.chip_whole.step, bf16[256,512]{1,0:T(8,128)(2,1)S(1)} %shard_map.66.chip_great.source, bf16[256,512]{1,0:T(8,128)(2,1)S(1)} %get-tuple-element.54.refs_0_), custom_call_target="tpu_custom_call" | custom-call | flops 268435456 | bytes 1572864 | tf_op jit(solution)/shard_map/pallas_call | solution.py:54
  17.3 0.6 %collective-permute-start.9 = (bf16[256,512]{1,0:T(8,128)(2,1)S(1)}, bf16[256,512]{1,0:T(8,128)(2,1)S(1)}, u32[]{:S(2)}, u32[]{:S(2)}) collective-permute-start(bf16[256,512]{1,0:T(8,128)(2,1)S(1)} %get-tuple-element.55), channel_id=1, source_target_pairs={{0,1},{1,0},{2,3},{3,2},{4,5},{5,7},{6,14},{7,4},{8,9},{9,8},{10,1... | collective-permute-start | bytes 786440 | tf_op jit(solution)/shard_map/ppermute | solution.py:469
  17.9 3.7 %collective-permute-done.5.state = bf16[256,512]{1,0:T(8,128)(2,1)S(1)} collective-permute-done((bf16[256,512]{1,0:T(8,128)(2,1)S(1)}, bf16[256,512]{1,0:T(8,128)(2,1)S(1)}, u32[]{:S(2)}, u32[]{:S(2)}) %collective-permute-start.5) | collective-permute-done | bytes 262176 | tf_op jit(solution)/shard_map/ppermute | solution.py:469
  21.7 2.6 %collective-permute-start.6 = (bf16[256,512]{1,0:T(8,128)(2,1)S(1)}, bf16[256,512]{1,0:T(8,128)(2,1)S(1)}, u32[]{:S(2)}, u32[]{:S(2)}) collective-permute-start(bf16[256,512]{1,0:T(8,128)(2,1)S(1)} %shard_map.73), channel_id=1, source_target_pairs={{0,1},{1,0},{2,3},{3,2},{4,5},{5,4},{6,7},{7,6},{8,9},{9,8},{10,11... | collective-permute-start | bytes 786440 | tf_op jit(solution)/shard_map/ppermute | solution.py:450
  24.3 0.2 collective-permute-done.9.state
  24.5 1.0 %collective-permute-done.6.lesser = bf16[256,512]{1,0:T(8,128)(2,1)S(1)} collective-permute-done((bf16[256,512]{1,0:T(8,128)(2,1)S(1)}, bf16[256,512]{1,0:T(8,128)(2,1)S(1)}, u32[]{:S(2)}, u32[]{:S(2)}) %collective-permute-start.6) | collective-permute-done | bytes 262176 | tf_op jit(solution)/shard_map/ppermute | solution.py:450
  25.4 0.0 collective-permute-done.10.taken
  25.4 1.3 %shard_map.77 = (bf16[2,128,256]{2,1,0:T(8,128)(2,1)S(1)}, bf16[2,128,256]{2,1,0:T(8,128)(2,1)S(1)}, bf16[2,128,256]{2,1,0:T(8,128)(2,1)S(1)}, bf16[2,128,256]{2,1,0:T(8,128)(2,1)S(1)}) custom-call(bf16[256,512]{1,0:T(8,128)(2,1)S(1)} %collective-permute-done.6.lesser, bf16[256,512]{1,0:T(8,128)(2,1)S(1)} %shard_map.76.greater, ...), custom_call_target="tpu_custom_call" | custom-call | flops 805306368 | bytes 3932160 | tf_op jit(solution)/shard_map/pallas_call | solution.py:54
  26.7 1.6 %collective-permute-start.11 = (bf16[2,128,256]{2,1,0:T(8,128)(2,1)S(1)}, bf16[2,128,256]{2,1,0:T(8,128)(2,1)S(1)}, u32[]{:S(2)}, u32[]{:S(2)}) collective-permute-start(bf16[2,128,256]{2,1,0:T(8,128)(2,1)S(1)} %get-tuple-element.60), channel_id=1, source_target_pairs={{0,8},{8,0},{16,24},{24,16},{1,9},{9,1},{17,25},{25,17},{2,10},{10... | collective-permute-start | bytes 393224 | tf_op jit(solution)/shard_map/ppermute | solution.py:472
  28.3 1.5 %collective-permute-start.12 = (bf16[2,128,256]{2,1,0:T(8,128)(2,1)S(1)}, bf16[2,128,256]{2,1,0:T(8,128)(2,1)S(1)}, u32[]{:S(2)}, u32[]{:S(2)}) collective-permute-start(bf16[2,128,256]{2,1,0:T(8,128)(2,1)S(1)} %get-tuple-element.61), channel_id=1, source_target_pairs={{0,16},{8,24},{16,0},{24,8},{1,17},{9,25},{17,1},{25,9},{2,18},{10... | collective-permute-start | bytes 393224 | tf_op jit(solution)/shard_map/ppermute | solution.py:472
  29.8 0.5 %collective-permute-start.13 = (bf16[2,128,256]{2,1,0:T(8,128)(2,1)S(1)}, bf16[2,128,256]{2,1,0:T(8,128)(2,1)S(1)}, u32[]{:S(2)}, u32[]{:S(2)}) collective-permute-start(bf16[2,128,256]{2,1,0:T(8,128)(2,1)S(1)} %get-tuple-element.62), channel_id=1, source_target_pairs={{0,24},{8,16},{16,8},{24,0},{1,25},{9,17},{17,9},{25,1},{2,26},{10... | collective-permute-start | bytes 393224 | tf_op jit(solution)/shard_map/ppermute | solution.py:472
  30.3 1.9 %collective-permute-done.11.refs_1_ = bf16[2,128,256]{2,1,0:T(8,128)(2,1)S(1)} collective-permute-done((bf16[2,128,256]{2,1,0:T(8,128)(2,1)S(1)}, bf16[2,128,256]{2,1,0:T(8,128)(2,1)S(1)}, u32[]{:S(2)}, u32[]{:S(2)}) %collective-permute-start.11) | collective-permute-done | bytes 131104 | tf_op jit(solution)/shard_map/ppermute | solution.py:472
  32.2 5.2 %collective-permute-done.12.refs_2_ = bf16[2,128,256]{2,1,0:T(8,128)(2,1)S(1)} collective-permute-done((bf16[2,128,256]{2,1,0:T(8,128)(2,1)S(1)}, bf16[2,128,256]{2,1,0:T(8,128)(2,1)S(1)}, u32[]{:S(2)}, u32[]{:S(2)}) %collective-permute-start.12) | collective-permute-done | bytes 131104 | tf_op jit(solution)/shard_map/ppermute | solution.py:472
  37.4 0.0 collective-permute-done.13.refs_3_
  37.4 0.2 collective-permute-start.14
  37.6 1.4 %collective-permute-done.14.swapped = bf16[4,128,256]{2,1,0:T(8,128)(2,1)S(1)} collective-permute-done((bf16[4,128,256]{2,1,0:T(8,128)(2,1)S(1)}, bf16[4,128,256]{2,1,0:T(8,128)(2,1)S(1)}, u32[]{:S(2)}, u32[]{:S(2)}) %collective-permute-start.14) | collective-permute-done | bytes 262176 | tf_op jit(solution)/shard_map/ppermute | solution.py:450
  39.0 0.4 shard_map.79
  39.4 0.7 %collective-permute-start.15 = (bf16[128,256]{1,0:T(8,128)(2,1)S(1)}, bf16[128,256]{1,0:T(8,128)(2,1)S(1)}, u32[]{:S(2)}, u32[]{:S(2)}) collective-permute-start(bf16[128,256]{1,0:T(8,128)(2,1)S(1)} %get-tuple-element.64), channel_id=1, source_target_pairs={{0,8},{8,0},{16,24},{24,16},{1,9},{9,1},{17,25},{25,17},{2,10},{10... | collective-permute-start | bytes 196616 | tf_op jit(solution)/shard_map/ppermute | solution.py:472
  40.2 1.4 %collective-permute-start.16 = (bf16[128,256]{1,0:T(8,128)(2,1)S(1)}, bf16[128,256]{1,0:T(8,128)(2,1)S(1)}, u32[]{:S(2)}, u32[]{:S(2)}) collective-permute-start(bf16[128,256]{1,0:T(8,128)(2,1)S(1)} %get-tuple-element.65), channel_id=1, source_target_pairs={{0,16},{8,24},{16,0},{24,8},{1,17},{9,25},{17,1},{25,9},{2,18},{10... | collective-permute-start | bytes 196616 | tf_op jit(solution)/shard_map/ppermute | solution.py:472
  41.5 1.5 %collective-permute-start.17 = (bf16[128,256]{1,0:T(8,128)(2,1)S(1)}, bf16[128,256]{1,0:T(8,128)(2,1)S(1)}, u32[]{:S(2)}, u32[]{:S(2)}) collective-permute-start(bf16[128,256]{1,0:T(8,128)(2,1)S(1)} %get-tuple-element.66), channel_id=1, source_target_pairs={{0,24},{8,16},{16,8},{24,0},{1,25},{9,17},{17,9},{25,1},{2,26},{10... | collective-permute-start | bytes 196616 | tf_op jit(solution)/shard_map/ppermute | solution.py:472
  43.0 0.8 %collective-permute-done.15.refs_1_ = bf16[128,256]{1,0:T(8,128)(2,1)S(1)} collective-permute-done((bf16[128,256]{1,0:T(8,128)(2,1)S(1)}, bf16[128,256]{1,0:T(8,128)(2,1)S(1)}, u32[]{:S(2)}, u32[]{:S(2)}) %collective-permute-start.15) | collective-permute-done | bytes 65568 | tf_op jit(solution)/shard_map/ppermute | solution.py:472
  43.8 0.7 %collective-permute-done.16.refs_2_ = bf16[128,256]{1,0:T(8,128)(2,1)S(1)} collective-permute-done((bf16[128,256]{1,0:T(8,128)(2,1)S(1)}, bf16[128,256]{1,0:T(8,128)(2,1)S(1)}, u32[]{:S(2)}, u32[]{:S(2)}) %collective-permute-start.16) | collective-permute-done | bytes 65568 | tf_op jit(solution)/shard_map/ppermute | solution.py:472
  44.4 2.3 %collective-permute-done.17.refs_3_ = bf16[128,256]{1,0:T(8,128)(2,1)S(1)} collective-permute-done((bf16[128,256]{1,0:T(8,128)(2,1)S(1)}, bf16[128,256]{1,0:T(8,128)(2,1)S(1)}, u32[]{:S(2)}, u32[]{:S(2)}) %collective-permute-start.17) | collective-permute-done | bytes 65568 | tf_op jit(solution)/shard_map/ppermute | solution.py:472
  46.7 0.7 %shard_map.80 = bf16[4,128,256]{2,1,0:T(8,128)(2,1)} custom-call(bf16[128,256]{1,0:T(8,128)(2,1)S(1)} %get-tuple-element.63.refs_0_, bf16[128,256]{1,0:T(8,128)(2,1)S(1)} %collective-permute-done.15.refs_1_, bf16[128,256]{1,0:T(8,128)(2,1)S(1)} %collective-permute-done.16.refs_2_, bf16[128,256]{1,0:T(8,128)(2,1)S(1)} %collective-permute-done.17.refs_3_), custom_call_target="tpu_custom_call" | custom-call | bytes 524288 | tf_op jit(solution)/shard_map/pallas_call | solution.py:54
  (5 shorter events, 0.1 us)
Async XLA Ops:
  4.5 1.6 %collective-permute-start.1 = (bf16[256,512]{1,0:T(8,128)(2,1)S(1)}, bf16[256,512]{1,0:T(8,128)(2,1)S(1)}, u32[]{:S(2)}, u32[]{:S(2)}) collective-permute-start(bf16[256,512]{1,0:T(8,128)(2,1)S(1)} %get-tuple-element.43.whole.later), channel_id=1, source_target_pairs={{0,1},{1,0},{2,3},{3,2},{4,5},{5,4},{6,7},{7,6},{8,9},{9,8},{10,11... | collective-permute-start | bytes 786440 | tf_op jit(solution)/shard_map/ppermute | solution.py:450
  4.6 1.9 %collective-permute-start = (bf16[256,512]{1,0:T(8,128)(2,1)S(1)}, bf16[256,512]{1,0:T(8,128)(2,1)S(1)}, u32[]{:S(2)}, u32[]{:S(2)}) collective-permute-start(bf16[256,512]{1,0:T(8,128)(2,1)S(1)} %get-tuple-element.42.upper.great_total), channel_id=1, source_target_pairs={{0,1},{1,0},{2,3},{3,2},{4,5},{5,4},{6,7},{7,6},{8,9},{9,8},{10,11... | collective-permute-start | bytes 786440 | tf_op jit(solution)/shard_map/ppermute | solution.py:450
  5.1 1.8 %collective-permute-start.2 = (bf16[256,512]{1,0:T(8,128)(2,1)S(1)}, bf16[256,512]{1,0:T(8,128)(2,1)S(1)}, u32[]{:S(2)}, u32[]{:S(2)}) collective-permute-start(bf16[256,512]{1,0:T(8,128)(2,1)S(1)} %get-tuple-element.44.upper.total), channel_id=1, source_target_pairs={{0,1},{1,0},{2,3},{3,2},{4,5},{5,4},{6,7},{7,6},{8,9},{9,8},{10,11... | collective-permute-start | bytes 786440 | tf_op jit(solution)/shard_map/ppermute | solution.py:450
  8.4 17.0 %collective-permute-start.10 = (bf16[1280,512]{1,0:T(8,128)(2,1)S(1)}, bf16[1280,512]{1,0:T(8,128)(2,1)S(1)}, u32[]{:S(2)}, u32[]{:S(2)}) collective-permute-start(bf16[1280,512]{1,0:T(8,128)(2,1)S(1)} %get-tuple-element.57.given), channel_id=1, source_target_pairs={{0,1},{1,0},{2,3},{3,2},{4,5},{5,4},{6,7},{7,6},{8,9},{9,8},{10,11... | collective-permute-start | bytes 3932168 | tf_op jit(solution)/shard_map/ppermute | solution.py:450
  9.5 3.0 %collective-permute-start.3 = (bf16[256,512]{1,0:T(8,128)(2,1)S(1)}, bf16[256,512]{1,0:T(8,128)(2,1)S(1)}, u32[]{:S(2)}, u32[]{:S(2)}) collective-permute-start(bf16[256,512]{1,0:T(8,128)(2,1)S(1)} %shard_map.68.joined), channel_id=1, source_target_pairs={{0,1},{1,3},{2,0},{3,2},{4,5},{5,4},{6,7},{7,6},{8,9},{9,11},{10,8... | collective-permute-start | bytes 786440 | tf_op jit(solution)/shard_map/ppermute | solution.py:469
  9.5 4.0 %collective-permute-start.7 = (bf16[256,512]{1,0:T(8,128)(2,1)S(1)}, bf16[256,512]{1,0:T(8,128)(2,1)S(1)}, u32[]{:S(2)}, u32[]{:S(2)}) collective-permute-start(bf16[256,512]{1,0:T(8,128)(2,1)S(1)} %shard_map.66.chip_great.source), channel_id=1, source_target_pairs={{0,1},{1,3},{2,0},{3,2},{4,5},{5,4},{6,7},{7,6},{8,9},{9,11},{10,8... | collective-permute-start | bytes 786440 | tf_op jit(solution)/shard_map/ppermute | solution.py:469
  13.0 1.6 %collective-permute-start.4 = (bf16[256,512]{1,0:T(8,128)(2,1)S(1)}, bf16[256,512]{1,0:T(8,128)(2,1)S(1)}, u32[]{:S(2)}, u32[]{:S(2)}) collective-permute-start(bf16[256,512]{1,0:T(8,128)(2,1)S(1)} %get-tuple-element.49), channel_id=1, source_target_pairs={{0,1},{1,0},{2,3},{3,5},{4,2},{5,4},{6,7},{7,6},{8,9},{9,8},{10,11... | collective-permute-start | bytes 786440 | tf_op jit(solution)/shard_map/ppermute | solution.py:469
  14.0 2.8 %collective-permute-start.8 = (bf16[256,512]{1,0:T(8,128)(2,1)S(1)}, bf16[256,512]{1,0:T(8,128)(2,1)S(1)}, u32[]{:S(2)}, u32[]{:S(2)}) collective-permute-start(bf16[256,512]{1,0:T(8,128)(2,1)S(1)} %get-tuple-element.53), channel_id=1, source_target_pairs={{0,1},{1,0},{2,3},{3,5},{4,2},{5,4},{6,7},{7,6},{8,9},{9,8},{10,11... | collective-permute-start | bytes 786440 | tf_op jit(solution)/shard_map/ppermute | solution.py:469
  15.2 6.5 %collective-permute-start.5 = (bf16[256,512]{1,0:T(8,128)(2,1)S(1)}, bf16[256,512]{1,0:T(8,128)(2,1)S(1)}, u32[]{:S(2)}, u32[]{:S(2)}) collective-permute-start(bf16[256,512]{1,0:T(8,128)(2,1)S(1)} %get-tuple-element.51), channel_id=1, source_target_pairs={{0,1},{1,0},{2,3},{3,2},{4,5},{5,7},{6,14},{7,4},{8,9},{9,8},{10,1... | collective-permute-start | bytes 786440 | tf_op jit(solution)/shard_map/ppermute | solution.py:469
  17.3 7.1 %collective-permute-start.9 = (bf16[256,512]{1,0:T(8,128)(2,1)S(1)}, bf16[256,512]{1,0:T(8,128)(2,1)S(1)}, u32[]{:S(2)}, u32[]{:S(2)}) collective-permute-start(bf16[256,512]{1,0:T(8,128)(2,1)S(1)} %get-tuple-element.55), channel_id=1, source_target_pairs={{0,1},{1,0},{2,3},{3,2},{4,5},{5,7},{6,14},{7,4},{8,9},{9,8},{10,1... | collective-permute-start | bytes 786440 | tf_op jit(solution)/shard_map/ppermute | solution.py:469
  21.7 3.8 %collective-permute-start.6 = (bf16[256,512]{1,0:T(8,128)(2,1)S(1)}, bf16[256,512]{1,0:T(8,128)(2,1)S(1)}, u32[]{:S(2)}, u32[]{:S(2)}) collective-permute-start(bf16[256,512]{1,0:T(8,128)(2,1)S(1)} %shard_map.73), channel_id=1, source_target_pairs={{0,1},{1,0},{2,3},{3,2},{4,5},{5,4},{6,7},{7,6},{8,9},{9,8},{10,11... | collective-permute-start | bytes 786440 | tf_op jit(solution)/shard_map/ppermute | solution.py:450
  26.7 5.5 %collective-permute-start.11 = (bf16[2,128,256]{2,1,0:T(8,128)(2,1)S(1)}, bf16[2,128,256]{2,1,0:T(8,128)(2,1)S(1)}, u32[]{:S(2)}, u32[]{:S(2)}) collective-permute-start(bf16[2,128,256]{2,1,0:T(8,128)(2,1)S(1)} %get-tuple-element.60), channel_id=1, source_target_pairs={{0,8},{8,0},{16,24},{24,16},{1,9},{9,1},{17,25},{25,17},{2,10},{10... | collective-permute-start | bytes 393224 | tf_op jit(solution)/shard_map/ppermute | solution.py:472
  28.3 9.1 %collective-permute-start.12 = (bf16[2,128,256]{2,1,0:T(8,128)(2,1)S(1)}, bf16[2,128,256]{2,1,0:T(8,128)(2,1)S(1)}, u32[]{:S(2)}, u32[]{:S(2)}) collective-permute-start(bf16[2,128,256]{2,1,0:T(8,128)(2,1)S(1)} %get-tuple-element.61), channel_id=1, source_target_pairs={{0,16},{8,24},{16,0},{24,8},{1,17},{9,25},{17,1},{25,9},{2,18},{10... | collective-permute-start | bytes 393224 | tf_op jit(solution)/shard_map/ppermute | solution.py:472
  29.8 7.6 %collective-permute-start.13 = (bf16[2,128,256]{2,1,0:T(8,128)(2,1)S(1)}, bf16[2,128,256]{2,1,0:T(8,128)(2,1)S(1)}, u32[]{:S(2)}, u32[]{:S(2)}) collective-permute-start(bf16[2,128,256]{2,1,0:T(8,128)(2,1)S(1)} %get-tuple-element.62), channel_id=1, source_target_pairs={{0,24},{8,16},{16,8},{24,0},{1,25},{9,17},{17,9},{25,1},{2,26},{10... | collective-permute-start | bytes 393224 | tf_op jit(solution)/shard_map/ppermute | solution.py:472
  37.4 1.6 %collective-permute-start.14 = (bf16[4,128,256]{2,1,0:T(8,128)(2,1)S(1)}, bf16[4,128,256]{2,1,0:T(8,128)(2,1)S(1)}, u32[]{:S(2)}, u32[]{:S(2)}) collective-permute-start(bf16[4,128,256]{2,1,0:T(8,128)(2,1)S(1)} %shard_map.78), channel_id=1, source_target_pairs={{0,1},{1,0},{2,3},{3,2},{4,5},{5,4},{6,7},{7,6},{8,9},{9,8},{10,11... | collective-permute-start | bytes 786440 | tf_op jit(solution)/shard_map/ppermute | solution.py:450
  39.4 4.3 %collective-permute-start.15 = (bf16[128,256]{1,0:T(8,128)(2,1)S(1)}, bf16[128,256]{1,0:T(8,128)(2,1)S(1)}, u32[]{:S(2)}, u32[]{:S(2)}) collective-permute-start(bf16[128,256]{1,0:T(8,128)(2,1)S(1)} %get-tuple-element.64), channel_id=1, source_target_pairs={{0,8},{8,0},{16,24},{24,16},{1,9},{9,1},{17,25},{25,17},{2,10},{10... | collective-permute-start | bytes 196616 | tf_op jit(solution)/shard_map/ppermute | solution.py:472
  40.2 4.3 %collective-permute-start.16 = (bf16[128,256]{1,0:T(8,128)(2,1)S(1)}, bf16[128,256]{1,0:T(8,128)(2,1)S(1)}, u32[]{:S(2)}, u32[]{:S(2)}) collective-permute-start(bf16[128,256]{1,0:T(8,128)(2,1)S(1)} %get-tuple-element.65), channel_id=1, source_target_pairs={{0,16},{8,24},{16,0},{24,8},{1,17},{9,25},{17,1},{25,9},{2,18},{10... | collective-permute-start | bytes 196616 | tf_op jit(solution)/shard_map/ppermute | solution.py:472
  41.5 5.2 %collective-permute-start.17 = (bf16[128,256]{1,0:T(8,128)(2,1)S(1)}, bf16[128,256]{1,0:T(8,128)(2,1)S(1)}, u32[]{:S(2)}, u32[]{:S(2)}) collective-permute-start(bf16[128,256]{1,0:T(8,128)(2,1)S(1)} %get-tuple-element.66), channel_id=1, source_target_pairs={{0,24},{8,16},{16,8},{24,0},{1,25},{9,17},{17,9},{25,1},{2,26},{10... | collective-permute-start | bytes 196616 | tf_op jit(solution)/shard_map/ppermute | solution.py:472

commit v4 on v3

--- a/solution.py
+++ b/solution.py
@@ -330,23 +330,31 @@
             given[base : base + rows, side : side + order] = pick(lessers)
 
 
-def finish_kernel(energies, lesser, greater, given, taken, own_parts, *refs):
-    pieces, doubled = refs[:energies], refs[energies]
+def finish_kernel(
+    energies, made, last, near, lesser, greater, given, taken, own_parts, *refs
+):
+    pieces, doubled = refs[: len(made)], refs[len(made)]
     rows, order = pieces[0].shape[1:]
     half = order // 2
     upper = lax.axis_index("domain") & 1
-
-    @pl.when(upper == 0)
+    at_last = (lax.axis_index("domain") >> 1) == last
+
+    @pl.when((upper == 0) & at_last)
     def _():
         doubled[...] = stacked(lesser[...])
 
+    @pl.when((upper == 0) & jnp.logical_not(at_last))
+    def _():
+        doubled[...] = stacked(near[...])
+
     @pl.when(upper == 1)
     def _():
         doubled[...] = stacked(greater[...])
 
+    span = slice(made[0] * rows, (made[-1] + 1) * rows)
     for source, slot in ((given, upper), (taken, 1 - upper)):
-        moved = times(source[: energies * rows], doubled[...]).astype(BF16)
-        for k in range(energies):
+        moved = times(source[span], doubled[...]).astype(BF16)
+        for i, k in enumerate(made):
             first = energies * rows + k * half
             right = stacked(source[first : first + half])
             if source is given:
@@ -354,8 +362,8 @@
             else:
                 base, side = parts_at(energies, rows, half, k)
                 part = source[base : base + rows, side : side + order]
-            pieces[k][slot] = (
-                times_adjoint(moved[k * rows : (k + 1) * rows], right) + part.astype(F32)
+            pieces[i][slot] = (
+                times_adjoint(moved[i * rows : (i + 1) * rows], right) + part.astype(F32)
             ).astype(BF16)
 
 
@@ -449,23 +457,24 @@
     def swap(x):
         return lax.ppermute(x, "domain", [(d, d ^ 1) for d in range(domains)])
 
-    def hop(x, z):
-        last = 2 * z - 1
-        if z < chips - 1 or energies % 2:
-            ring = [last, last + 2, last + 1, last - 1]
+    def hop(x, z, lower=False):
+        source, target = 2 * z - 1, 2 * z + (not lower)
+        aside = target ^ 1
+        if z < chips - 1 or lower or energies % 4:
+            ring = [source, target, aside, source - 1]
         else:
-            ring = [last, last + 2, last - 1]
+            ring = [source, target, source - 1]
         onward = dict(zip(ring, ring[1:] + ring[:1]))
         route = []
         for e in range(energies):
             for d in range(domains):
                 if d in onward:
-                    target = (e, onward[d])
-                elif d == last + 1:
-                    target = (e ^ 1, d)
+                    place = (e, onward[d])
+                elif d == aside:
+                    place = (e ^ 2, d)
                 else:
-                    target = (e, d ^ 1)
-                route.append((e * domains + d, target[0] * domains + target[1]))
+                    place = (e, d ^ 1)
+                route.append((e * domains + d, place[0] * domains + place[1]))
         return lax.ppermute(x, ("energy", "domain"), route)
 
     def across(x, k):
@@ -562,21 +571,27 @@
     less, great = joined_less, chip_great
     less_in, great_in = (), ()
     for z in range(1, chips):
-        less, great = hop(less, z), hop(great, z)
+        less = hop(less, z, lower=z == chips - 1)
+        great = hop(great, z)
         if z < chips - 1:
             less, *less_in = step_on(z, less, less_in, chip_less)
             great, *great_in = step_on(z, great, great_in, chip_great)
         else:
-            less_in = keep_last(less, less_in)
             great_in = keep_last(great, great_in)
-    pieces = kernel_call(
-        functools.partial(finish_kernel, energies),
-        [jax.ShapeDtypeStruct((2, rows, order), BF16)] * energies,
-        (swap(*less_in), *great_in, given, taken, own_parts),
-        6 * unit,
-        scratch=[pltpu.VMEM((2 * order, 2 * order), BF16)],
-    )
-    pieces = [pieces[0]] + [across(pieces[k], k) for k in range(1, energies)]
+    near = swap(*less_in) if less_in else jnp.zeros_like(less)
+
+    def finish(made):
+        return kernel_call(
+            functools.partial(finish_kernel, energies, made, chips - 1),
+            [jax.ShapeDtypeStruct((2, rows, order), BF16)] * len(made),
+            (near, less, *great_in, given, taken, own_parts),
+            6 * len(made) / energies * unit,
+            scratch=[pltpu.VMEM((2 * order, 2 * order), BF16)],
+        )
+
+    pieces = finish(range(1, energies))
+    pieces = [across(piece, k + 1) for k, piece in enumerate(pieces)]
+    pieces = [*finish(range(1)), *pieces]
     (packed,) = kernel_call(
         functools.partial(pack_kernel, energies),
         [jax.ShapeDtypeStruct((energies, rows, order), BF16)],

time: 48.2 us -> 48.3 us (level)
  Pallas kernels: 10.9 us -> 11.4 us
    ppermute x6, waiting for transfers between devices: 6.87 us -> 10.3 us  [hop(): return lax.ppermute(x, ('energy', 'domain'), route)]
    ppermute x6, waiting for transfers between devices: 10.8 us -> 8.24 us  [across(): return lax.ppermute(x, 'energy', [(e, e ^ k) for e in range(energies)])]
    ppermute x6, waiting for transfers between devices: 3.76 us -> 2.91 us  [swap(): return lax.ppermute(x, 'domain', [(d, d ^ 1) for d in range(domains)])]
    ppermute x6, starting transfers between devices: 3.32 us -> 2.82 us  [hop(): return lax.ppermute(x, ('energy', 'domain'), route)]
  transfers between devices with their start and end apart: 18 -> 18, of which waited for: 14 -> 13; matrix products, arithmetic and copies ran while one was open for 0% -> 0% of each run, Pallas kernels for 5% -> 7%
where the time goes in v4:
time: 48.3 us; the launch traced here: 47.4 us
  waiting for transfers between devices  21.4 us (44%)
  starting transfers between devices  14.5 us (30%)
  Pallas kernels  11.4 us (24%)
    pallas_call x17, Pallas kernels, kernel_call(): pl.pallas_call(body, out_shape=outs, in_specs=in_specs or [VMEM] * len(op...  11.4 us
    ppermute x6, waiting for transfers between devices, hop(): return lax.ppermute(x, ('energy', 'domain'), route)  10.3 us
    ppermute x6, waiting for transfers between devices, across(): return lax.ppermute(x, 'energy', [(e, e ^ k) for e in range(energies)])  8.24 us
    ppermute x6, starting transfers between devices, across(): return lax.ppermute(x, 'energy', [(e, e ^ k) for e in range(energies)])  7.11 us
    ppermute x6, starting transfers between devices, swap(): return lax.ppermute(x, 'domain', [(d, d ^ 1) for d in range(domains)])  4.54 us
    ppermute x6, waiting for transfers between devices, swap(): return lax.ppermute(x, 'domain', [(d, d ^ 1) for d in range(domains)])  2.91 us
    ppermute x6, starting transfers between devices, hop(): return lax.ppermute(x, ('energy', 'domain'), route)  2.82 us
  transfers between devices with their start and end apart: 18, of which 13 were waited for; matrix products, arithmetic and copies ran while one was open for 0% of the time, Pallas kernels for 7%

profile of v4, /device:TPU:24, one launch (start us, length us, event | category | flops | bytes accessed | tf_op | source)
XLA Modules:
  0.0 47.4 jit_solution(3581189247700437852)
XLA Ops:
  0.0 3.0 %shard_map.64 = (bf16[2,256,512]{2,1,0:T(8,128)(2,1)S(1)}, bf16[2,256,512]{2,1,0:T(8,128)(2,1)S(1)}, bf16[2,256,512]{2,1,0:T(8,128)(2,1)S(1)}, bf16[1,256,512]{2...) custom-call(bf16[1,2,256,512]{3,2,1,0:T(8,128)(2,1)} %retarded.1, ...), custom_call_target="tpu_custom_call" | custom-call | flops 939524096 | bytes 4718592 | tf_op jit(solution)/shard_map/pallas_call | solution.py:54
  3.0 1.5 %shard_map.65 = (bf16[256,512]{1,0:T(8,128)(2,1)S(1)}, bf16[2,256,512]{2,1,0:T(8,128)(2,1)S(1)}, bf16[256,512]{1,0:T(8,128)(2,1)S(1)}, bf16[256,512]{1,0:T(8,128)(2,1)S(1)}) custom-call(bf16[2,256,512]{2,1,0:T(8,128)(2,1)S(1)} %get-tuple-element.35.retarded, bf16[2,256,512]{2,1,0:T(8,128)(2,1)S(1)} %get-tuple-element.36.coupling, ...), custom_call_target="tpu_custom_call" | custom-call | flops 1073741824 | bytes 3145728 | tf_op jit(solution)/shard_map/pallas_call | solution.py:54
  4.5 0.1 collective-permute-start.1
  4.6 0.5 %collective-permute-start = (bf16[256,512]{1,0:T(8,128)(2,1)S(1)}, bf16[256,512]{1,0:T(8,128)(2,1)S(1)}, u32[]{:S(2)}, u32[]{:S(2)}) collective-permute-start(bf16[256,512]{1,0:T(8,128)(2,1)S(1)} %get-tuple-element.41.upper.great_total), channel_id=1, source_target_pairs={{0,1},{1,0},{2,3},{3,2},{4,5},{5,4},{6,7},{7,6},{8,9},{9,8},{10,11... | collective-permute-start | bytes 786440 | tf_op jit(solution)/shard_map/ppermute | solution.py:458
  5.1 0.1 collective-permute-start.2
  5.2 0.9 %collective-permute-done.1.earlier.lower_whole = bf16[256,512]{1,0:T(8,128)(2,1)S(1)} collective-permute-done((bf16[256,512]{1,0:T(8,128)(2,1)S(1)}, bf16[256,512]{1,0:T(8,128)(2,1)S(1)}, u32[]{:S(2)}, u32[]{:S(2)}) %collective-permute-start.1) | collective-permute-done | bytes 262176 | tf_op jit(solution)/shard_map/ppermute | solution.py:458
  6.1 0.3 shard_map.67.chip_whole.step
  6.4 0.1 collective-permute-done.lower.lower_great
  6.5 0.4 collective-permute-done.2.lower
  6.9 0.6 %shard_map.69 = (bf16[2,256,512]{2,1,0:T(8,128)(2,1)S(1)}, bf16[256,512]{1,0:T(8,128)(2,1)S(1)}) custom-call(bf16[256,512]{1,0:T(8,128)(2,1)S(1)} %get-tuple-element.42.whole.later, bf16[256,512]{1,0:T(8,128)(2,1)S(1)} %shard_map.68.joined, bf16[256,512]{1,0:T(8,128)(2,1)S(1)} %get-tuple-element.39.first_step, ...), custom_call_target="tpu_custom_call" | custom-call | flops 536870912 | bytes 2883584 | tf_op jit(solution)/shard_map/pallas_call | solution.py:54
  7.4 1.0 %shard_map.70 = (bf16[1280,512]{1,0:T(8,128)(2,1)S(1)}, bf16[512,256]{1,0:T(8,128)(2,1)S(1)}, s32[4,8,128]{2,1,0:T(8,128)S(1)}) custom-call(s32[2,2]{1,0:T(2,128)} %tiles.1, s32[4]{0:T(128)} %offsets.1, bf16[256,512]{1,0:T(8,128)(2,1)S(1)} %get-tuple-element.39.first_step, bf16[1,256,512]{2,1,0:T(8,128)(2,1)S(1)} %get-tuple-element.38.later_steps, ...), custom_call_target="tpu_custom_call" | custom-call | flops 402653184 | bytes 4735008 | tf_op jit(solution)/shard_map/pallas_call | solution.py:54
  8.4 1.1 %collective-permute-start.10 = (bf16[1280,512]{1,0:T(8,128)(2,1)S(1)}, bf16[1280,512]{1,0:T(8,128)(2,1)S(1)}, u32[]{:S(2)}, u32[]{:S(2)}) collective-permute-start(bf16[1280,512]{1,0:T(8,128)(2,1)S(1)} %get-tuple-element.56.given), channel_id=1, source_target_pairs={{0,1},{1,0},{2,3},{3,2},{4,5},{5,4},{6,7},{7,6},{8,9},{9,8},{10,11... | collective-permute-start | bytes 3932168 | tf_op jit(solution)/shard_map/ppermute | solution.py:458
  9.5 0.1 collective-permute-start.7
  9.5 0.5 collective-permute-start.3
  10.0 2.5 %collective-permute-done.7.state = bf16[256,512]{1,0:T(8,128)(2,1)S(1)} collective-permute-done((bf16[256,512]{1,0:T(8,128)(2,1)S(1)}, bf16[256,512]{1,0:T(8,128)(2,1)S(1)}, u32[]{:S(2)}, u32[]{:S(2)}) %collective-permute-start.7) | collective-permute-done | bytes 262176 | tf_op jit(solution)/shard_map/ppermute | solution.py:478
  12.5 0.5 %shard_map.73 = (bf16[256,512]{1,0:T(8,128)(2,1)S(1)}, bf16[256,512]{1,0:T(8,128)(2,1)S(1)}) custom-call(bf16[256,512]{1,0:T(8,128)(2,1)S(1)} %collective-permute-done.7.state, bf16[256,512]{1,0:T(8,128)(2,1)S(1)} %shard_map.67.chip_whole.step, bf16[256,512]{1,0:T(8,128)(2,1)S(1)} %shard_map.66.chip_great.source), custom_call_target="tpu_custom_call" | custom-call | flops 268435456 | bytes 1310720 | tf_op jit(solution)/shard_map/pallas_call | solution.py:54
  13.0 0.4 collective-permute-start.8
  13.5 0.0 collective-permute-done.3.state
  13.5 0.5 %shard_map.71 = (bf16[256,512]{1,0:T(8,128)(2,1)S(1)}, bf16[256,512]{1,0:T(8,128)(2,1)S(1)}) custom-call(bf16[256,512]{1,0:T(8,128)(2,1)S(1)} %collective-permute-done.3.state, bf16[256,512]{1,0:T(8,128)(2,1)S(1)} %shard_map.67.chip_whole.step, bf16[256,512]{1,0:T(8,128)(2,1)S(1)} %get-tuple-element.47.source), custom_call_target="tpu_custom_call" | custom-call | flops 268435456 | bytes 1310720 | tf_op jit(solution)/shard_map/pallas_call | solution.py:54
  14.0 0.2 collective-permute-start.4
  14.2 0.4 collective-permute-done.8.state
  14.6 0.5 %shard_map.74 = (bf16[256,512]{1,0:T(8,128)(2,1)S(1)}, bf16[256,512]{1,0:T(8,128)(2,1)S(1)}) custom-call(bf16[256,512]{1,0:T(8,128)(2,1)S(1)} %collective-permute-done.8.state, bf16[256,512]{1,0:T(8,128)(2,1)S(1)} %shard_map.67.chip_whole.step, bf16[256,512]{1,0:T(8,128)(2,1)S(1)} %shard_map.66.chip_great.source, bf16[256,512]{1,0:T(8,128)(2,1)S(1)} %get-tuple-element.53.refs_0_), custom_call_target="tpu_custom_call" | custom-call | flops 268435456 | bytes 1572864 | tf_op jit(solution)/shard_map/pallas_call | solution.py:54
  15.2 1.6 %collective-permute-start.9 = (bf16[256,512]{1,0:T(8,128)(2,1)S(1)}, bf16[256,512]{1,0:T(8,128)(2,1)S(1)}, u32[]{:S(2)}, u32[]{:S(2)}) collective-permute-start(bf16[256,512]{1,0:T(8,128)(2,1)S(1)} %get-tuple-element.54), channel_id=1, source_target_pairs={{0,1},{1,0},{2,3},{3,2},{4,5},{5,7},{6,22},{7,4},{8,9},{9,8},{10,1... | collective-permute-start | bytes 786440 | tf_op jit(solution)/shard_map/ppermute | solution.py:478
  16.8 0.0 collective-permute-done.4.state
  16.8 0.5 %shard_map.72 = (bf16[256,512]{1,0:T(8,128)(2,1)S(1)}, bf16[256,512]{1,0:T(8,128)(2,1)S(1)}) custom-call(bf16[256,512]{1,0:T(8,128)(2,1)S(1)} %collective-permute-done.4.state, bf16[256,512]{1,0:T(8,128)(2,1)S(1)} %shard_map.67.chip_whole.step, bf16[256,512]{1,0:T(8,128)(2,1)S(1)} %get-tuple-element.47.source, bf16[256,512]{1,0:T(8,128)(2,1)S(1)} %get-tuple-element.49.refs_0_), custom_call_target="tpu_custom_call" | custom-call | flops 268435456 | bytes 1572864 | tf_op jit(solution)/shard_map/pallas_call | solution.py:54
  17.3 2.8 %collective-permute-start.5 = (bf16[256,512]{1,0:T(8,128)(2,1)S(1)}, bf16[256,512]{1,0:T(8,128)(2,1)S(1)}, u32[]{:S(2)}, u32[]{:S(2)}) collective-permute-start(bf16[256,512]{1,0:T(8,128)(2,1)S(1)} %get-tuple-element.50), channel_id=1, source_target_pairs={{0,1},{1,0},{2,3},{3,2},{4,5},{5,4},{6,7},{7,6},{8,9},{9,8},{10,11... | collective-permute-start | bytes 786440 | tf_op jit(solution)/shard_map/ppermute | solution.py:458
  20.1 0.1 collective-permute-start.6
  20.2 1.4 %collective-permute-done.9.state = bf16[256,512]{1,0:T(8,128)(2,1)S(1)} collective-permute-done((bf16[256,512]{1,0:T(8,128)(2,1)S(1)}, bf16[256,512]{1,0:T(8,128)(2,1)S(1)}, u32[]{:S(2)}, u32[]{:S(2)}) %collective-permute-start.9) | collective-permute-done | bytes 262176 | tf_op jit(solution)/shard_map/ppermute | solution.py:478
  21.7 0.0 collective-permute-done.5.near
  21.7 5.9 %collective-permute-done.6.lesser = bf16[256,512]{1,0:T(8,128)(2,1)S(1)} collective-permute-done((bf16[256,512]{1,0:T(8,128)(2,1)S(1)}, bf16[256,512]{1,0:T(8,128)(2,1)S(1)}, u32[]{:S(2)}, u32[]{:S(2)}) %collective-permute-start.6) | collective-permute-done | bytes 262176 | tf_op jit(solution)/shard_map/ppermute | solution.py:478
  27.5 0.0 collective-permute-done.10.taken
  27.5 1.1 %shard_map.77 = (bf16[2,128,256]{2,1,0:T(8,128)(2,1)S(1)}, bf16[2,128,256]{2,1,0:T(8,128)(2,1)S(1)}, bf16[2,128,256]{2,1,0:T(8,128)(2,1)S(1)}) custom-call(bf16[256,512]{1,0:T(8,128)(2,1)S(1)} %collective-permute-done.5.near, bf16[256,512]{1,0:T(8,128)(2,1)S(1)} %collective-permute-done.6.lesser, bf16[256,512]{1,0:T(8,128)(2,1)S(1)} %shard_map.75.greater, ...), custom_call_target="tpu_custom_call" | custom-call | flops 603979776 | bytes 4063232 | tf_op jit(solution)/shard_map/pallas_call | solution.py:54
  28.6 1.0 %collective-permute-start.11 = (bf16[2,128,256]{2,1,0:T(8,128)(2,1)S(1)}, bf16[2,128,256]{2,1,0:T(8,128)(2,1)S(1)}, u32[]{:S(2)}, u32[]{:S(2)}) collective-permute-start(bf16[2,128,256]{2,1,0:T(8,128)(2,1)S(1)} %get-tuple-element.58), channel_id=1, source_target_pairs={{0,8},{8,0},{16,24},{24,16},{1,9},{9,1},{17,25},{25,17},{2,10},{10... | collective-permute-start | bytes 393224 | tf_op jit(solution)/shard_map/ppermute | solution.py:481
  29.6 1.5 %collective-permute-start.12 = (bf16[2,128,256]{2,1,0:T(8,128)(2,1)S(1)}, bf16[2,128,256]{2,1,0:T(8,128)(2,1)S(1)}, u32[]{:S(2)}, u32[]{:S(2)}) collective-permute-start(bf16[2,128,256]{2,1,0:T(8,128)(2,1)S(1)} %get-tuple-element.59), channel_id=1, source_target_pairs={{0,16},{8,24},{16,0},{24,8},{1,17},{9,25},{17,1},{25,9},{2,18},{10... | collective-permute-start | bytes 393224 | tf_op jit(solution)/shard_map/ppermute | solution.py:481
  31.1 1.1 %collective-permute-start.13 = (bf16[2,128,256]{2,1,0:T(8,128)(2,1)S(1)}, bf16[2,128,256]{2,1,0:T(8,128)(2,1)S(1)}, u32[]{:S(2)}, u32[]{:S(2)}) collective-permute-start(bf16[2,128,256]{2,1,0:T(8,128)(2,1)S(1)} %get-tuple-element.60), channel_id=1, source_target_pairs={{0,24},{8,16},{16,8},{24,0},{1,25},{9,17},{17,9},{25,1},{2,26},{10... | collective-permute-start | bytes 393224 | tf_op jit(solution)/shard_map/ppermute | solution.py:481
  32.2 0.7 %shard_map.76.refs_0_ = bf16[2,128,256]{2,1,0:T(8,128)(2,1)S(1)} custom-call(bf16[256,512]{1,0:T(8,128)(2,1)S(1)} %collective-permute-done.5.near, bf16[256,512]{1,0:T(8,128)(2,1)S(1)} %collective-permute-done.6.lesser, bf16[256,512]{1,0:T(8,128)(2,1)S(1)} %shard_map.75.greater, bf16[1280,512]{1,0:T(8,128)(2,1)S(1)} %get-tuple-element.56.given, ...), custom_call_target="tpu_custom_call" | custom-call | flops 201326592 | bytes 3801088 | tf_op jit(solution)/shard_map/pallas_call | solution.py:54
  32.8 1.9 %collective-permute-done.11.refs_1_ = bf16[2,128,256]{2,1,0:T(8,128)(2,1)S(1)} collective-permute-done((bf16[2,128,256]{2,1,0:T(8,128)(2,1)S(1)}, bf16[2,128,256]{2,1,0:T(8,128)(2,1)S(1)}, u32[]{:S(2)}, u32[]{:S(2)}) %collective-permute-start.11) | collective-permute-done | bytes 131104 | tf_op jit(solution)/shard_map/ppermute | solution.py:481
  34.8 2.6 %collective-permute-done.12.refs_2_ = bf16[2,128,256]{2,1,0:T(8,128)(2,1)S(1)} collective-permute-done((bf16[2,128,256]{2,1,0:T(8,128)(2,1)S(1)}, bf16[2,128,256]{2,1,0:T(8,128)(2,1)S(1)}, u32[]{:S(2)}, u32[]{:S(2)}) %collective-permute-start.12) | collective-permute-done | bytes 131104 | tf_op jit(solution)/shard_map/ppermute | solution.py:481
  37.4 0.0 collective-permute-done.13.refs_3_
  37.4 0.1 collective-permute-start.14
  37.5 1.5 %collective-permute-done.14.swapped = bf16[4,128,256]{2,1,0:T(8,128)(2,1)S(1)} collective-permute-done((bf16[4,128,256]{2,1,0:T(8,128)(2,1)S(1)}, bf16[4,128,256]{2,1,0:T(8,128)(2,1)S(1)}, u32[]{:S(2)}, u32[]{:S(2)}) %collective-permute-start.14) | collective-permute-done | bytes 262176 | tf_op jit(solution)/shard_map/ppermute | solution.py:458
  39.0 0.4 shard_map.79
  39.4 1.2 %collective-permute-start.15 = (bf16[128,256]{1,0:T(8,128)(2,1)S(1)}, bf16[128,256]{1,0:T(8,128)(2,1)S(1)}, u32[]{:S(2)}, u32[]{:S(2)}) collective-permute-start(bf16[128,256]{1,0:T(8,128)(2,1)S(1)} %get-tuple-element.62), channel_id=1, source_target_pairs={{0,8},{8,0},{16,24},{24,16},{1,9},{9,1},{17,25},{25,17},{2,10},{10... | collective-permute-start | bytes 196616 | tf_op jit(solution)/shard_map/ppermute | solution.py:481
  40.6 0.9 %collective-permute-start.16 = (bf16[128,256]{1,0:T(8,128)(2,1)S(1)}, bf16[128,256]{1,0:T(8,128)(2,1)S(1)}, u32[]{:S(2)}, u32[]{:S(2)}) collective-permute-start(bf16[128,256]{1,0:T(8,128)(2,1)S(1)} %get-tuple-element.63), channel_id=1, source_target_pairs={{0,16},{8,24},{16,0},{24,8},{1,17},{9,25},{17,1},{25,9},{2,18},{10... | collective-permute-start | bytes 196616 | tf_op jit(solution)/shard_map/ppermute | solution.py:481
  41.5 1.4 %collective-permute-start.17 = (bf16[128,256]{1,0:T(8,128)(2,1)S(1)}, bf16[128,256]{1,0:T(8,128)(2,1)S(1)}, u32[]{:S(2)}, u32[]{:S(2)}) collective-permute-start(bf16[128,256]{1,0:T(8,128)(2,1)S(1)} %get-tuple-element.64), channel_id=1, source_target_pairs={{0,24},{8,16},{16,8},{24,0},{1,25},{9,17},{17,9},{25,1},{2,26},{10... | collective-permute-start | bytes 196616 | tf_op jit(solution)/shard_map/ppermute | solution.py:481
  42.9 0.8 %collective-permute-done.15.refs_1_ = bf16[128,256]{1,0:T(8,128)(2,1)S(1)} collective-permute-done((bf16[128,256]{1,0:T(8,128)(2,1)S(1)}, bf16[128,256]{1,0:T(8,128)(2,1)S(1)}, u32[]{:S(2)}, u32[]{:S(2)}) %collective-permute-start.15) | collective-permute-done | bytes 65568 | tf_op jit(solution)/shard_map/ppermute | solution.py:481
  43.7 1.8 %collective-permute-done.16.refs_2_ = bf16[128,256]{1,0:T(8,128)(2,1)S(1)} collective-permute-done((bf16[128,256]{1,0:T(8,128)(2,1)S(1)}, bf16[128,256]{1,0:T(8,128)(2,1)S(1)}, u32[]{:S(2)}, u32[]{:S(2)}) %collective-permute-start.16) | collective-permute-done | bytes 65568 | tf_op jit(solution)/shard_map/ppermute | solution.py:481
  45.5 1.1 %collective-permute-done.17.refs_3_ = bf16[128,256]{1,0:T(8,128)(2,1)S(1)} collective-permute-done((bf16[128,256]{1,0:T(8,128)(2,1)S(1)}, bf16[128,256]{1,0:T(8,128)(2,1)S(1)}, u32[]{:S(2)}, u32[]{:S(2)}) %collective-permute-start.17) | collective-permute-done | bytes 65568 | tf_op jit(solution)/shard_map/ppermute | solution.py:481
  46.7 0.7 %shard_map.80 = bf16[4,128,256]{2,1,0:T(8,128)(2,1)} custom-call(bf16[128,256]{1,0:T(8,128)(2,1)S(1)} %get-tuple-element.61.refs_0_, bf16[128,256]{1,0:T(8,128)(2,1)S(1)} %collective-permute-done.15.refs_1_, bf16[128,256]{1,0:T(8,128)(2,1)S(1)} %collective-permute-done.16.refs_2_, bf16[128,256]{1,0:T(8,128)(2,1)S(1)} %collective-permute-done.17.refs_3_), custom_call_target="tpu_custom_call" | custom-call | bytes 524288 | tf_op jit(solution)/shard_map/pallas_call | solution.py:54
  (4 shorter events, 0.0 us)
Async XLA Ops:
  4.5 1.6 %collective-permute-start.1 = (bf16[256,512]{1,0:T(8,128)(2,1)S(1)}, bf16[256,512]{1,0:T(8,128)(2,1)S(1)}, u32[]{:S(2)}, u32[]{:S(2)}) collective-permute-start(bf16[256,512]{1,0:T(8,128)(2,1)S(1)} %get-tuple-element.42.whole.later), channel_id=1, source_target_pairs={{0,1},{1,0},{2,3},{3,2},{4,5},{5,4},{6,7},{7,6},{8,9},{9,8},{10,11... | collective-permute-start | bytes 786440 | tf_op jit(solution)/shard_map/ppermute | solution.py:458
  4.6 1.9 %collective-permute-start = (bf16[256,512]{1,0:T(8,128)(2,1)S(1)}, bf16[256,512]{1,0:T(8,128)(2,1)S(1)}, u32[]{:S(2)}, u32[]{:S(2)}) collective-permute-start(bf16[256,512]{1,0:T(8,128)(2,1)S(1)} %get-tuple-element.41.upper.great_total), channel_id=1, source_target_pairs={{0,1},{1,0},{2,3},{3,2},{4,5},{5,4},{6,7},{7,6},{8,9},{9,8},{10,11... | collective-permute-start | bytes 786440 | tf_op jit(solution)/shard_map/ppermute | solution.py:458
  5.1 1.8 %collective-permute-start.2 = (bf16[256,512]{1,0:T(8,128)(2,1)S(1)}, bf16[256,512]{1,0:T(8,128)(2,1)S(1)}, u32[]{:S(2)}, u32[]{:S(2)}) collective-permute-start(bf16[256,512]{1,0:T(8,128)(2,1)S(1)} %get-tuple-element.43.upper.total), channel_id=1, source_target_pairs={{0,1},{1,0},{2,3},{3,2},{4,5},{5,4},{6,7},{7,6},{8,9},{9,8},{10,11... | collective-permute-start | bytes 786440 | tf_op jit(solution)/shard_map/ppermute | solution.py:458
  8.4 19.1 %collective-permute-start.10 = (bf16[1280,512]{1,0:T(8,128)(2,1)S(1)}, bf16[1280,512]{1,0:T(8,128)(2,1)S(1)}, u32[]{:S(2)}, u32[]{:S(2)}) collective-permute-start(bf16[1280,512]{1,0:T(8,128)(2,1)S(1)} %get-tuple-element.56.given), channel_id=1, source_target_pairs={{0,1},{1,0},{2,3},{3,2},{4,5},{5,4},{6,7},{7,6},{8,9},{9,8},{10,11... | collective-permute-start | bytes 3932168 | tf_op jit(solution)/shard_map/ppermute | solution.py:458
  9.5 3.0 %collective-permute-start.7 = (bf16[256,512]{1,0:T(8,128)(2,1)S(1)}, bf16[256,512]{1,0:T(8,128)(2,1)S(1)}, u32[]{:S(2)}, u32[]{:S(2)}) collective-permute-start(bf16[256,512]{1,0:T(8,128)(2,1)S(1)} %shard_map.66.chip_great.source), channel_id=1, source_target_pairs={{0,1},{1,3},{2,0},{3,2},{4,5},{5,4},{6,7},{7,6},{8,9},{9,11},{10,8... | collective-permute-start | bytes 786440 | tf_op jit(solution)/shard_map/ppermute | solution.py:478
  9.5 4.0 %collective-permute-start.3 = (bf16[256,512]{1,0:T(8,128)(2,1)S(1)}, bf16[256,512]{1,0:T(8,128)(2,1)S(1)}, u32[]{:S(2)}, u32[]{:S(2)}) collective-permute-start(bf16[256,512]{1,0:T(8,128)(2,1)S(1)} %shard_map.68.joined), channel_id=1, source_target_pairs={{0,1},{1,3},{2,0},{3,2},{4,5},{5,4},{6,7},{7,6},{8,9},{9,11},{10,8... | collective-permute-start | bytes 786440 | tf_op jit(solution)/shard_map/ppermute | solution.py:478
  13.0 1.6 %collective-permute-start.8 = (bf16[256,512]{1,0:T(8,128)(2,1)S(1)}, bf16[256,512]{1,0:T(8,128)(2,1)S(1)}, u32[]{:S(2)}, u32[]{:S(2)}) collective-permute-start(bf16[256,512]{1,0:T(8,128)(2,1)S(1)} %get-tuple-element.52), channel_id=1, source_target_pairs={{0,1},{1,0},{2,3},{3,5},{4,2},{5,4},{6,7},{7,6},{8,9},{9,8},{10,11... | collective-permute-start | bytes 786440 | tf_op jit(solution)/shard_map/ppermute | solution.py:478
  14.0 2.8 %collective-permute-start.4 = (bf16[256,512]{1,0:T(8,128)(2,1)S(1)}, bf16[256,512]{1,0:T(8,128)(2,1)S(1)}, u32[]{:S(2)}, u32[]{:S(2)}) collective-permute-start(bf16[256,512]{1,0:T(8,128)(2,1)S(1)} %get-tuple-element.48), channel_id=1, source_target_pairs={{0,1},{1,0},{2,3},{3,5},{4,2},{5,4},{6,7},{7,6},{8,9},{9,8},{10,11... | collective-permute-start | bytes 786440 | tf_op jit(solution)/shard_map/ppermute | solution.py:478
  15.2 6.5 %collective-permute-start.9 = (bf16[256,512]{1,0:T(8,128)(2,1)S(1)}, bf16[256,512]{1,0:T(8,128)(2,1)S(1)}, u32[]{:S(2)}, u32[]{:S(2)}) collective-permute-start(bf16[256,512]{1,0:T(8,128)(2,1)S(1)} %get-tuple-element.54), channel_id=1, source_target_pairs={{0,1},{1,0},{2,3},{3,2},{4,5},{5,7},{6,22},{7,4},{8,9},{9,8},{10,1... | collective-permute-start | bytes 786440 | tf_op jit(solution)/shard_map/ppermute | solution.py:478
  17.3 4.3 %collective-permute-start.5 = (bf16[256,512]{1,0:T(8,128)(2,1)S(1)}, bf16[256,512]{1,0:T(8,128)(2,1)S(1)}, u32[]{:S(2)}, u32[]{:S(2)}) collective-permute-start(bf16[256,512]{1,0:T(8,128)(2,1)S(1)} %get-tuple-element.50), channel_id=1, source_target_pairs={{0,1},{1,0},{2,3},{3,2},{4,5},{5,4},{6,7},{7,6},{8,9},{9,8},{10,11... | collective-permute-start | bytes 786440 | tf_op jit(solution)/shard_map/ppermute | solution.py:458
  20.1 7.4 %collective-permute-start.6 = (bf16[256,512]{1,0:T(8,128)(2,1)S(1)}, bf16[256,512]{1,0:T(8,128)(2,1)S(1)}, u32[]{:S(2)}, u32[]{:S(2)}) collective-permute-start(bf16[256,512]{1,0:T(8,128)(2,1)S(1)} %get-tuple-element.51), channel_id=1, source_target_pairs={{0,1},{1,0},{2,3},{3,2},{4,5},{5,6},{6,7},{7,4},{8,9},{9,8},{10,11... | collective-permute-start | bytes 786440 | tf_op jit(solution)/shard_map/ppermute | solution.py:478
  28.6 6.1 %collective-permute-start.11 = (bf16[2,128,256]{2,1,0:T(8,128)(2,1)S(1)}, bf16[2,128,256]{2,1,0:T(8,128)(2,1)S(1)}, u32[]{:S(2)}, u32[]{:S(2)}) collective-permute-start(bf16[2,128,256]{2,1,0:T(8,128)(2,1)S(1)} %get-tuple-element.58), channel_id=1, source_target_pairs={{0,8},{8,0},{16,24},{24,16},{1,9},{9,1},{17,25},{25,17},{2,10},{10... | collective-permute-start | bytes 393224 | tf_op jit(solution)/shard_map/ppermute | solution.py:481
  29.6 7.8 %collective-permute-start.12 = (bf16[2,128,256]{2,1,0:T(8,128)(2,1)S(1)}, bf16[2,128,256]{2,1,0:T(8,128)(2,1)S(1)}, u32[]{:S(2)}, u32[]{:S(2)}) collective-permute-start(bf16[2,128,256]{2,1,0:T(8,128)(2,1)S(1)} %get-tuple-element.59), channel_id=1, source_target_pairs={{0,16},{8,24},{16,0},{24,8},{1,17},{9,25},{17,1},{25,9},{2,18},{10... | collective-permute-start | bytes 393224 | tf_op jit(solution)/shard_map/ppermute | solution.py:481
  31.1 6.3 %collective-permute-start.13 = (bf16[2,128,256]{2,1,0:T(8,128)(2,1)S(1)}, bf16[2,128,256]{2,1,0:T(8,128)(2,1)S(1)}, u32[]{:S(2)}, u32[]{:S(2)}) collective-permute-start(bf16[2,128,256]{2,1,0:T(8,128)(2,1)S(1)} %get-tuple-element.60), channel_id=1, source_target_pairs={{0,24},{8,16},{16,8},{24,0},{1,25},{9,17},{17,9},{25,1},{2,26},{10... | collective-permute-start | bytes 393224 | tf_op jit(solution)/shard_map/ppermute | solution.py:481
  37.4 1.6 %collective-permute-start.14 = (bf16[4,128,256]{2,1,0:T(8,128)(2,1)S(1)}, bf16[4,128,256]{2,1,0:T(8,128)(2,1)S(1)}, u32[]{:S(2)}, u32[]{:S(2)}) collective-permute-start(bf16[4,128,256]{2,1,0:T(8,128)(2,1)S(1)} %shard_map.78), channel_id=1, source_target_pairs={{0,1},{1,0},{2,3},{3,2},{4,5},{5,4},{6,7},{7,6},{8,9},{9,8},{10,11... | collective-permute-start | bytes 786440 | tf_op jit(solution)/shard_map/ppermute | solution.py:458
  39.4 4.3 %collective-permute-start.15 = (bf16[128,256]{1,0:T(8,128)(2,1)S(1)}, bf16[128,256]{1,0:T(8,128)(2,1)S(1)}, u32[]{:S(2)}, u32[]{:S(2)}) collective-permute-start(bf16[128,256]{1,0:T(8,128)(2,1)S(1)} %get-tuple-element.62), channel_id=1, source_target_pairs={{0,8},{8,0},{16,24},{24,16},{1,9},{9,1},{17,25},{25,17},{2,10},{10... | collective-permute-start | bytes 196616 | tf_op jit(solution)/shard_map/ppermute | solution.py:481
  40.6 5.0 %collective-permute-start.16 = (bf16[128,256]{1,0:T(8,128)(2,1)S(1)}, bf16[128,256]{1,0:T(8,128)(2,1)S(1)}, u32[]{:S(2)}, u32[]{:S(2)}) collective-permute-start(bf16[128,256]{1,0:T(8,128)(2,1)S(1)} %get-tuple-element.63), channel_id=1, source_target_pairs={{0,16},{8,24},{16,0},{24,8},{1,17},{9,25},{17,1},{25,9},{2,18},{10... | collective-permute-start | bytes 196616 | tf_op jit(solution)/shard_map/ppermute | solution.py:481
  41.5 5.2 %collective-permute-start.17 = (bf16[128,256]{1,0:T(8,128)(2,1)S(1)}, bf16[128,256]{1,0:T(8,128)(2,1)S(1)}, u32[]{:S(2)}, u32[]{:S(2)}) collective-permute-start(bf16[128,256]{1,0:T(8,128)(2,1)S(1)} %get-tuple-element.64), channel_id=1, source_target_pairs={{0,24},{8,16},{16,8},{24,0},{1,25},{9,17},{17,9},{25,1},{2,26},{10... | collective-permute-start | bytes 196616 | tf_op jit(solution)/shard_map/ppermute | solution.py:481

commit v5 on v4

--- a/solution.py
+++ b/solution.py
@@ -48,7 +48,9 @@
     )
 
 
-def kernel_call(body, outs, operands, flops, in_specs=None, scratch=(), out_specs=None):
+def kernel_call(
+    body, outs, operands, flops, in_specs=None, scratch=(), out_specs=None, aliases=None
+):
     moved = sum(x.size * x.dtype.itemsize for x in operands)
     moved += sum(math.prod(o.shape) * o.dtype.itemsize for o in outs)
     return pl.pallas_call(
@@ -57,6 +59,7 @@
         in_specs=in_specs or [VMEM] * len(operands),
         out_specs=out_specs or [VMEM] * len(outs),
         scratch_shapes=list(scratch),
+        input_output_aliases=aliases or {},
         compiler_params=pltpu.CompilerParams(vmem_limit_bytes=VMEM_LIMIT),
         cost_estimate=pl.CostEstimate(
             flops=int(flops), bytes_accessed=moved, transcendentals=0
@@ -174,10 +177,6 @@
     kept, (out, chosen) = (refs[0] if len(refs) == 3 else None), refs[-2:]
     out[...] = advance(state[...], step[...], source[...])
     keep(z, state, kept, chosen)
-
-
-def keep_kernel(z, state, *refs):
-    keep(z, state, refs[0] if len(refs) == 2 else None, refs[-1])
 
 
 def parts_at(energies, rows, half, k):
@@ -330,22 +329,14 @@
             given[base : base + rows, side : side + order] = pick(lessers)
 
 
-def finish_kernel(
-    energies, made, last, near, lesser, greater, given, taken, own_parts, *refs
-):
-    pieces, doubled = refs[: len(made)], refs[len(made)]
+def tiles_kernel(energies, made, greater, lesser, given, taken, own_parts, pieces, doubled):
     rows, order = pieces[0].shape[1:]
     half = order // 2
     upper = lax.axis_index("domain") & 1
-    at_last = (lax.axis_index("domain") >> 1) == last
-
-    @pl.when((upper == 0) & at_last)
+
+    @pl.when(upper == 0)
     def _():
         doubled[...] = stacked(lesser[...])
-
-    @pl.when((upper == 0) & jnp.logical_not(at_last))
-    def _():
-        doubled[...] = stacked(near[...])
 
     @pl.when(upper == 1)
     def _():
@@ -365,6 +356,35 @@
             pieces[i][slot] = (
                 times_adjoint(moved[i * rows : (i + 1) * rows], right) + part.astype(F32)
             ).astype(BF16)
+
+
+def finish_kernel(energies, made, last, on_last, lesser, greater, *refs):
+    operands, refs = refs[:3], refs[3:]
+    pieces, doubled = refs[-1 - len(made) : -1], refs[-1]
+    at_last = (lax.axis_index("domain") >> 1) == last
+
+    @pl.when(at_last if on_last else jnp.logical_not(at_last))
+    def _():
+        tiles_kernel(energies, made, greater, lesser, *operands, pieces, doubled)
+
+
+def finish_own_kernel(energies, last, near, kept, lesser, greater, *refs):
+    operands, (piece, doubled, arrived_less, arrived_great) = refs[:3], refs[3:]
+    at_last = (lax.axis_index("domain") >> 1) == last
+
+    @pl.when(at_last)
+    def _():
+        arrived_less[...] = lesser[...]
+        arrived_great[...] = greater[...]
+
+    @pl.when(jnp.logical_not(at_last))
+    def _():
+        arrived_less[...] = near[...]
+        arrived_great[...] = kept[...]
+
+    tiles_kernel(
+        energies, range(1), arrived_great, arrived_less, *operands, [piece], doubled
+    )
 
 
 def pack_kernel(energies, *refs):
@@ -563,11 +583,6 @@
             2 * unit,
         )
 
-    def keep_last(state, kept):
-        return kernel_call(
-            functools.partial(keep_kernel, chips - 1), [block], (state, *kept), 0
-        )
-
     less, great = joined_less, chip_great
     less_in, great_in = (), ()
     for z in range(1, chips):
@@ -576,22 +591,33 @@
         if z < chips - 1:
             less, *less_in = step_on(z, less, less_in, chip_less)
             great, *great_in = step_on(z, great, great_in, chip_great)
-        else:
-            great_in = keep_last(great, great_in)
-    near = swap(*less_in) if less_in else jnp.zeros_like(less)
-
-    def finish(made):
-        return kernel_call(
-            functools.partial(finish_kernel, energies, made, chips - 1),
-            [jax.ShapeDtypeStruct((2, rows, order), BF16)] * len(made),
-            (near, less, *great_in, given, taken, own_parts),
-            6 * len(made) / energies * unit,
-            scratch=[pltpu.VMEM((2 * order, 2 * order), BF16)],
+    if not less_in:
+        less_in, great_in = [jnp.zeros_like(less)], [jnp.zeros_like(great)]
+    near, kept = swap(*less_in), great_in[0]
+    shared = (given, taken, own_parts)
+    double = pltpu.VMEM((2 * order, 2 * order), BF16)
+    sent = range(1, energies)
+    pair = jax.ShapeDtypeStruct((2, rows, order), BF16)
+    pieces = ()
+    for on_last, arrived in ((False, (near, kept)), (True, (less, great))):
+        operands = (*arrived, *shared, *pieces)
+        pieces = kernel_call(
+            functools.partial(finish_kernel, energies, sent, chips - 1, on_last),
+            [pair] * len(sent),
+            operands,
+            5 * unit,
+            scratch=[double],
+            aliases={len(operands) - len(pieces) + i: i for i in range(len(pieces))},
         )
-
-    pieces = finish(range(1, energies))
-    pieces = [across(piece, k + 1) for k, piece in enumerate(pieces)]
-    pieces = [*finish(range(1)), *pieces]
+    pieces = [across(piece, k) for k, piece in zip(sent, pieces)]
+    (own,) = kernel_call(
+        functools.partial(finish_own_kernel, energies, chips - 1),
+        [pair],
+        (near, kept, less, great, *shared),
+        2 * unit,
+        scratch=[double] + [pltpu.VMEM((order, 2 * order), BF16)] * 2,
+    )
+    pieces = [own, *pieces]
     (packed,) = kernel_call(
         functools.partial(pack_kernel, energies),
         [jax.ShapeDtypeStruct((energies, rows, order), BF16)],

time: 48.3 us -> 46.6 us (0.965)
  the two profiles are of different devices: /device:TPU:24 before, /device:TPU:16 now
where the time goes in v5:
time: 46.6 us; the launch traced here: 46.5 us
  waiting for transfers between devices  19.4 us (42%)
  starting transfers between devices  15.5 us (33%)
  Pallas kernels  11.4 us (24%)
    pallas_call x17, Pallas kernels, kernel_call(): pl.pallas_call(body, out_shape=outs, in_specs=in_specs or [VMEM] * len(op...  11.4 us
    ppermute x6, waiting for transfers between devices, hop(): return lax.ppermute(x, ('energy', 'domain'), route)  9.11 us
    ppermute x6, waiting for transfers between devices, across(): return lax.ppermute(x, 'energy', [(e, e ^ k) for e in range(energies)])  7.41 us
    ppermute x6, starting transfers between devices, across(): return lax.ppermute(x, 'energy', [(e, e ^ k) for e in range(energies)])  7.04 us
    ppermute x6, starting transfers between devices, hop(): return lax.ppermute(x, ('energy', 'domain'), route)  5.62 us
    ppermute x6, waiting for transfers between devices, swap(): return lax.ppermute(x, 'domain', [(d, d ^ 1) for d in range(domains)])  2.91 us
    ppermute x6, starting transfers between devices, swap(): return lax.ppermute(x, 'domain', [(d, d ^ 1) for d in range(domains)])  2.87 us
  transfers between devices with their start and end apart: 18, of which 15 were waited for; matrix products, arithmetic and copies ran while one was open for 0% of the time, Pallas kernels for 9%

profile of v5, /device:TPU:16, one launch (start us, length us, event | category | flops | bytes accessed | tf_op | source)
XLA Modules:
  0.0 46.5 jit_solution(8248396084992804674)
XLA Ops:
  0.0 3.0 %shard_map.64 = (bf16[2,256,512]{2,1,0:T(8,128)(2,1)S(1)}, bf16[2,256,512]{2,1,0:T(8,128)(2,1)S(1)}, bf16[2,256,512]{2,1,0:T(8,128)(2,1)S(1)}, bf16[1,256,512]{2...) custom-call(bf16[1,2,256,512]{3,2,1,0:T(8,128)(2,1)} %retarded.1, ...), custom_call_target="tpu_custom_call" | custom-call | flops 939524096 | bytes 4718592 | tf_op jit(solution)/shard_map/pallas_call | solution.py:56
  3.0 1.5 %shard_map.65 = (bf16[256,512]{1,0:T(8,128)(2,1)S(1)}, bf16[2,256,512]{2,1,0:T(8,128)(2,1)S(1)}, bf16[256,512]{1,0:T(8,128)(2,1)S(1)}, bf16[256,512]{1,0:T(8,128)(2,1)S(1)}) custom-call(bf16[2,256,512]{2,1,0:T(8,128)(2,1)S(1)} %get-tuple-element.38.retarded, bf16[2,256,512]{2,1,0:T(8,128)(2,1)S(1)} %get-tuple-element.39.coupling, ...), custom_call_target="tpu_custom_call" | custom-call | flops 1073741824 | bytes 3145728 | tf_op jit(solution)/shard_map/pallas_call | solution.py:56
  4.5 0.1 collective-permute-start.1
  4.6 0.5 %collective-permute-start = (bf16[256,512]{1,0:T(8,128)(2,1)S(1)}, bf16[256,512]{1,0:T(8,128)(2,1)S(1)}, u32[]{:S(2)}, u32[]{:S(2)}) collective-permute-start(bf16[256,512]{1,0:T(8,128)(2,1)S(1)} %get-tuple-element.44.upper.great_total), channel_id=1, source_target_pairs={{0,1},{1,0},{2,3},{3,2},{4,5},{5,4},{6,7},{7,6},{8,9},{9,8},{10,11... | collective-permute-start | bytes 786440 | tf_op jit(solution)/shard_map/ppermute | solution.py:478
  5.1 0.1 collective-permute-start.2
  5.2 0.9 %collective-permute-done.1.earlier.lower_whole = bf16[256,512]{1,0:T(8,128)(2,1)S(1)} collective-permute-done((bf16[256,512]{1,0:T(8,128)(2,1)S(1)}, bf16[256,512]{1,0:T(8,128)(2,1)S(1)}, u32[]{:S(2)}, u32[]{:S(2)}) %collective-permute-start.1) | collective-permute-done | bytes 262176 | tf_op jit(solution)/shard_map/ppermute | solution.py:478
  6.1 0.3 shard_map.67.chip_whole.step
  6.4 0.1 collective-permute-done.lower.lower_great
  6.5 0.4 collective-permute-done.2.lower
  6.9 0.6 %shard_map.69 = (bf16[2,256,512]{2,1,0:T(8,128)(2,1)S(1)}, bf16[256,512]{1,0:T(8,128)(2,1)S(1)}) custom-call(bf16[256,512]{1,0:T(8,128)(2,1)S(1)} %get-tuple-element.45.whole.later, bf16[256,512]{1,0:T(8,128)(2,1)S(1)} %shard_map.68.joined, bf16[256,512]{1,0:T(8,128)(2,1)S(1)} %get-tuple-element.42.first_step, ...), custom_call_target="tpu_custom_call" | custom-call | flops 536870912 | bytes 2883584 | tf_op jit(solution)/shard_map/pallas_call | solution.py:56
  7.4 1.0 %shard_map.70 = (bf16[1280,512]{1,0:T(8,128)(2,1)S(1)}, bf16[512,256]{1,0:T(8,128)(2,1)S(1)}, s32[4,8,128]{2,1,0:T(8,128)S(1)}) custom-call(s32[2,2]{1,0:T(2,128)} %tiles.1, s32[4]{0:T(128)} %offsets.1, bf16[256,512]{1,0:T(8,128)(2,1)S(1)} %get-tuple-element.42.first_step, bf16[1,256,512]{2,1,0:T(8,128)(2,1)S(1)} %get-tuple-element.41.later_steps, ...), custom_call_target="tpu_custom_call" | custom-call | flops 402653184 | bytes 4735008 | tf_op jit(solution)/shard_map/pallas_call | solution.py:56
  8.4 1.1 %collective-permute-start.10 = (bf16[1280,512]{1,0:T(8,128)(2,1)S(1)}, bf16[1280,512]{1,0:T(8,128)(2,1)S(1)}, u32[]{:S(2)}, u32[]{:S(2)}) collective-permute-start(bf16[1280,512]{1,0:T(8,128)(2,1)S(1)} %get-tuple-element.59.refs_0_), channel_id=1, source_target_pairs={{0,1},{1,0},{2,3},{3,2},{4,5},{5,4},{6,7},{7,6},{8,9},{9,8},{10,11... | collective-permute-start | bytes 3932168 | tf_op jit(solution)/shard_map/ppermute | solution.py:478
  9.5 0.1 collective-permute-start.3
  9.5 0.5 collective-permute-start.6
  10.0 2.5 %collective-permute-done.3.state = bf16[256,512]{1,0:T(8,128)(2,1)S(1)} collective-permute-done((bf16[256,512]{1,0:T(8,128)(2,1)S(1)}, bf16[256,512]{1,0:T(8,128)(2,1)S(1)}, u32[]{:S(2)}, u32[]{:S(2)}) %collective-permute-start.3) | collective-permute-done | bytes 262176 | tf_op jit(solution)/shard_map/ppermute | solution.py:498
  12.5 0.5 %shard_map.71 = (bf16[256,512]{1,0:T(8,128)(2,1)S(1)}, bf16[256,512]{1,0:T(8,128)(2,1)S(1)}) custom-call(bf16[256,512]{1,0:T(8,128)(2,1)S(1)} %collective-permute-done.3.state, bf16[256,512]{1,0:T(8,128)(2,1)S(1)} %shard_map.67.chip_whole.step, bf16[256,512]{1,0:T(8,128)(2,1)S(1)} %get-tuple-element.50.source), custom_call_target="tpu_custom_call" | custom-call | flops 268435456 | bytes 1310720 | tf_op jit(solution)/shard_map/pallas_call | solution.py:56
  13.0 1.4 %collective-permute-start.4 = (bf16[256,512]{1,0:T(8,128)(2,1)S(1)}, bf16[256,512]{1,0:T(8,128)(2,1)S(1)}, u32[]{:S(2)}, u32[]{:S(2)}) collective-permute-start(bf16[256,512]{1,0:T(8,128)(2,1)S(1)} %get-tuple-element.51), channel_id=1, source_target_pairs={{0,1},{1,0},{2,3},{3,5},{4,2},{5,4},{6,7},{7,6},{8,9},{9,8},{10,11... | collective-permute-start | bytes 786440 | tf_op jit(solution)/shard_map/ppermute | solution.py:498
  14.4 0.0 collective-permute-done.6.state
  14.4 0.5 %shard_map.73 = (bf16[256,512]{1,0:T(8,128)(2,1)S(1)}, bf16[256,512]{1,0:T(8,128)(2,1)S(1)}) custom-call(bf16[256,512]{1,0:T(8,128)(2,1)S(1)} %collective-permute-done.6.state, bf16[256,512]{1,0:T(8,128)(2,1)S(1)} %shard_map.67.chip_whole.step, bf16[256,512]{1,0:T(8,128)(2,1)S(1)} %shard_map.66.chip_great.source), custom_call_target="tpu_custom_call" | custom-call | flops 268435456 | bytes 1310720 | tf_op jit(solution)/shard_map/pallas_call | solution.py:56
  15.0 2.3 %collective-permute-start.7 = (bf16[256,512]{1,0:T(8,128)(2,1)S(1)}, bf16[256,512]{1,0:T(8,128)(2,1)S(1)}, u32[]{:S(2)}, u32[]{:S(2)}) collective-permute-start(bf16[256,512]{1,0:T(8,128)(2,1)S(1)} %get-tuple-element.54), channel_id=1, source_target_pairs={{0,1},{1,0},{2,3},{3,5},{4,2},{5,4},{6,7},{7,6},{8,9},{9,8},{10,11... | collective-permute-start | bytes 786440 | tf_op jit(solution)/shard_map/ppermute | solution.py:498
  17.2 1.1 %collective-permute-done.4.state = bf16[256,512]{1,0:T(8,128)(2,1)S(1)} collective-permute-done((bf16[256,512]{1,0:T(8,128)(2,1)S(1)}, bf16[256,512]{1,0:T(8,128)(2,1)S(1)}, u32[]{:S(2)}, u32[]{:S(2)}) %collective-permute-start.4) | collective-permute-done | bytes 262176 | tf_op jit(solution)/shard_map/ppermute | solution.py:498
  18.3 0.5 %shard_map.72 = (bf16[256,512]{1,0:T(8,128)(2,1)S(1)}, bf16[256,512]{1,0:T(8,128)(2,1)S(1)}) custom-call(bf16[256,512]{1,0:T(8,128)(2,1)S(1)} %collective-permute-done.4.state, bf16[256,512]{1,0:T(8,128)(2,1)S(1)} %shard_map.67.chip_whole.step, bf16[256,512]{1,0:T(8,128)(2,1)S(1)} %get-tuple-element.50.source, bf16[256,512]{1,0:T(8,128)(2,1)S(1)} %get-tuple-element.52.refs_0_), custom_call_target="tpu_custom_call" | custom-call | flops 268435456 | bytes 1572864 | tf_op jit(solution)/shard_map/pallas_call | solution.py:56
  18.8 1.1 %collective-permute-start.5 = (bf16[256,512]{1,0:T(8,128)(2,1)S(1)}, bf16[256,512]{1,0:T(8,128)(2,1)S(1)}, u32[]{:S(2)}, u32[]{:S(2)}) collective-permute-start(bf16[256,512]{1,0:T(8,128)(2,1)S(1)} %get-tuple-element.53), channel_id=1, source_target_pairs={{0,1},{1,0},{2,3},{3,2},{4,5},{5,4},{6,7},{7,6},{8,9},{9,8},{10,11... | collective-permute-start | bytes 786440 | tf_op jit(solution)/shard_map/ppermute | solution.py:478
  19.9 0.1 collective-permute-start.8
  20.0 1.1 %collective-permute-done.7.state = bf16[256,512]{1,0:T(8,128)(2,1)S(1)} collective-permute-done((bf16[256,512]{1,0:T(8,128)(2,1)S(1)}, bf16[256,512]{1,0:T(8,128)(2,1)S(1)}, u32[]{:S(2)}, u32[]{:S(2)}) %collective-permute-start.7) | collective-permute-done | bytes 262176 | tf_op jit(solution)/shard_map/ppermute | solution.py:498
  21.1 0.5 %shard_map.74 = (bf16[256,512]{1,0:T(8,128)(2,1)S(1)}, bf16[256,512]{1,0:T(8,128)(2,1)S(1)}) custom-call(bf16[256,512]{1,0:T(8,128)(2,1)S(1)} %collective-permute-done.7.state, bf16[256,512]{1,0:T(8,128)(2,1)S(1)} %shard_map.67.chip_whole.step, bf16[256,512]{1,0:T(8,128)(2,1)S(1)} %shard_map.66.chip_great.source, bf16[256,512]{1,0:T(8,128)(2,1)S(1)} %get-tuple-element.55.refs_0_), custom_call_target="tpu_custom_call" | custom-call | flops 268435456 | bytes 1572864 | tf_op jit(solution)/shard_map/pallas_call | solution.py:56
  21.7 1.4 %collective-permute-start.9 = (bf16[256,512]{1,0:T(8,128)(2,1)S(1)}, bf16[256,512]{1,0:T(8,128)(2,1)S(1)}, u32[]{:S(2)}, u32[]{:S(2)}) collective-permute-start(bf16[256,512]{1,0:T(8,128)(2,1)S(1)} %get-tuple-element.58), channel_id=1, source_target_pairs={{0,1},{1,0},{2,3},{3,2},{4,5},{5,7},{6,22},{7,4},{8,9},{9,8},{10,1... | collective-permute-start | bytes 786440 | tf_op jit(solution)/shard_map/ppermute | solution.py:498
  23.1 0.0 collective-permute-done.5.near.lesser
  23.1 0.0 collective-permute-done.10.refs_1_
  23.1 1.1 %shard_map.76 = (bf16[2,128,256]{2,1,0:T(8,128)(2,1)S(1)}, bf16[2,128,256]{2,1,0:T(8,128)(2,1)S(1)}, bf16[2,128,256]{2,1,0:T(8,128)(2,1)S(1)}) custom-call(bf16[256,512]{1,0:T(8,128)(2,1)S(1)} %collective-permute-done.5.near.lesser, bf16[256,512]{1,0:T(8,128)(2,1)S(1)} %get-tuple-element.56.kept.greater, bf16[1280,512]{1,0:T(8,128)(2,1)S(1)} %get-tuple-element.59.refs_0_, ...), custom_call_target="tpu_custom_call" | custom-call | flops 671088640 | bytes 3801088 | tf_op jit(solution)/shard_map/pallas_call | solution.py:56
  24.1 1.6 %collective-permute-done.8.lesser = bf16[256,512]{1,0:T(8,128)(2,1)S(1)} collective-permute-done((bf16[256,512]{1,0:T(8,128)(2,1)S(1)}, bf16[256,512]{1,0:T(8,128)(2,1)S(1)}, u32[]{:S(2)}, u32[]{:S(2)}) %collective-permute-start.8) | collective-permute-done | bytes 262176 | tf_op jit(solution)/shard_map/ppermute | solution.py:498
  25.7 2.8 %collective-permute-done.9.greater = bf16[256,512]{1,0:T(8,128)(2,1)S(1)} collective-permute-done((bf16[256,512]{1,0:T(8,128)(2,1)S(1)}, bf16[256,512]{1,0:T(8,128)(2,1)S(1)}, u32[]{:S(2)}, u32[]{:S(2)}) %collective-permute-start.9) | collective-permute-done | bytes 262176 | tf_op jit(solution)/shard_map/ppermute | solution.py:498
  28.5 1.5 %collective-permute-start.11 = (bf16[2,128,256]{2,1,0:T(8,128)(2,1)S(1)}, bf16[2,128,256]{2,1,0:T(8,128)(2,1)S(1)}, u32[]{:S(2)}, u32[]{:S(2)}) collective-permute-start(bf16[2,128,256]{2,1,0:T(8,128)(2,1)S(1)} %get-tuple-element.64), channel_id=1, source_target_pairs={{0,8},{8,0},{16,24},{24,16},{1,9},{9,1},{17,25},{25,17},{2,10},{10... | collective-permute-start | bytes 393224 | tf_op jit(solution)/shard_map/ppermute | solution.py:501
  30.0 1.5 %collective-permute-start.12 = (bf16[2,128,256]{2,1,0:T(8,128)(2,1)S(1)}, bf16[2,128,256]{2,1,0:T(8,128)(2,1)S(1)}, u32[]{:S(2)}, u32[]{:S(2)}) collective-permute-start(bf16[2,128,256]{2,1,0:T(8,128)(2,1)S(1)} %get-tuple-element.65), channel_id=1, source_target_pairs={{0,16},{8,24},{16,0},{24,8},{1,17},{9,25},{17,1},{25,9},{2,18},{10... | collective-permute-start | bytes 393224 | tf_op jit(solution)/shard_map/ppermute | solution.py:501
  31.6 0.5 %collective-permute-start.13 = (bf16[2,128,256]{2,1,0:T(8,128)(2,1)S(1)}, bf16[2,128,256]{2,1,0:T(8,128)(2,1)S(1)}, u32[]{:S(2)}, u32[]{:S(2)}) collective-permute-start(bf16[2,128,256]{2,1,0:T(8,128)(2,1)S(1)} %get-tuple-element.66), channel_id=1, source_target_pairs={{0,24},{8,16},{16,8},{24,0},{1,25},{9,17},{17,9},{25,1},{2,26},{10... | collective-permute-start | bytes 393224 | tf_op jit(solution)/shard_map/ppermute | solution.py:501
  32.0 0.7 %shard_map.75.refs_0_ = bf16[2,128,256]{2,1,0:T(8,128)(2,1)S(1)} custom-call(bf16[256,512]{1,0:T(8,128)(2,1)S(1)} %collective-permute-done.5.near.lesser, bf16[256,512]{1,0:T(8,128)(2,1)S(1)} %get-tuple-element.56.kept.greater, bf16[256,512]{1,0:T(8,128)(2,1)S(1)} %collective-permute-done.8.lesser, bf16[256,512]{1,0:T(8,128)(2,1)S(1)} %collective-permute-done.9.greater, ...), custom_call_target="tpu_custom_call" | custom-call | flops 268435456 | bytes 4063232 | tf_op jit(solution)/shard_map/pallas_call | solution.py:56
  32.7 1.3 %collective-permute-done.11.refs_1_ = bf16[2,128,256]{2,1,0:T(8,128)(2,1)S(1)} collective-permute-done((bf16[2,128,256]{2,1,0:T(8,128)(2,1)S(1)}, bf16[2,128,256]{2,1,0:T(8,128)(2,1)S(1)}, u32[]{:S(2)}, u32[]{:S(2)}) %collective-permute-start.11) | collective-permute-done | bytes 131104 | tf_op jit(solution)/shard_map/ppermute | solution.py:501
  34.0 1.2 %collective-permute-done.12.refs_2_ = bf16[2,128,256]{2,1,0:T(8,128)(2,1)S(1)} collective-permute-done((bf16[2,128,256]{2,1,0:T(8,128)(2,1)S(1)}, bf16[2,128,256]{2,1,0:T(8,128)(2,1)S(1)}, u32[]{:S(2)}, u32[]{:S(2)}) %collective-permute-start.12) | collective-permute-done | bytes 131104 | tf_op jit(solution)/shard_map/ppermute | solution.py:501
  35.2 2.2 %collective-permute-done.13.refs_3_ = bf16[2,128,256]{2,1,0:T(8,128)(2,1)S(1)} collective-permute-done((bf16[2,128,256]{2,1,0:T(8,128)(2,1)S(1)}, bf16[2,128,256]{2,1,0:T(8,128)(2,1)S(1)}, u32[]{:S(2)}, u32[]{:S(2)}) %collective-permute-start.13) | collective-permute-done | bytes 131104 | tf_op jit(solution)/shard_map/ppermute | solution.py:501
  37.4 0.1 collective-permute-start.14
  37.5 1.5 %collective-permute-done.14.swapped = bf16[4,128,256]{2,1,0:T(8,128)(2,1)S(1)} collective-permute-done((bf16[4,128,256]{2,1,0:T(8,128)(2,1)S(1)}, bf16[4,128,256]{2,1,0:T(8,128)(2,1)S(1)}, u32[]{:S(2)}, u32[]{:S(2)}) %collective-permute-start.14) | collective-permute-done | bytes 262176 | tf_op jit(solution)/shard_map/ppermute | solution.py:478
  39.0 0.4 shard_map.79
  39.4 0.6 %collective-permute-start.15 = (bf16[128,256]{1,0:T(8,128)(2,1)S(1)}, bf16[128,256]{1,0:T(8,128)(2,1)S(1)}, u32[]{:S(2)}, u32[]{:S(2)}) collective-permute-start(bf16[128,256]{1,0:T(8,128)(2,1)S(1)} %get-tuple-element.68), channel_id=1, source_target_pairs={{0,8},{8,0},{16,24},{24,16},{1,9},{9,1},{17,25},{25,17},{2,10},{10... | collective-permute-start | bytes 196616 | tf_op jit(solution)/shard_map/ppermute | solution.py:501
  40.0 0.5 %collective-permute-start.16 = (bf16[128,256]{1,0:T(8,128)(2,1)S(1)}, bf16[128,256]{1,0:T(8,128)(2,1)S(1)}, u32[]{:S(2)}, u32[]{:S(2)}) collective-permute-start(bf16[128,256]{1,0:T(8,128)(2,1)S(1)} %get-tuple-element.69), channel_id=1, source_target_pairs={{0,16},{8,24},{16,0},{24,8},{1,17},{9,25},{17,1},{25,9},{2,18},{10... | collective-permute-start | bytes 196616 | tf_op jit(solution)/shard_map/ppermute | solution.py:501
  40.6 2.4 %collective-permute-start.17 = (bf16[128,256]{1,0:T(8,128)(2,1)S(1)}, bf16[128,256]{1,0:T(8,128)(2,1)S(1)}, u32[]{:S(2)}, u32[]{:S(2)}) collective-permute-start(bf16[128,256]{1,0:T(8,128)(2,1)S(1)} %get-tuple-element.70), channel_id=1, source_target_pairs={{0,24},{8,16},{16,8},{24,0},{1,25},{9,17},{17,9},{25,1},{2,26},{10... | collective-permute-start | bytes 196616 | tf_op jit(solution)/shard_map/ppermute | solution.py:501
  43.0 0.9 %collective-permute-done.15.refs_1_ = bf16[128,256]{1,0:T(8,128)(2,1)S(1)} collective-permute-done((bf16[128,256]{1,0:T(8,128)(2,1)S(1)}, bf16[128,256]{1,0:T(8,128)(2,1)S(1)}, u32[]{:S(2)}, u32[]{:S(2)}) %collective-permute-start.15) | collective-permute-done | bytes 65568 | tf_op jit(solution)/shard_map/ppermute | solution.py:501
  43.9 1.1 %collective-permute-done.16.refs_2_ = bf16[128,256]{1,0:T(8,128)(2,1)S(1)} collective-permute-done((bf16[128,256]{1,0:T(8,128)(2,1)S(1)}, bf16[128,256]{1,0:T(8,128)(2,1)S(1)}, u32[]{:S(2)}, u32[]{:S(2)}) %collective-permute-start.16) | collective-permute-done | bytes 65568 | tf_op jit(solution)/shard_map/ppermute | solution.py:501
  45.0 0.7 %collective-permute-done.17.refs_3_ = bf16[128,256]{1,0:T(8,128)(2,1)S(1)} collective-permute-done((bf16[128,256]{1,0:T(8,128)(2,1)S(1)}, bf16[128,256]{1,0:T(8,128)(2,1)S(1)}, u32[]{:S(2)}, u32[]{:S(2)}) %collective-permute-start.17) | collective-permute-done | bytes 65568 | tf_op jit(solution)/shard_map/ppermute | solution.py:501
  45.7 0.7 %shard_map.80 = bf16[4,128,256]{2,1,0:T(8,128)(2,1)} custom-call(bf16[128,256]{1,0:T(8,128)(2,1)S(1)} %get-tuple-element.67.refs_0_, bf16[128,256]{1,0:T(8,128)(2,1)S(1)} %collective-permute-done.15.refs_1_, bf16[128,256]{1,0:T(8,128)(2,1)S(1)} %collective-permute-done.16.refs_2_, bf16[128,256]{1,0:T(8,128)(2,1)S(1)} %collective-permute-done.17.refs_3_), custom_call_target="tpu_custom_call" | custom-call | bytes 524288 | tf_op jit(solution)/shard_map/pallas_call | solution.py:56
  (4 shorter events, 0.0 us)
Async XLA Ops:
  4.5 1.6 %collective-permute-start.1 = (bf16[256,512]{1,0:T(8,128)(2,1)S(1)}, bf16[256,512]{1,0:T(8,128)(2,1)S(1)}, u32[]{:S(2)}, u32[]{:S(2)}) collective-permute-start(bf16[256,512]{1,0:T(8,128)(2,1)S(1)} %get-tuple-element.45.whole.later), channel_id=1, source_target_pairs={{0,1},{1,0},{2,3},{3,2},{4,5},{5,4},{6,7},{7,6},{8,9},{9,8},{10,11... | collective-permute-start | bytes 786440 | tf_op jit(solution)/shard_map/ppermute | solution.py:478
  4.6 1.9 %collective-permute-start = (bf16[256,512]{1,0:T(8,128)(2,1)S(1)}, bf16[256,512]{1,0:T(8,128)(2,1)S(1)}, u32[]{:S(2)}, u32[]{:S(2)}) collective-permute-start(bf16[256,512]{1,0:T(8,128)(2,1)S(1)} %get-tuple-element.44.upper.great_total), channel_id=1, source_target_pairs={{0,1},{1,0},{2,3},{3,2},{4,5},{5,4},{6,7},{7,6},{8,9},{9,8},{10,11... | collective-permute-start | bytes 786440 | tf_op jit(solution)/shard_map/ppermute | solution.py:478
  5.1 1.8 %collective-permute-start.2 = (bf16[256,512]{1,0:T(8,128)(2,1)S(1)}, bf16[256,512]{1,0:T(8,128)(2,1)S(1)}, u32[]{:S(2)}, u32[]{:S(2)}) collective-permute-start(bf16[256,512]{1,0:T(8,128)(2,1)S(1)} %get-tuple-element.46.upper.total), channel_id=1, source_target_pairs={{0,1},{1,0},{2,3},{3,2},{4,5},{5,4},{6,7},{7,6},{8,9},{9,8},{10,11... | collective-permute-start | bytes 786440 | tf_op jit(solution)/shard_map/ppermute | solution.py:478
  8.4 14.6 %collective-permute-start.10 = (bf16[1280,512]{1,0:T(8,128)(2,1)S(1)}, bf16[1280,512]{1,0:T(8,128)(2,1)S(1)}, u32[]{:S(2)}, u32[]{:S(2)}) collective-permute-start(bf16[1280,512]{1,0:T(8,128)(2,1)S(1)} %get-tuple-element.59.refs_0_), channel_id=1, source_target_pairs={{0,1},{1,0},{2,3},{3,2},{4,5},{5,4},{6,7},{7,6},{8,9},{9,8},{10,11... | collective-permute-start | bytes 3932168 | tf_op jit(solution)/shard_map/ppermute | solution.py:478
  9.5 3.0 %collective-permute-start.3 = (bf16[256,512]{1,0:T(8,128)(2,1)S(1)}, bf16[256,512]{1,0:T(8,128)(2,1)S(1)}, u32[]{:S(2)}, u32[]{:S(2)}) collective-permute-start(bf16[256,512]{1,0:T(8,128)(2,1)S(1)} %shard_map.68.joined), channel_id=1, source_target_pairs={{0,1},{1,3},{2,0},{3,2},{4,5},{5,4},{6,7},{7,6},{8,9},{9,11},{10,8... | collective-permute-start | bytes 786440 | tf_op jit(solution)/shard_map/ppermute | solution.py:498
  9.5 4.9 %collective-permute-start.6 = (bf16[256,512]{1,0:T(8,128)(2,1)S(1)}, bf16[256,512]{1,0:T(8,128)(2,1)S(1)}, u32[]{:S(2)}, u32[]{:S(2)}) collective-permute-start(bf16[256,512]{1,0:T(8,128)(2,1)S(1)} %shard_map.66.chip_great.source), channel_id=1, source_target_pairs={{0,1},{1,3},{2,0},{3,2},{4,5},{5,4},{6,7},{7,6},{8,9},{9,11},{10,8... | collective-permute-start | bytes 786440 | tf_op jit(solution)/shard_map/ppermute | solution.py:498
  13.0 5.3 %collective-permute-start.4 = (bf16[256,512]{1,0:T(8,128)(2,1)S(1)}, bf16[256,512]{1,0:T(8,128)(2,1)S(1)}, u32[]{:S(2)}, u32[]{:S(2)}) collective-permute-start(bf16[256,512]{1,0:T(8,128)(2,1)S(1)} %get-tuple-element.51), channel_id=1, source_target_pairs={{0,1},{1,0},{2,3},{3,5},{4,2},{5,4},{6,7},{7,6},{8,9},{9,8},{10,11... | collective-permute-start | bytes 786440 | tf_op jit(solution)/shard_map/ppermute | solution.py:498
  15.0 6.2 %collective-permute-start.7 = (bf16[256,512]{1,0:T(8,128)(2,1)S(1)}, bf16[256,512]{1,0:T(8,128)(2,1)S(1)}, u32[]{:S(2)}, u32[]{:S(2)}) collective-permute-start(bf16[256,512]{1,0:T(8,128)(2,1)S(1)} %get-tuple-element.54), channel_id=1, source_target_pairs={{0,1},{1,0},{2,3},{3,5},{4,2},{5,4},{6,7},{7,6},{8,9},{9,8},{10,11... | collective-permute-start | bytes 786440 | tf_op jit(solution)/shard_map/ppermute | solution.py:498
  18.8 4.2 %collective-permute-start.5 = (bf16[256,512]{1,0:T(8,128)(2,1)S(1)}, bf16[256,512]{1,0:T(8,128)(2,1)S(1)}, u32[]{:S(2)}, u32[]{:S(2)}) collective-permute-start(bf16[256,512]{1,0:T(8,128)(2,1)S(1)} %get-tuple-element.53), channel_id=1, source_target_pairs={{0,1},{1,0},{2,3},{3,2},{4,5},{5,4},{6,7},{7,6},{8,9},{9,8},{10,11... | collective-permute-start | bytes 786440 | tf_op jit(solution)/shard_map/ppermute | solution.py:478
  19.9 5.8 %collective-permute-start.8 = (bf16[256,512]{1,0:T(8,128)(2,1)S(1)}, bf16[256,512]{1,0:T(8,128)(2,1)S(1)}, u32[]{:S(2)}, u32[]{:S(2)}) collective-permute-start(bf16[256,512]{1,0:T(8,128)(2,1)S(1)} %get-tuple-element.57), channel_id=1, source_target_pairs={{0,1},{1,0},{2,3},{3,2},{4,5},{5,6},{6,7},{7,4},{8,9},{9,8},{10,11... | collective-permute-start | bytes 786440 | tf_op jit(solution)/shard_map/ppermute | solution.py:498
  21.7 6.9 %collective-permute-start.9 = (bf16[256,512]{1,0:T(8,128)(2,1)S(1)}, bf16[256,512]{1,0:T(8,128)(2,1)S(1)}, u32[]{:S(2)}, u32[]{:S(2)}) collective-permute-start(bf16[256,512]{1,0:T(8,128)(2,1)S(1)} %get-tuple-element.58), channel_id=1, source_target_pairs={{0,1},{1,0},{2,3},{3,2},{4,5},{5,7},{6,22},{7,4},{8,9},{9,8},{10,1... | collective-permute-start | bytes 786440 | tf_op jit(solution)/shard_map/ppermute | solution.py:498
  28.5 5.4 %collective-permute-start.11 = (bf16[2,128,256]{2,1,0:T(8,128)(2,1)S(1)}, bf16[2,128,256]{2,1,0:T(8,128)(2,1)S(1)}, u32[]{:S(2)}, u32[]{:S(2)}) collective-permute-start(bf16[2,128,256]{2,1,0:T(8,128)(2,1)S(1)} %get-tuple-element.64), channel_id=1, source_target_pairs={{0,8},{8,0},{16,24},{24,16},{1,9},{9,1},{17,25},{25,17},{2,10},{10... | collective-permute-start | bytes 393224 | tf_op jit(solution)/shard_map/ppermute | solution.py:501
  30.0 5.2 %collective-permute-start.12 = (bf16[2,128,256]{2,1,0:T(8,128)(2,1)S(1)}, bf16[2,128,256]{2,1,0:T(8,128)(2,1)S(1)}, u32[]{:S(2)}, u32[]{:S(2)}) collective-permute-start(bf16[2,128,256]{2,1,0:T(8,128)(2,1)S(1)} %get-tuple-element.65), channel_id=1, source_target_pairs={{0,16},{8,24},{16,0},{24,8},{1,17},{9,25},{17,1},{25,9},{2,18},{10... | collective-permute-start | bytes 393224 | tf_op jit(solution)/shard_map/ppermute | solution.py:501
  31.6 5.9 %collective-permute-start.13 = (bf16[2,128,256]{2,1,0:T(8,128)(2,1)S(1)}, bf16[2,128,256]{2,1,0:T(8,128)(2,1)S(1)}, u32[]{:S(2)}, u32[]{:S(2)}) collective-permute-start(bf16[2,128,256]{2,1,0:T(8,128)(2,1)S(1)} %get-tuple-element.66), channel_id=1, source_target_pairs={{0,24},{8,16},{16,8},{24,0},{1,25},{9,17},{17,9},{25,1},{2,26},{10... | collective-permute-start | bytes 393224 | tf_op jit(solution)/shard_map/ppermute | solution.py:501
  37.4 1.6 %collective-permute-start.14 = (bf16[4,128,256]{2,1,0:T(8,128)(2,1)S(1)}, bf16[4,128,256]{2,1,0:T(8,128)(2,1)S(1)}, u32[]{:S(2)}, u32[]{:S(2)}) collective-permute-start(bf16[4,128,256]{2,1,0:T(8,128)(2,1)S(1)} %shard_map.78), channel_id=1, source_target_pairs={{0,1},{1,0},{2,3},{3,2},{4,5},{5,4},{6,7},{7,6},{8,9},{9,8},{10,11... | collective-permute-start | bytes 786440 | tf_op jit(solution)/shard_map/ppermute | solution.py:478
  39.4 4.5 %collective-permute-start.15 = (bf16[128,256]{1,0:T(8,128)(2,1)S(1)}, bf16[128,256]{1,0:T(8,128)(2,1)S(1)}, u32[]{:S(2)}, u32[]{:S(2)}) collective-permute-start(bf16[128,256]{1,0:T(8,128)(2,1)S(1)} %get-tuple-element.68), channel_id=1, source_target_pairs={{0,8},{8,0},{16,24},{24,16},{1,9},{9,1},{17,25},{25,17},{2,10},{10... | collective-permute-start | bytes 196616 | tf_op jit(solution)/shard_map/ppermute | solution.py:501
  40.0 5.0 %collective-permute-start.16 = (bf16[128,256]{1,0:T(8,128)(2,1)S(1)}, bf16[128,256]{1,0:T(8,128)(2,1)S(1)}, u32[]{:S(2)}, u32[]{:S(2)}) collective-permute-start(bf16[128,256]{1,0:T(8,128)(2,1)S(1)} %get-tuple-element.69), channel_id=1, source_target_pairs={{0,16},{8,24},{16,0},{24,8},{1,17},{9,25},{17,1},{25,9},{2,18},{10... | collective-permute-start | bytes 196616 | tf_op jit(solution)/shard_map/ppermute | solution.py:501
  40.6 5.2 %collective-permute-start.17 = (bf16[128,256]{1,0:T(8,128)(2,1)S(1)}, bf16[128,256]{1,0:T(8,128)(2,1)S(1)}, u32[]{:S(2)}, u32[]{:S(2)}) collective-permute-start(bf16[128,256]{1,0:T(8,128)(2,1)S(1)} %get-tuple-element.70), channel_id=1, source_target_pairs={{0,24},{8,16},{16,8},{24,0},{1,25},{9,17},{17,9},{25,1},{2,26},{10... | collective-permute-start | bytes 196616 | tf_op jit(solution)/shard_map/ppermute | solution.py:501

commit v6 on v5

--- a/solution.py
+++ b/solution.py
@@ -85,6 +85,44 @@
             part.wait()
 
 
+def on_first_chip():
+    return (lax.axis_index("domain") >> 1) == 0
+
+
+def lesser_chain(blocks, retarded, coupling, sigma, later_steps, sources, total, ready):
+    state = None
+    for k in range(blocks):
+        ready("r", k)
+        ready("l", k)
+        source = injected(retarded[k], sigma[k])
+        sources[k] = source
+        if k > 0:
+            ready("c", k)
+            step = product(retarded[k], coupling[k])
+            later_steps[k - 1] = step
+        state = source if k == 0 else advance(state, step, source)
+    total[...] = state
+
+
+def greater_chain(
+    blocks, retarded, coupling, sigma, later_steps, first_step, sources, total, whole
+):
+    state = chain = None
+    for k in range(blocks):
+        source = injected(retarded[k], sigma[k])
+        sources[k] = source
+        if k == 0:
+            chain = product(retarded[0], coupling[0])
+            first_step[...] = chain
+            state = source
+        else:
+            step = later_steps[k - 1]
+            chain = product(step, chain)
+            state = advance(state, step, source)
+    total[...] = state
+    whole[...] = chain
+
+
 def first_kernel(
     blocks,
     retarded,
@@ -93,11 +131,11 @@
     greater,
     held_retarded,
     held_coupling,
+    held_lesser,
     held_greater,
     later_steps,
     sources,
     total,
-    held_lesser,
     sem,
 ):
     copies = {}
@@ -111,54 +149,138 @@
         copies["g", k] = (greater.at[0, k], held_greater.at[k])
     for index, (key, (source, target)) in enumerate(copies.items()):
         copies[key] = Copies(source, target, sem.at[index])
-    state = None
-    for k in range(blocks):
-        copies["r", k].wait()
-        copies["l", k].wait()
-        source = injected(held_retarded[k], held_lesser[k])
-        sources[k] = source
-        if k > 0:
-            copies["c", k].wait()
-            step = product(held_retarded[k], held_coupling[k])
-            later_steps[k - 1] = step
-        state = source if k == 0 else advance(state, step, source)
-    total[...] = state
-    copies["c", 0].wait()
-    for k in range(blocks):
-        copies["g", k].wait()
+    early = [key for key in copies if key[0] in "rl" or (key[0] == "c" and key[1] > 0)]
+    first_chip = on_first_chip()
+
+    @pl.when(first_chip)
+    def _():
+        lesser_chain(
+            blocks,
+            held_retarded,
+            held_coupling,
+            held_lesser,
+            later_steps,
+            sources,
+            total,
+            lambda *key: copies[key].wait(),
+        )
+
+    @pl.when(jnp.logical_not(first_chip))
+    def _():
+        for key in early:
+            copies[key].wait()
+
+    for key in copies:
+        if key not in early:
+            copies[key].wait()
 
 
 def second_kernel(
-    blocks, retarded, coupling, greater, later_steps, first_step, sources, total, whole
+    blocks,
+    retarded,
+    coupling,
+    lesser,
+    greater,
+    given_steps,
+    given_sources,
+    given_total,
+    later_steps,
+    less_sources,
+    less_total,
+    first_step,
+    great_sources,
+    great_total,
+    whole,
 ):
-    state = chain = None
-    for k in range(blocks):
-        source = injected(retarded[k], greater[k])
-        sources[k] = source
-        if k == 0:
-            chain = product(retarded[0], coupling[0])
-            first_step[...] = chain
-            state = source
-        else:
-            step = later_steps[k - 1]
-            chain = product(step, chain)
-            state = advance(state, step, source)
-    total[...] = state
-    whole[...] = chain
-
-
-def join_kernel(every_chip, lower, whole, upper, out):
-    needed = (lax.axis_index("domain") & 1) == 1
-    if not every_chip:
-        needed &= (lax.axis_index("domain") >> 1) == 0
-
-    @pl.when(needed)
+    first_chip = on_first_chip()
+
+    @pl.when(first_chip)
+    def _():
+        greater_chain(
+            blocks,
+            retarded,
+            coupling,
+            greater,
+            given_steps,
+            first_step,
+            great_sources,
+            great_total,
+            whole,
+        )
+        less_total[...] = given_total[...]
+
+    @pl.when(jnp.logical_not(first_chip))
+    def _():
+        lesser_chain(
+            blocks,
+            retarded,
+            coupling,
+            lesser,
+            later_steps,
+            less_sources,
+            less_total,
+            lambda *key: None,
+        )
+
+
+def third_kernel(
+    blocks,
+    retarded,
+    coupling,
+    greater,
+    later_steps,
+    given_step,
+    given_sources,
+    given_total,
+    given_whole,
+    first_step,
+    sources,
+    total,
+    whole,
+):
+    first_chip = on_first_chip()
+
+    @pl.when(first_chip)
+    def _():
+        total[...] = given_total[...]
+        whole[...] = given_whole[...]
+
+    @pl.when(jnp.logical_not(first_chip))
+    def _():
+        greater_chain(
+            blocks,
+            retarded,
+            coupling,
+            greater,
+            later_steps,
+            first_step,
+            sources,
+            total,
+            whole,
+        )
+
+
+def join_first_kernel(lower, whole, upper, out):
+    @pl.when(lax.axis_index("domain") == 1)
     def _():
         out[...] = advance(lower[...], whole[...], upper[...])
 
 
-def chain_kernel(later, earlier, out):
-    out[...] = product(later[...], earlier[...])
+def join_kernel(joined, lower, lower_whole, whole, upper, chip, chip_whole):
+    on_upper = (lax.axis_index("domain") & 1) == 1
+    first_chip = on_first_chip()
+
+    @pl.when(on_upper)
+    def _():
+        chip_whole[...] = product(whole[...], lower_whole[...])
+
+    @pl.when(on_upper & first_chip)
+    def _():
+        chip[...] = joined[...]
+
+    @pl.when(on_upper & jnp.logical_not(first_chip))
+    def _():
+        chip[...] = advance(lower[...], whole[...], upper[...])
 
 
 def keep(z, state, kept, out):
@@ -175,7 +297,11 @@
 
 def advance_kernel(z, state, step, source, *refs):
     kept, (out, chosen) = (refs[0] if len(refs) == 3 else None), refs[-2:]
-    out[...] = advance(state[...], step[...], source[...])
+
+    @pl.when((lax.axis_index("domain") >> 1) == z)
+    def _():
+        out[...] = advance(state[...], step[...], source[...])
+
     keep(z, state, kept, chosen)
 
 
@@ -215,7 +341,7 @@
     states,
     chip,
 ):
-    first_chip = (lax.axis_index("domain") >> 1) == 0
+    first_chip = on_first_chip()
 
     @pl.when(first_chip)
     def _():
@@ -500,41 +626,48 @@
     def across(x, k):
         return lax.ppermute(x, "energy", [(e, e ^ k) for e in range(energies)])
 
-    held_retarded, held_coupling, held_greater, later_steps, less_sources, less_total = (
-        kernel_call(
-            functools.partial(first_kernel, blocks),
-            [series(blocks)] * 3 + [series(blocks - 1), series(blocks), block],
-            in_place(retarded, coupling, sigma_lesser, sigma_greater),
-            (5 * blocks - 3) * unit,
-            in_specs=[HBM] * 4,
-            scratch=[
-                pltpu.VMEM((blocks, order, 2 * order), BF16),
-                pltpu.SemaphoreType.DMA((4 * blocks, 2)),
-            ],
-        )
+    held_retarded, held_coupling, held_less, held_great, *less_set = kernel_call(
+        functools.partial(first_kernel, blocks),
+        [series(blocks)] * 4 + [series(blocks - 1), series(blocks), block],
+        in_place(retarded, coupling, sigma_lesser, sigma_greater),
+        (5 * blocks - 3) * unit,
+        in_specs=[HBM] * 4,
+        scratch=[pltpu.SemaphoreType.DMA((4 * blocks, 2))],
+    )
+    early_less = less_set[2]
+    lower_less = swap(early_less)
+    later_steps, less_sources, less_total, *great_set = kernel_call(
+        functools.partial(second_kernel, blocks),
+        [series(blocks - 1), series(blocks), block]
+        + [block, series(blocks), block, block],
+        (held_retarded, held_coupling, held_less, held_great, *less_set),
+        (5 * blocks - 2) * unit,
+        aliases={4: 0, 5: 1},
+    )
+    early_great, early_whole = great_set[2:]
+    (joined_less,) = kernel_call(
+        join_first_kernel, [block], (lower_less, early_whole, early_less), 2 * unit
     )
     lower_less = swap(less_total)
+    lower_great = swap(early_great)
     first_step, great_sources, great_total, whole = kernel_call(
-        functools.partial(second_kernel, blocks),
+        functools.partial(third_kernel, blocks),
         [block, series(blocks), block, block],
-        (held_retarded, held_coupling, held_greater, later_steps),
+        (held_retarded, held_coupling, held_great, later_steps, *great_set),
         (5 * blocks - 2) * unit,
+        aliases={4: 0, 5: 1},
+    )
+    (joined_great,) = kernel_call(
+        join_first_kernel, [block], (lower_great, early_whole, early_great), 2 * unit
     )
     lower_great = swap(great_total)
     lower_whole = swap(whole)
-    (joined_less,) = kernel_call(
-        functools.partial(join_kernel, False),
-        [block],
-        (lower_less, whole, less_total),
-        2 * unit,
-    )
-    (chip_great,) = kernel_call(
-        functools.partial(join_kernel, True),
-        [block],
-        (lower_great, whole, great_total),
-        2 * unit,
-    )
-    (chip_whole,) = kernel_call(chain_kernel, [block], (whole, lower_whole), unit)
+    chip_great, chip_whole = kernel_call(
+        join_kernel,
+        [block] * 2,
+        (joined_great, lower_great, lower_whole, whole, great_total),
+        3 * unit,
+    )
     lessers, chip_less = kernel_call(
         functools.partial(prepare_lesser_kernel, blocks),
         [series(blocks), block],
@@ -583,7 +716,7 @@
             2 * unit,
         )
 
-    less, great = joined_less, chip_great
+    less, great = joined_less, joined_great
     less_in, great_in = (), ()
     for z in range(1, chips):
         less = hop(less, z, lower=z == chips - 1)

time: 46.6 us -> 47.7 us (1.024)
  starting transfers between devices: 15.5 us -> 17.5 us
  Pallas kernels: 11.4 us -> 10.2 us
    pallas_call x17 -> x18, Pallas kernels: 11.4 us -> 10.2 us  [kernel_call(): pl.pallas_call(body, out_shape=outs, in_specs=in_specs or [VMEM] * len(op...]
    ppermute x6, starting transfers between devices: 5.62 us -> 6.65 us  [hop(): return lax.ppermute(x, ('energy', 'domain'), route)]
    ppermute x6 -> x8, starting transfers between devices: 2.87 us -> 3.78 us  [swap(): return lax.ppermute(x, 'domain', [(d, d ^ 1) for d in range(domains)])]
    ppermute x6 -> x8, waiting for transfers between devices: 2.91 us -> 3.22 us  [swap(): return lax.ppermute(x, 'domain', [(d, d ^ 1) for d in range(domains)])]
  transfers between devices with their start and end apart: 18 -> 20, of which waited for: 15 -> 15; matrix products, arithmetic and copies ran while one was open for 0% -> 0% of each run, Pallas kernels for 9% -> 12%
where the time goes in v6:
time: 47.7 us; the launch traced here: 47.5 us
  waiting for transfers between devices  19.7 us (41%)
  starting transfers between devices  17.5 us (37%)
  Pallas kernels  10.2 us (21%)
    pallas_call x18, Pallas kernels, kernel_call(): pl.pallas_call(body, out_shape=outs, in_specs=in_specs or [VMEM] * len(op...  10.2 us
    ppermute x6, waiting for transfers between devices, hop(): return lax.ppermute(x, ('energy', 'domain'), route)  9.12 us
    ppermute x6, waiting for transfers between devices, across(): return lax.ppermute(x, 'energy', [(e, e ^ k) for e in range(energies)])  7.41 us
    ppermute x6, starting transfers between devices, across(): return lax.ppermute(x, 'energy', [(e, e ^ k) for e in range(energies)])  7.04 us
    ppermute x6, starting transfers between devices, hop(): return lax.ppermute(x, ('energy', 'domain'), route)  6.65 us
    ppermute x8, starting transfers between devices, swap(): return lax.ppermute(x, 'domain', [(d, d ^ 1) for d in range(domains)])  3.78 us
    ppermute x8, waiting for transfers between devices, swap(): return lax.ppermute(x, 'domain', [(d, d ^ 1) for d in range(domains)])  3.22 us
  transfers between devices with their start and end apart: 20, of which 15 were waited for; matrix products, arithmetic and copies ran while one was open for 0% of the time, Pallas kernels for 12%

profile of v6, /device:TPU:16, one launch (start us, length us, event | category | flops | bytes accessed | tf_op | source)
XLA Modules:
  0.0 47.5 jit_solution(8847658692491336418)
XLA Ops:
  0.0 1.7 %shard_map.64 = (bf16[2,256,512]{2,1,0:T(8,128)(2,1)S(1)}, bf16[2,256,512]{2,1,0:T(8,128)(2,1)S(1)}, bf16[2,256,512]{2,1,0:T(8,128)(2,1)S(1)}, bf16[2,256,512]{2...) custom-call(bf16[1,2,256,512]{3,2,1,0:T(8,128)(2,1)} %retarded.1, ...), custom_call_target="tpu_custom_call" | custom-call | flops 939524096 | bytes 5242880 | tf_op jit(solution)/shard_map/pallas_call | solution.py:56
  1.7 0.1 collective-permute-start.3
  1.8 1.4 %shard_map.65 = (bf16[1,256,512]{2,1,0:T(8,128)(2,1)S(1)}, bf16[2,256,512]{2,1,0:T(8,128)(2,1)S(1)}, bf16[256,512]{1,0:T(8,128)(2,1)S(1)}, bf16[256,512]{1,0:T(8...) custom-call(bf16[2,256,512]{2,1,0:T(8,128)(2,1)S(1)} %get-tuple-elem, ...), custom_call_target="tpu_custom_call", output_to_operand_aliasing={{0}: (4, {}), {1}: (5, {})} | custom-call | flops 1073741824 | bytes 5505024 | tf_op jit(solution)/shard_map/pallas_call | solution.py:56
  3.3 0.6 %collective-permute-start.1 = (bf16[256,512]{1,0:T(8,128)(2,1)S(1)}, bf16[256,512]{1,0:T(8,128)(2,1)S(1)}, u32[]{:S(2)}, u32[]{:S(2)}) collective-permute-start(bf16[256,512]{1,0:T(8,128)(2,1)S(1)} %get-tuple-element.58.given_total.upper), channel_id=1, source_target_pairs={{0,1},{1,0},{2,3},{3,2},{4,5},{5,4},{6,7},{7,6},{8,9},{9,8},{10,11... | collective-permute-start | bytes 786440 | tf_op jit(solution)/shard_map/ppermute | solution.py:604
  3.8 1.5 %shard_map.66 = (bf16[256,512]{1,0:T(8,128)(2,1)S(1)}, bf16[2,256,512]{2,1,0:T(8,128)(2,1)S(1)}, bf16[256,512]{1,0:T(8,128)(2,1)S(1)}, bf16[256,512]{1,0:T(8,128)(2,1)S(1)}) custom-call(bf16[2,256,512]{2,1,0:T(8,128)(2,1)S(1)} %get-tuple-element.48.retarded, ...), custom_call_target="tpu_custom_call", output_to_operand_aliasing={{0}: (4, {}), {1}: (5, {})} | custom-call | flops 1073741824 | bytes 4456448 | tf_op jit(solution)/shard_map/pallas_call | solution.py:56
  5.3 0.1 collective-permute-start
  5.4 0.5 %collective-permute-start.2 = (bf16[256,512]{1,0:T(8,128)(2,1)S(1)}, bf16[256,512]{1,0:T(8,128)(2,1)S(1)}, u32[]{:S(2)}, u32[]{:S(2)}) collective-permute-start(bf16[256,512]{1,0:T(8,128)(2,1)S(1)} %get-tuple-element.63.whole), channel_id=1, source_target_pairs={{0,1},{1,0},{2,3},{3,2},{4,5},{5,4},{6,7},{7,6},{8,9},{9,8},{10,11... | collective-permute-start | bytes 786440 | tf_op jit(solution)/shard_map/ppermute | solution.py:604
  5.9 0.1 collective-permute-start.4
  6.0 0.0 collective-permute-done.1.lower
  6.0 0.0 collective-permute-done.3.lower
  6.0 0.9 %collective-permute-done.lower.lower_great = bf16[256,512]{1,0:T(8,128)(2,1)S(1)} collective-permute-done((bf16[256,512]{1,0:T(8,128)(2,1)S(1)}, bf16[256,512]{1,0:T(8,128)(2,1)S(1)}, u32[]{:S(2)}, u32[]{:S(2)}) %collective-permute-start) | collective-permute-done | bytes 262176 | tf_op jit(solution)/shard_map/ppermute | solution.py:604
  6.9 0.4 collective-permute-done.2.lower_whole
  7.3 0.4 collective-permute-done.4.lower
  7.7 0.6 %shard_map.70 = (bf16[2,256,512]{2,1,0:T(8,128)(2,1)S(1)}, bf16[256,512]{1,0:T(8,128)(2,1)S(1)}) custom-call(bf16[256,512]{1,0:T(8,128)(2,1)S(1)} %get-tuple-element.63.whole, bf16[256,512]{1,0:T(8,128)(2,1)S(1)} %shard_map.69.joined, bf16[256,512]{1,0:T(8,128)(2,1)S(1)} %get-tuple-element.60.first_step, ...), custom_call_target="tpu_custom_call" | custom-call | flops 536870912 | bytes 2883584 | tf_op jit(solution)/shard_map/pallas_call | solution.py:56
  8.2 1.0 %shard_map.71 = (bf16[1280,512]{1,0:T(8,128)(2,1)S(1)}, bf16[512,256]{1,0:T(8,128)(2,1)S(1)}, s32[4,8,128]{2,1,0:T(8,128)S(1)}) custom-call(s32[2,2]{1,0:T(2,128)} %tiles.1, s32[4]{0:T(128)} %offsets.1, bf16[256,512]{1,0:T(8,128)(2,1)S(1)} %get-tuple-element.60.first_step, bf16[1,256,512]{2,1,0:T(8,128)(2,1)S(1)} %get-tuple-element.55.later_steps, ...), custom_call_target="tpu_custom_call" | custom-call | flops 402653184 | bytes 4735008 | tf_op jit(solution)/shard_map/pallas_call | solution.py:56
  9.2 1.3 %collective-permute-start.12 = (bf16[1280,512]{1,0:T(8,128)(2,1)S(1)}, bf16[1280,512]{1,0:T(8,128)(2,1)S(1)}, u32[]{:S(2)}, u32[]{:S(2)}) collective-permute-start(bf16[1280,512]{1,0:T(8,128)(2,1)S(1)} %get-tuple-element.79.refs_0_), channel_id=1, source_target_pairs={{0,1},{1,0},{2,3},{3,2},{4,5},{5,4},{6,7},{7,6},{8,9},{9,8},{10,11... | collective-permute-start | bytes 3932168 | tf_op jit(solution)/shard_map/ppermute | solution.py:604
  10.6 0.1 collective-permute-start.5
  10.6 0.5 collective-permute-start.8
  11.1 2.5 %collective-permute-done.5.state = bf16[256,512]{1,0:T(8,128)(2,1)S(1)} collective-permute-done((bf16[256,512]{1,0:T(8,128)(2,1)S(1)}, bf16[256,512]{1,0:T(8,128)(2,1)S(1)}, u32[]{:S(2)}, u32[]{:S(2)}) %collective-permute-start.5) | collective-permute-done | bytes 262176 | tf_op jit(solution)/shard_map/ppermute | solution.py:624
  13.6 1.9 %collective-permute-start.6 = (bf16[256,512]{1,0:T(8,128)(2,1)S(1)}, bf16[256,512]{1,0:T(8,128)(2,1)S(1)}, u32[]{:S(2)}, u32[]{:S(2)}) collective-permute-start(bf16[256,512]{1,0:T(8,128)(2,1)S(1)} %get-tuple-element.71), channel_id=1, source_target_pairs={{0,1},{1,0},{2,3},{3,5},{4,2},{5,4},{6,7},{7,6},{8,9},{9,8},{10,11... | collective-permute-start | bytes 786440 | tf_op jit(solution)/shard_map/ppermute | solution.py:624
  15.5 0.0 collective-permute-done.8.state
  15.5 2.8 %collective-permute-start.9 = (bf16[256,512]{1,0:T(8,128)(2,1)S(1)}, bf16[256,512]{1,0:T(8,128)(2,1)S(1)}, u32[]{:S(2)}, u32[]{:S(2)}) collective-permute-start(bf16[256,512]{1,0:T(8,128)(2,1)S(1)} %get-tuple-element.74), channel_id=1, source_target_pairs={{0,1},{1,0},{2,3},{3,5},{4,2},{5,4},{6,7},{7,6},{8,9},{9,8},{10,11... | collective-permute-start | bytes 786440 | tf_op jit(solution)/shard_map/ppermute | solution.py:624
  18.3 1.1 %collective-permute-done.6.state = bf16[256,512]{1,0:T(8,128)(2,1)S(1)} collective-permute-done((bf16[256,512]{1,0:T(8,128)(2,1)S(1)}, bf16[256,512]{1,0:T(8,128)(2,1)S(1)}, u32[]{:S(2)}, u32[]{:S(2)}) %collective-permute-start.6) | collective-permute-done | bytes 262176 | tf_op jit(solution)/shard_map/ppermute | solution.py:624
  19.4 0.5 %shard_map.73 = (bf16[256,512]{1,0:T(8,128)(2,1)S(1)}, bf16[256,512]{1,0:T(8,128)(2,1)S(1)}) custom-call(bf16[256,512]{1,0:T(8,128)(2,1)S(1)} %collective-permute-done.6.state, bf16[256,512]{1,0:T(8,128)(2,1)S(1)} %get-tuple-element.65.chip_whole.step, bf16[256,512]{1,0:T(8,128)(2,1)S(1)} %get-tuple-element.70.source, ...), custom_call_target="tpu_custom_call" | custom-call | flops 268435456 | bytes 1572864 | tf_op jit(solution)/shard_map/pallas_call | solution.py:56
  19.9 1.1 %collective-permute-start.7 = (bf16[256,512]{1,0:T(8,128)(2,1)S(1)}, bf16[256,512]{1,0:T(8,128)(2,1)S(1)}, u32[]{:S(2)}, u32[]{:S(2)}) collective-permute-start(bf16[256,512]{1,0:T(8,128)(2,1)S(1)} %get-tuple-element.73), channel_id=1, source_target_pairs={{0,1},{1,0},{2,3},{3,2},{4,5},{5,4},{6,7},{7,6},{8,9},{9,8},{10,11... | collective-permute-start | bytes 786440 | tf_op jit(solution)/shard_map/ppermute | solution.py:604
  21.0 0.1 collective-permute-start.10
  21.1 1.1 %collective-permute-done.9.state = bf16[256,512]{1,0:T(8,128)(2,1)S(1)} collective-permute-done((bf16[256,512]{1,0:T(8,128)(2,1)S(1)}, bf16[256,512]{1,0:T(8,128)(2,1)S(1)}, u32[]{:S(2)}, u32[]{:S(2)}) %collective-permute-start.9) | collective-permute-done | bytes 262176 | tf_op jit(solution)/shard_map/ppermute | solution.py:624
  22.2 0.5 %shard_map.75 = (bf16[256,512]{1,0:T(8,128)(2,1)S(1)}, bf16[256,512]{1,0:T(8,128)(2,1)S(1)}) custom-call(bf16[256,512]{1,0:T(8,128)(2,1)S(1)} %collective-permute-done.9.state, bf16[256,512]{1,0:T(8,128)(2,1)S(1)} %get-tuple-element.65.chip_whole.step, bf16[256,512]{1,0:T(8,128)(2,1)S(1)} %get-tuple-element.64.chip_great.source, ...), custom_call_target="tpu_custom_call" | custom-call | flops 268435456 | bytes 1572864 | tf_op jit(solution)/shard_map/pallas_call | solution.py:56
  22.7 1.4 %collective-permute-start.11 = (bf16[256,512]{1,0:T(8,128)(2,1)S(1)}, bf16[256,512]{1,0:T(8,128)(2,1)S(1)}, u32[]{:S(2)}, u32[]{:S(2)}) collective-permute-start(bf16[256,512]{1,0:T(8,128)(2,1)S(1)} %get-tuple-element.78), channel_id=1, source_target_pairs={{0,1},{1,0},{2,3},{3,2},{4,5},{5,7},{6,22},{7,4},{8,9},{9,8},{10,1... | collective-permute-start | bytes 786440 | tf_op jit(solution)/shard_map/ppermute | solution.py:624
  24.1 0.0 collective-permute-done.7.near.lesser
  24.1 0.0 collective-permute-done.12.refs_1_
  24.1 1.1 %shard_map.77 = (bf16[2,128,256]{2,1,0:T(8,128)(2,1)S(1)}, bf16[2,128,256]{2,1,0:T(8,128)(2,1)S(1)}, bf16[2,128,256]{2,1,0:T(8,128)(2,1)S(1)}) custom-call(bf16[256,512]{1,0:T(8,128)(2,1)S(1)} %collective-permute-done.7.near.lesser, bf16[256,512]{1,0:T(8,128)(2,1)S(1)} %get-tuple-element.76.kept.greater, bf16[1280,512]{1,0:T(8,128)(2,1)S(1)} %get-tuple-element.79.refs_0_, ...), custom_call_target="tpu_custom_call" | custom-call | flops 671088640 | bytes 3801088 | tf_op jit(solution)/shard_map/pallas_call | solution.py:56
  25.2 1.6 %collective-permute-done.10.lesser = bf16[256,512]{1,0:T(8,128)(2,1)S(1)} collective-permute-done((bf16[256,512]{1,0:T(8,128)(2,1)S(1)}, bf16[256,512]{1,0:T(8,128)(2,1)S(1)}, u32[]{:S(2)}, u32[]{:S(2)}) %collective-permute-start.10) | collective-permute-done | bytes 262176 | tf_op jit(solution)/shard_map/ppermute | solution.py:624
  26.8 2.8 %collective-permute-done.11.greater = bf16[256,512]{1,0:T(8,128)(2,1)S(1)} collective-permute-done((bf16[256,512]{1,0:T(8,128)(2,1)S(1)}, bf16[256,512]{1,0:T(8,128)(2,1)S(1)}, u32[]{:S(2)}, u32[]{:S(2)}) %collective-permute-start.11) | collective-permute-done | bytes 262176 | tf_op jit(solution)/shard_map/ppermute | solution.py:624
  29.6 1.5 %collective-permute-start.13 = (bf16[2,128,256]{2,1,0:T(8,128)(2,1)S(1)}, bf16[2,128,256]{2,1,0:T(8,128)(2,1)S(1)}, u32[]{:S(2)}, u32[]{:S(2)}) collective-permute-start(bf16[2,128,256]{2,1,0:T(8,128)(2,1)S(1)} %get-tuple-element.84), channel_id=1, source_target_pairs={{0,8},{8,0},{16,24},{24,16},{1,9},{9,1},{17,25},{25,17},{2,10},{10... | collective-permute-start | bytes 393224 | tf_op jit(solution)/shard_map/ppermute | solution.py:627
  31.1 1.5 %collective-permute-start.14 = (bf16[2,128,256]{2,1,0:T(8,128)(2,1)S(1)}, bf16[2,128,256]{2,1,0:T(8,128)(2,1)S(1)}, u32[]{:S(2)}, u32[]{:S(2)}) collective-permute-start(bf16[2,128,256]{2,1,0:T(8,128)(2,1)S(1)} %get-tuple-element.85), channel_id=1, source_target_pairs={{0,16},{8,24},{16,0},{24,8},{1,17},{9,25},{17,1},{25,9},{2,18},{10... | collective-permute-start | bytes 393224 | tf_op jit(solution)/shard_map/ppermute | solution.py:627
  32.6 0.5 %collective-permute-start.15 = (bf16[2,128,256]{2,1,0:T(8,128)(2,1)S(1)}, bf16[2,128,256]{2,1,0:T(8,128)(2,1)S(1)}, u32[]{:S(2)}, u32[]{:S(2)}) collective-permute-start(bf16[2,128,256]{2,1,0:T(8,128)(2,1)S(1)} %get-tuple-element.86), channel_id=1, source_target_pairs={{0,24},{8,16},{16,8},{24,0},{1,25},{9,17},{17,9},{25,1},{2,26},{10... | collective-permute-start | bytes 393224 | tf_op jit(solution)/shard_map/ppermute | solution.py:627
  33.1 0.7 %shard_map.76.refs_0_ = bf16[2,128,256]{2,1,0:T(8,128)(2,1)S(1)} custom-call(bf16[256,512]{1,0:T(8,128)(2,1)S(1)} %collective-permute-done.7.near.lesser, bf16[256,512]{1,0:T(8,128)(2,1)S(1)} %get-tuple-element.76.kept.greater, bf16[256,512]{1,0:T(8,128)(2,1)S(1)} %collective-permute-done.10.lesser, bf16[256,512]{1,0:T(8,128)(2,1)S(1)} %collective-permute-done.11.greater, ...), custom_call_target="tpu_custom_call" | custom-call | flops 268435456 | bytes 4063232 | tf_op jit(solution)/shard_map/pallas_call | solution.py:56
  33.8 1.4 %collective-permute-done.13.refs_1_ = bf16[2,128,256]{2,1,0:T(8,128)(2,1)S(1)} collective-permute-done((bf16[2,128,256]{2,1,0:T(8,128)(2,1)S(1)}, bf16[2,128,256]{2,1,0:T(8,128)(2,1)S(1)}, u32[]{:S(2)}, u32[]{:S(2)}) %collective-permute-start.13) | collective-permute-done | bytes 131104 | tf_op jit(solution)/shard_map/ppermute | solution.py:627
  35.2 1.2 %collective-permute-done.14.refs_2_ = bf16[2,128,256]{2,1,0:T(8,128)(2,1)S(1)} collective-permute-done((bf16[2,128,256]{2,1,0:T(8,128)(2,1)S(1)}, bf16[2,128,256]{2,1,0:T(8,128)(2,1)S(1)}, u32[]{:S(2)}, u32[]{:S(2)}) %collective-permute-start.14) | collective-permute-done | bytes 131104 | tf_op jit(solution)/shard_map/ppermute | solution.py:627
  36.5 2.0 %collective-permute-done.15.refs_3_ = bf16[2,128,256]{2,1,0:T(8,128)(2,1)S(1)} collective-permute-done((bf16[2,128,256]{2,1,0:T(8,128)(2,1)S(1)}, bf16[2,128,256]{2,1,0:T(8,128)(2,1)S(1)}, u32[]{:S(2)}, u32[]{:S(2)}) %collective-permute-start.15) | collective-permute-done | bytes 131104 | tf_op jit(solution)/shard_map/ppermute | solution.py:627
  38.5 0.1 collective-permute-start.16
  38.6 1.5 %collective-permute-done.16.swapped = bf16[4,128,256]{2,1,0:T(8,128)(2,1)S(1)} collective-permute-done((bf16[4,128,256]{2,1,0:T(8,128)(2,1)S(1)}, bf16[4,128,256]{2,1,0:T(8,128)(2,1)S(1)}, u32[]{:S(2)}, u32[]{:S(2)}) %collective-permute-start.16) | collective-permute-done | bytes 262176 | tf_op jit(solution)/shard_map/ppermute | solution.py:604
  40.1 0.4 shard_map.80
  40.5 0.6 %collective-permute-start.17 = (bf16[128,256]{1,0:T(8,128)(2,1)S(1)}, bf16[128,256]{1,0:T(8,128)(2,1)S(1)}, u32[]{:S(2)}, u32[]{:S(2)}) collective-permute-start(bf16[128,256]{1,0:T(8,128)(2,1)S(1)} %get-tuple-element.88), channel_id=1, source_target_pairs={{0,8},{8,0},{16,24},{24,16},{1,9},{9,1},{17,25},{25,17},{2,10},{10... | collective-permute-start | bytes 196616 | tf_op jit(solution)/shard_map/ppermute | solution.py:627
  41.1 0.5 %collective-permute-start.18 = (bf16[128,256]{1,0:T(8,128)(2,1)S(1)}, bf16[128,256]{1,0:T(8,128)(2,1)S(1)}, u32[]{:S(2)}, u32[]{:S(2)}) collective-permute-start(bf16[128,256]{1,0:T(8,128)(2,1)S(1)} %get-tuple-element.89), channel_id=1, source_target_pairs={{0,16},{8,24},{16,0},{24,8},{1,17},{9,25},{17,1},{25,9},{2,18},{10... | collective-permute-start | bytes 196616 | tf_op jit(solution)/shard_map/ppermute | solution.py:627
  41.6 2.4 %collective-permute-start.19 = (bf16[128,256]{1,0:T(8,128)(2,1)S(1)}, bf16[128,256]{1,0:T(8,128)(2,1)S(1)}, u32[]{:S(2)}, u32[]{:S(2)}) collective-permute-start(bf16[128,256]{1,0:T(8,128)(2,1)S(1)} %get-tuple-element.90), channel_id=1, source_target_pairs={{0,24},{8,16},{16,8},{24,0},{1,25},{9,17},{17,9},{25,1},{2,26},{10... | collective-permute-start | bytes 196616 | tf_op jit(solution)/shard_map/ppermute | solution.py:627
  44.1 0.9 %collective-permute-done.17.refs_1_ = bf16[128,256]{1,0:T(8,128)(2,1)S(1)} collective-permute-done((bf16[128,256]{1,0:T(8,128)(2,1)S(1)}, bf16[128,256]{1,0:T(8,128)(2,1)S(1)}, u32[]{:S(2)}, u32[]{:S(2)}) %collective-permute-start.17) | collective-permute-done | bytes 65568 | tf_op jit(solution)/shard_map/ppermute | solution.py:627
  45.0 1.1 %collective-permute-done.18.refs_2_ = bf16[128,256]{1,0:T(8,128)(2,1)S(1)} collective-permute-done((bf16[128,256]{1,0:T(8,128)(2,1)S(1)}, bf16[128,256]{1,0:T(8,128)(2,1)S(1)}, u32[]{:S(2)}, u32[]{:S(2)}) %collective-permute-start.18) | collective-permute-done | bytes 65568 | tf_op jit(solution)/shard_map/ppermute | solution.py:627
  46.1 0.7 %collective-permute-done.19.refs_3_ = bf16[128,256]{1,0:T(8,128)(2,1)S(1)} collective-permute-done((bf16[128,256]{1,0:T(8,128)(2,1)S(1)}, bf16[128,256]{1,0:T(8,128)(2,1)S(1)}, u32[]{:S(2)}, u32[]{:S(2)}) %collective-permute-start.19) | collective-permute-done | bytes 65568 | tf_op jit(solution)/shard_map/ppermute | solution.py:627
  46.8 0.7 %shard_map.81 = bf16[4,128,256]{2,1,0:T(8,128)(2,1)} custom-call(bf16[128,256]{1,0:T(8,128)(2,1)S(1)} %get-tuple-element.87.refs_0_, bf16[128,256]{1,0:T(8,128)(2,1)S(1)} %collective-permute-done.17.refs_1_, bf16[128,256]{1,0:T(8,128)(2,1)S(1)} %collective-permute-done.18.refs_2_, bf16[128,256]{1,0:T(8,128)(2,1)S(1)} %collective-permute-done.19.refs_3_), custom_call_target="tpu_custom_call" | custom-call | bytes 524288 | tf_op jit(solution)/shard_map/pallas_call | solution.py:56
  (7 shorter events, 0.1 us)
Async XLA Ops:
  1.7 4.2 %collective-permute-start.3 = (bf16[256,512]{1,0:T(8,128)(2,1)S(1)}, bf16[256,512]{1,0:T(8,128)(2,1)S(1)}, u32[]{:S(2)}, u32[]{:S(2)}) collective-permute-start(bf16[256,512]{1,0:T(8,128)(2,1)S(1)} %get-tuple-element.54.given_total.upper), channel_id=1, source_target_pairs={{0,1},{1,0},{2,3},{3,2},{4,5},{5,4},{6,7},{7,6},{8,9},{9,8},{10,11... | collective-permute-start | bytes 786440 | tf_op jit(solution)/shard_map/ppermute | solution.py:604
  3.3 2.7 %collective-permute-start.1 = (bf16[256,512]{1,0:T(8,128)(2,1)S(1)}, bf16[256,512]{1,0:T(8,128)(2,1)S(1)}, u32[]{:S(2)}, u32[]{:S(2)}) collective-permute-start(bf16[256,512]{1,0:T(8,128)(2,1)S(1)} %get-tuple-element.58.given_total.upper), channel_id=1, source_target_pairs={{0,1},{1,0},{2,3},{3,2},{4,5},{5,4},{6,7},{7,6},{8,9},{9,8},{10,11... | collective-permute-start | bytes 786440 | tf_op jit(solution)/shard_map/ppermute | solution.py:604
  5.3 1.6 %collective-permute-start = (bf16[256,512]{1,0:T(8,128)(2,1)S(1)}, bf16[256,512]{1,0:T(8,128)(2,1)S(1)}, u32[]{:S(2)}, u32[]{:S(2)}) collective-permute-start(bf16[256,512]{1,0:T(8,128)(2,1)S(1)} %get-tuple-element.62.upper.great_total), channel_id=1, source_target_pairs={{0,1},{1,0},{2,3},{3,2},{4,5},{5,4},{6,7},{7,6},{8,9},{9,8},{10,11... | collective-permute-start | bytes 786440 | tf_op jit(solution)/shard_map/ppermute | solution.py:604
  5.4 1.9 %collective-permute-start.2 = (bf16[256,512]{1,0:T(8,128)(2,1)S(1)}, bf16[256,512]{1,0:T(8,128)(2,1)S(1)}, u32[]{:S(2)}, u32[]{:S(2)}) collective-permute-start(bf16[256,512]{1,0:T(8,128)(2,1)S(1)} %get-tuple-element.63.whole), channel_id=1, source_target_pairs={{0,1},{1,0},{2,3},{3,2},{4,5},{5,4},{6,7},{7,6},{8,9},{9,8},{10,11... | collective-permute-start | bytes 786440 | tf_op jit(solution)/shard_map/ppermute | solution.py:604
  5.9 1.8 %collective-permute-start.4 = (bf16[256,512]{1,0:T(8,128)(2,1)S(1)}, bf16[256,512]{1,0:T(8,128)(2,1)S(1)}, u32[]{:S(2)}, u32[]{:S(2)}) collective-permute-start(bf16[256,512]{1,0:T(8,128)(2,1)S(1)} %get-tuple-element.67.total), channel_id=1, source_target_pairs={{0,1},{1,0},{2,3},{3,2},{4,5},{5,4},{6,7},{7,6},{8,9},{9,8},{10,11... | collective-permute-start | bytes 786440 | tf_op jit(solution)/shard_map/ppermute | solution.py:604
  9.2 14.9 %collective-permute-start.12 = (bf16[1280,512]{1,0:T(8,128)(2,1)S(1)}, bf16[1280,512]{1,0:T(8,128)(2,1)S(1)}, u32[]{:S(2)}, u32[]{:S(2)}) collective-permute-start(bf16[1280,512]{1,0:T(8,128)(2,1)S(1)} %get-tuple-element.79.refs_0_), channel_id=1, source_target_pairs={{0,1},{1,0},{2,3},{3,2},{4,5},{5,4},{6,7},{7,6},{8,9},{9,8},{10,11... | collective-permute-start | bytes 3932168 | tf_op jit(solution)/shard_map/ppermute | solution.py:604
  10.6 3.0 %collective-permute-start.5 = (bf16[256,512]{1,0:T(8,128)(2,1)S(1)}, bf16[256,512]{1,0:T(8,128)(2,1)S(1)}, u32[]{:S(2)}, u32[]{:S(2)}) collective-permute-start(bf16[256,512]{1,0:T(8,128)(2,1)S(1)} %shard_map.69.joined), channel_id=1, source_target_pairs={{0,1},{1,3},{2,0},{3,2},{4,5},{5,4},{6,7},{7,6},{8,9},{9,11},{10,8... | collective-permute-start | bytes 786440 | tf_op jit(solution)/shard_map/ppermute | solution.py:624
  10.6 4.9 %collective-permute-start.8 = (bf16[256,512]{1,0:T(8,128)(2,1)S(1)}, bf16[256,512]{1,0:T(8,128)(2,1)S(1)}, u32[]{:S(2)}, u32[]{:S(2)}) collective-permute-start(bf16[256,512]{1,0:T(8,128)(2,1)S(1)} %shard_map.67.joined), channel_id=1, source_target_pairs={{0,1},{1,3},{2,0},{3,2},{4,5},{5,4},{6,7},{7,6},{8,9},{9,11},{10,8... | collective-permute-start | bytes 786440 | tf_op jit(solution)/shard_map/ppermute | solution.py:624
  13.6 5.8 %collective-permute-start.6 = (bf16[256,512]{1,0:T(8,128)(2,1)S(1)}, bf16[256,512]{1,0:T(8,128)(2,1)S(1)}, u32[]{:S(2)}, u32[]{:S(2)}) collective-permute-start(bf16[256,512]{1,0:T(8,128)(2,1)S(1)} %get-tuple-element.71), channel_id=1, source_target_pairs={{0,1},{1,0},{2,3},{3,5},{4,2},{5,4},{6,7},{7,6},{8,9},{9,8},{10,11... | collective-permute-start | bytes 786440 | tf_op jit(solution)/shard_map/ppermute | solution.py:624
  15.5 6.7 %collective-permute-start.9 = (bf16[256,512]{1,0:T(8,128)(2,1)S(1)}, bf16[256,512]{1,0:T(8,128)(2,1)S(1)}, u32[]{:S(2)}, u32[]{:S(2)}) collective-permute-start(bf16[256,512]{1,0:T(8,128)(2,1)S(1)} %get-tuple-element.74), channel_id=1, source_target_pairs={{0,1},{1,0},{2,3},{3,5},{4,2},{5,4},{6,7},{7,6},{8,9},{9,8},{10,11... | collective-permute-start | bytes 786440 | tf_op jit(solution)/shard_map/ppermute | solution.py:624
  19.9 4.2 %collective-permute-start.7 = (bf16[256,512]{1,0:T(8,128)(2,1)S(1)}, bf16[256,512]{1,0:T(8,128)(2,1)S(1)}, u32[]{:S(2)}, u32[]{:S(2)}) collective-permute-start(bf16[256,512]{1,0:T(8,128)(2,1)S(1)} %get-tuple-element.73), channel_id=1, source_target_pairs={{0,1},{1,0},{2,3},{3,2},{4,5},{5,4},{6,7},{7,6},{8,9},{9,8},{10,11... | collective-permute-start | bytes 786440 | tf_op jit(solution)/shard_map/ppermute | solution.py:604
  21.0 5.8 %collective-permute-start.10 = (bf16[256,512]{1,0:T(8,128)(2,1)S(1)}, bf16[256,512]{1,0:T(8,128)(2,1)S(1)}, u32[]{:S(2)}, u32[]{:S(2)}) collective-permute-start(bf16[256,512]{1,0:T(8,128)(2,1)S(1)} %get-tuple-element.77), channel_id=1, source_target_pairs={{0,1},{1,0},{2,3},{3,2},{4,5},{5,6},{6,7},{7,4},{8,9},{9,8},{10,11... | collective-permute-start | bytes 786440 | tf_op jit(solution)/shard_map/ppermute | solution.py:624
  22.7 6.9 %collective-permute-start.11 = (bf16[256,512]{1,0:T(8,128)(2,1)S(1)}, bf16[256,512]{1,0:T(8,128)(2,1)S(1)}, u32[]{:S(2)}, u32[]{:S(2)}) collective-permute-start(bf16[256,512]{1,0:T(8,128)(2,1)S(1)} %get-tuple-element.78), channel_id=1, source_target_pairs={{0,1},{1,0},{2,3},{3,2},{4,5},{5,7},{6,22},{7,4},{8,9},{9,8},{10,1... | collective-permute-start | bytes 786440 | tf_op jit(solution)/shard_map/ppermute | solution.py:624
  29.6 5.6 %collective-permute-start.13 = (bf16[2,128,256]{2,1,0:T(8,128)(2,1)S(1)}, bf16[2,128,256]{2,1,0:T(8,128)(2,1)S(1)}, u32[]{:S(2)}, u32[]{:S(2)}) collective-permute-start(bf16[2,128,256]{2,1,0:T(8,128)(2,1)S(1)} %get-tuple-element.84), channel_id=1, source_target_pairs={{0,8},{8,0},{16,24},{24,16},{1,9},{9,1},{17,25},{25,17},{2,10},{10... | collective-permute-start | bytes 393224 | tf_op jit(solution)/shard_map/ppermute | solution.py:627
  31.1 5.4 %collective-permute-start.14 = (bf16[2,128,256]{2,1,0:T(8,128)(2,1)S(1)}, bf16[2,128,256]{2,1,0:T(8,128)(2,1)S(1)}, u32[]{:S(2)}, u32[]{:S(2)}) collective-permute-start(bf16[2,128,256]{2,1,0:T(8,128)(2,1)S(1)} %get-tuple-element.85), channel_id=1, source_target_pairs={{0,16},{8,24},{16,0},{24,8},{1,17},{9,25},{17,1},{25,9},{2,18},{10... | collective-permute-start | bytes 393224 | tf_op jit(solution)/shard_map/ppermute | solution.py:627
  32.6 5.9 %collective-permute-start.15 = (bf16[2,128,256]{2,1,0:T(8,128)(2,1)S(1)}, bf16[2,128,256]{2,1,0:T(8,128)(2,1)S(1)}, u32[]{:S(2)}, u32[]{:S(2)}) collective-permute-start(bf16[2,128,256]{2,1,0:T(8,128)(2,1)S(1)} %get-tuple-element.86), channel_id=1, source_target_pairs={{0,24},{8,16},{16,8},{24,0},{1,25},{9,17},{17,9},{25,1},{2,26},{10... | collective-permute-start | bytes 393224 | tf_op jit(solution)/shard_map/ppermute | solution.py:627
  38.5 1.6 %collective-permute-start.16 = (bf16[4,128,256]{2,1,0:T(8,128)(2,1)S(1)}, bf16[4,128,256]{2,1,0:T(8,128)(2,1)S(1)}, u32[]{:S(2)}, u32[]{:S(2)}) collective-permute-start(bf16[4,128,256]{2,1,0:T(8,128)(2,1)S(1)} %shard_map.79), channel_id=1, source_target_pairs={{0,1},{1,0},{2,3},{3,2},{4,5},{5,4},{6,7},{7,6},{8,9},{9,8},{10,11... | collective-permute-start | bytes 786440 | tf_op jit(solution)/shard_map/ppermute | solution.py:604
  40.5 4.4 %collective-permute-start.17 = (bf16[128,256]{1,0:T(8,128)(2,1)S(1)}, bf16[128,256]{1,0:T(8,128)(2,1)S(1)}, u32[]{:S(2)}, u32[]{:S(2)}) collective-permute-start(bf16[128,256]{1,0:T(8,128)(2,1)S(1)} %get-tuple-element.88), channel_id=1, source_target_pairs={{0,8},{8,0},{16,24},{24,16},{1,9},{9,1},{17,25},{25,17},{2,10},{10... | collective-permute-start | bytes 196616 | tf_op jit(solution)/shard_map/ppermute | solution.py:627
  41.1 5.0 %collective-permute-start.18 = (bf16[128,256]{1,0:T(8,128)(2,1)S(1)}, bf16[128,256]{1,0:T(8,128)(2,1)S(1)}, u32[]{:S(2)}, u32[]{:S(2)}) collective-permute-start(bf16[128,256]{1,0:T(8,128)(2,1)S(1)} %get-tuple-element.89), channel_id=1, source_target_pairs={{0,16},{8,24},{16,0},{24,8},{1,17},{9,25},{17,1},{25,9},{2,18},{10... | collective-permute-start | bytes 196616 | tf_op jit(solution)/shard_map/ppermute | solution.py:627
  41.6 5.2 %collective-permute-start.19 = (bf16[128,256]{1,0:T(8,128)(2,1)S(1)}, bf16[128,256]{1,0:T(8,128)(2,1)S(1)}, u32[]{:S(2)}, u32[]{:S(2)}) collective-permute-start(bf16[128,256]{1,0:T(8,128)(2,1)S(1)} %get-tuple-element.90), channel_id=1, source_target_pairs={{0,24},{8,16},{16,8},{24,0},{1,25},{9,17},{17,9},{25,1},{2,26},{10... | collective-permute-start | bytes 196616 | tf_op jit(solution)/shard_map/ppermute | solution.py:627

commit v7 on v6

--- a/solution.py
+++ b/solution.py
@@ -266,21 +266,23 @@
         out[...] = advance(lower[...], whole[...], upper[...])
 
 
-def join_kernel(joined, lower, lower_whole, whole, upper, chip, chip_whole):
+def join_kernel(joined, lower, whole, upper, chip):
     on_upper = (lax.axis_index("domain") & 1) == 1
     first_chip = on_first_chip()
 
-    @pl.when(on_upper)
+    @pl.when(on_upper & first_chip)
+    def _():
+        chip[...] = joined[...]
+
+    @pl.when(on_upper & jnp.logical_not(first_chip))
+    def _():
+        chip[...] = advance(lower[...], whole[...], upper[...])
+
+
+def join_whole_kernel(whole, lower_whole, chip_whole):
+    @pl.when((lax.axis_index("domain") & 1) == 1)
     def _():
         chip_whole[...] = product(whole[...], lower_whole[...])
-
-    @pl.when(on_upper & first_chip)
-    def _():
-        chip[...] = joined[...]
-
-    @pl.when(on_upper & jnp.logical_not(first_chip))
-    def _():
-        chip[...] = advance(lower[...], whole[...], upper[...])
 
 
 def keep(z, state, kept, out):
@@ -327,31 +329,6 @@
 
     for k in range(1, blocks - 1):
         states[k] = advance(states[k - 1], later_steps[k - 1], sources[k])
-
-
-def prepare_lesser_kernel(
-    blocks,
-    whole,
-    joined,
-    first_step,
-    later_steps,
-    sources,
-    lower,
-    total,
-    states,
-    chip,
-):
-    first_chip = on_first_chip()
-
-    @pl.when(first_chip)
-    def _():
-        chip[...] = joined[...]
-
-    @pl.when(jnp.logical_not(first_chip))
-    def _():
-        chip[...] = advance(lower[...], whole[...], total[...])
-
-    states_of(blocks, first_step, later_steps, sources, lower, total, chip, states)
 
 
 def prepare_kernel(
@@ -362,6 +339,10 @@
     offsets,
     first_step,
     later_steps,
+    lesser_sources,
+    lower_less,
+    less_total,
+    chip_less,
     greater_sources,
     lower_great,
     great_total,
@@ -369,11 +350,11 @@
     lower_whole,
     whole,
     chip_whole,
-    lessers,
     given,
     own_parts,
     shifts,
     chains,
+    lessers,
     greaters,
     held_tiles,
     held_offsets,
@@ -390,16 +371,11 @@
     order = first_step.shape[0]
     half = order // 2
     rows = blocks * chosen * half // energies
-    states_of(
-        blocks,
-        first_step,
-        later_steps,
-        greater_sources,
-        lower_great,
-        great_total,
-        chip_great,
-        greaters,
-    )
+    for sources, lower, total, chip, states in (
+        (lesser_sources, lower_less, less_total, chip_less, lessers),
+        (greater_sources, lower_great, great_total, chip_great, greaters),
+    ):
+        states_of(blocks, first_step, later_steps, sources, lower, total, chip, states)
 
     @pl.when(upper == 0)
     def _():
@@ -605,18 +581,20 @@
 
     def hop(x, z, lower=False):
         source, target = 2 * z - 1, 2 * z + (not lower)
-        aside = target ^ 1
-        if z < chips - 1 or lower or energies % 4:
-            ring = [source, target, aside, source - 1]
+        before, aside = source - 1, target ^ 1
+        if energies % 4 or lower or z == 1 < chips - 1:
+            ring = [source, target, aside, before]
+        elif z < chips - 1:
+            ring = [source, target]
         else:
-            ring = [source, target, source - 1]
+            ring = [source, target, before]
         onward = dict(zip(ring, ring[1:] + ring[:1]))
         route = []
         for e in range(energies):
             for d in range(domains):
                 if d in onward:
                     place = (e, onward[d])
-                elif d == aside:
+                elif d in (before, aside):
                     place = (e ^ 2, d)
                 else:
                     place = (e, d ^ 1)
@@ -662,17 +640,12 @@
     )
     lower_great = swap(great_total)
     lower_whole = swap(whole)
-    chip_great, chip_whole = kernel_call(
-        join_kernel,
-        [block] * 2,
-        (joined_great, lower_great, lower_whole, whole, great_total),
-        3 * unit,
-    )
-    lessers, chip_less = kernel_call(
-        functools.partial(prepare_lesser_kernel, blocks),
-        [series(blocks), block],
-        (whole, joined_less, first_step, later_steps, less_sources, lower_less, less_total),
-        4 * unit,
+    (chip_less,) = kernel_call(
+        join_kernel, [block], (joined_less, lower_less, whole, less_total), 2 * unit
+    )
+    (chip_whole,) = kernel_call(join_whole_kernel, [block], (whole, lower_whole), unit)
+    (chip_great,) = kernel_call(
+        join_kernel, [block], (joined_great, lower_great, whole, great_total), 2 * unit
     )
     given, own_parts, shifts = kernel_call(
         functools.partial(prepare_kernel, blocks, energies, chosen),
@@ -687,6 +660,10 @@
             *in_place(tiles, offsets),
             first_step,
             later_steps,
+            less_sources,
+            lower_less,
+            less_total,
+            chip_less,
             great_sources,
             lower_great,
             great_total,
@@ -694,11 +671,10 @@
             lower_whole,
             whole,
             chip_whole,
-            lessers,
         ),
-        3 * unit,
-        in_specs=[HBM] * 2 + [VMEM] * 10,
-        scratch=[pltpu.VMEM((blocks, order, 2 * order), BF16)] * 2
+        5 * unit,
+        in_specs=[HBM] * 2 + [VMEM] * 13,
+        scratch=[pltpu.VMEM((blocks, order, 2 * order), BF16)] * 3
         + [
             pltpu.SMEM(tiles.shape, jnp.int32),
             pltpu.SMEM(offsets.shape, jnp.int32),

time: 47.7 us -> 47.8 us (level)
  the two profiles are of different devices: /device:TPU:16 before, /device:TPU:20 now
where the time goes in v7:
time: 47.8 us; the launch traced here: 47.7 us
  waiting for transfers between devices  23.8 us (50%)
  starting transfers between devices  14.1 us (29%)
  Pallas kernels  9.65 us (20%)
    ppermute x6, waiting for transfers between devices, hop(): return lax.ppermute(x, ('energy', 'domain'), route)  12.9 us
    pallas_call x19, Pallas kernels, kernel_call(): pl.pallas_call(body, out_shape=outs, in_specs=in_specs or [VMEM] * len(op...  9.65 us
    ppermute x6, waiting for transfers between devices, across(): return lax.ppermute(x, 'energy', [(e, e ^ k) for e in range(energies)])  7.41 us
    ppermute x6, starting transfers between devices, across(): return lax.ppermute(x, 'energy', [(e, e ^ k) for e in range(energies)])  7.04 us
    ppermute x8, starting transfers between devices, swap(): return lax.ppermute(x, 'domain', [(d, d ^ 1) for d in range(domains)])  3.54 us
    ppermute x6, starting transfers between devices, hop(): return lax.ppermute(x, ('energy', 'domain'), route)  3.5 us
    ppermute x8, waiting for transfers between devices, swap(): return lax.ppermute(x, 'domain', [(d, d ^ 1) for d in range(domains)])  3.46 us
  transfers between devices with their start and end apart: 20, of which 17 were waited for; matrix products, arithmetic and copies ran while one was open for 0% of the time, Pallas kernels for 6%

profile of v7, /device:TPU:20, one launch (start us, length us, event | category | flops | bytes accessed | tf_op | source)
XLA Modules:
  0.0 47.7 jit_solution(9630341001043850179)
XLA Ops:
  0.0 1.7 %shard_map.64 = (bf16[2,256,512]{2,1,0:T(8,128)(2,1)S(1)}, bf16[2,256,512]{2,1,0:T(8,128)(2,1)S(1)}, bf16[2,256,512]{2,1,0:T(8,128)(2,1)S(1)}, bf16[2,256,512]{2...) custom-call(bf16[1,2,256,512]{3,2,1,0:T(8,128)(2,1)} %retarded.1, ...), custom_call_target="tpu_custom_call" | custom-call | flops 939524096 | bytes 5242880 | tf_op jit(solution)/shard_map/pallas_call | solution.py:56
  1.7 1.4 %shard_map.65 = (bf16[1,256,512]{2,1,0:T(8,128)(2,1)S(1)}, bf16[2,256,512]{2,1,0:T(8,128)(2,1)S(1)}, bf16[256,512]{1,0:T(8,128)(2,1)S(1)}, bf16[256,512]{1,0:T(8...) custom-call(bf16[2,256,512]{2,1,0:T(8,128)(2,1)S(1)} %get-tuple-elem, ...), custom_call_target="tpu_custom_call", output_to_operand_aliasing={{0}: (4, {}), {1}: (5, {})} | custom-call | flops 1073741824 | bytes 5505024 | tf_op jit(solution)/shard_map/pallas_call | solution.py:56
  3.2 1.5 %shard_map.66 = (bf16[256,512]{1,0:T(8,128)(2,1)S(1)}, bf16[2,256,512]{2,1,0:T(8,128)(2,1)S(1)}, bf16[256,512]{1,0:T(8,128)(2,1)S(1)}, bf16[256,512]{1,0:T(8,128)(2,1)S(1)}) custom-call(bf16[2,256,512]{2,1,0:T(8,128)(2,1)S(1)} %get-tuple-element.44.retarded, ...), custom_call_target="tpu_custom_call", output_to_operand_aliasing={{0}: (4, {}), {1}: (5, {})} | custom-call | flops 1073741824 | bytes 4456448 | tf_op jit(solution)/shard_map/pallas_call | solution.py:56
  4.7 0.1 collective-permute-start.4
  4.8 0.5 %collective-permute-start.1 = (bf16[256,512]{1,0:T(8,128)(2,1)S(1)}, bf16[256,512]{1,0:T(8,128)(2,1)S(1)}, u32[]{:S(2)}, u32[]{:S(2)}) collective-permute-start(bf16[256,512]{1,0:T(8,128)(2,1)S(1)} %get-tuple-element.50.given_total.upper), channel_id=1, source_target_pairs={{0,1},{1,0},{2,3},{3,2},{4,5},{5,4},{6,7},{7,6},{8,9},{9,8},{10,11... | collective-permute-start | bytes 786440 | tf_op jit(solution)/shard_map/ppermute | solution.py:580
  5.3 0.1 collective-permute-start.3
  5.4 0.4 collective-permute-start
  5.8 0.1 collective-permute-start.2
  5.9 0.4 collective-permute-done.4.lower_whole
  6.3 0.4 collective-permute-done.1.lower
  6.7 0.4 collective-permute-done.3.lower
  7.1 0.4 collective-permute-done.lower.lower_less
  7.4 0.4 collective-permute-done.2.lower.lower_great
  7.8 1.0 %shard_map.72 = (bf16[1280,512]{1,0:T(8,128)(2,1)S(1)}, bf16[512,256]{1,0:T(8,128)(2,1)S(1)}, s32[4,8,128]{2,1,0:T(8,128)S(1)}) custom-call(s32[2,2]{1,0:T(2,128)} %tiles.1, s32[4]{0:T(128)} %offsets.1, bf16[256,512]{1,0:T(8,128)(2,1)S(1)} %get-tuple-element.56.first_step, bf16[1,256,512]{2,1,0:T(8,128)(2,1)S(1)} %get-tuple-element.51.later_steps, ...), custom_call_target="tpu_custom_call" | custom-call | flops 671088640 | bytes 5521440 | tf_op jit(solution)/shard_map/pallas_call | solution.py:56
  8.8 1.6 %collective-permute-start.12 = (bf16[1280,512]{1,0:T(8,128)(2,1)S(1)}, bf16[1280,512]{1,0:T(8,128)(2,1)S(1)}, u32[]{:S(2)}, u32[]{:S(2)}) collective-permute-start(bf16[1280,512]{1,0:T(8,128)(2,1)S(1)} %get-tuple-element.71.refs_0_), channel_id=1, source_target_pairs={{0,1},{1,0},{2,3},{3,2},{4,5},{5,4},{6,7},{7,6},{8,9},{9,8},{10,11... | collective-permute-start | bytes 3932168 | tf_op jit(solution)/shard_map/ppermute | solution.py:580
  10.4 0.1 collective-permute-start.5
  10.4 0.5 collective-permute-start.8
  10.9 2.5 %collective-permute-done.5.state = bf16[256,512]{1,0:T(8,128)(2,1)S(1)} collective-permute-done((bf16[256,512]{1,0:T(8,128)(2,1)S(1)}, bf16[256,512]{1,0:T(8,128)(2,1)S(1)}, u32[]{:S(2)}, u32[]{:S(2)}) %collective-permute-start.5) | collective-permute-done | bytes 262176 | tf_op jit(solution)/shard_map/ppermute | solution.py:602
  13.5 0.6 %collective-permute-start.6 = (bf16[256,512]{1,0:T(8,128)(2,1)S(1)}, bf16[256,512]{1,0:T(8,128)(2,1)S(1)}, u32[]{:S(2)}, u32[]{:S(2)}) collective-permute-start(bf16[256,512]{1,0:T(8,128)(2,1)S(1)} %get-tuple-element.63), channel_id=1, source_target_pairs={{0,1},{1,0},{2,18},{3,5},{4,20},{5,3},{6,7},{7,6},{8,9},{9,8},{10,... | collective-permute-start | bytes 786440 | tf_op jit(solution)/shard_map/ppermute | solution.py:602
  14.0 0.0 collective-permute-done.8.state
  14.0 1.6 %collective-permute-start.9 = (bf16[256,512]{1,0:T(8,128)(2,1)S(1)}, bf16[256,512]{1,0:T(8,128)(2,1)S(1)}, u32[]{:S(2)}, u32[]{:S(2)}) collective-permute-start(bf16[256,512]{1,0:T(8,128)(2,1)S(1)} %get-tuple-element.66), channel_id=1, source_target_pairs={{0,1},{1,0},{2,18},{3,5},{4,20},{5,3},{6,7},{7,6},{8,9},{9,8},{10,... | collective-permute-start | bytes 786440 | tf_op jit(solution)/shard_map/ppermute | solution.py:602
  15.6 4.3 %collective-permute-done.6.state = bf16[256,512]{1,0:T(8,128)(2,1)S(1)} collective-permute-done((bf16[256,512]{1,0:T(8,128)(2,1)S(1)}, bf16[256,512]{1,0:T(8,128)(2,1)S(1)}, u32[]{:S(2)}, u32[]{:S(2)}) %collective-permute-start.6) | collective-permute-done | bytes 262176 | tf_op jit(solution)/shard_map/ppermute | solution.py:602
  19.9 0.5 %shard_map.74 = (bf16[256,512]{1,0:T(8,128)(2,1)S(1)}, bf16[256,512]{1,0:T(8,128)(2,1)S(1)}) custom-call(bf16[256,512]{1,0:T(8,128)(2,1)S(1)} %collective-permute-done.6.state, bf16[256,512]{1,0:T(8,128)(2,1)S(1)} %shard_map.71.chip_whole.step, bf16[256,512]{1,0:T(8,128)(2,1)S(1)} %shard_map.68.chip_less.source, bf16[256,512]{1,0:T(8,128)(2,1)S(1)} %get-tuple-element.64.refs_0_), custom_call_target="tpu_custom_call" | custom-call | flops 268435456 | bytes 1572864 | tf_op jit(solution)/shard_map/pallas_call | solution.py:56
  20.4 0.7 %collective-permute-start.7 = (bf16[256,512]{1,0:T(8,128)(2,1)S(1)}, bf16[256,512]{1,0:T(8,128)(2,1)S(1)}, u32[]{:S(2)}, u32[]{:S(2)}) collective-permute-start(bf16[256,512]{1,0:T(8,128)(2,1)S(1)} %get-tuple-element.65), channel_id=1, source_target_pairs={{0,1},{1,0},{2,3},{3,2},{4,5},{5,4},{6,7},{7,6},{8,9},{9,8},{10,11... | collective-permute-start | bytes 786440 | tf_op jit(solution)/shard_map/ppermute | solution.py:580
  21.1 0.1 collective-permute-start.10
  21.2 1.5 %collective-permute-done.9.state = bf16[256,512]{1,0:T(8,128)(2,1)S(1)} collective-permute-done((bf16[256,512]{1,0:T(8,128)(2,1)S(1)}, bf16[256,512]{1,0:T(8,128)(2,1)S(1)}, u32[]{:S(2)}, u32[]{:S(2)}) %collective-permute-start.9) | collective-permute-done | bytes 262176 | tf_op jit(solution)/shard_map/ppermute | solution.py:602
  22.7 0.5 %shard_map.76 = (bf16[256,512]{1,0:T(8,128)(2,1)S(1)}, bf16[256,512]{1,0:T(8,128)(2,1)S(1)}) custom-call(bf16[256,512]{1,0:T(8,128)(2,1)S(1)} %collective-permute-done.9.state, bf16[256,512]{1,0:T(8,128)(2,1)S(1)} %shard_map.71.chip_whole.step, bf16[256,512]{1,0:T(8,128)(2,1)S(1)} %shard_map.70.chip_great.source, bf16[256,512]{1,0:T(8,128)(2,1)S(1)} %get-tuple-element.67.refs_0_), custom_call_target="tpu_custom_call" | custom-call | flops 268435456 | bytes 1572864 | tf_op jit(solution)/shard_map/pallas_call | solution.py:56
  23.2 0.7 %collective-permute-start.11 = (bf16[256,512]{1,0:T(8,128)(2,1)S(1)}, bf16[256,512]{1,0:T(8,128)(2,1)S(1)}, u32[]{:S(2)}, u32[]{:S(2)}) collective-permute-start(bf16[256,512]{1,0:T(8,128)(2,1)S(1)} %get-tuple-element.70), channel_id=1, source_target_pairs={{0,1},{1,0},{2,3},{3,2},{4,5},{5,7},{6,22},{7,4},{8,9},{9,8},{10,1... | collective-permute-start | bytes 786440 | tf_op jit(solution)/shard_map/ppermute | solution.py:602
  24.0 0.0 collective-permute-done.7.near.lesser
  24.0 0.0 collective-permute-done.12.refs_1_
  24.0 1.1 %shard_map.78 = (bf16[2,128,256]{2,1,0:T(8,128)(2,1)S(1)}, bf16[2,128,256]{2,1,0:T(8,128)(2,1)S(1)}, bf16[2,128,256]{2,1,0:T(8,128)(2,1)S(1)}) custom-call(bf16[256,512]{1,0:T(8,128)(2,1)S(1)} %collective-permute-done.7.near.lesser, bf16[256,512]{1,0:T(8,128)(2,1)S(1)} %get-tuple-element.68.kept.greater, bf16[1280,512]{1,0:T(8,128)(2,1)S(1)} %get-tuple-element.71.refs_0_, ...), custom_call_target="tpu_custom_call" | custom-call | flops 671088640 | bytes 3801088 | tf_op jit(solution)/shard_map/pallas_call | solution.py:56
  25.1 1.9 %collective-permute-done.10.lesser = bf16[256,512]{1,0:T(8,128)(2,1)S(1)} collective-permute-done((bf16[256,512]{1,0:T(8,128)(2,1)S(1)}, bf16[256,512]{1,0:T(8,128)(2,1)S(1)}, u32[]{:S(2)}, u32[]{:S(2)}) %collective-permute-start.10) | collective-permute-done | bytes 262176 | tf_op jit(solution)/shard_map/ppermute | solution.py:602
  26.9 2.8 %collective-permute-done.11.greater = bf16[256,512]{1,0:T(8,128)(2,1)S(1)} collective-permute-done((bf16[256,512]{1,0:T(8,128)(2,1)S(1)}, bf16[256,512]{1,0:T(8,128)(2,1)S(1)}, u32[]{:S(2)}, u32[]{:S(2)}) %collective-permute-start.11) | collective-permute-done | bytes 262176 | tf_op jit(solution)/shard_map/ppermute | solution.py:602
  29.7 1.5 %collective-permute-start.13 = (bf16[2,128,256]{2,1,0:T(8,128)(2,1)S(1)}, bf16[2,128,256]{2,1,0:T(8,128)(2,1)S(1)}, u32[]{:S(2)}, u32[]{:S(2)}) collective-permute-start(bf16[2,128,256]{2,1,0:T(8,128)(2,1)S(1)} %get-tuple-element.76), channel_id=1, source_target_pairs={{0,8},{8,0},{16,24},{24,16},{1,9},{9,1},{17,25},{25,17},{2,10},{10... | collective-permute-start | bytes 393224 | tf_op jit(solution)/shard_map/ppermute | solution.py:605
  31.2 0.5 %collective-permute-start.14 = (bf16[2,128,256]{2,1,0:T(8,128)(2,1)S(1)}, bf16[2,128,256]{2,1,0:T(8,128)(2,1)S(1)}, u32[]{:S(2)}, u32[]{:S(2)}) collective-permute-start(bf16[2,128,256]{2,1,0:T(8,128)(2,1)S(1)} %get-tuple-element.77), channel_id=1, source_target_pairs={{0,16},{8,24},{16,0},{24,8},{1,17},{9,25},{17,1},{25,9},{2,18},{10... | collective-permute-start | bytes 393224 | tf_op jit(solution)/shard_map/ppermute | solution.py:605
  31.7 1.5 %collective-permute-start.15 = (bf16[2,128,256]{2,1,0:T(8,128)(2,1)S(1)}, bf16[2,128,256]{2,1,0:T(8,128)(2,1)S(1)}, u32[]{:S(2)}, u32[]{:S(2)}) collective-permute-start(bf16[2,128,256]{2,1,0:T(8,128)(2,1)S(1)} %get-tuple-element.78), channel_id=1, source_target_pairs={{0,24},{8,16},{16,8},{24,0},{1,25},{9,17},{17,9},{25,1},{2,26},{10... | collective-permute-start | bytes 393224 | tf_op jit(solution)/shard_map/ppermute | solution.py:605
  33.2 0.7 %shard_map.77.refs_0_ = bf16[2,128,256]{2,1,0:T(8,128)(2,1)S(1)} custom-call(bf16[256,512]{1,0:T(8,128)(2,1)S(1)} %collective-permute-done.7.near.lesser, bf16[256,512]{1,0:T(8,128)(2,1)S(1)} %get-tuple-element.68.kept.greater, bf16[256,512]{1,0:T(8,128)(2,1)S(1)} %collective-permute-done.10.lesser, bf16[256,512]{1,0:T(8,128)(2,1)S(1)} %collective-permute-done.11.greater, ...), custom_call_target="tpu_custom_call" | custom-call | flops 268435456 | bytes 4063232 | tf_op jit(solution)/shard_map/pallas_call | solution.py:56
  33.9 1.2 %collective-permute-done.13.refs_1_ = bf16[2,128,256]{2,1,0:T(8,128)(2,1)S(1)} collective-permute-done((bf16[2,128,256]{2,1,0:T(8,128)(2,1)S(1)}, bf16[2,128,256]{2,1,0:T(8,128)(2,1)S(1)}, u32[]{:S(2)}, u32[]{:S(2)}) %collective-permute-start.13) | collective-permute-done | bytes 131104 | tf_op jit(solution)/shard_map/ppermute | solution.py:605
  35.1 1.1 %collective-permute-done.14.refs_2_ = bf16[2,128,256]{2,1,0:T(8,128)(2,1)S(1)} collective-permute-done((bf16[2,128,256]{2,1,0:T(8,128)(2,1)S(1)}, bf16[2,128,256]{2,1,0:T(8,128)(2,1)S(1)}, u32[]{:S(2)}, u32[]{:S(2)}) %collective-permute-start.14) | collective-permute-done | bytes 131104 | tf_op jit(solution)/shard_map/ppermute | solution.py:605
  36.2 1.4 %collective-permute-done.15.refs_3_ = bf16[2,128,256]{2,1,0:T(8,128)(2,1)S(1)} collective-permute-done((bf16[2,128,256]{2,1,0:T(8,128)(2,1)S(1)}, bf16[2,128,256]{2,1,0:T(8,128)(2,1)S(1)}, u32[]{:S(2)}, u32[]{:S(2)}) %collective-permute-start.15) | collective-permute-done | bytes 131104 | tf_op jit(solution)/shard_map/ppermute | solution.py:605
  37.6 0.1 collective-permute-start.16
  37.7 1.5 %collective-permute-done.16.swapped = bf16[4,128,256]{2,1,0:T(8,128)(2,1)S(1)} collective-permute-done((bf16[4,128,256]{2,1,0:T(8,128)(2,1)S(1)}, bf16[4,128,256]{2,1,0:T(8,128)(2,1)S(1)}, u32[]{:S(2)}, u32[]{:S(2)}) %collective-permute-start.16) | collective-permute-done | bytes 262176 | tf_op jit(solution)/shard_map/ppermute | solution.py:580
  39.2 0.4 shard_map.81
  39.6 0.6 %collective-permute-start.17 = (bf16[128,256]{1,0:T(8,128)(2,1)S(1)}, bf16[128,256]{1,0:T(8,128)(2,1)S(1)}, u32[]{:S(2)}, u32[]{:S(2)}) collective-permute-start(bf16[128,256]{1,0:T(8,128)(2,1)S(1)} %get-tuple-element.80), channel_id=1, source_target_pairs={{0,8},{8,0},{16,24},{24,16},{1,9},{9,1},{17,25},{25,17},{2,10},{10... | collective-permute-start | bytes 196616 | tf_op jit(solution)/shard_map/ppermute | solution.py:605
  40.2 1.5 %collective-permute-start.18 = (bf16[128,256]{1,0:T(8,128)(2,1)S(1)}, bf16[128,256]{1,0:T(8,128)(2,1)S(1)}, u32[]{:S(2)}, u32[]{:S(2)}) collective-permute-start(bf16[128,256]{1,0:T(8,128)(2,1)S(1)} %get-tuple-element.81), channel_id=1, source_target_pairs={{0,16},{8,24},{16,0},{24,8},{1,17},{9,25},{17,1},{25,9},{2,18},{10... | collective-permute-start | bytes 196616 | tf_op jit(solution)/shard_map/ppermute | solution.py:605
  41.8 1.4 %collective-permute-start.19 = (bf16[128,256]{1,0:T(8,128)(2,1)S(1)}, bf16[128,256]{1,0:T(8,128)(2,1)S(1)}, u32[]{:S(2)}, u32[]{:S(2)}) collective-permute-start(bf16[128,256]{1,0:T(8,128)(2,1)S(1)} %get-tuple-element.82), channel_id=1, source_target_pairs={{0,24},{8,16},{16,8},{24,0},{1,25},{9,17},{17,9},{25,1},{2,26},{10... | collective-permute-start | bytes 196616 | tf_op jit(solution)/shard_map/ppermute | solution.py:605
  43.2 0.9 %collective-permute-done.17.refs_1_ = bf16[128,256]{1,0:T(8,128)(2,1)S(1)} collective-permute-done((bf16[128,256]{1,0:T(8,128)(2,1)S(1)}, bf16[128,256]{1,0:T(8,128)(2,1)S(1)}, u32[]{:S(2)}, u32[]{:S(2)}) %collective-permute-start.17) | collective-permute-done | bytes 65568 | tf_op jit(solution)/shard_map/ppermute | solution.py:605
  44.0 0.5 collective-permute-done.18.refs_2_
  44.5 2.4 %collective-permute-done.19.refs_3_ = bf16[128,256]{1,0:T(8,128)(2,1)S(1)} collective-permute-done((bf16[128,256]{1,0:T(8,128)(2,1)S(1)}, bf16[128,256]{1,0:T(8,128)(2,1)S(1)}, u32[]{:S(2)}, u32[]{:S(2)}) %collective-permute-start.19) | collective-permute-done | bytes 65568 | tf_op jit(solution)/shard_map/ppermute | solution.py:605
  46.9 0.7 %shard_map.82 = bf16[4,128,256]{2,1,0:T(8,128)(2,1)} custom-call(bf16[128,256]{1,0:T(8,128)(2,1)S(1)} %get-tuple-element.79.refs_0_, bf16[128,256]{1,0:T(8,128)(2,1)S(1)} %collective-permute-done.17.refs_1_, bf16[128,256]{1,0:T(8,128)(2,1)S(1)} %collective-permute-done.18.refs_2_, bf16[128,256]{1,0:T(8,128)(2,1)S(1)} %collective-permute-done.19.refs_3_), custom_call_target="tpu_custom_call" | custom-call | bytes 524288 | tf_op jit(solution)/shard_map/pallas_call | solution.py:56
  (9 shorter events, 0.1 us)
Async XLA Ops:
  4.7 1.6 %collective-permute-start.4 = (bf16[256,512]{1,0:T(8,128)(2,1)S(1)}, bf16[256,512]{1,0:T(8,128)(2,1)S(1)}, u32[]{:S(2)}, u32[]{:S(2)}) collective-permute-start(bf16[256,512]{1,0:T(8,128)(2,1)S(1)} %get-tuple-element.59.whole), channel_id=1, source_target_pairs={{0,1},{1,0},{2,3},{3,2},{4,5},{5,4},{6,7},{7,6},{8,9},{9,8},{10,11... | collective-permute-start | bytes 786440 | tf_op jit(solution)/shard_map/ppermute | solution.py:580
  4.8 1.9 %collective-permute-start.1 = (bf16[256,512]{1,0:T(8,128)(2,1)S(1)}, bf16[256,512]{1,0:T(8,128)(2,1)S(1)}, u32[]{:S(2)}, u32[]{:S(2)}) collective-permute-start(bf16[256,512]{1,0:T(8,128)(2,1)S(1)} %get-tuple-element.50.given_total.upper), channel_id=1, source_target_pairs={{0,1},{1,0},{2,3},{3,2},{4,5},{5,4},{6,7},{7,6},{8,9},{9,8},{10,11... | collective-permute-start | bytes 786440 | tf_op jit(solution)/shard_map/ppermute | solution.py:580
  5.3 1.8 %collective-permute-start.3 = (bf16[256,512]{1,0:T(8,128)(2,1)S(1)}, bf16[256,512]{1,0:T(8,128)(2,1)S(1)}, u32[]{:S(2)}, u32[]{:S(2)}) collective-permute-start(bf16[256,512]{1,0:T(8,128)(2,1)S(1)} %get-tuple-element.54.given_total.upper), channel_id=1, source_target_pairs={{0,1},{1,0},{2,3},{3,2},{4,5},{5,4},{6,7},{7,6},{8,9},{9,8},{10,11... | collective-permute-start | bytes 786440 | tf_op jit(solution)/shard_map/ppermute | solution.py:580
  5.4 2.1 %collective-permute-start = (bf16[256,512]{1,0:T(8,128)(2,1)S(1)}, bf16[256,512]{1,0:T(8,128)(2,1)S(1)}, u32[]{:S(2)}, u32[]{:S(2)}) collective-permute-start(bf16[256,512]{1,0:T(8,128)(2,1)S(1)} %get-tuple-element.58.upper.less_total), channel_id=1, source_target_pairs={{0,1},{1,0},{2,3},{3,2},{4,5},{5,4},{6,7},{7,6},{8,9},{9,8},{10,11... | collective-permute-start | bytes 786440 | tf_op jit(solution)/shard_map/ppermute | solution.py:580
  5.8 2.0 %collective-permute-start.2 = (bf16[256,512]{1,0:T(8,128)(2,1)S(1)}, bf16[256,512]{1,0:T(8,128)(2,1)S(1)}, u32[]{:S(2)}, u32[]{:S(2)}) collective-permute-start(bf16[256,512]{1,0:T(8,128)(2,1)S(1)} %get-tuple-element.61.upper.great_total), channel_id=1, source_target_pairs={{0,1},{1,0},{2,3},{3,2},{4,5},{5,4},{6,7},{7,6},{8,9},{9,8},{10,11... | collective-permute-start | bytes 786440 | tf_op jit(solution)/shard_map/ppermute | solution.py:580
  8.8 15.2 %collective-permute-start.12 = (bf16[1280,512]{1,0:T(8,128)(2,1)S(1)}, bf16[1280,512]{1,0:T(8,128)(2,1)S(1)}, u32[]{:S(2)}, u32[]{:S(2)}) collective-permute-start(bf16[1280,512]{1,0:T(8,128)(2,1)S(1)} %get-tuple-element.71.refs_0_), channel_id=1, source_target_pairs={{0,1},{1,0},{2,3},{3,2},{4,5},{5,4},{6,7},{7,6},{8,9},{9,8},{10,11... | collective-permute-start | bytes 3932168 | tf_op jit(solution)/shard_map/ppermute | solution.py:580
  10.4 3.0 %collective-permute-start.5 = (bf16[256,512]{1,0:T(8,128)(2,1)S(1)}, bf16[256,512]{1,0:T(8,128)(2,1)S(1)}, u32[]{:S(2)}, u32[]{:S(2)}) collective-permute-start(bf16[256,512]{1,0:T(8,128)(2,1)S(1)} %shard_map.67.joined), channel_id=1, source_target_pairs={{0,1},{1,3},{2,0},{3,2},{4,5},{5,4},{6,7},{7,6},{8,9},{9,11},{10,8... | collective-permute-start | bytes 786440 | tf_op jit(solution)/shard_map/ppermute | solution.py:602
  10.4 3.6 %collective-permute-start.8 = (bf16[256,512]{1,0:T(8,128)(2,1)S(1)}, bf16[256,512]{1,0:T(8,128)(2,1)S(1)}, u32[]{:S(2)}, u32[]{:S(2)}) collective-permute-start(bf16[256,512]{1,0:T(8,128)(2,1)S(1)} %shard_map.69.joined), channel_id=1, source_target_pairs={{0,1},{1,3},{2,0},{3,2},{4,5},{5,4},{6,7},{7,6},{8,9},{9,11},{10,8... | collective-permute-start | bytes 786440 | tf_op jit(solution)/shard_map/ppermute | solution.py:602
  13.5 6.4 %collective-permute-start.6 = (bf16[256,512]{1,0:T(8,128)(2,1)S(1)}, bf16[256,512]{1,0:T(8,128)(2,1)S(1)}, u32[]{:S(2)}, u32[]{:S(2)}) collective-permute-start(bf16[256,512]{1,0:T(8,128)(2,1)S(1)} %get-tuple-element.63), channel_id=1, source_target_pairs={{0,1},{1,0},{2,18},{3,5},{4,20},{5,3},{6,7},{7,6},{8,9},{9,8},{10,... | collective-permute-start | bytes 786440 | tf_op jit(solution)/shard_map/ppermute | solution.py:602
  14.0 8.7 %collective-permute-start.9 = (bf16[256,512]{1,0:T(8,128)(2,1)S(1)}, bf16[256,512]{1,0:T(8,128)(2,1)S(1)}, u32[]{:S(2)}, u32[]{:S(2)}) collective-permute-start(bf16[256,512]{1,0:T(8,128)(2,1)S(1)} %get-tuple-element.66), channel_id=1, source_target_pairs={{0,1},{1,0},{2,18},{3,5},{4,20},{5,3},{6,7},{7,6},{8,9},{9,8},{10,... | collective-permute-start | bytes 786440 | tf_op jit(solution)/shard_map/ppermute | solution.py:602
  20.4 3.6 %collective-permute-start.7 = (bf16[256,512]{1,0:T(8,128)(2,1)S(1)}, bf16[256,512]{1,0:T(8,128)(2,1)S(1)}, u32[]{:S(2)}, u32[]{:S(2)}) collective-permute-start(bf16[256,512]{1,0:T(8,128)(2,1)S(1)} %get-tuple-element.65), channel_id=1, source_target_pairs={{0,1},{1,0},{2,3},{3,2},{4,5},{5,4},{6,7},{7,6},{8,9},{9,8},{10,11... | collective-permute-start | bytes 786440 | tf_op jit(solution)/shard_map/ppermute | solution.py:580
  21.1 5.8 %collective-permute-start.10 = (bf16[256,512]{1,0:T(8,128)(2,1)S(1)}, bf16[256,512]{1,0:T(8,128)(2,1)S(1)}, u32[]{:S(2)}, u32[]{:S(2)}) collective-permute-start(bf16[256,512]{1,0:T(8,128)(2,1)S(1)} %get-tuple-element.69), channel_id=1, source_target_pairs={{0,1},{1,0},{2,3},{3,2},{4,5},{5,6},{6,7},{7,4},{8,9},{9,8},{10,11... | collective-permute-start | bytes 786440 | tf_op jit(solution)/shard_map/ppermute | solution.py:602
  23.2 6.5 %collective-permute-start.11 = (bf16[256,512]{1,0:T(8,128)(2,1)S(1)}, bf16[256,512]{1,0:T(8,128)(2,1)S(1)}, u32[]{:S(2)}, u32[]{:S(2)}) collective-permute-start(bf16[256,512]{1,0:T(8,128)(2,1)S(1)} %get-tuple-element.70), channel_id=1, source_target_pairs={{0,1},{1,0},{2,3},{3,2},{4,5},{5,7},{6,22},{7,4},{8,9},{9,8},{10,1... | collective-permute-start | bytes 786440 | tf_op jit(solution)/shard_map/ppermute | solution.py:602
  29.7 5.4 %collective-permute-start.13 = (bf16[2,128,256]{2,1,0:T(8,128)(2,1)S(1)}, bf16[2,128,256]{2,1,0:T(8,128)(2,1)S(1)}, u32[]{:S(2)}, u32[]{:S(2)}) collective-permute-start(bf16[2,128,256]{2,1,0:T(8,128)(2,1)S(1)} %get-tuple-element.76), channel_id=1, source_target_pairs={{0,8},{8,0},{16,24},{24,16},{1,9},{9,1},{17,25},{25,17},{2,10},{10... | collective-permute-start | bytes 393224 | tf_op jit(solution)/shard_map/ppermute | solution.py:605
  31.2 5.0 %collective-permute-start.14 = (bf16[2,128,256]{2,1,0:T(8,128)(2,1)S(1)}, bf16[2,128,256]{2,1,0:T(8,128)(2,1)S(1)}, u32[]{:S(2)}, u32[]{:S(2)}) collective-permute-start(bf16[2,128,256]{2,1,0:T(8,128)(2,1)S(1)} %get-tuple-element.77), channel_id=1, source_target_pairs={{0,16},{8,24},{16,0},{24,8},{1,17},{9,25},{17,1},{25,9},{2,18},{10... | collective-permute-start | bytes 393224 | tf_op jit(solution)/shard_map/ppermute | solution.py:605
  31.7 5.9 %collective-permute-start.15 = (bf16[2,128,256]{2,1,0:T(8,128)(2,1)S(1)}, bf16[2,128,256]{2,1,0:T(8,128)(2,1)S(1)}, u32[]{:S(2)}, u32[]{:S(2)}) collective-permute-start(bf16[2,128,256]{2,1,0:T(8,128)(2,1)S(1)} %get-tuple-element.78), channel_id=1, source_target_pairs={{0,24},{8,16},{16,8},{24,0},{1,25},{9,17},{17,9},{25,1},{2,26},{10... | collective-permute-start | bytes 393224 | tf_op jit(solution)/shard_map/ppermute | solution.py:605
  37.6 1.6 %collective-permute-start.16 = (bf16[4,128,256]{2,1,0:T(8,128)(2,1)S(1)}, bf16[4,128,256]{2,1,0:T(8,128)(2,1)S(1)}, u32[]{:S(2)}, u32[]{:S(2)}) collective-permute-start(bf16[4,128,256]{2,1,0:T(8,128)(2,1)S(1)} %shard_map.80), channel_id=1, source_target_pairs={{0,1},{1,0},{2,3},{3,2},{4,5},{5,4},{6,7},{7,6},{8,9},{9,8},{10,11... | collective-permute-start | bytes 786440 | tf_op jit(solution)/shard_map/ppermute | solution.py:580
  39.6 4.4 %collective-permute-start.17 = (bf16[128,256]{1,0:T(8,128)(2,1)S(1)}, bf16[128,256]{1,0:T(8,128)(2,1)S(1)}, u32[]{:S(2)}, u32[]{:S(2)}) collective-permute-start(bf16[128,256]{1,0:T(8,128)(2,1)S(1)} %get-tuple-element.80), channel_id=1, source_target_pairs={{0,8},{8,0},{16,24},{24,16},{1,9},{9,1},{17,25},{25,17},{2,10},{10... | collective-permute-start | bytes 196616 | tf_op jit(solution)/shard_map/ppermute | solution.py:605
  40.2 4.3 %collective-permute-start.18 = (bf16[128,256]{1,0:T(8,128)(2,1)S(1)}, bf16[128,256]{1,0:T(8,128)(2,1)S(1)}, u32[]{:S(2)}, u32[]{:S(2)}) collective-permute-start(bf16[128,256]{1,0:T(8,128)(2,1)S(1)} %get-tuple-element.81), channel_id=1, source_target_pairs={{0,16},{8,24},{16,0},{24,8},{1,17},{9,25},{17,1},{25,9},{2,18},{10... | collective-permute-start | bytes 196616 | tf_op jit(solution)/shard_map/ppermute | solution.py:605
  41.8 5.2 %collective-permute-start.19 = (bf16[128,256]{1,0:T(8,128)(2,1)S(1)}, bf16[128,256]{1,0:T(8,128)(2,1)S(1)}, u32[]{:S(2)}, u32[]{:S(2)}) collective-permute-start(bf16[128,256]{1,0:T(8,128)(2,1)S(1)} %get-tuple-element.82), channel_id=1, source_target_pairs={{0,24},{8,16},{16,8},{24,0},{1,25},{9,17},{17,9},{25,1},{2,26},{10... | collective-permute-start | bytes 196616 | tf_op jit(solution)/shard_map/ppermute | solution.py:605

commit v8 on v7

--- a/solution.py
+++ b/solution.py
@@ -300,7 +300,7 @@
 def advance_kernel(z, state, step, source, *refs):
     kept, (out, chosen) = (refs[0] if len(refs) == 3 else None), refs[-2:]
 
-    @pl.when((lax.axis_index("domain") >> 1) == z)
+    @pl.when(lax.axis_index("domain") == 2 * z + 1)
     def _():
         out[...] = advance(state[...], step[...], source[...])
 
@@ -582,10 +582,8 @@
     def hop(x, z, lower=False):
         source, target = 2 * z - 1, 2 * z + (not lower)
         before, aside = source - 1, target ^ 1
-        if energies % 4 or lower or z == 1 < chips - 1:
+        if energies % 4 or lower or z < chips - 1:
             ring = [source, target, aside, before]
-        elif z < chips - 1:
-            ring = [source, target]
         else:
             ring = [source, target, before]
         onward = dict(zip(ring, ring[1:] + ring[:1]))
@@ -594,7 +592,7 @@
             for d in range(domains):
                 if d in onward:
                     place = (e, onward[d])
-                elif d in (before, aside):
+                elif d == aside:
                     place = (e ^ 2, d)
                 else:
                     place = (e, d ^ 1)

time: 47.8 us -> 47.5 us (level)
  starting transfers between devices: 14.1 us -> 19.2 us
  waiting for transfers between devices: 23.8 us -> 19.4 us
  Pallas kernels: 9.65 us -> 8.64 us
    ppermute x6, waiting for transfers between devices: 12.9 us -> 8.58 us  [hop(): return lax.ppermute(x, ('energy', 'domain'), route)]
    ppermute x6, starting transfers between devices: 3.5 us -> 7.2 us  [hop(): return lax.ppermute(x, ('energy', 'domain'), route)]
    ppermute x8, starting transfers between devices: 3.54 us -> 4.95 us  [swap(): return lax.ppermute(x, 'domain', [(d, d ^ 1) for d in range(domains)])]
    pallas_call x19, Pallas kernels: 9.65 us -> 8.64 us  [kernel_call(): pl.pallas_call(body, out_shape=outs, in_specs=in_specs or [VMEM] * len(op...]
  transfers between devices with their start and end apart: 20 -> 20, of which waited for: 17 -> 17; matrix products, arithmetic and copies ran while one was open for 0% -> 0% of each run, Pallas kernels for 6% -> 4%
where the time goes in v8:
time: 47.5 us; the launch traced here: 47.4 us
  waiting for transfers between devices  19.4 us (41%)
  starting transfers between devices  19.2 us (40%)
  Pallas kernels  8.64 us (18%)
    pallas_call x19, Pallas kernels, kernel_call(): pl.pallas_call(body, out_shape=outs, in_specs=in_specs or [VMEM] * len(op...  8.64 us
    ppermute x6, waiting for transfers between devices, hop(): return lax.ppermute(x, ('energy', 'domain'), route)  8.58 us
    ppermute x6, waiting for transfers between devices, across(): return lax.ppermute(x, 'energy', [(e, e ^ k) for e in range(energies)])  7.41 us
    ppermute x6, starting transfers between devices, hop(): return lax.ppermute(x, ('energy', 'domain'), route)  7.2 us
    ppermute x6, starting transfers between devices, across(): return lax.ppermute(x, 'energy', [(e, e ^ k) for e in range(energies)])  7.04 us
    ppermute x8, starting transfers between devices, swap(): return lax.ppermute(x, 'domain', [(d, d ^ 1) for d in range(domains)])  4.95 us
    ppermute x8, waiting for transfers between devices, swap(): return lax.ppermute(x, 'domain', [(d, d ^ 1) for d in range(domains)])  3.46 us
  transfers between devices with their start and end apart: 20, of which 17 were waited for; matrix products, arithmetic and copies ran while one was open for 0% of the time, Pallas kernels for 4%

profile of v8, /device:TPU:20, one launch (start us, length us, event | category | flops | bytes accessed | tf_op | source)
XLA Modules:
  0.0 47.4 jit_solution(8622482382267037981)
XLA Ops:
  0.0 1.7 %shard_map.64 = (bf16[2,256,512]{2,1,0:T(8,128)(2,1)S(1)}, bf16[2,256,512]{2,1,0:T(8,128)(2,1)S(1)}, bf16[2,256,512]{2,1,0:T(8,128)(2,1)S(1)}, bf16[2,256,512]{2...) custom-call(bf16[1,2,256,512]{3,2,1,0:T(8,128)(2,1)} %retarded.1, ...), custom_call_target="tpu_custom_call" | custom-call | flops 939524096 | bytes 5242880 | tf_op jit(solution)/shard_map/pallas_call | solution.py:56
  1.7 1.4 %shard_map.65 = (bf16[1,256,512]{2,1,0:T(8,128)(2,1)S(1)}, bf16[2,256,512]{2,1,0:T(8,128)(2,1)S(1)}, bf16[256,512]{1,0:T(8,128)(2,1)S(1)}, bf16[256,512]{1,0:T(8...) custom-call(bf16[2,256,512]{2,1,0:T(8,128)(2,1)S(1)} %get-tuple-elem, ...), custom_call_target="tpu_custom_call", output_to_operand_aliasing={{0}: (4, {}), {1}: (5, {})} | custom-call | flops 1073741824 | bytes 5505024 | tf_op jit(solution)/shard_map/pallas_call | solution.py:56
  3.2 1.5 %shard_map.66 = (bf16[256,512]{1,0:T(8,128)(2,1)S(1)}, bf16[2,256,512]{2,1,0:T(8,128)(2,1)S(1)}, bf16[256,512]{1,0:T(8,128)(2,1)S(1)}, bf16[256,512]{1,0:T(8,128)(2,1)S(1)}) custom-call(bf16[2,256,512]{2,1,0:T(8,128)(2,1)S(1)} %get-tuple-element.44.retarded, ...), custom_call_target="tpu_custom_call", output_to_operand_aliasing={{0}: (4, {}), {1}: (5, {})} | custom-call | flops 1073741824 | bytes 4456448 | tf_op jit(solution)/shard_map/pallas_call | solution.py:56
  4.7 0.1 collective-permute-start.4
  4.8 0.5 %collective-permute-start.1 = (bf16[256,512]{1,0:T(8,128)(2,1)S(1)}, bf16[256,512]{1,0:T(8,128)(2,1)S(1)}, u32[]{:S(2)}, u32[]{:S(2)}) collective-permute-start(bf16[256,512]{1,0:T(8,128)(2,1)S(1)} %get-tuple-element.50.given_total.upper), channel_id=1, source_target_pairs={{0,1},{1,0},{2,3},{3,2},{4,5},{5,4},{6,7},{7,6},{8,9},{9,8},{10,11... | collective-permute-start | bytes 786440 | tf_op jit(solution)/shard_map/ppermute | solution.py:580
  5.3 0.1 collective-permute-start.3
  5.4 0.4 collective-permute-start
  5.8 0.1 collective-permute-start.2
  5.9 0.4 collective-permute-done.4.lower_whole
  6.3 0.4 collective-permute-done.1.lower
  6.7 0.4 collective-permute-done.3.lower
  7.1 0.4 collective-permute-done.lower.lower_less
  7.4 0.4 collective-permute-done.2.lower.lower_great
  7.8 1.0 %shard_map.72 = (bf16[1280,512]{1,0:T(8,128)(2,1)S(1)}, bf16[512,256]{1,0:T(8,128)(2,1)S(1)}, s32[4,8,128]{2,1,0:T(8,128)S(1)}) custom-call(s32[2,2]{1,0:T(2,128)} %tiles.1, s32[4]{0:T(128)} %offsets.1, bf16[256,512]{1,0:T(8,128)(2,1)S(1)} %get-tuple-element.56.first_step, bf16[1,256,512]{2,1,0:T(8,128)(2,1)S(1)} %get-tuple-element.51.later_steps, ...), custom_call_target="tpu_custom_call" | custom-call | flops 671088640 | bytes 5521440 | tf_op jit(solution)/shard_map/pallas_call | solution.py:56
  8.8 1.6 %collective-permute-start.12 = (bf16[1280,512]{1,0:T(8,128)(2,1)S(1)}, bf16[1280,512]{1,0:T(8,128)(2,1)S(1)}, u32[]{:S(2)}, u32[]{:S(2)}) collective-permute-start(bf16[1280,512]{1,0:T(8,128)(2,1)S(1)} %get-tuple-element.71.refs_0_), channel_id=1, source_target_pairs={{0,1},{1,0},{2,3},{3,2},{4,5},{5,4},{6,7},{7,6},{8,9},{9,8},{10,11... | collective-permute-start | bytes 3932168 | tf_op jit(solution)/shard_map/ppermute | solution.py:580
  10.4 0.1 collective-permute-start.5
  10.4 0.5 collective-permute-start.8
  10.9 2.5 %collective-permute-done.5.state = bf16[256,512]{1,0:T(8,128)(2,1)S(1)} collective-permute-done((bf16[256,512]{1,0:T(8,128)(2,1)S(1)}, bf16[256,512]{1,0:T(8,128)(2,1)S(1)}, u32[]{:S(2)}, u32[]{:S(2)}) %collective-permute-start.5) | collective-permute-done | bytes 262176 | tf_op jit(solution)/shard_map/ppermute | solution.py:600
  13.5 1.4 %collective-permute-start.6 = (bf16[256,512]{1,0:T(8,128)(2,1)S(1)}, bf16[256,512]{1,0:T(8,128)(2,1)S(1)}, u32[]{:S(2)}, u32[]{:S(2)}) collective-permute-start(bf16[256,512]{1,0:T(8,128)(2,1)S(1)} %get-tuple-element.63), channel_id=1, source_target_pairs={{0,1},{1,0},{2,3},{3,5},{4,2},{5,4},{6,7},{7,6},{8,9},{9,8},{10,11... | collective-permute-start | bytes 786440 | tf_op jit(solution)/shard_map/ppermute | solution.py:600
  14.8 0.0 collective-permute-done.8.state
  14.9 2.8 %collective-permute-start.9 = (bf16[256,512]{1,0:T(8,128)(2,1)S(1)}, bf16[256,512]{1,0:T(8,128)(2,1)S(1)}, u32[]{:S(2)}, u32[]{:S(2)}) collective-permute-start(bf16[256,512]{1,0:T(8,128)(2,1)S(1)} %get-tuple-element.66), channel_id=1, source_target_pairs={{0,1},{1,0},{2,3},{3,5},{4,2},{5,4},{6,7},{7,6},{8,9},{9,8},{10,11... | collective-permute-start | bytes 786440 | tf_op jit(solution)/shard_map/ppermute | solution.py:600
  17.6 1.1 %collective-permute-done.6.state = bf16[256,512]{1,0:T(8,128)(2,1)S(1)} collective-permute-done((bf16[256,512]{1,0:T(8,128)(2,1)S(1)}, bf16[256,512]{1,0:T(8,128)(2,1)S(1)}, u32[]{:S(2)}, u32[]{:S(2)}) %collective-permute-start.6) | collective-permute-done | bytes 262176 | tf_op jit(solution)/shard_map/ppermute | solution.py:600
  18.7 2.1 %collective-permute-start.7 = (bf16[256,512]{1,0:T(8,128)(2,1)S(1)}, bf16[256,512]{1,0:T(8,128)(2,1)S(1)}, u32[]{:S(2)}, u32[]{:S(2)}) collective-permute-start(bf16[256,512]{1,0:T(8,128)(2,1)S(1)} %get-tuple-element.65), channel_id=1, source_target_pairs={{0,1},{1,0},{2,3},{3,2},{4,5},{5,4},{6,7},{7,6},{8,9},{9,8},{10,11... | collective-permute-start | bytes 786440 | tf_op jit(solution)/shard_map/ppermute | solution.py:580
  20.9 0.1 collective-permute-start.10
  21.0 0.6 %collective-permute-done.9.state = bf16[256,512]{1,0:T(8,128)(2,1)S(1)} collective-permute-done((bf16[256,512]{1,0:T(8,128)(2,1)S(1)}, bf16[256,512]{1,0:T(8,128)(2,1)S(1)}, u32[]{:S(2)}, u32[]{:S(2)}) %collective-permute-start.9) | collective-permute-done | bytes 262176 | tf_op jit(solution)/shard_map/ppermute | solution.py:600
  21.6 2.4 %collective-permute-start.11 = (bf16[256,512]{1,0:T(8,128)(2,1)S(1)}, bf16[256,512]{1,0:T(8,128)(2,1)S(1)}, u32[]{:S(2)}, u32[]{:S(2)}) collective-permute-start(bf16[256,512]{1,0:T(8,128)(2,1)S(1)} %get-tuple-element.70), channel_id=1, source_target_pairs={{0,1},{1,0},{2,3},{3,2},{4,5},{5,7},{6,22},{7,4},{8,9},{9,8},{10,1... | collective-permute-start | bytes 786440 | tf_op jit(solution)/shard_map/ppermute | solution.py:600
  24.0 0.0 collective-permute-done.7.near.lesser
  24.0 0.0 collective-permute-done.12.refs_1_
  24.0 1.1 %shard_map.78 = (bf16[2,128,256]{2,1,0:T(8,128)(2,1)S(1)}, bf16[2,128,256]{2,1,0:T(8,128)(2,1)S(1)}, bf16[2,128,256]{2,1,0:T(8,128)(2,1)S(1)}) custom-call(bf16[256,512]{1,0:T(8,128)(2,1)S(1)} %collective-permute-done.7.near.lesser, bf16[256,512]{1,0:T(8,128)(2,1)S(1)} %get-tuple-element.68.kept.greater, bf16[1280,512]{1,0:T(8,128)(2,1)S(1)} %get-tuple-element.71.refs_0_, ...), custom_call_target="tpu_custom_call" | custom-call | flops 671088640 | bytes 3801088 | tf_op jit(solution)/shard_map/pallas_call | solution.py:56
  25.1 1.6 %collective-permute-done.10.lesser = bf16[256,512]{1,0:T(8,128)(2,1)S(1)} collective-permute-done((bf16[256,512]{1,0:T(8,128)(2,1)S(1)}, bf16[256,512]{1,0:T(8,128)(2,1)S(1)}, u32[]{:S(2)}, u32[]{:S(2)}) %collective-permute-start.10) | collective-permute-done | bytes 262176 | tf_op jit(solution)/shard_map/ppermute | solution.py:600
  26.7 2.8 %collective-permute-done.11.greater = bf16[256,512]{1,0:T(8,128)(2,1)S(1)} collective-permute-done((bf16[256,512]{1,0:T(8,128)(2,1)S(1)}, bf16[256,512]{1,0:T(8,128)(2,1)S(1)}, u32[]{:S(2)}, u32[]{:S(2)}) %collective-permute-start.11) | collective-permute-done | bytes 262176 | tf_op jit(solution)/shard_map/ppermute | solution.py:600
  29.5 1.5 %collective-permute-start.13 = (bf16[2,128,256]{2,1,0:T(8,128)(2,1)S(1)}, bf16[2,128,256]{2,1,0:T(8,128)(2,1)S(1)}, u32[]{:S(2)}, u32[]{:S(2)}) collective-permute-start(bf16[2,128,256]{2,1,0:T(8,128)(2,1)S(1)} %get-tuple-element.76), channel_id=1, source_target_pairs={{0,8},{8,0},{16,24},{24,16},{1,9},{9,1},{17,25},{25,17},{2,10},{10... | collective-permute-start | bytes 393224 | tf_op jit(solution)/shard_map/ppermute | solution.py:603
  30.9 0.5 %collective-permute-start.14 = (bf16[2,128,256]{2,1,0:T(8,128)(2,1)S(1)}, bf16[2,128,256]{2,1,0:T(8,128)(2,1)S(1)}, u32[]{:S(2)}, u32[]{:S(2)}) collective-permute-start(bf16[2,128,256]{2,1,0:T(8,128)(2,1)S(1)} %get-tuple-element.77), channel_id=1, source_target_pairs={{0,16},{8,24},{16,0},{24,8},{1,17},{9,25},{17,1},{25,9},{2,18},{10... | collective-permute-start | bytes 393224 | tf_op jit(solution)/shard_map/ppermute | solution.py:603
  31.4 1.5 %collective-permute-start.15 = (bf16[2,128,256]{2,1,0:T(8,128)(2,1)S(1)}, bf16[2,128,256]{2,1,0:T(8,128)(2,1)S(1)}, u32[]{:S(2)}, u32[]{:S(2)}) collective-permute-start(bf16[2,128,256]{2,1,0:T(8,128)(2,1)S(1)} %get-tuple-element.78), channel_id=1, source_target_pairs={{0,24},{8,16},{16,8},{24,0},{1,25},{9,17},{17,9},{25,1},{2,26},{10... | collective-permute-start | bytes 393224 | tf_op jit(solution)/shard_map/ppermute | solution.py:603
  33.0 0.7 %shard_map.77.refs_0_ = bf16[2,128,256]{2,1,0:T(8,128)(2,1)S(1)} custom-call(bf16[256,512]{1,0:T(8,128)(2,1)S(1)} %collective-permute-done.7.near.lesser, bf16[256,512]{1,0:T(8,128)(2,1)S(1)} %get-tuple-element.68.kept.greater, bf16[256,512]{1,0:T(8,128)(2,1)S(1)} %collective-permute-done.10.lesser, bf16[256,512]{1,0:T(8,128)(2,1)S(1)} %collective-permute-done.11.greater, ...), custom_call_target="tpu_custom_call" | custom-call | flops 268435456 | bytes 4063232 | tf_op jit(solution)/shard_map/pallas_call | solution.py:56
  33.7 1.4 %collective-permute-done.13.refs_1_ = bf16[2,128,256]{2,1,0:T(8,128)(2,1)S(1)} collective-permute-done((bf16[2,128,256]{2,1,0:T(8,128)(2,1)S(1)}, bf16[2,128,256]{2,1,0:T(8,128)(2,1)S(1)}, u32[]{:S(2)}, u32[]{:S(2)}) %collective-permute-start.13) | collective-permute-done | bytes 131104 | tf_op jit(solution)/shard_map/ppermute | solution.py:603
  35.1 0.8 %collective-permute-done.14.refs_2_ = bf16[2,128,256]{2,1,0:T(8,128)(2,1)S(1)} collective-permute-done((bf16[2,128,256]{2,1,0:T(8,128)(2,1)S(1)}, bf16[2,128,256]{2,1,0:T(8,128)(2,1)S(1)}, u32[]{:S(2)}, u32[]{:S(2)}) %collective-permute-start.14) | collective-permute-done | bytes 131104 | tf_op jit(solution)/shard_map/ppermute | solution.py:603
  35.9 1.4 %collective-permute-done.15.refs_3_ = bf16[2,128,256]{2,1,0:T(8,128)(2,1)S(1)} collective-permute-done((bf16[2,128,256]{2,1,0:T(8,128)(2,1)S(1)}, bf16[2,128,256]{2,1,0:T(8,128)(2,1)S(1)}, u32[]{:S(2)}, u32[]{:S(2)}) %collective-permute-start.15) | collective-permute-done | bytes 131104 | tf_op jit(solution)/shard_map/ppermute | solution.py:603
  37.3 0.1 collective-permute-start.16
  37.4 1.5 %collective-permute-done.16.swapped = bf16[4,128,256]{2,1,0:T(8,128)(2,1)S(1)} collective-permute-done((bf16[4,128,256]{2,1,0:T(8,128)(2,1)S(1)}, bf16[4,128,256]{2,1,0:T(8,128)(2,1)S(1)}, u32[]{:S(2)}, u32[]{:S(2)}) %collective-permute-start.16) | collective-permute-done | bytes 262176 | tf_op jit(solution)/shard_map/ppermute | solution.py:580
  38.9 0.4 shard_map.81
  39.3 0.6 %collective-permute-start.17 = (bf16[128,256]{1,0:T(8,128)(2,1)S(1)}, bf16[128,256]{1,0:T(8,128)(2,1)S(1)}, u32[]{:S(2)}, u32[]{:S(2)}) collective-permute-start(bf16[128,256]{1,0:T(8,128)(2,1)S(1)} %get-tuple-element.80), channel_id=1, source_target_pairs={{0,8},{8,0},{16,24},{24,16},{1,9},{9,1},{17,25},{25,17},{2,10},{10... | collective-permute-start | bytes 196616 | tf_op jit(solution)/shard_map/ppermute | solution.py:603
  40.0 1.5 %collective-permute-start.18 = (bf16[128,256]{1,0:T(8,128)(2,1)S(1)}, bf16[128,256]{1,0:T(8,128)(2,1)S(1)}, u32[]{:S(2)}, u32[]{:S(2)}) collective-permute-start(bf16[128,256]{1,0:T(8,128)(2,1)S(1)} %get-tuple-element.81), channel_id=1, source_target_pairs={{0,16},{8,24},{16,0},{24,8},{1,17},{9,25},{17,1},{25,9},{2,18},{10... | collective-permute-start | bytes 196616 | tf_op jit(solution)/shard_map/ppermute | solution.py:603
  41.5 1.4 %collective-permute-start.19 = (bf16[128,256]{1,0:T(8,128)(2,1)S(1)}, bf16[128,256]{1,0:T(8,128)(2,1)S(1)}, u32[]{:S(2)}, u32[]{:S(2)}) collective-permute-start(bf16[128,256]{1,0:T(8,128)(2,1)S(1)} %get-tuple-element.82), channel_id=1, source_target_pairs={{0,24},{8,16},{16,8},{24,0},{1,25},{9,17},{17,9},{25,1},{2,26},{10... | collective-permute-start | bytes 196616 | tf_op jit(solution)/shard_map/ppermute | solution.py:603
  42.9 0.9 %collective-permute-done.17.refs_1_ = bf16[128,256]{1,0:T(8,128)(2,1)S(1)} collective-permute-done((bf16[128,256]{1,0:T(8,128)(2,1)S(1)}, bf16[128,256]{1,0:T(8,128)(2,1)S(1)}, u32[]{:S(2)}, u32[]{:S(2)}) %collective-permute-start.17) | collective-permute-done | bytes 65568 | tf_op jit(solution)/shard_map/ppermute | solution.py:603
  43.8 0.5 %collective-permute-done.18.refs_2_ = bf16[128,256]{1,0:T(8,128)(2,1)S(1)} collective-permute-done((bf16[128,256]{1,0:T(8,128)(2,1)S(1)}, bf16[128,256]{1,0:T(8,128)(2,1)S(1)}, u32[]{:S(2)}, u32[]{:S(2)}) %collective-permute-start.18) | collective-permute-done | bytes 65568 | tf_op jit(solution)/shard_map/ppermute | solution.py:603
  44.2 2.4 %collective-permute-done.19.refs_3_ = bf16[128,256]{1,0:T(8,128)(2,1)S(1)} collective-permute-done((bf16[128,256]{1,0:T(8,128)(2,1)S(1)}, bf16[128,256]{1,0:T(8,128)(2,1)S(1)}, u32[]{:S(2)}, u32[]{:S(2)}) %collective-permute-start.19) | collective-permute-done | bytes 65568 | tf_op jit(solution)/shard_map/ppermute | solution.py:603
  46.7 0.7 %shard_map.82 = bf16[4,128,256]{2,1,0:T(8,128)(2,1)} custom-call(bf16[128,256]{1,0:T(8,128)(2,1)S(1)} %get-tuple-element.79.refs_0_, bf16[128,256]{1,0:T(8,128)(2,1)S(1)} %collective-permute-done.17.refs_1_, bf16[128,256]{1,0:T(8,128)(2,1)S(1)} %collective-permute-done.18.refs_2_, bf16[128,256]{1,0:T(8,128)(2,1)S(1)} %collective-permute-done.19.refs_3_), custom_call_target="tpu_custom_call" | custom-call | bytes 524288 | tf_op jit(solution)/shard_map/pallas_call | solution.py:56
  (11 shorter events, 0.1 us)
Async XLA Ops:
  4.7 1.6 %collective-permute-start.4 = (bf16[256,512]{1,0:T(8,128)(2,1)S(1)}, bf16[256,512]{1,0:T(8,128)(2,1)S(1)}, u32[]{:S(2)}, u32[]{:S(2)}) collective-permute-start(bf16[256,512]{1,0:T(8,128)(2,1)S(1)} %get-tuple-element.59.whole), channel_id=1, source_target_pairs={{0,1},{1,0},{2,3},{3,2},{4,5},{5,4},{6,7},{7,6},{8,9},{9,8},{10,11... | collective-permute-start | bytes 786440 | tf_op jit(solution)/shard_map/ppermute | solution.py:580
  4.8 1.9 %collective-permute-start.1 = (bf16[256,512]{1,0:T(8,128)(2,1)S(1)}, bf16[256,512]{1,0:T(8,128)(2,1)S(1)}, u32[]{:S(2)}, u32[]{:S(2)}) collective-permute-start(bf16[256,512]{1,0:T(8,128)(2,1)S(1)} %get-tuple-element.50.given_total.upper), channel_id=1, source_target_pairs={{0,1},{1,0},{2,3},{3,2},{4,5},{5,4},{6,7},{7,6},{8,9},{9,8},{10,11... | collective-permute-start | bytes 786440 | tf_op jit(solution)/shard_map/ppermute | solution.py:580
  5.3 1.8 %collective-permute-start.3 = (bf16[256,512]{1,0:T(8,128)(2,1)S(1)}, bf16[256,512]{1,0:T(8,128)(2,1)S(1)}, u32[]{:S(2)}, u32[]{:S(2)}) collective-permute-start(bf16[256,512]{1,0:T(8,128)(2,1)S(1)} %get-tuple-element.54.given_total.upper), channel_id=1, source_target_pairs={{0,1},{1,0},{2,3},{3,2},{4,5},{5,4},{6,7},{7,6},{8,9},{9,8},{10,11... | collective-permute-start | bytes 786440 | tf_op jit(solution)/shard_map/ppermute | solution.py:580
  5.4 2.1 %collective-permute-start = (bf16[256,512]{1,0:T(8,128)(2,1)S(1)}, bf16[256,512]{1,0:T(8,128)(2,1)S(1)}, u32[]{:S(2)}, u32[]{:S(2)}) collective-permute-start(bf16[256,512]{1,0:T(8,128)(2,1)S(1)} %get-tuple-element.58.upper.less_total), channel_id=1, source_target_pairs={{0,1},{1,0},{2,3},{3,2},{4,5},{5,4},{6,7},{7,6},{8,9},{9,8},{10,11... | collective-permute-start | bytes 786440 | tf_op jit(solution)/shard_map/ppermute | solution.py:580
  5.8 2.0 %collective-permute-start.2 = (bf16[256,512]{1,0:T(8,128)(2,1)S(1)}, bf16[256,512]{1,0:T(8,128)(2,1)S(1)}, u32[]{:S(2)}, u32[]{:S(2)}) collective-permute-start(bf16[256,512]{1,0:T(8,128)(2,1)S(1)} %get-tuple-element.61.upper.great_total), channel_id=1, source_target_pairs={{0,1},{1,0},{2,3},{3,2},{4,5},{5,4},{6,7},{7,6},{8,9},{9,8},{10,11... | collective-permute-start | bytes 786440 | tf_op jit(solution)/shard_map/ppermute | solution.py:580
  8.8 15.2 %collective-permute-start.12 = (bf16[1280,512]{1,0:T(8,128)(2,1)S(1)}, bf16[1280,512]{1,0:T(8,128)(2,1)S(1)}, u32[]{:S(2)}, u32[]{:S(2)}) collective-permute-start(bf16[1280,512]{1,0:T(8,128)(2,1)S(1)} %get-tuple-element.71.refs_0_), channel_id=1, source_target_pairs={{0,1},{1,0},{2,3},{3,2},{4,5},{5,4},{6,7},{7,6},{8,9},{9,8},{10,11... | collective-permute-start | bytes 3932168 | tf_op jit(solution)/shard_map/ppermute | solution.py:580
  10.4 3.0 %collective-permute-start.5 = (bf16[256,512]{1,0:T(8,128)(2,1)S(1)}, bf16[256,512]{1,0:T(8,128)(2,1)S(1)}, u32[]{:S(2)}, u32[]{:S(2)}) collective-permute-start(bf16[256,512]{1,0:T(8,128)(2,1)S(1)} %shard_map.67.joined), channel_id=1, source_target_pairs={{0,1},{1,3},{2,0},{3,2},{4,5},{5,4},{6,7},{7,6},{8,9},{9,11},{10,8... | collective-permute-start | bytes 786440 | tf_op jit(solution)/shard_map/ppermute | solution.py:600
  10.4 4.4 %collective-permute-start.8 = (bf16[256,512]{1,0:T(8,128)(2,1)S(1)}, bf16[256,512]{1,0:T(8,128)(2,1)S(1)}, u32[]{:S(2)}, u32[]{:S(2)}) collective-permute-start(bf16[256,512]{1,0:T(8,128)(2,1)S(1)} %shard_map.69.joined), channel_id=1, source_target_pairs={{0,1},{1,3},{2,0},{3,2},{4,5},{5,4},{6,7},{7,6},{8,9},{9,11},{10,8... | collective-permute-start | bytes 786440 | tf_op jit(solution)/shard_map/ppermute | solution.py:600
  13.5 5.3 %collective-permute-start.6 = (bf16[256,512]{1,0:T(8,128)(2,1)S(1)}, bf16[256,512]{1,0:T(8,128)(2,1)S(1)}, u32[]{:S(2)}, u32[]{:S(2)}) collective-permute-start(bf16[256,512]{1,0:T(8,128)(2,1)S(1)} %get-tuple-element.63), channel_id=1, source_target_pairs={{0,1},{1,0},{2,3},{3,5},{4,2},{5,4},{6,7},{7,6},{8,9},{9,8},{10,11... | collective-permute-start | bytes 786440 | tf_op jit(solution)/shard_map/ppermute | solution.py:600
  14.9 6.7 %collective-permute-start.9 = (bf16[256,512]{1,0:T(8,128)(2,1)S(1)}, bf16[256,512]{1,0:T(8,128)(2,1)S(1)}, u32[]{:S(2)}, u32[]{:S(2)}) collective-permute-start(bf16[256,512]{1,0:T(8,128)(2,1)S(1)} %get-tuple-element.66), channel_id=1, source_target_pairs={{0,1},{1,0},{2,3},{3,5},{4,2},{5,4},{6,7},{7,6},{8,9},{9,8},{10,11... | collective-permute-start | bytes 786440 | tf_op jit(solution)/shard_map/ppermute | solution.py:600
  18.7 5.3 %collective-permute-start.7 = (bf16[256,512]{1,0:T(8,128)(2,1)S(1)}, bf16[256,512]{1,0:T(8,128)(2,1)S(1)}, u32[]{:S(2)}, u32[]{:S(2)}) collective-permute-start(bf16[256,512]{1,0:T(8,128)(2,1)S(1)} %get-tuple-element.65), channel_id=1, source_target_pairs={{0,1},{1,0},{2,3},{3,2},{4,5},{5,4},{6,7},{7,6},{8,9},{9,8},{10,11... | collective-permute-start | bytes 786440 | tf_op jit(solution)/shard_map/ppermute | solution.py:580
  20.9 5.8 %collective-permute-start.10 = (bf16[256,512]{1,0:T(8,128)(2,1)S(1)}, bf16[256,512]{1,0:T(8,128)(2,1)S(1)}, u32[]{:S(2)}, u32[]{:S(2)}) collective-permute-start(bf16[256,512]{1,0:T(8,128)(2,1)S(1)} %get-tuple-element.69), channel_id=1, source_target_pairs={{0,1},{1,0},{2,3},{3,2},{4,5},{5,6},{6,7},{7,4},{8,9},{9,8},{10,11... | collective-permute-start | bytes 786440 | tf_op jit(solution)/shard_map/ppermute | solution.py:600
  21.6 7.9 %collective-permute-start.11 = (bf16[256,512]{1,0:T(8,128)(2,1)S(1)}, bf16[256,512]{1,0:T(8,128)(2,1)S(1)}, u32[]{:S(2)}, u32[]{:S(2)}) collective-permute-start(bf16[256,512]{1,0:T(8,128)(2,1)S(1)} %get-tuple-element.70), channel_id=1, source_target_pairs={{0,1},{1,0},{2,3},{3,2},{4,5},{5,7},{6,22},{7,4},{8,9},{9,8},{10,1... | collective-permute-start | bytes 786440 | tf_op jit(solution)/shard_map/ppermute | solution.py:600
  29.5 5.6 %collective-permute-start.13 = (bf16[2,128,256]{2,1,0:T(8,128)(2,1)S(1)}, bf16[2,128,256]{2,1,0:T(8,128)(2,1)S(1)}, u32[]{:S(2)}, u32[]{:S(2)}) collective-permute-start(bf16[2,128,256]{2,1,0:T(8,128)(2,1)S(1)} %get-tuple-element.76), channel_id=1, source_target_pairs={{0,8},{8,0},{16,24},{24,16},{1,9},{9,1},{17,25},{25,17},{2,10},{10... | collective-permute-start | bytes 393224 | tf_op jit(solution)/shard_map/ppermute | solution.py:603
  30.9 5.0 %collective-permute-start.14 = (bf16[2,128,256]{2,1,0:T(8,128)(2,1)S(1)}, bf16[2,128,256]{2,1,0:T(8,128)(2,1)S(1)}, u32[]{:S(2)}, u32[]{:S(2)}) collective-permute-start(bf16[2,128,256]{2,1,0:T(8,128)(2,1)S(1)} %get-tuple-element.77), channel_id=1, source_target_pairs={{0,16},{8,24},{16,0},{24,8},{1,17},{9,25},{17,1},{25,9},{2,18},{10... | collective-permute-start | bytes 393224 | tf_op jit(solution)/shard_map/ppermute | solution.py:603
  31.4 5.9 %collective-permute-start.15 = (bf16[2,128,256]{2,1,0:T(8,128)(2,1)S(1)}, bf16[2,128,256]{2,1,0:T(8,128)(2,1)S(1)}, u32[]{:S(2)}, u32[]{:S(2)}) collective-permute-start(bf16[2,128,256]{2,1,0:T(8,128)(2,1)S(1)} %get-tuple-element.78), channel_id=1, source_target_pairs={{0,24},{8,16},{16,8},{24,0},{1,25},{9,17},{17,9},{25,1},{2,26},{10... | collective-permute-start | bytes 393224 | tf_op jit(solution)/shard_map/ppermute | solution.py:603
  37.3 1.6 %collective-permute-start.16 = (bf16[4,128,256]{2,1,0:T(8,128)(2,1)S(1)}, bf16[4,128,256]{2,1,0:T(8,128)(2,1)S(1)}, u32[]{:S(2)}, u32[]{:S(2)}) collective-permute-start(bf16[4,128,256]{2,1,0:T(8,128)(2,1)S(1)} %shard_map.80), channel_id=1, source_target_pairs={{0,1},{1,0},{2,3},{3,2},{4,5},{5,4},{6,7},{7,6},{8,9},{9,8},{10,11... | collective-permute-start | bytes 786440 | tf_op jit(solution)/shard_map/ppermute | solution.py:580
  39.3 4.4 %collective-permute-start.17 = (bf16[128,256]{1,0:T(8,128)(2,1)S(1)}, bf16[128,256]{1,0:T(8,128)(2,1)S(1)}, u32[]{:S(2)}, u32[]{:S(2)}) collective-permute-start(bf16[128,256]{1,0:T(8,128)(2,1)S(1)} %get-tuple-element.80), channel_id=1, source_target_pairs={{0,8},{8,0},{16,24},{24,16},{1,9},{9,1},{17,25},{25,17},{2,10},{10... | collective-permute-start | bytes 196616 | tf_op jit(solution)/shard_map/ppermute | solution.py:603
  40.0 4.3 %collective-permute-start.18 = (bf16[128,256]{1,0:T(8,128)(2,1)S(1)}, bf16[128,256]{1,0:T(8,128)(2,1)S(1)}, u32[]{:S(2)}, u32[]{:S(2)}) collective-permute-start(bf16[128,256]{1,0:T(8,128)(2,1)S(1)} %get-tuple-element.81), channel_id=1, source_target_pairs={{0,16},{8,24},{16,0},{24,8},{1,17},{9,25},{17,1},{25,9},{2,18},{10... | collective-permute-start | bytes 196616 | tf_op jit(solution)/shard_map/ppermute | solution.py:603
  41.5 5.2 %collective-permute-start.19 = (bf16[128,256]{1,0:T(8,128)(2,1)S(1)}, bf16[128,256]{1,0:T(8,128)(2,1)S(1)}, u32[]{:S(2)}, u32[]{:S(2)}) collective-permute-start(bf16[128,256]{1,0:T(8,128)(2,1)S(1)} %get-tuple-element.82), channel_id=1, source_target_pairs={{0,24},{8,16},{16,8},{24,0},{1,25},{9,17},{17,9},{25,1},{2,26},{10... | collective-permute-start | bytes 196616 | tf_op jit(solution)/shard_map/ppermute | solution.py:603
